TPU v7x, 32 devices: a whole 2x2x4 slice. The times are simulated.
32 devices in a mesh: dp: 16 (over z, x, core), tensor: 2 (over y).
Axes of the slice: x: 2, y: 2, z: 4, core: 2. Of those that a mesh axis runs over, the one named last changes fastest.
Arguments:
- tokens: bfloat16 [24576, 768], P(('dp', 'tensor')), may hold values from -6 to 6
- token_mask: int32 [1536, 16], P('dp'), may hold values from 0 to 1, as said below
- norm_gains: float32 [2, 768], replicated, may hold values from 0.5 to 1.5
- gain_moments: float32 [2, 768], replicated, may hold values from 76.8 to 614.4
- cotangent: bfloat16 [1536, 768], P(('dp', 'tensor')), may hold values from -6 to 6
- master: float32 [768, 96, 96], P(('dp', 'tensor'))
- stat_left: float32 [768, 96, 96], P(('dp', 'tensor')), as said below
- stat_right: float32 [768, 96, 96], P(('dp', 'tensor')), as said below
- root_left: float32 [768, 96, 96], P(('dp', 'tensor')), as said below
- root_right: float32 [768, 96, 96], P(('dp', 'tensor')), as said below
Outputs:
- pooled: float32 [1536, 768], P(('dp', 'tensor'))
- input_grad: float32 [24576, 768], P(('dp', 'tensor'))
- gain_grads: float32 [2, 768], replicated
- gain_moments_new: float32 [2, 768], replicated
- norm_gains_new: float32 [2, 768], replicated
- grad_blocks: float32 [768, 96, 96], P(('dp', 'tensor'))
- left_new: float32 [768, 96, 96], P(('dp', 'tensor'))
- right_new: float32 [768, 96, 96], P(('dp', 'tensor'))
- master_new: float32 [768, 96, 96], P(('dp', 'tensor'))
- master_copy: bfloat16 [768, 96, 96], P(('dp', 'tensor'))
Inputs may be any that keep to these rules, and one draw needn't show every extreme that they name: `token_mask`: each caption's mask is 1 on its first n slots and 0 after, n from 4 to 16; the first caption has n = 4 and the last n = 16. `stat_left`: each block is symmetric positive definite. `stat_right`: each block is symmetric positive definite. `root_left`: each block is symmetric positive definite. `root_right`: each block is symmetric positive definite.
All inputs are finite; a program needn't handle non-finite values.
Results may differ from a plain program's by a relative error of at most 0.0097.
Values may be sent and summed in bfloat16 or wider, within the bound.
No kernel may reach another device: no remote copies, remote signals or barrier semaphores. Data moves between devices by JAX's collectives and lax.ppermute only.
A program may use at most 192 MiB of HBM per device.

v0:
```python
import functools

import jax
import jax.numpy as jnp
from jax import lax
from jax.experimental import pallas as pl
from jax.experimental.pallas import tpu as pltpu
from jax.sharding import PartitionSpec as P

D = 768
HEADS = 12
HD = 64
FF = 3072
BLOCK = 96
SLOTS = 16
HALVES = 2
STRIP = 4 * BLOCK
STRIPS = 96
OWN = 6
GROUP = 128
CAPS = GROUP // SLOTS
PAIR = 2 * HD

EPSILON = 1e-06
DECAY_RATE = 0.5
STEP_RATE = 0.25
GAIN_RATE = 0.3
MASKED_SCORE = -1e30
PRECISE = lax.Precision.HIGHEST
F32 = jnp.float32
BF16 = jnp.bfloat16


def mm(left, right, left_dim=1, right_dim=0):
    return lax.dot_general(
        left, right, (((left_dim,), (right_dim,)), ((), ())), preferred_element_type=F32
    )


def side_by_side(ref, lead, count):
    parts = [ref[lead + (slice(None), i)].reshape(-1, STRIP) for i in range(count)]
    return jnp.concatenate(parts, axis=1)


def norm_parts(values):
    center = values - jnp.mean(values, axis=-1, keepdims=True)
    inverse = lax.rsqrt(jnp.mean(center * center, axis=-1, keepdims=True) + EPSILON)
    return center * inverse, inverse


def norm_back(xhat, inverse, gain, grad):
    scaled = grad * gain
    return inverse * (
        scaled
        - jnp.mean(scaled, axis=-1, keepdims=True)
        - xhat * jnp.mean(scaled * xhat, axis=-1, keepdims=True)
    )


def split_pair(values):
    first = lax.broadcasted_iota(jnp.int32, (GROUP, PAIR), 1) < HD
    zero = jnp.zeros_like(values)
    return jnp.concatenate(
        [jnp.where(first, values, zero), jnp.where(first, zero, values)], axis=0
    )


def join_pair(stacked):
    first = lax.broadcasted_iota(jnp.int32, (GROUP, PAIR), 1) < HD
    return jnp.where(first, stacked[:GROUP], stacked[GROUP:])


def caption_of():
    return lax.broadcasted_iota(jnp.int32, (SLOTS, 2 * GROUP), 1) % GROUP // SLOTS


def compact(full, caption):
    kept = full[0:SLOTS]
    for i in range(1, CAPS):
        kept = jnp.where(caption == i, full[i * SLOTS : (i + 1) * SLOTS], kept)
    return kept


def expand(kept, caption):
    zero = jnp.zeros_like(kept)
    return jnp.concatenate(
        [jnp.where(caption == i, kept, zero).astype(BF16) for i in range(CAPS)], axis=0
    )


def pair_probs(queries, key_rows, bias, caption):
    scores = compact(mm(key_rows, queries, 1, 1), caption) * HD ** (-0.5) + bias
    shifted = jnp.exp(scores - jnp.max(scores, axis=0, keepdims=True))
    return shifted / jnp.sum(shifted, axis=0, keepdims=True)


def key_bias(mask):
    bias = jnp.where(mask > 0, 0.0, MASKED_SCORE)
    return jnp.concatenate([bias, bias], axis=1)


def span_of(i, size=GROUP):
    return pl.ds(pl.multiple_of(i * size, size), size)


def attention_forward(
    tok, gains, mask, by_three, by_two, normed, qkv, attended, after, normed_two, w_qkv, w_out, sems
):
    rows = tok.shape[0]
    copies = []
    for half in range(HALVES):
        copies.append(
            pltpu.make_async_copy(by_three.at[half, 0:8], w_qkv.at[half], sems.at[half])
        )
    for half in range(HALVES):
        copies.append(
            pltpu.make_async_copy(by_two.at[half, 12:16], w_out.at[half], sems.at[2 + half])
        )
    for copy in copies:
        copy.start()

    @pl.loop(0, rows // GROUP)
    def _(i):
        span = span_of(i)
        xhat, _ = norm_parts(tok[span, :].astype(F32))
        normed[span, :] = (xhat * gains[0:1, :]).astype(BF16)

    for half in range(HALVES):
        copies[half].wait()
        mixed = mm(normed[...], side_by_side(w_qkv, (half,), 3)).astype(BF16)
        for part in range(3):
            qkv[3 * half + part] = mixed[:, part * STRIP : (part + 1) * STRIP]

    @pl.loop(0, rows // GROUP)
    def _(i):
        span = span_of(i)
        bias = key_bias(mask[i])
        caption = caption_of()
        for half in range(HALVES):
            for pair in range(STRIP // PAIR):
                lanes = slice(pair * PAIR, (pair + 1) * PAIR)
                wide = slice(half * STRIP + pair * PAIR, half * STRIP + (pair + 1) * PAIR)
                probs = pair_probs(
                    split_pair(qkv[3 * half, span, lanes]),
                    qkv[3 * half + 1, span, lanes],
                    bias,
                    caption,
                )
                mixed = mm(expand(probs, caption), qkv[3 * half + 2, span, lanes], 0, 0)
                attended[span, wide] = join_pair(mixed).astype(BF16)

    copies[2].wait()
    copies[3].wait()
    weight = jnp.concatenate([side_by_side(w_out, (half,), 2) for half in range(HALVES)], axis=0)
    after[...] = mm(attended[...], weight)

    @pl.loop(0, rows // GROUP)
    def _(i):
        span = span_of(i)
        summed = tok[span, :].astype(F32) + after[span, :]
        after[span, :] = summed
        xhat, _ = norm_parts(summed)
        normed_two[span, :] = (xhat * gains[1:2, :]).astype(BF16)


GELU_A = 0.7978845608028654
GELU_B = 0.044715


def gelu_both(v):
    square = v * v
    inner = jnp.tanh(GELU_A * v * (1.0 + GELU_B * square))
    half_up = 0.5 * (1.0 + inner)
    slope = half_up + (0.5 * GELU_A) * v * (1.0 - inner * inner) * (1.0 + (3.0 * GELU_B) * square)
    return v * half_up, slope


class Emitter:
    def __init__(self, targets, runs, coords):
        self.core = coords[0]
        self.whole = targets[0] if len(targets) == 1 else None
        self.batches = [] if self.whole is not None else list(zip(runs, targets[0::2], targets[1::2]))

    def store(self, value, half, strip, planes):
        if self.whole is not None:
            self.whole[half, strip] = value
            return
        plane = strip // (4 * OWN)
        place = (strip // (2 * OWN)) % 2
        owner = (strip // OWN) % 2
        for run, kept, sent in self.batches:
            inside = [z for z in planes if z in run]
            if not inside:
                continue
            here = True if len(inside) == len(planes) else (plane >= run[0]) & (plane <= run[-1])
            spot = (plane - run[0], half, place, strip % OWN)

            @pl.when(here & (owner == self.core))
            def _():
                kept[spot] = value

            @pl.when(here & (owner != self.core))
            def _():
                sent[spot] = value


def mlp_both(coords, normed_two, out_low, w_up, w_down, *rest):
    hidden, grad_normed_two, *targets, grad_up = rest
    step = pl.program_id(0)
    rows = normed_two.shape[0]
    emit = Emitter(targets, ((2, 3), (1,)), coords)

    @pl.when(step == 0)
    def _():
        grad_normed_two[...] = jnp.zeros_like(grad_normed_two)

    up_weight = side_by_side(w_up, (0,), 2)
    down_weight = side_by_side(w_down, (0,), 2)
    chunk = 256
    for i in range(rows // chunk):
        span = slice(i * chunk, (i + 1) * chunk)
        act, slope = gelu_both(mm(normed_two[span, :], up_weight))
        hidden[step, span, :] = act.astype(BF16)
        grad = (mm(out_low[span, :], down_weight, 1, 1) * slope).astype(BF16)
        grad_up[span, :] = grad
        grad_normed_two[span, :] += mm(grad, up_weight, 1, 1)

    half = step // 2
    column = lax.rem(step, 2)
    down_grad = mm(hidden[step], out_low[...], 0, 0).astype(BF16)
    up_grad = mm(normed_two[...], grad_up[...], 0, 0).astype(BF16)
    for row in range(8):
        for part in range(2):
            block = slice(row * BLOCK, (row + 1) * BLOCK), slice(part * STRIP, (part + 1) * STRIP)
            emit.store(down_grad[block], half, 64 + 16 * column + 2 * row + part, (2, 3))
            planes = (1,) if row < 4 else (2,)
            emit.store(up_grad[block], half, 32 + 4 * row + 2 * column + part, planes)


def mlp_out(after, hidden, share, w_down, pooled, total):
    step = pl.program_id(0)
    rows = after.shape[0]
    product = mm(hidden[step], side_by_side(w_down, (0,), 2))

    @pl.when(step == 0)
    def _():
        total[...] = after[...] + product

    @pl.when(step > 0)
    def _():
        total[...] += product

    @pl.when(step == pl.num_programs(0) - 1)
    def _():
        @pl.loop(0, rows // GROUP)
        def _(i):
            weighted = (total[span_of(i), :] * share[span_of(i), :]).reshape(CAPS, SLOTS, D)
            pooled[span_of(i, CAPS), :] = jnp.sum(weighted, axis=1)


def output_backward(held, coords, gains, attended, after, grad_out, grad_normed_two, by_two, *rest):
    grad_after, gain_part, grad_att, *targets = rest[held:-3]
    after_low, w_out, weight_sem = rest[-3:]
    rows = after.shape[0]
    emit = Emitter(targets, ((1,),), coords)
    copies = [
        pltpu.make_async_copy(by_two.at[half, 12:16], w_out.at[half], weight_sem.at[half])
        for half in range(HALVES)
    ]
    for copy in copies:
        copy.start()
    gain_part[...] = jnp.zeros_like(gain_part)

    @pl.loop(0, rows // GROUP)
    def _(i):
        span = span_of(i)
        xhat, inverse = norm_parts(after[span, :])
        grad = grad_normed_two[span, :]
        gain_part[...] += jnp.sum(grad * xhat, axis=0, keepdims=True)
        value = grad_out[span, :] + norm_back(xhat, inverse, gains[1:2, :], grad)
        grad_after[span, :] = value
        after_low[span, :] = value.astype(BF16)

    for copy in copies:
        copy.wait()
    weight = jnp.concatenate([side_by_side(w_out, (half,), 2) for half in range(HALVES)], axis=0)
    grad_att[...] = mm(after_low[...], weight, 1, 1).astype(BF16)
    grad_w = mm(attended[...], after_low[...], 0, 0).astype(BF16)
    for half in range(HALVES):
        for row in range(4):
            for part in range(2):
                top = (4 * half + row) * BLOCK
                value = grad_w[top : top + BLOCK, part * STRIP : (part + 1) * STRIP]
                emit.store(value, half, 24 + 2 * row + part, (1,))


def attention_backward(held, coords, mask, normed, qkv, grad_att, *rest):
    grad_mixed, *targets = rest[held:]
    rows = normed.shape[0]
    emit = Emitter(targets, ((0,),), coords)

    @pl.loop(0, rows // GROUP)
    def _(i):
        span = span_of(i)
        bias = key_bias(mask[i])
        caption = caption_of()
        scale = HD ** (-0.5)
        for half in range(HALVES):
            for pair in range(STRIP // PAIR):
                lanes = slice(pair * PAIR, (pair + 1) * PAIR)
                wide = slice(half * STRIP + pair * PAIR, half * STRIP + (pair + 1) * PAIR)
                queries = split_pair(qkv[3 * half, span, lanes])
                key_rows = qkv[3 * half + 1, span, lanes]
                value_rows = qkv[3 * half + 2, span, lanes]
                probs = pair_probs(queries, key_rows, bias, caption)
                grads = split_pair(grad_att[span, wide])
                grad_probs = compact(mm(value_rows, grads, 1, 1), caption)
                inner = jnp.sum(probs * grad_probs, axis=0, keepdims=True)
                grad_scores = expand(probs * (grad_probs - inner), caption)
                grad_mixed[3 * half, span, lanes] = (
                    join_pair(mm(grad_scores, key_rows, 0, 0)) * scale
                ).astype(BF16)
                grad_mixed[3 * half + 1, span, lanes] = (mm(grad_scores, queries) * scale).astype(
                    BF16
                )
                grad_mixed[3 * half + 2, span, lanes] = mm(expand(probs, caption), grads).astype(
                    BF16
                )

    for half in range(HALVES):
        grads = jnp.concatenate([grad_mixed[3 * half + part] for part in range(3)], axis=1)
        grad_w = mm(normed[...], grads, 0, 0).astype(BF16)
        for row in range(8):
            for part in range(3):
                strip = 3 * row + part
                value = grad_w[row * BLOCK : (row + 1) * BLOCK, part * STRIP : (part + 1) * STRIP]
                emit.store(value, half, strip, (0,))


def input_backward(tok, gains, grad_mixed, grad_after, gain_two, w_qkv, input_grad, gain_part):
    half = pl.program_id(0)
    rows = tok.shape[0]
    grads = jnp.concatenate([grad_mixed[3 * half + part] for part in range(3)], axis=1)
    back = mm(grads, side_by_side(w_qkv, (0,), 3), 1, 1)

    @pl.when(half == 0)
    def _():
        input_grad[...] = back

    @pl.when(half == HALVES - 1)
    def _():
        input_grad[...] += back
        gain_part[0] = jnp.zeros_like(gain_two)
        gain_part[1] = gain_two[...]

        @pl.loop(0, rows // GROUP)
        def _(i):
            span = span_of(i)
            xhat, inverse = norm_parts(tok[span, :].astype(F32))
            grad = input_grad[span, :]
            gain_part[0] += jnp.sum(grad * xhat, axis=0, keepdims=True)
            input_grad[span, :] = grad_after[span, :] + norm_back(
                xhat, inverse, gains[0:1, :], grad
            )


def shape_of(*shape, dtype=BF16):
    return jax.ShapeDtypeStruct(shape, dtype)


HBM = pl.BlockSpec(memory_space=pl.ANY)
VMEM = pl.BlockSpec(memory_space=pltpu.VMEM)
SMEM = pl.BlockSpec(memory_space=pltpu.SMEM)


def call(kernel, name, in_specs, outs, scratch, flops, args, grid=(1,), aliases=None, mib=10):
    args = tuple(
        pltpu.with_memory_space_constraint(a, pltpu.HBM) if a.ndim == 5 else a for a in args
    )
    moved = sum(math_size(a.shape) * a.dtype.itemsize for a in args)
    moved += sum(math_size(s.shape) * s.dtype.itemsize for _, s in outs)
    return pl.pallas_call(
        kernel,
        grid=grid,
        in_specs=in_specs,
        out_specs=[spec for spec, _ in outs],
        out_shape=[shape for _, shape in outs],
        scratch_shapes=scratch,
        input_output_aliases=aliases or {},
        compiler_params=pltpu.CompilerParams(
            dimension_semantics=("arbitrary",) * len(grid), vmem_limit_bytes=mib << 20
        ),
        cost_estimate=pl.CostEstimate(flops=flops, bytes_accessed=moved, transcendentals=0),
        name=name,
    )(*args)


def math_size(shape):
    size = 1
    for extent in shape:
        size *= extent
    return size


UNIT = 2 * 768 * 768 * 768


def run_forward(tok, gains, mask, strips):
    rows = tok.shape[0]
    by_three = strips.reshape(HALVES, 32, 3, BLOCK, STRIP)
    by_two = strips.reshape(HALVES, 48, 2, BLOCK, STRIP)
    return call(
        attention_forward,
        "attention_forward",
        [VMEM, VMEM, VMEM, HBM, HBM],
        [
            (VMEM, shape_of(rows, D)),
            (VMEM, shape_of(6, rows, STRIP)),
            (VMEM, shape_of(rows, D)),
            (VMEM, shape_of(rows, D, dtype=F32)),
            (VMEM, shape_of(rows, D)),
        ],
        [
            pltpu.VMEM((HALVES, 8, 3, BLOCK, STRIP), BF16),
            pltpu.VMEM((HALVES, 4, 2, BLOCK, STRIP), BF16),
            pltpu.SemaphoreType.DMA((4,)),
        ],
        5 * UNIT,
        (tok, gains, mask, by_three, by_two),
        mib=10,
    )


def targets_of(runs, split):
    if split:
        shapes = [shape_of(len(run), HALVES, 2, OWN, BLOCK, STRIP) for run in runs for _ in range(2)]
    else:
        shapes = [shape_of(HALVES, STRIPS, BLOCK, STRIP)]
    return [(VMEM, shape) for shape in shapes]


def up_spec():
    return pl.BlockSpec((1, 8, 2, BLOCK, STRIP), lambda i: (i // 2, 1, i % 2, 0, 0))


def down_spec():
    return pl.BlockSpec((1, 8, 2, BLOCK, STRIP), lambda i: (i // 2, 4 + i % 2, 0, 0, 0))


def run_mlp(coords, normed_two, out_low, strips, split):
    rows = normed_two.shape[0]
    by_four = strips.reshape(HALVES, 24, 4, BLOCK, STRIP)
    by_two = strips.reshape(HALVES, 48, 2, BLOCK, STRIP)
    return call(
        mlp_both,
        "mlp_both",
        [SMEM, VMEM, VMEM, up_spec(), down_spec()],
        [(VMEM, shape_of(4, rows, D)), (VMEM, shape_of(rows, D, dtype=F32))]
        + targets_of(((2, 3), (1,)), split),
        [pltpu.VMEM((rows, D), BF16)],
        20 * UNIT,
        (coords, normed_two, out_low, by_four, by_two),
        grid=(4,),
        mib=16,
    )


def run_mlp_out(after, hidden, share, strips):
    rows = after.shape[0]
    by_two = strips.reshape(HALVES, 48, 2, BLOCK, STRIP)
    return call(
        mlp_out,
        "mlp_out",
        [VMEM, VMEM, VMEM, down_spec()],
        [(VMEM, shape_of(rows // SLOTS, D, dtype=F32))],
        [pltpu.VMEM((rows, D), F32)],
        4 * UNIT,
        (after, hidden, share, by_two),
        grid=(4,),
        mib=8,
    )[0]


def run_output(coords, gains, attended, after, grad_out, grad_two, strips, held, split):
    rows = after.shape[0]
    by_two = strips.reshape(HALVES, 48, 2, BLOCK, STRIP)
    return call(
        functools.partial(output_backward, len(held)),
        "output_backward",
        [SMEM, VMEM, VMEM, VMEM, VMEM, VMEM, HBM] + [VMEM] * len(held),
        [
            (VMEM, shape_of(rows, D, dtype=F32)),
            (VMEM, shape_of(1, D, dtype=F32)),
            (VMEM, shape_of(rows, D)),
        ]
        + targets_of(((1,),), split),
        [
            pltpu.VMEM((rows, D), BF16),
            pltpu.VMEM((HALVES, 4, 2, BLOCK, STRIP), BF16),
            pltpu.SemaphoreType.DMA((HALVES,)),
        ],
        2 * UNIT,
        (coords, gains, attended, after, grad_out, grad_two, by_two, *held),
        aliases={7 + i: 3 + i for i in range(len(held))},
        mib=12,
    )


def run_backward(coords, mask, normed, qkv, grad_att, held, split):
    rows = normed.shape[0]
    return call(
        functools.partial(attention_backward, len(held)),
        "attention_backward",
        [SMEM, VMEM, VMEM, VMEM, VMEM] + [VMEM] * len(held),
        [(VMEM, shape_of(6, rows, STRIP))] + targets_of(((0,),), split),
        [],
        7 * UNIT,
        (coords, mask, normed, qkv, grad_att, *held),
        aliases={5 + i: 1 + i for i in range(len(held))},
        mib=8,
    )


def run_input(tok, gains, grad_mixed, grad_after, gain_two, strips):
    rows = tok.shape[0]
    by_three = strips.reshape(HALVES, 32, 3, BLOCK, STRIP)
    return call(
        input_backward,
        "input_backward",
        [
            VMEM,
            VMEM,
            VMEM,
            VMEM,
            VMEM,
            pl.BlockSpec((1, 8, 3, BLOCK, STRIP), lambda i: (i, 0, 0, 0, 0)),
        ],
        [
            (VMEM, shape_of(rows, D, dtype=F32)),
            (VMEM, shape_of(2, 1, D, dtype=F32)),
        ],
        [],
        3 * UNIT,
        (tok, gains, grad_mixed, grad_after, gain_two, by_three),
        grid=(HALVES,),
        mib=10,
    )


def to_strips(blocks):
    count = blocks.shape[0] // 4
    return blocks.reshape(count, 4, BLOCK, BLOCK).transpose(0, 2, 1, 3).reshape(count, BLOCK, STRIP)


def to_blocks(strips):
    count = strips.shape[0]
    return strips.reshape(count, BLOCK, 4, BLOCK).transpose(0, 2, 1, 3).reshape(-1, BLOCK, BLOCK)


EVERY = ("tensor", "dp")


def gather_weights(master):
    low = master.astype(BF16)
    own = low.shape[0]
    if own % 4 == 0:
        strips = to_strips(low).reshape(-1, STRIP)
        strips = lax.all_gather(strips, EVERY, axis=0, tiled=True)
        return strips.reshape(HALVES, STRIPS, BLOCK, STRIP)
    blocks = lax.all_gather(low, EVERY, axis=0, tiled=True)
    return to_strips(blocks).reshape(HALVES, STRIPS, BLOCK, STRIP)


def scatter_flat(strips, own):
    if own % 4 == 0:
        mine = lax.psum_scatter(
            strips.reshape(-1, STRIP), EVERY, scatter_dimension=0, tiled=True
        )
        return to_blocks(mine.reshape(-1, BLOCK, STRIP)).astype(F32)
    blocks = to_blocks(strips.reshape(-1, BLOCK, STRIP))
    return lax.psum_scatter(blocks, EVERY, scatter_dimension=0, tiled=True).astype(F32)


def fence(*values):
    return lax.optimization_barrier(values)


OTHER_CORE = [(i, i ^ 1) for i in range(16)]
OTHER_X = [(i, i ^ 2) for i in range(16)]
OTHER_Y = [(0, 1), (1, 0)]


def by_plane(*moves):
    return [(4 * a + i, 4 * b + i) for a, b in moves for i in range(4)]


def split_sum(coords, kept, arrived, sent_one, sent_two, kept_one, kept_two):
    place, half = coords[1], coords[3]

    @pl.loop(0, 2 * kept.shape[0])
    def _(step):
        plane, i = step // 2, lax.rem(step, 2)
        one, two = pl.ds(0, 3), pl.ds(3, 3)
        sent_one[plane, i] = kept[plane, 1 - half, i, one] + arrived[plane, 1 - half, i, one]
        kept_one[plane, i] = kept[plane, half, i, one] + arrived[plane, half, i, one]
        sent_two[plane, i] = kept[plane, i, 1 - place, two] + arrived[plane, i, 1 - place, two]
        kept_two[plane, i] = kept[plane, i, place, two] + arrived[plane, i, place, two]


def split_again(coords, one, two, one_in, two_in, sent_one, sent_two, kept_one, kept_two):
    place, half = coords[1], coords[3]

    @pl.loop(0, one.shape[0])
    def _(plane):
        sent_one[plane] = one[plane, 1 - place] + one_in[plane, 1 - place]
        kept_one[plane] = one[plane, place] + one_in[plane, place]
        sent_two[plane] = two[plane, 1 - half] + two_in[plane, 1 - half]
        kept_two[plane] = two[plane, half] + two_in[plane, half]


def join_sum(coords, one, two, one_in, two_in, *outs):
    for i, out in enumerate(outs):
        plane = 0 if len(outs) == 1 else lax.rem(coords[2] + i, 2)
        out[0:3] = one[plane] + one_in[plane]
        out[3:6] = two[plane] + two_in[plane]


def sum_of(left, right, out):
    @pl.loop(0, left.shape[0])
    def _(i):
        out[i] = left[i] + right[i]


def run_split(coords, kept, arrived):
    shape = shape_of(kept.shape[0], 2, 3, BLOCK, STRIP)
    outs = call(
        split_sum,
        "split_sum",
        [SMEM, VMEM, VMEM],
        [(VMEM, shape)] * 4,
        [],
        math_size(kept.shape),
        (coords, kept, arrived),
        mib=4,
    )
    return outs[:2], outs[2:]


def run_again(coords, kept, arrived):
    shape = shape_of(kept[0].shape[0], 3, BLOCK, STRIP)
    outs = call(
        split_again,
        "split_again",
        [SMEM] + [VMEM] * 4,
        [(VMEM, shape)] * 4,
        [],
        2 * math_size(kept[0].shape),
        (coords, *kept, *arrived),
        mib=4,
    )
    return outs[:2], outs[2:]


def run_join(coords, kept, arrived):
    return call(
        join_sum,
        "join_sum",
        [SMEM] + [VMEM] * 4,
        [(VMEM, shape_of(OWN, BLOCK, STRIP))] * kept[0].shape[0],
        [],
        2 * math_size(kept[0].shape),
        (coords, *kept, *arrived),
        mib=4,
    )


def run_sum(left, right):
    return call(
        sum_of,
        "sum_of",
        [VMEM] * 2,
        [(VMEM, jax.ShapeDtypeStruct(left.shape, left.dtype))],
        [],
        math_size(left.shape),
        (left, right),
        mib=4,
    )[0]


def core_hop(sent):
    return lax.ppermute(sent, "dp", OTHER_CORE)


def first_hop(sent):
    return lax.ppermute(sent[0], "tensor", OTHER_Y), lax.ppermute(sent[1], "dp", OTHER_X)


def second_hop(sent):
    return lax.ppermute(sent[0], "dp", OTHER_X), lax.ppermute(sent[1], "tensor", OTHER_Y)


def precise(left, right, left_dim=1, right_dim=0):
    left_high, right_high = left.astype(BF16), right.astype(BF16)
    left_low = (left - left_high.astype(F32)).astype(BF16)
    right_low = (right - right_high.astype(F32)).astype(BF16)
    small = mm(left_high, right_low, left_dim, right_dim) + mm(
        left_low, right_high, left_dim, right_dim
    )
    return mm(left_high, right_high, left_dim, right_dim) + small


def update(
    coords, high, high_in, one, one_in, zero, zero_in, master, stat_left, stat_right, root_left, root_right, *outs
):
    grad_out, left_out, right_out, master_out, copy_out, grad = outs
    plane = coords[2]
    strip = pl.program_id(0)
    for condition, own, arrived in (
        (plane >= 2, high, high_in),
        (plane == 1, one, one_in),
        (plane == 0, zero, zero_in),
    ):

        @pl.when(condition)
        def _():
            grad[...] = own[strip].astype(F32) + arrived[strip].astype(F32)

    for i in range(4):
        block = 4 * strip + i
        g = grad[:, i * BLOCK : (i + 1) * BLOCK]
        grad_out[i] = g
        left_out[i] = DECAY_RATE * stat_left[block] + (1.0 - DECAY_RATE) * precise(g, g, 1, 1)
        right_out[i] = DECAY_RATE * stat_right[block] + (1.0 - DECAY_RATE) * precise(g, g, 0, 0)
        direction = precise(root_left[block], precise(g, root_right[block]))
        new = master[block] - STEP_RATE * direction
        master_out[i] = new
        copy_out[i] = new.astype(BF16)


def run_update(coords, sums, blocks):
    count = blocks[0].shape[0]
    tile = pl.BlockSpec((4, BLOCK, BLOCK), lambda i: (i, 0, 0))
    shape = shape_of(count, BLOCK, BLOCK, dtype=F32)
    return call(
        update,
        "update",
        [SMEM] + [VMEM] * (len(sums) + len(blocks)),
        [(tile, shape)] * 4 + [(tile, shape_of(count, BLOCK, BLOCK))],
        [pltpu.VMEM((BLOCK, STRIP), F32)],
        12 * 2 * count * BLOCK**3,
        (coords, *sums, *blocks),
        grid=(count // 4,),
        mib=12,
    )


def sum_hops():
    hops = []
    for axis in ("tensor", "dp"):
        size, step = lax.axis_size(axis), 1
        while step < size:
            hops.append((axis, [(i, i ^ step) for i in range(size)]))
            step *= 2
    return hops


def add_hop(value, hop):
    return run_sum(value, lax.ppermute(value, *hop))


def plain_update(grad, master, stat_left, stat_right, root_left, root_right):
    left_new = DECAY_RATE * stat_left + (1.0 - DECAY_RATE) * jnp.einsum(
        "nij,nkj->nik", grad, grad, precision=PRECISE
    )
    right_new = DECAY_RATE * stat_right + (1.0 - DECAY_RATE) * jnp.einsum(
        "nji,njk->nik", grad, grad, precision=PRECISE
    )
    right_side = jnp.einsum("nij,njk->nik", grad, root_right, precision=PRECISE)
    direction = jnp.einsum("nij,njk->nik", root_left, right_side, precision=PRECISE)
    master_new = master - STEP_RATE * direction
    return grad, left_new, right_new, master_new, master_new.astype(BF16)


def body(
    tokens,
    token_mask,
    norm_gains,
    gain_moments,
    cotangent,
    master,
    stat_left,
    stat_right,
    root_left,
    root_right,
):
    rows = tokens.shape[0]
    own_caps = cotangent.shape[0]
    own = master.shape[0]
    split = lax.axis_size("dp") == 16 and lax.axis_size("tensor") == 2
    dp_pos, half = lax.axis_index("dp"), lax.axis_index("tensor")
    coords = jnp.stack([dp_pos % 2, dp_pos // 2 % 2, dp_pos // 4, half]).astype(jnp.int32)
    strips = gather_weights(master)
    group_mask = token_mask.astype(F32)
    own_mask = lax.dynamic_slice_in_dim(group_mask, half * own_caps, own_caps, 0)
    share = (own_mask / jnp.sum(own_mask, axis=1, keepdims=True)).reshape(rows, 1)
    mask = jnp.repeat(own_mask.reshape(rows // GROUP, CAPS, SLOTS), SLOTS, axis=1).swapaxes(1, 2)
    cot = cotangent.astype(F32)
    grad_out = (cot[:, None, :] * share.reshape(own_caps, SLOTS, 1)).reshape(rows, D)
    out_low = grad_out.astype(BF16)
    normed, qkv, attended, after, normed_two = run_forward(tokens, norm_gains, mask, strips)
    hidden, grad_two, *held = run_mlp(coords, normed_two, out_low, strips, split)
    hops = sum_hops()
    blocks = (master, stat_left, stat_right, root_left, root_right)
    if not split:
        grad_after, gain_two, grad_att, *held = run_output(
            coords, norm_gains, attended, after, grad_out, grad_two, strips, held, split
        )
        grad_mixed, *held = run_backward(coords, mask, normed, qkv, grad_att, held, split)
        input_grad, gain_grads = run_input(
            tokens, norm_gains, grad_mixed, grad_after, gain_two, strips
        )
        pooled = run_mlp_out(after, hidden, share, strips)
        for hop in hops:
            gain_grads = add_hop(gain_grads, hop)
        updated = plain_update(scatter_flat(held[0], own), *blocks)
    else:
        upper_kept, upper_sent, one_kept, one_sent = held
        upper_in = core_hop(upper_sent)
        grad_after, gain_two, grad_att, *one = run_output(
            coords, norm_gains, attended, after, grad_out, grad_two, strips, (one_kept, one_sent), split
        )
        upper_in, grad_att, one = fence(upper_in, grad_att, one)

        upper_sent, upper_kept = run_split(coords, upper_kept, upper_in)
        upper_sent, grad_att, one = fence(upper_sent, grad_att, one)
        upper_in = first_hop(upper_sent)
        one_in = core_hop(one[1])
        grad_mixed, *zero = run_backward(coords, mask, normed, qkv, grad_att, [], split)
        upper_in, one_in, grad_mixed, zero = fence(upper_in, one_in, grad_mixed, zero)

        upper_sent, upper_kept = run_again(coords, upper_kept, upper_in)
        one_sent, one_kept = run_split(coords, one[0], one_in)
        upper_sent, one_sent, zero, grad_mixed = fence(upper_sent, one_sent, zero, grad_mixed)
        zero_in = core_hop(zero[1])
        upper_in = second_hop(upper_sent)
        one_in = first_hop(one_sent)
        input_grad, gain_grads = run_input(
            tokens, norm_gains, grad_mixed, grad_after, gain_two, strips
        )
        zero_in, gain_grads, hidden = fence(zero_in, gain_grads, hidden)

        zero_sent, zero_kept = run_split(coords, zero[0], zero_in)
        zero_sent, gain_grads, hidden = fence(zero_sent, gain_grads, hidden)
        zero_in = first_hop(zero_sent)
        gain_grads = add_hop(gain_grads, hops[0])
        pooled = run_mlp_out(after, hidden, share, strips)
        upper_in, one_in, gain_grads, pooled = fence(upper_in, one_in, gain_grads, pooled)

        one_sent, one_kept = run_again(coords, one_kept, one_in)
        one_in = second_hop(one_sent)
        high, other = run_join(coords, upper_kept, upper_in)
        high_in = lax.ppermute(other, "dp", by_plane((0, 1), (1, 0), (2, 3), (3, 2)))
        gain_grads = add_hop(gain_grads, hops[1])
        zero_in, one_in, high_in, gain_grads = fence(zero_in, one_in, high_in, gain_grads)

        zero_sent, zero_kept = run_again(coords, zero_kept, zero_in)
        zero_in = second_hop(zero_sent)
        (one_sum,) = run_join(coords, one_kept, one_in)
        one_in = lax.ppermute(one_sum, "dp", by_plane((0, 1), (2, 3)))
        high = run_sum(high, high_in)
        high_in = lax.ppermute(high, "dp", by_plane((0, 2), (1, 3)))
        gain_grads = add_hop(gain_grads, hops[2])
        zero_in, one_in, gain_grads = fence(zero_in, one_in, gain_grads)

        (zero_sum,) = run_join(coords, zero_kept, zero_in)
        zero_in = lax.ppermute(zero_sum, "dp", by_plane((1, 0), (3, 2)))
        one_sum = run_sum(one_sum, one_in)
        one_in = lax.ppermute(one_sum, "dp", by_plane((3, 1)))
        gain_grads = add_hop(gain_grads, hops[3])
        zero_in, high_in, gain_grads = fence(zero_in, high_in, gain_grads)

        zero_sum = run_sum(zero_sum, zero_in)
        zero_in = lax.ppermute(zero_sum, "dp", by_plane((2, 0)))
        gain_grads = add_hop(gain_grads, hops[4])
        updated = run_update(coords, (high, high_in, one_sum, one_in, zero_sum, zero_in), blocks)
    gain_grads = gain_grads.reshape(2, D)
    moments_new = DECAY_RATE * gain_moments + (1.0 - DECAY_RATE) * gain_grads * gain_grads
    gains_new = norm_gains - GAIN_RATE * gain_grads / (jnp.sqrt(moments_new) + 1e-08)
    return (pooled, input_grad, gain_grads, moments_new, gains_new, *updated)


def solution(mesh):
    rows = P(("dp", "tensor"), None)
    blocks = P(("dp", "tensor"), None, None)
    return jax.shard_map(
        body,
        mesh=mesh,
        in_specs=(rows, P("dp", None), P(), P(), rows) + (blocks,) * 5,
        out_specs=(rows, rows, P(), P(), P()) + (blocks,) * 5,
        check_vma=False,
    )
```

profile of v0, /device:TPU:0, one launch (start us, length us, event | category | flops | bytes accessed | tf_op | source)
XLA Modules:
  0.0 307.1 jit_solution(1750737226362280461)
XLA Ops:
  7.2 1.4 convert_element_type.13
  8.9 1.2 reshape_reshape.8
  11.3 0.8 reshape.43
  12.1 2.1 bitcast_multiply_fusion
  14.2 103.2 %all-gather.2.cloned.1.call-done = bf16[18432,384]{1,0:T(8,128)(2,1)} async-done(((bf16[576,384]{1,0:T(8,128)(2,1)}), bf16[18432,384]{1,0:T(8,128)(2,1)}) %all-gather.2.cloned.1.call-update) | async-done | bytes 14155792 | tf_op jit(solution)/shard_map/all_gather | solution.py:568
  117.4 0.8 copy-done.27
  118.2 12.9 %attention_forward.1 = (bf16[768,768]{1,0:T(8,128)(2,1)S(1)}, bf16[6,768,384]{2,1,0:T(8,128)(2,1)S(1)}, bf16[768,768]{1,0:T(8,128)(2,1)S(1)}, f32[768,768]{1,0:T(8,128)S(1)}, bf16[768,768]{1,0:T(8,128)(2,1)S(1)}) custom-call(bf16[768,768]{1,0:T(8,128)(2,1)S(1)} %copy-done.1, f32[2,768]{1,0:T(2,128)S(1)} %copy-done.29, f32[6,16,128]{2,1,0:T(8,128)S(1)} %bitcast.23, ...), custom_call_target="tpu_custom_call" | custom-call | flops 4529848320 | bytes 38983680 | tf_op jit(solution)/shard_map/attention_forward/pallas_call | solution.py:382
  131.2 26.6 %mlp_both.1 = (bf16[4,768,768]{2,1,0:T(8,128)(2,1)S(1)}, f32[768,768]{1,0:T(8,128)S(1)}, bf16[2,2,2,6,96,384]{5,4,3,2,1,0:T(8,128)(2,1)S(1)}, bf16[2,2,2,6,96,38...) custom-call(s32[4]{0:T(128)S(1)} %pad_add_fusion.coords, ...), custom_call_target="tpu_custom_call" | custom-call | flops 18119393280 | bytes 48365584 | tf_op jit(solution)/shard_map/mlp_both/pallas_call | solution.py:382
  157.8 2.1 copy-done.3
  160.2 5.0 %output_backward.1 = (f32[768,768]{1,0:T(8,128)S(1)}, f32[1,768]{1,0:T(1,128)S(1)}, bf16[768,768]{1,0:T(8,128)(2,1)S(1)}, bf16[1,2,2,6,96,384]{5,4,3,2,1,0:T(8,128)(2,1)S(1)}, bf16[1,2,2,6,96,384]{5,4,3,2,1,0:T(8,128)(2,1)S(1)}) custom-call(s32[4]{0:T(128)S(1)} %pad_add_fusion.coords, ...), custom_call_target="tpu_custom_call", output_to_operand_aliasing={{3}: (7, {}), {4}: (8, {})} | custom-call | flops 1811939328 | bytes 33039376 | tf_op jit(solution)/shard_map/output_backward/pallas_call | solution.py:382
  165.2 1.4 copy-done.7
  166.6 1.1 split_sum.3
  167.7 0.9 copy-done.17
  168.9 1.5 collective-permute-start.1
  170.4 0.6 collective-permute-start.2
  170.9 17.9 %attention_backward.1 = (bf16[6,768,384]{2,1,0:T(8,128)(2,1)S(1)}, bf16[1,2,2,6,96,384]{5,4,3,2,1,0:T(8,128)(2,1)S(1)}, bf16[1,2,2,6,96,384]{5,4,3,2,1,0:T(8,128)(2,1)}) custom-call(s32[4]{0:T(128)S(1)} %pad_add_fusion.coords, f32[6,16,128]{2,1,0:T(8,128)S(1)} %bitcast.24, bf16[768,768]{1,0:T(8,128)(2,1)S(1)} %get-tuple-element.132.normed, ...), custom_call_target="tpu_custom_call" | custom-call | flops 6341787648 | bytes 13025296 | tf_op jit(solution)/shard_map/attention_backward/pallas_call | solution.py:382
  188.8 1.2 copy-done.9
  190.1 0.7 collective-permute-done.1.one_in
  190.7 1.2 collective-permute-done.2.two_in
  191.9 1.0 split_sum.4
  193.0 0.8 copy-done.22
  193.8 2.7 split_again.3
  196.5 0.8 copy-done.23
  197.3 0.8 copy-done.25
  198.0 0.8 copy-done.32
  198.8 0.8 copy-done.33
  199.6 1.7 reshape.47.share
  201.3 0.6 collective-permute-start.4
  201.8 1.4 collective-permute-start.5
  203.3 0.6 collective-permute-start.6
  203.9 1.5 collective-permute-start.7
  205.3 2.0 copy-done.6
  207.3 1.7 copy-done.8
  209.0 8.9 %input_backward.1 = (f32[768,768]{1,0:T(8,128)}, f32[2,1,768]{2,1,0:T(1,128)S(1)}) custom-call(bf16[768,768]{1,0:T(8,128)(2,1)S(1)} %copy-done.1, f32[2,768]{1,0:T(2,128)S(1)} %copy-done.29, bf16[6,768,384]{2,1,0:T(8,128)(2,1)S(1)} %copy-done.6, f32[768,768]{1,0:T(8,128)S(1)} %copy-done.8, f32[1,768]{1,0:T(1,128)S(1)} %get-tuple-element.157.gain_two, ...), custom_call_target="tpu_custom_call" | custom-call | flops 2717908992 | bytes 23608320 | tf_op jit(solution)/shard_map/input_backward/pallas_call | solution.py:382
  217.9 1.8 split_sum.5
  219.8 0.8 copy-done.19
  220.6 0.8 copy-done.20
  221.9 2.3 copy-done.4
  224.2 8.2 %mlp_out.1 = f32[48,768]{1,0:T(8,128)} custom-call(f32[768,768]{1,0:T(8,128)S(1)} %get-tuple-element.114.after, bf16[4,768,768]{2,1,0:T(8,128)(2,1)S(1)} %copy-done.4, f32[768,1]{1,0:T(8,128)S(1)} %copy-done.11, bf16[2,48,2,96,384]{4,3,2,1,0:T(8,128)(2,1)} %bitcast.31), custom_call_target="tpu_custom_call" | custom-call | flops 3623878656 | bytes 21384192 | tf_op jit(solution)/shard_map/mlp_out/pallas_call | solution.py:382
  232.5 1.5 collective-permute-start.10
  234.0 0.6 collective-permute-start.11
  234.6 0.7 join_sum.3
  235.3 0.7 collective-permute-start.14
  236.0 1.6 split_again.4
  237.6 1.5 collective-permute-start.12
  239.7 10.0 %collective-permute-done.12.one_in = bf16[1,3,96,384]{3,2,1,0:T(8,128)(2,1)S(1)} collective-permute-done((bf16[1,3,96,384]{3,2,1,0:T(8,128)(2,1)S(1)}, bf16[1,3,96,384]{3,2,1,0:T(8,128)(2,1)S(1)}, u32[]{:S(2)}, u32[]{:S(2)}) %collective-permute-start.12) | collective-permute-done | bytes 221216 | tf_op jit(solution)/shard_map/ppermute | solution.py:699
  249.7 0.6 join_sum.4.left
  250.3 2.5 collective-permute-start.18
  252.9 1.6 split_again.5
  254.6 0.6 collective-permute-start.16
  255.2 1.4 collective-permute-start.17
  256.6 0.6 collective-permute-start.19
  257.3 3.5 %collective-permute-start.21 = (bf16[6,96,384]{2,1,0:T(8,128)(2,1)S(1)}, bf16[6,96,384]{2,1,0:T(8,128)(2,1)S(1)}, u32[]{:S(2)}, u32[]{:S(2)}) collective-permute-start(bf16[6,96,384]{2,1,0:T(8,128)(2,1)S(1)} %sum_of.11.high), channel_id=1, source_target_pairs={{0,16},{2,18},{4,20},{6,22},{8,24},{10,26},{12,28},{14,30},{1,17},... | collective-permute-start | bytes 1327112 | tf_op jit(solution)/shard_map/ppermute | solution.py:871
  261.1 1.9 collective-permute-done.18.right
  263.0 0.6 join_sum.5.left
  263.6 1.4 collective-permute-start.20
  265.0 2.7 collective-permute-start.22
  267.8 0.7 collective-permute-start.24
  268.5 5.6 %collective-permute-done.22.right = f32[2,1,768]{2,1,0:T(1,128)S(1)} collective-permute-done((f32[2,1,768]{2,1,0:T(1,128)S(1)}, f32[2,1,768]{2,1,0:T(1,128)S(1)}, u32[]{:S(2)}, u32[]{:S(2)}) %collective-permute-start.22) | collective-permute-done | bytes 6176 | tf_op jit(solution)/shard_map/ppermute | solution.py:768
  274.2 1.3 collective-permute-start.25
  275.5 7.1 %collective-permute-start.23 = (f32[2,1,768]{2,1,0:T(1,128)S(1)}, f32[2,1,768]{2,1,0:T(1,128)S(1)}, u32[]{:S(2)}, u32[]{:S(2)}) collective-permute-start(f32[2,1,768]{2,1,0:T(1,128)S(1)} %sum_of.12.left), channel_id=1, source_target_pairs={{0,16},{2,18},{4,20},{6,22},{8,24},{10,26},{12,28},{14,30},{16,0},... | collective-permute-start | bytes 18440 | tf_op jit(solution)/shard_map/ppermute | solution.py:768
  282.6 8.4 %collective-permute-done.23.right = f32[2,1,768]{2,1,0:T(1,128)S(1)} collective-permute-done((f32[2,1,768]{2,1,0:T(1,128)S(1)}, f32[2,1,768]{2,1,0:T(1,128)S(1)}, u32[]{:S(2)}, u32[]{:S(2)}) %collective-permute-start.23) | collective-permute-done | bytes 6176 | tf_op jit(solution)/shard_map/ppermute | solution.py:768
  291.0 0.6 divide_subtract_fusion
  291.7 8.5 %update.1 = (f32[24,96,96]{2,1,0:T(8,128)}, f32[24,96,96]{2,1,0:T(8,128)}, f32[24,96,96]{2,1,0:T(8,128)}, f32[24,96,96]{2,1,0:T(8,128)}, bf16[24,96,96]{2,1,0:T(8,128)(2,1)}) custom-call(s32[4]{0:T(128)S(1)} %pad_add_fusion.coords, bf16[6,96,384]{2,1,0:T(8,128)(2,1)S(1)} %sum_of.11.high, bf16[6,96,384]{2,1,0:T(8,128)(2,1)S(1)} %collective-permute-done.21.high_in, ...), custom_call_target="tpu_custom_call" | custom-call | flops 509607936 | bytes 11059216 | tf_op jit(solution)/shard_map/update/pallas_call | solution.py:382
  (118 shorter events, 4.0 us)
Async XLA Ops:
  7.2 110.2 %all-gather.2.cloned.1.call-start = ((), (), s32[]{:S(2)}) async-start(), calls=%async_computation | async-start | bytes 14598144 | tf_op jit(solution)/shard_map/all_gather | solution.py:568
  8.6 1.6 copy-start.42
  8.6 1.9 copy-start.41
  12.1 105.3 %copy-start.1 = (bf16[768,768]{1,0:T(8,128)(2,1)S(1)}, bf16[768,768]{1,0:T(8,128)(2,1)}, u32[]{:S(2)}) copy-start(bf16[768,768]{1,0:T(8,128)(2,1)} %tok.3) | copy-start | bytes 3538948
  12.1 105.3 %copy-start.29 = (f32[2,768]{1,0:T(2,128)S(1)}, f32[2,768]{1,0:T(2,128)}, u32[]{:S(2)}) copy-start(f32[2,768]{1,0:T(2,128)} %gains.5) | copy-start | bytes 18436
  117.4 0.8 copy-start.27
  118.2 13.0 %copy-start.16 = (bf16[768,768]{1,0:T(8,128)(2,1)S(1)}, bf16[768,768]{1,0:T(8,128)(2,1)}, u32[]{:S(2)}) copy-start(bf16[768,768]{1,0:T(8,128)(2,1)} %get-tuple-element.216.out_low) | copy-start | bytes 3538948
  131.2 29.0 %copy-start = (f32[768,768]{1,0:T(8,128)S(1)}, f32[768,768]{1,0:T(8,128)}, u32[]{:S(2)}) copy-start(f32[768,768]{1,0:T(8,128)} %get-tuple-element.215.grad_out) | copy-start | bytes 7077892
  157.8 2.1 copy-start.3
  159.9 6.7 %collective-permute-start = (bf16[2,2,2,6,96,384]{5,4,3,2,1,0:T(8,128)(2,1)S(1)}, bf16[2,2,2,6,96,384]{5,4,3,2,1,0:T(8,128)(2,1)S(1)}, u32[]{:S(2)}, u32[]{:S(2)}) collective-permute-start(bf16[2,2,2,6,96,384]{5,4,3,2,1,0:T(8,128)(2,1)S(1)} %get-tuple-element.112), channel_id=1, source_target_pairs={{0,2},{2,0},{4,6},{6,4},{8,10},{10,8},{12,14},{14,12},{16,18},{18,... | collective-permute-start | bytes 10616840 | tf_op jit(solution)/shard_map/ppermute | solution.py:691
  165.2 1.4 copy-start.7
  166.6 4.3 %copy-start.28 = (f32[6,128,16]{1,2,0:T(8,128)S(1)}, f32[6,128,16]{1,2,0:T(8,128)}, u32[]{:S(2)}) copy-start(f32[6,128,16]{1,2,0:T(8,128)} %reshape.43) | copy-start | bytes 147460
  167.7 0.9 copy-start.17
  168.6 20.2 %copy-start.18 = (bf16[2,2,3,96,384]{4,3,2,1,0:T(8,128)(2,1)}, bf16[2,2,3,96,384]{4,3,2,1,0:T(8,128)(2,1)S(1)}, u32[]{:S(2)}) copy-start(bf16[2,2,3,96,384]{4,3,2,1,0:T(8,128)(2,1)S(1)} %get-tuple-element.123.two) | copy-start | bytes 2654212
  168.6 23.3 %collective-permute-start.3 = (bf16[1,2,2,6,96,384]{5,4,3,2,1,0:T(8,128)(2,1)S(1)}, bf16[1,2,2,6,96,384]{5,4,3,2,1,0:T(8,128)(2,1)S(1)}, u32[]{:S(2)}, u32[]{:S(2)}) collective-permute-start(bf16[1,2,2,6,96,384]{5,4,3,2,1,0:T(8,128)(2,1)S(1)} %get-tuple-element.131), channel_id=1, source_target_pairs={{0,2},{2,0},{4,6},{6,4},{8,10},{10,8},{12,14},{14,12},{16,18},{18,... | collective-permute-start | bytes 5308424 | tf_op jit(solution)/shard_map/ppermute | solution.py:691
  168.9 21.8 %collective-permute-start.1 = (bf16[2,2,3,96,384]{4,3,2,1,0:T(8,128)(2,1)S(1)}, bf16[2,2,3,96,384]{4,3,2,1,0:T(8,128)(2,1)S(1)}, u32[]{:S(2)}, u32[]{:S(2)}) collective-permute-start(bf16[2,2,3,96,384]{4,3,2,1,0:T(8,128)(2,1)S(1)} %get-tuple-element.129), channel_id=1, source_target_pairs={{0,1},{1,0},{2,3},{3,2},{4,5},{5,4},{6,7},{7,6},{8,9},{9,8},{10,11... | collective-permute-start | bytes 2654216 | tf_op jit(solution)/shard_map/ppermute | solution.py:695
  170.4 21.5 %collective-permute-start.2 = (bf16[2,2,3,96,384]{4,3,2,1,0:T(8,128)(2,1)S(1)}, bf16[2,2,3,96,384]{4,3,2,1,0:T(8,128)(2,1)S(1)}, u32[]{:S(2)}, u32[]{:S(2)}) collective-permute-start(bf16[2,2,3,96,384]{4,3,2,1,0:T(8,128)(2,1)S(1)} %get-tuple-element.130), channel_id=1, source_target_pairs={{0,4},{2,6},{4,0},{6,2},{8,12},{10,14},{12,8},{14,10},{16,20},{18,... | collective-permute-start | bytes 2654216 | tf_op jit(solution)/shard_map/ppermute | solution.py:695
  188.8 1.3 copy-start.9
  190.0 2.9 copy-start.5
  190.7 3.0 copy-start.34
  191.9 1.9 copy-start.35
  192.9 0.8 copy-start.22
  193.7 2.7 copy-start.21
  193.7 2.7 copy-start.30
  193.7 2.8 copy-start.31
  199.6 18.4 %collective-permute-start.8 = (bf16[1,2,2,6,96,384]{5,4,3,2,1,0:T(8,128)(2,1)}, bf16[1,2,2,6,96,384]{5,4,3,2,1,0:T(8,128)(2,1)}, u32[]{:S(2)}, u32[]{:S(2)}) collective-permute-start(bf16[1,2,2,6,96,384]{5,4,3,2,1,0:T(8,128)(2,1)} %get-tuple-element.154), channel_id=1, source_target_pairs={{0,2},{2,0},{4,6},{6,4},{8,10},{10,8},{12,14},{14,12},{16,18},{18,... | collective-permute-start | bytes 5308424 | tf_op jit(solution)/shard_map/ppermute | solution.py:691
  201.3 32.7 %collective-permute-start.4 = (bf16[2,3,96,384]{3,2,1,0:T(8,128)(2,1)}, bf16[2,3,96,384]{3,2,1,0:T(8,128)(2,1)S(1)}, u32[]{:S(2)}, u32[]{:S(2)}) collective-permute-start(bf16[2,3,96,384]{3,2,1,0:T(8,128)(2,1)} %copy-done.33), channel_id=1, source_target_pairs={{0,4},{2,6},{4,0},{6,2},{8,12},{10,14},{12,8},{14,10},{16,20},{18,... | collective-permute-start | bytes 1327112 | tf_op jit(solution)/shard_map/ppermute | solution.py:699
  201.8 32.7 %collective-permute-start.5 = (bf16[2,3,96,384]{3,2,1,0:T(8,128)(2,1)}, bf16[2,3,96,384]{3,2,1,0:T(8,128)(2,1)S(1)}, u32[]{:S(2)}, u32[]{:S(2)}) collective-permute-start(bf16[2,3,96,384]{3,2,1,0:T(8,128)(2,1)} %copy-done.32), channel_id=1, source_target_pairs={{0,1},{1,0},{2,3},{3,2},{4,5},{5,4},{6,7},{7,6},{8,9},{9,8},{10,11... | collective-permute-start | bytes 1327112 | tf_op jit(solution)/shard_map/ppermute | solution.py:699
  203.3 31.3 %collective-permute-start.6 = (bf16[1,2,3,96,384]{4,3,2,1,0:T(8,128)(2,1)}, bf16[1,2,3,96,384]{4,3,2,1,0:T(8,128)(2,1)S(1)}, u32[]{:S(2)}, u32[]{:S(2)}) collective-permute-start(bf16[1,2,3,96,384]{4,3,2,1,0:T(8,128)(2,1)} %copy-done.31), channel_id=1, source_target_pairs={{0,1},{1,0},{2,3},{3,2},{4,5},{5,4},{6,7},{7,6},{8,9},{9,8},{10,11... | collective-permute-start | bytes 1327112 | tf_op jit(solution)/shard_map/ppermute | solution.py:695
  203.9 30.7 %collective-permute-start.7 = (bf16[1,2,3,96,384]{4,3,2,1,0:T(8,128)(2,1)}, bf16[1,2,3,96,384]{4,3,2,1,0:T(8,128)(2,1)S(1)}, u32[]{:S(2)}, u32[]{:S(2)}) collective-permute-start(bf16[1,2,3,96,384]{4,3,2,1,0:T(8,128)(2,1)} %copy-done.30), channel_id=1, source_target_pairs={{0,4},{2,6},{4,0},{6,2},{8,12},{10,14},{12,8},{14,10},{16,20},{18,... | collective-permute-start | bytes 1327112 | tf_op jit(solution)/shard_map/ppermute | solution.py:695
  205.3 2.0 copy-start.6
  207.3 1.7 copy-start.8
  209.0 8.9 %copy-start.10 = (bf16[1,2,2,6,96,384]{5,4,3,2,1,0:T(8,128)(2,1)S(1)}, bf16[1,2,2,6,96,384]{5,4,3,2,1,0:T(8,128)(2,1)}, u32[]{:S(2)}) copy-start(bf16[1,2,2,6,96,384]{5,4,3,2,1,0:T(8,128)(2,1)} %copy-done.9) | copy-start | bytes 5308420
  217.9 3.9 %copy-start.11 = (f32[768,1]{1,0:T(8,128)S(1)}, f32[768,1]{1,0:T(8,128)}, u32[]{:S(2)}) copy-start(f32[768,1]{1,0:T(8,128)} %reshape.47.share) | copy-start | bytes 9220
  221.3 11.1 %collective-permute-start.9 = (f32[2,1,768]{2,1,0:T(1,128)S(1)}, f32[2,1,768]{2,1,0:T(1,128)S(1)}, u32[]{:S(2)}, u32[]{:S(2)}) collective-permute-start(f32[2,1,768]{2,1,0:T(1,128)S(1)} %get-tuple-element.165.left), channel_id=1, source_target_pairs={{0,1},{1,0},{2,3},{3,2},{4,5},{5,4},{6,7},{7,6},{8,9},{9,8},{10,11... | collective-permute-start | bytes 18440 | tf_op jit(solution)/shard_map/ppermute | solution.py:768
  221.9 2.3 copy-start.4
  224.2 10.4 %copy-start.24 = (bf16[2,3,96,384]{3,2,1,0:T(8,128)(2,1)S(1)}, bf16[2,3,96,384]{3,2,1,0:T(8,128)(2,1)}, u32[]{:S(2)}) copy-start(bf16[2,3,96,384]{3,2,1,0:T(8,128)(2,1)} %copy-done.23) | copy-start | bytes 1327108
  224.2 10.4 %copy-start.26 = (bf16[2,3,96,384]{3,2,1,0:T(8,128)(2,1)S(1)}, bf16[2,3,96,384]{3,2,1,0:T(8,128)(2,1)}, u32[]{:S(2)}) copy-start(bf16[2,3,96,384]{3,2,1,0:T(8,128)(2,1)} %copy-done.25) | copy-start | bytes 1327108
  232.5 17.2 %collective-permute-start.10 = (bf16[1,2,3,96,384]{4,3,2,1,0:T(8,128)(2,1)S(1)}, bf16[1,2,3,96,384]{4,3,2,1,0:T(8,128)(2,1)S(1)}, u32[]{:S(2)}, u32[]{:S(2)}) collective-permute-start(bf16[1,2,3,96,384]{4,3,2,1,0:T(8,128)(2,1)S(1)} %get-tuple-element.171), channel_id=1, source_target_pairs={{0,1},{1,0},{2,3},{3,2},{4,5},{5,4},{6,7},{7,6},{8,9},{9,8},{10,11... | collective-permute-start | bytes 1327112 | tf_op jit(solution)/shard_map/ppermute | solution.py:695
  234.0 15.7 %collective-permute-start.11 = (bf16[1,2,3,96,384]{4,3,2,1,0:T(8,128)(2,1)S(1)}, bf16[1,2,3,96,384]{4,3,2,1,0:T(8,128)(2,1)S(1)}, u32[]{:S(2)}, u32[]{:S(2)}) collective-permute-start(bf16[1,2,3,96,384]{4,3,2,1,0:T(8,128)(2,1)S(1)} %get-tuple-element.172), channel_id=1, source_target_pairs={{0,4},{2,6},{4,0},{6,2},{8,12},{10,14},{12,8},{14,10},{16,20},{18,... | collective-permute-start | bytes 1327112 | tf_op jit(solution)/shard_map/ppermute | solution.py:695
  234.6 1.4 copy-start.38
  234.6 1.4 copy-start.39
  235.3 14.4 %collective-permute-start.14 = (bf16[6,96,384]{2,1,0:T(8,128)(2,1)S(1)}, bf16[6,96,384]{2,1,0:T(8,128)(2,1)S(1)}, u32[]{:S(2)}, u32[]{:S(2)}) collective-permute-start(bf16[6,96,384]{2,1,0:T(8,128)(2,1)S(1)} %get-tuple-element.183), channel_id=1, source_target_pairs={{0,8},{2,10},{4,12},{6,14},{8,0},{10,2},{12,4},{14,6},{16,24},{18,... | collective-permute-start | bytes 1327112 | tf_op jit(solution)/shard_map/ppermute | solution.py:862
  236.0 3.1 %collective-permute-start.15 = (f32[2,1,768]{2,1,0:T(1,128)S(1)}, f32[2,1,768]{2,1,0:T(1,128)S(1)}, u32[]{:S(2)}, u32[]{:S(2)}) collective-permute-start(f32[2,1,768]{2,1,0:T(1,128)S(1)} %sum_of.8.left), channel_id=1, source_target_pairs={{0,2},{2,0},{4,6},{6,4},{8,10},{10,8},{12,14},{14,12},{16,18},{18,... | collective-permute-start | bytes 18440 | tf_op jit(solution)/shard_map/ppermute | solution.py:768
  237.6 12.1 %collective-permute-start.12 = (bf16[1,3,96,384]{3,2,1,0:T(8,128)(2,1)S(1)}, bf16[1,3,96,384]{3,2,1,0:T(8,128)(2,1)S(1)}, u32[]{:S(2)}, u32[]{:S(2)}) collective-permute-start(bf16[1,3,96,384]{3,2,1,0:T(8,128)(2,1)S(1)} %get-tuple-element.177), channel_id=1, source_target_pairs={{0,4},{2,6},{4,0},{6,2},{8,12},{10,14},{12,8},{14,10},{16,20},{18,... | collective-permute-start | bytes 663560 | tf_op jit(solution)/shard_map/ppermute | solution.py:699
  239.1 10.6 %collective-permute-start.13 = (bf16[1,3,96,384]{3,2,1,0:T(8,128)(2,1)S(1)}, bf16[1,3,96,384]{3,2,1,0:T(8,128)(2,1)S(1)}, u32[]{:S(2)}, u32[]{:S(2)}) collective-permute-start(bf16[1,3,96,384]{3,2,1,0:T(8,128)(2,1)S(1)} %get-tuple-element.178), channel_id=1, source_target_pairs={{0,1},{1,0},{2,3},{3,2},{4,5},{5,4},{6,7},{7,6},{8,9},{9,8},{10,11... | collective-permute-start | bytes 663560 | tf_op jit(solution)/shard_map/ppermute | solution.py:699
  249.7 3.2 %copy-start.36 = (bf16[1,2,3,96,384]{4,3,2,1,0:T(8,128)(2,1)}, bf16[1,2,3,96,384]{4,3,2,1,0:T(8,128)(2,1)S(1)}, u32[]{:S(2)}) copy-start(bf16[1,2,3,96,384]{4,3,2,1,0:T(8,128)(2,1)S(1)} %collective-permute-done.10.one_in) | copy-start | bytes 1327108
  249.7 3.2 %copy-start.37 = (bf16[1,2,3,96,384]{4,3,2,1,0:T(8,128)(2,1)}, bf16[1,2,3,96,384]{4,3,2,1,0:T(8,128)(2,1)S(1)}, u32[]{:S(2)}) copy-start(bf16[1,2,3,96,384]{4,3,2,1,0:T(8,128)(2,1)S(1)} %collective-permute-done.11.two_in) | copy-start | bytes 1327108
  250.3 12.6 %collective-permute-start.18 = (bf16[6,96,384]{2,1,0:T(8,128)(2,1)S(1)}, bf16[6,96,384]{2,1,0:T(8,128)(2,1)S(1)}, u32[]{:S(2)}, u32[]{:S(2)}) collective-permute-start(bf16[6,96,384]{2,1,0:T(8,128)(2,1)S(1)} %join_sum.4.left), channel_id=1, source_target_pairs={{0,8},{2,10},{4,12},{6,14},{16,24},{18,26},{20,28},{22,30},{1,9},{... | collective-permute-start | bytes 1327112 | tf_op jit(solution)/shard_map/ppermute | solution.py:869
  252.9 38.8 %copy-start.15 = (f32[24,96,96]{2,1,0:T(8,128)S(1)}, f32[24,96,96]{2,1,0:T(8,128)}, u32[]{:S(2)}) copy-start(f32[24,96,96]{2,1,0:T(8,128)} %root_right.1) | copy-start | bytes 2654212
  254.6 6.2 %collective-permute-start.16 = (bf16[1,3,96,384]{3,2,1,0:T(8,128)(2,1)S(1)}, bf16[1,3,96,384]{3,2,1,0:T(8,128)(2,1)S(1)}, u32[]{:S(2)}, u32[]{:S(2)}) collective-permute-start(bf16[1,3,96,384]{3,2,1,0:T(8,128)(2,1)S(1)} %get-tuple-element.189), channel_id=1, source_target_pairs={{0,4},{2,6},{4,0},{6,2},{8,12},{10,14},{12,8},{14,10},{16,20},{18,... | collective-permute-start | bytes 663560 | tf_op jit(solution)/shard_map/ppermute | solution.py:699
  255.2 5.9 %collective-permute-start.17 = (bf16[1,3,96,384]{3,2,1,0:T(8,128)(2,1)S(1)}, bf16[1,3,96,384]{3,2,1,0:T(8,128)(2,1)S(1)}, u32[]{:S(2)}, u32[]{:S(2)}) collective-permute-start(bf16[1,3,96,384]{3,2,1,0:T(8,128)(2,1)S(1)} %get-tuple-element.190), channel_id=1, source_target_pairs={{0,1},{1,0},{2,3},{3,2},{4,5},{5,4},{6,7},{7,6},{8,9},{9,8},{10,11... | collective-permute-start | bytes 663560 | tf_op jit(solution)/shard_map/ppermute | solution.py:699
  256.6 4.2 %collective-permute-start.19 = (f32[2,1,768]{2,1,0:T(1,128)S(1)}, f32[2,1,768]{2,1,0:T(1,128)S(1)}, u32[]{:S(2)}, u32[]{:S(2)}) collective-permute-start(f32[2,1,768]{2,1,0:T(1,128)S(1)} %sum_of.9.left), channel_id=1, source_target_pairs={{0,4},{2,6},{4,0},{6,2},{8,12},{10,14},{12,8},{14,10},{16,20},{18,... | collective-permute-start | bytes 18440 | tf_op jit(solution)/shard_map/ppermute | solution.py:768
  257.2 34.4 %copy-start.14 = (f32[24,96,96]{2,1,0:T(8,128)S(1)}, f32[24,96,96]{2,1,0:T(8,128)}, u32[]{:S(2)}) copy-start(f32[24,96,96]{2,1,0:T(8,128)} %root_left.1) | copy-start | bytes 2654212
  257.3 16.8 %collective-permute-start.21 = (bf16[6,96,384]{2,1,0:T(8,128)(2,1)S(1)}, bf16[6,96,384]{2,1,0:T(8,128)(2,1)S(1)}, u32[]{:S(2)}, u32[]{:S(2)}) collective-permute-start(bf16[6,96,384]{2,1,0:T(8,128)(2,1)S(1)} %sum_of.11.high), channel_id=1, source_target_pairs={{0,16},{2,18},{4,20},{6,22},{8,24},{10,26},{12,28},{14,30},{1,17},... | collective-permute-start | bytes 1327112 | tf_op jit(solution)/shard_map/ppermute | solution.py:871
  263.0 28.1 %copy-start.43 = (f32[2,768]{1,0:T(2,128)S(1)}, f32[2,768]{1,0:T(2,128)}, u32[]{:S(2)}) copy-start(f32[2,768]{1,0:T(2,128)} %param.13) | copy-start | bytes 18436
  263.0 28.7 %copy-start.2 = (f32[24,96,96]{2,1,0:T(8,128)S(1)}, f32[24,96,96]{2,1,0:T(8,128)}, u32[]{:S(2)}) copy-start(f32[24,96,96]{2,1,0:T(8,128)} %master.1) | copy-start | bytes 2654212
  263.0 28.7 %copy-start.12 = (f32[24,96,96]{2,1,0:T(8,128)S(1)}, f32[24,96,96]{2,1,0:T(8,128)}, u32[]{:S(2)}) copy-start(f32[24,96,96]{2,1,0:T(8,128)} %stat_left.1) | copy-start | bytes 2654212
  263.0 28.7 %copy-start.13 = (f32[24,96,96]{2,1,0:T(8,128)S(1)}, f32[24,96,96]{2,1,0:T(8,128)}, u32[]{:S(2)}) copy-start(f32[24,96,96]{2,1,0:T(8,128)} %stat_right.1) | copy-start | bytes 2654212
  263.6 10.5 %collective-permute-start.20 = (bf16[6,96,384]{2,1,0:T(8,128)(2,1)S(1)}, bf16[6,96,384]{2,1,0:T(8,128)(2,1)S(1)}, u32[]{:S(2)}, u32[]{:S(2)}) collective-permute-start(bf16[6,96,384]{2,1,0:T(8,128)(2,1)S(1)} %join_sum.5.left), channel_id=1, source_target_pairs={{8,0},{10,2},{12,4},{14,6},{24,16},{26,18},{28,20},{30,22},{9,1},{... | collective-permute-start | bytes 1327112 | tf_op jit(solution)/shard_map/ppermute | solution.py:876
  265.0 9.1 %collective-permute-start.22 = (f32[2,1,768]{2,1,0:T(1,128)S(1)}, f32[2,1,768]{2,1,0:T(1,128)S(1)}, u32[]{:S(2)}, u32[]{:S(2)}) collective-permute-start(f32[2,1,768]{2,1,0:T(1,128)S(1)} %sum_of.10.left), channel_id=1, source_target_pairs={{0,8},{2,10},{4,12},{6,14},{8,0},{10,2},{12,4},{14,6},{16,24},{18,... | collective-permute-start | bytes 18440 | tf_op jit(solution)/shard_map/ppermute | solution.py:768
  267.8 23.8 %collective-permute-start.24 = (bf16[6,96,384]{2,1,0:T(8,128)(2,1)S(1)}, bf16[6,96,384]{2,1,0:T(8,128)(2,1)S(1)}, u32[]{:S(2)}, u32[]{:S(2)}) collective-permute-start(bf16[6,96,384]{2,1,0:T(8,128)(2,1)S(1)} %sum_of.14.one), channel_id=1, source_target_pairs={{24,8},{26,10},{28,12},{30,14},{25,9},{27,11},{29,13},{31,15}} | collective-permute-start | bytes 1327112 | tf_op jit(solution)/shard_map/ppermute | solution.py:878
  274.2 17.4 %collective-permute-start.25 = (bf16[6,96,384]{2,1,0:T(8,128)(2,1)S(1)}, bf16[6,96,384]{2,1,0:T(8,128)(2,1)S(1)}, u32[]{:S(2)}, u32[]{:S(2)}) collective-permute-start(bf16[6,96,384]{2,1,0:T(8,128)(2,1)S(1)} %sum_of.15.zero), channel_id=1, source_target_pairs={{16,0},{18,2},{20,4},{22,6},{17,1},{19,3},{21,5},{23,7}} | collective-permute-start | bytes 1327112 | tf_op jit(solution)/shard_map/ppermute | solution.py:883
  275.5 15.5 %collective-permute-start.23 = (f32[2,1,768]{2,1,0:T(1,128)S(1)}, f32[2,1,768]{2,1,0:T(1,128)S(1)}, u32[]{:S(2)}, u32[]{:S(2)}) collective-permute-start(f32[2,1,768]{2,1,0:T(1,128)S(1)} %sum_of.12.left), channel_id=1, source_target_pairs={{0,16},{2,18},{4,20},{6,22},{8,24},{10,26},{12,28},{14,30},{16,0},... | collective-permute-start | bytes 18440 | tf_op jit(solution)/shard_map/ppermute | solution.py:768
  (7 other events, 5.2 us)
Sparse Core Ops, SparseCore 0:
  11.5 105.8 all-gather.1
where the time goes:
time: 308 us; the launch traced here: 307 us
  waiting for transfers between devices  131 us (43%)
  Pallas kernels  100 us (32%)
  starting transfers between devices  33.9 us (11%)
  local copies, waits for them, and re-layouts  22.8 us (7%)
  between operations  14.6 us (5%)
  other arithmetic  4.32 us (1%)
    all_gather x1, waiting for transfers between devices, gather_weights(): strips = lax.all_gather(strips, EVERY, axis=0, tiled=True)  103 us
    pallas_call x24, Pallas kernels, call(): pl.pallas_call(kernel, grid=grid, in_specs=in_specs, out_specs=[spec for...  100 us
    unnamed x89, local copies, waits for them, and re-layouts  18.5 us
    ppermute x5, waiting for transfers between devices, add_hop(): return run_sum(value, lax.ppermute(value, *hop))  14 us
    ppermute x5, starting transfers between devices, add_hop(): return run_sum(value, lax.ppermute(value, *hop))  11 us
    ppermute x3, waiting for transfers between devices, second_hop(): lax.ppermute(sent[0], 'dp', OTHER_X)  10 us
  transfers between devices with their start and end apart: 27, of which 8 were waited for; matrix products, arithmetic and copies ran while one was open for 2% of the time, Pallas kernels for 15%

commit v1 on v0

--- a/solution.py
+++ b/solution.py
@@ -19,6 +19,8 @@
 OWN = 6
 GROUP = 128
 CAPS = GROUP // SLOTS
+UPPER = (2, 3)
+LOWER = (0, 1)
 PAIR = 2 * HD
 
 EPSILON = 1e-06
@@ -37,9 +39,14 @@
     )
 
 
-def side_by_side(ref, lead, count):
-    parts = [ref[lead + (slice(None), i)].reshape(-1, STRIP) for i in range(count)]
+def weight_of(ref, half, rows, columns):
+    parts = [ref[half, rows, column].reshape(-1, STRIP) for column in columns]
     return jnp.concatenate(parts, axis=1)
+
+
+def out_weight(by_two):
+    halves = [weight_of(by_two, half, slice(12, 16), (0, 1)) for half in range(HALVES)]
+    return jnp.concatenate(halves, axis=0)
 
 
 def norm_parts(values):
@@ -103,21 +110,18 @@
     return pl.ds(pl.multiple_of(i * size, size), size)
 
 
+def pool(values, share):
+    parts = [
+        values[:, i : i + PAIR] * share for i in range(0, values.shape[1], PAIR)
+    ]
+    weighted = jnp.concatenate(parts, axis=1)
+    return jnp.sum(weighted.reshape(-1, SLOTS, values.shape[1]), axis=1)
+
+
 def attention_forward(
-    tok, gains, mask, by_three, by_two, normed, qkv, attended, after, normed_two, w_qkv, w_out, sems
+    tok, gains, mask, share, by_three, by_two, normed, qkv, attended, after, normed_two, after_pooled
 ):
     rows = tok.shape[0]
-    copies = []
-    for half in range(HALVES):
-        copies.append(
-            pltpu.make_async_copy(by_three.at[half, 0:8], w_qkv.at[half], sems.at[half])
-        )
-    for half in range(HALVES):
-        copies.append(
-            pltpu.make_async_copy(by_two.at[half, 12:16], w_out.at[half], sems.at[2 + half])
-        )
-    for copy in copies:
-        copy.start()
 
     @pl.loop(0, rows // GROUP)
     def _(i):
@@ -126,8 +130,7 @@
         normed[span, :] = (xhat * gains[0:1, :]).astype(BF16)
 
     for half in range(HALVES):
-        copies[half].wait()
-        mixed = mm(normed[...], side_by_side(w_qkv, (half,), 3)).astype(BF16)
+        mixed = mm(normed[...], weight_of(by_three, half, slice(0, 8), range(3))).astype(BF16)
         for part in range(3):
             qkv[3 * half + part] = mixed[:, part * STRIP : (part + 1) * STRIP]
 
@@ -149,16 +152,14 @@
                 mixed = mm(expand(probs, caption), qkv[3 * half + 2, span, lanes], 0, 0)
                 attended[span, wide] = join_pair(mixed).astype(BF16)
 
-    copies[2].wait()
-    copies[3].wait()
-    weight = jnp.concatenate([side_by_side(w_out, (half,), 2) for half in range(HALVES)], axis=0)
-    after[...] = mm(attended[...], weight)
+    after[...] = mm(attended[...], out_weight(by_two))
 
     @pl.loop(0, rows // GROUP)
     def _(i):
         span = span_of(i)
         summed = tok[span, :].astype(F32) + after[span, :]
         after[span, :] = summed
+        after_pooled[span_of(i, CAPS), :] = pool(summed, share[span, :])
         xhat, _ = norm_parts(summed)
         normed_two[span, :] = (xhat * gains[1:2, :]).astype(BF16)
 
@@ -192,7 +193,7 @@
             inside = [z for z in planes if z in run]
             if not inside:
                 continue
-            here = True if len(inside) == len(planes) else (plane >= run[0]) & (plane <= run[-1])
+            here = len(inside) == len(planes) or (plane >= run[0]) & (plane <= run[-1])
             spot = (plane - run[0], half, place, strip % OWN)
 
             @pl.when(here & (owner == self.core))
@@ -204,30 +205,33 @@
                 sent[spot] = value
 
 
-def mlp_both(coords, normed_two, out_low, w_up, w_down, *rest):
-    hidden, grad_normed_two, *targets, grad_up = rest
+def mlp_both(coords, normed_two, out_low, share, by_four, by_two, *rest):
+    hidden_pooled, grad_normed_two, *targets, hidden, grad_up = rest
     step = pl.program_id(0)
     rows = normed_two.shape[0]
-    emit = Emitter(targets, ((2, 3), (1,)), coords)
+    emit = Emitter(targets, (UPPER, LOWER), coords)
+    half = step // 2
+    column = lax.rem(step, 2)
 
     @pl.when(step == 0)
     def _():
         grad_normed_two[...] = jnp.zeros_like(grad_normed_two)
 
-    up_weight = side_by_side(w_up, (0,), 2)
-    down_weight = side_by_side(w_down, (0,), 2)
+    up_weight = weight_of(by_four, half, slice(8, 16), (2 * column, 2 * column + 1))
+    down_weight = weight_of(by_two, half, pl.ds(32 + 8 * column, 8), (0, 1))
     chunk = 256
     for i in range(rows // chunk):
         span = slice(i * chunk, (i + 1) * chunk)
         act, slope = gelu_both(mm(normed_two[span, :], up_weight))
-        hidden[step, span, :] = act.astype(BF16)
+        act = act.astype(BF16)
+        hidden[span, :] = act
+        caps = slice(i * chunk // SLOTS, (i + 1) * chunk // SLOTS)
+        hidden_pooled[step, caps, :] = pool(act.astype(F32), share[span, :])
         grad = (mm(out_low[span, :], down_weight, 1, 1) * slope).astype(BF16)
         grad_up[span, :] = grad
         grad_normed_two[span, :] += mm(grad, up_weight, 1, 1)
 
-    half = step // 2
-    column = lax.rem(step, 2)
-    down_grad = mm(hidden[step], out_low[...], 0, 0).astype(BF16)
+    down_grad = mm(hidden[...], out_low[...], 0, 0).astype(BF16)
     up_grad = mm(normed_two[...], grad_up[...], 0, 0).astype(BF16)
     for row in range(8):
         for part in range(2):
@@ -237,38 +241,22 @@
             emit.store(up_grad[block], half, 32 + 4 * row + 2 * column + part, planes)
 
 
-def mlp_out(after, hidden, share, w_down, pooled, total):
-    step = pl.program_id(0)
+def pool_out(after_pooled, hidden_pooled, by_two, pooled):
+    pooled[...] = after_pooled[...]
+    for step in range(4):
+        value = hidden_pooled[step]
+        high = value.astype(BF16)
+        low = (value - high.astype(F32)).astype(BF16)
+        start = 32 + 8 * (step % 2)
+        weight = weight_of(by_two, step // 2, slice(start, start + 8), (0, 1))
+        both = mm(jnp.concatenate([high, low], axis=0), weight)
+        pooled[...] += both[: value.shape[0]] + both[value.shape[0] :]
+
+
+def output_backward(held, coords, gains, attended, after, grad_out, grad_normed_two, by_two, *rest):
+    grad_after, gain_part, grad_att, *targets, after_low = rest[held:]
     rows = after.shape[0]
-    product = mm(hidden[step], side_by_side(w_down, (0,), 2))
-
-    @pl.when(step == 0)
-    def _():
-        total[...] = after[...] + product
-
-    @pl.when(step > 0)
-    def _():
-        total[...] += product
-
-    @pl.when(step == pl.num_programs(0) - 1)
-    def _():
-        @pl.loop(0, rows // GROUP)
-        def _(i):
-            weighted = (total[span_of(i), :] * share[span_of(i), :]).reshape(CAPS, SLOTS, D)
-            pooled[span_of(i, CAPS), :] = jnp.sum(weighted, axis=1)
-
-
-def output_backward(held, coords, gains, attended, after, grad_out, grad_normed_two, by_two, *rest):
-    grad_after, gain_part, grad_att, *targets = rest[held:-3]
-    after_low, w_out, weight_sem = rest[-3:]
-    rows = after.shape[0]
-    emit = Emitter(targets, ((1,),), coords)
-    copies = [
-        pltpu.make_async_copy(by_two.at[half, 12:16], w_out.at[half], weight_sem.at[half])
-        for half in range(HALVES)
-    ]
-    for copy in copies:
-        copy.start()
+    emit = Emitter(targets, (LOWER,), coords)
     gain_part[...] = jnp.zeros_like(gain_part)
 
     @pl.loop(0, rows // GROUP)
@@ -281,10 +269,7 @@
         grad_after[span, :] = value
         after_low[span, :] = value.astype(BF16)
 
-    for copy in copies:
-        copy.wait()
-    weight = jnp.concatenate([side_by_side(w_out, (half,), 2) for half in range(HALVES)], axis=0)
-    grad_att[...] = mm(after_low[...], weight, 1, 1).astype(BF16)
+    grad_att[...] = mm(after_low[...], out_weight(by_two), 1, 1).astype(BF16)
     grad_w = mm(attended[...], after_low[...], 0, 0).astype(BF16)
     for half in range(HALVES):
         for row in range(4):
@@ -297,7 +282,7 @@
 def attention_backward(held, coords, mask, normed, qkv, grad_att, *rest):
     grad_mixed, *targets = rest[held:]
     rows = normed.shape[0]
-    emit = Emitter(targets, ((0,),), coords)
+    emit = Emitter(targets, (LOWER,), coords)
 
     @pl.loop(0, rows // GROUP)
     def _(i):
@@ -337,46 +322,32 @@
                 emit.store(value, half, strip, (0,))
 
 
-def input_backward(tok, gains, grad_mixed, grad_after, gain_two, w_qkv, input_grad, gain_part):
-    half = pl.program_id(0)
+def input_backward(tok, gains, grad_mixed, grad_after, gain_two, by_three, input_grad, gain_part):
     rows = tok.shape[0]
-    grads = jnp.concatenate([grad_mixed[3 * half + part] for part in range(3)], axis=1)
-    back = mm(grads, side_by_side(w_qkv, (0,), 3), 1, 1)
-
-    @pl.when(half == 0)
-    def _():
-        input_grad[...] = back
-
-    @pl.when(half == HALVES - 1)
-    def _():
-        input_grad[...] += back
-        gain_part[0] = jnp.zeros_like(gain_two)
-        gain_part[1] = gain_two[...]
-
-        @pl.loop(0, rows // GROUP)
-        def _(i):
-            span = span_of(i)
-            xhat, inverse = norm_parts(tok[span, :].astype(F32))
-            grad = input_grad[span, :]
-            gain_part[0] += jnp.sum(grad * xhat, axis=0, keepdims=True)
-            input_grad[span, :] = grad_after[span, :] + norm_back(
-                xhat, inverse, gains[0:1, :], grad
-            )
+    grads = jnp.concatenate([grad_mixed[part] for part in range(6)], axis=1)
+    halves = [weight_of(by_three, half, slice(0, 8), range(3)) for half in range(HALVES)]
+    input_grad[...] = mm(grads, jnp.concatenate(halves, axis=1), 1, 1)
+    gain_part[0] = jnp.zeros_like(gain_two)
+    gain_part[1] = gain_two[...]
+
+    @pl.loop(0, rows // GROUP)
+    def _(i):
+        span = span_of(i)
+        xhat, inverse = norm_parts(tok[span, :].astype(F32))
+        grad = input_grad[span, :]
+        gain_part[0] += jnp.sum(grad * xhat, axis=0, keepdims=True)
+        input_grad[span, :] = grad_after[span, :] + norm_back(xhat, inverse, gains[0:1, :], grad)
 
 
 def shape_of(*shape, dtype=BF16):
     return jax.ShapeDtypeStruct(shape, dtype)
 
 
-HBM = pl.BlockSpec(memory_space=pl.ANY)
 VMEM = pl.BlockSpec(memory_space=pltpu.VMEM)
 SMEM = pl.BlockSpec(memory_space=pltpu.SMEM)
 
 
 def call(kernel, name, in_specs, outs, scratch, flops, args, grid=(1,), aliases=None, mib=10):
-    args = tuple(
-        pltpu.with_memory_space_constraint(a, pltpu.HBM) if a.ndim == 5 else a for a in args
-    )
     moved = sum(math_size(a.shape) * a.dtype.itemsize for a in args)
     moved += sum(math_size(s.shape) * s.dtype.itemsize for _, s in outs)
     return pl.pallas_call(
@@ -390,7 +361,7 @@
         compiler_params=pltpu.CompilerParams(
             dimension_semantics=("arbitrary",) * len(grid), vmem_limit_bytes=mib << 20
         ),
-        cost_estimate=pl.CostEstimate(flops=flops, bytes_accessed=moved, transcendentals=0),
+        cost_estimate=pl.CostEstimate(flops=1, bytes_accessed=1, transcendentals=0),
         name=name,
     )(*args)
 
@@ -405,29 +376,28 @@
 UNIT = 2 * 768 * 768 * 768
 
 
-def run_forward(tok, gains, mask, strips):
+def by_count(strips, count):
+    return strips.reshape(HALVES, STRIPS // count, count, BLOCK, STRIP)
+
+
+def run_forward(tok, gains, mask, share, strips):
     rows = tok.shape[0]
-    by_three = strips.reshape(HALVES, 32, 3, BLOCK, STRIP)
-    by_two = strips.reshape(HALVES, 48, 2, BLOCK, STRIP)
     return call(
         attention_forward,
         "attention_forward",
-        [VMEM, VMEM, VMEM, HBM, HBM],
+        [VMEM] * 6,
         [
             (VMEM, shape_of(rows, D)),
             (VMEM, shape_of(6, rows, STRIP)),
             (VMEM, shape_of(rows, D)),
             (VMEM, shape_of(rows, D, dtype=F32)),
             (VMEM, shape_of(rows, D)),
+            (VMEM, shape_of(rows // SLOTS, D, dtype=F32)),
         ],
-        [
-            pltpu.VMEM((HALVES, 8, 3, BLOCK, STRIP), BF16),
-            pltpu.VMEM((HALVES, 4, 2, BLOCK, STRIP), BF16),
-            pltpu.SemaphoreType.DMA((4,)),
-        ],
+        [],
         5 * UNIT,
-        (tok, gains, mask, by_three, by_two),
-        mib=10,
+        (tok, gains, mask, share, by_count(strips, 3), by_count(strips, 2)),
+        mib=3,
     )
 
 
@@ -439,70 +409,55 @@
     return [(VMEM, shape) for shape in shapes]
 
 
-def up_spec():
-    return pl.BlockSpec((1, 8, 2, BLOCK, STRIP), lambda i: (i // 2, 1, i % 2, 0, 0))
-
-
-def down_spec():
-    return pl.BlockSpec((1, 8, 2, BLOCK, STRIP), lambda i: (i // 2, 4 + i % 2, 0, 0, 0))
-
-
-def run_mlp(coords, normed_two, out_low, strips, split):
+def run_mlp(coords, normed_two, out_low, share, strips, split):
     rows = normed_two.shape[0]
-    by_four = strips.reshape(HALVES, 24, 4, BLOCK, STRIP)
-    by_two = strips.reshape(HALVES, 48, 2, BLOCK, STRIP)
     return call(
         mlp_both,
         "mlp_both",
-        [SMEM, VMEM, VMEM, up_spec(), down_spec()],
-        [(VMEM, shape_of(4, rows, D)), (VMEM, shape_of(rows, D, dtype=F32))]
-        + targets_of(((2, 3), (1,)), split),
-        [pltpu.VMEM((rows, D), BF16)],
+        [SMEM] + [VMEM] * 5,
+        [
+            (VMEM, shape_of(4, rows // SLOTS, D, dtype=F32)),
+            (VMEM, shape_of(rows, D, dtype=F32)),
+        ]
+        + targets_of((UPPER, LOWER), split),
+        [pltpu.VMEM((rows, D), BF16), pltpu.VMEM((rows, D), BF16)],
         20 * UNIT,
-        (coords, normed_two, out_low, by_four, by_two),
+        (coords, normed_two, out_low, share, by_count(strips, 4), by_count(strips, 2)),
         grid=(4,),
-        mib=16,
-    )
-
-
-def run_mlp_out(after, hidden, share, strips):
-    rows = after.shape[0]
-    by_two = strips.reshape(HALVES, 48, 2, BLOCK, STRIP)
-    return call(
-        mlp_out,
-        "mlp_out",
-        [VMEM, VMEM, VMEM, down_spec()],
-        [(VMEM, shape_of(rows // SLOTS, D, dtype=F32))],
-        [pltpu.VMEM((rows, D), F32)],
-        4 * UNIT,
-        (after, hidden, share, by_two),
-        grid=(4,),
-        mib=8,
+        mib=7,
+    )
+
+
+def run_pool(after_pooled, hidden_pooled, strips):
+    return call(
+        pool_out,
+        "pool_out",
+        [VMEM] * 3,
+        [(VMEM, jax.ShapeDtypeStruct(after_pooled.shape, F32))],
+        [],
+        UNIT // 2,
+        (after_pooled, hidden_pooled, by_count(strips, 2)),
+        mib=4,
     )[0]
 
 
 def run_output(coords, gains, attended, after, grad_out, grad_two, strips, held, split):
     rows = after.shape[0]
-    by_two = strips.reshape(HALVES, 48, 2, BLOCK, STRIP)
     return call(
         functools.partial(output_backward, len(held)),
         "output_backward",
-        [SMEM, VMEM, VMEM, VMEM, VMEM, VMEM, HBM] + [VMEM] * len(held),
+        [SMEM] + [VMEM] * (6 + len(held)),
         [
             (VMEM, shape_of(rows, D, dtype=F32)),
             (VMEM, shape_of(1, D, dtype=F32)),
             (VMEM, shape_of(rows, D)),
         ]
-        + targets_of(((1,),), split),
-        [
-            pltpu.VMEM((rows, D), BF16),
-            pltpu.VMEM((HALVES, 4, 2, BLOCK, STRIP), BF16),
-            pltpu.SemaphoreType.DMA((HALVES,)),
-        ],
+        + targets_of((LOWER,), split),
+        [pltpu.VMEM((rows, D), BF16)],
         2 * UNIT,
-        (coords, gains, attended, after, grad_out, grad_two, by_two, *held),
+        (coords, gains, attended, after, grad_out, grad_two, by_count(strips, 2), *held),
         aliases={7 + i: 3 + i for i in range(len(held))},
-        mib=12,
+        mib=6,
     )
 
 
@@ -512,38 +467,26 @@
         functools.partial(attention_backward, len(held)),
         "attention_backward",
         [SMEM, VMEM, VMEM, VMEM, VMEM] + [VMEM] * len(held),
-        [(VMEM, shape_of(6, rows, STRIP))] + targets_of(((0,),), split),
+        [(VMEM, shape_of(6, rows, STRIP))] + targets_of((LOWER,), split),
         [],
         7 * UNIT,
         (coords, mask, normed, qkv, grad_att, *held),
         aliases={5 + i: 1 + i for i in range(len(held))},
-        mib=8,
+        mib=6,
     )
 
 
 def run_input(tok, gains, grad_mixed, grad_after, gain_two, strips):
     rows = tok.shape[0]
-    by_three = strips.reshape(HALVES, 32, 3, BLOCK, STRIP)
     return call(
         input_backward,
         "input_backward",
-        [
-            VMEM,
-            VMEM,
-            VMEM,
-            VMEM,
-            VMEM,
-            pl.BlockSpec((1, 8, 3, BLOCK, STRIP), lambda i: (i, 0, 0, 0, 0)),
-        ],
-        [
-            (VMEM, shape_of(rows, D, dtype=F32)),
-            (VMEM, shape_of(2, 1, D, dtype=F32)),
-        ],
+        [VMEM] * 6,
+        [(VMEM, shape_of(rows, D, dtype=F32)), (VMEM, shape_of(2, 1, D, dtype=F32))],
         [],
         3 * UNIT,
-        (tok, gains, grad_mixed, grad_after, gain_two, by_three),
-        grid=(HALVES,),
-        mib=10,
+        (tok, gains, grad_mixed, grad_after, gain_two, by_count(strips, 3)),
+        mib=5,
     )
 
 
@@ -571,6 +514,146 @@
     return to_strips(blocks).reshape(HALVES, STRIPS, BLOCK, STRIP)
 
 
+def pack(master, out):
+    for strip in range(master.shape[0] // 4):
+        parts = [master[4 * strip + i].astype(BF16) for i in range(4)]
+        out[0, strip] = jnp.concatenate(parts, axis=1)
+
+
+def take_halves(by_x, by_y, from_x, from_y):
+    for plane in range(by_x.shape[0]):
+        from_x[plane] = by_x[plane, 0:3]
+        from_y[plane] = by_y[plane, 3:6]
+
+
+def take_both(one, two, out):
+    out[0] = one[0]
+    out[1] = two[0]
+
+
+def place_own(held, planes, coords, own, by_x, by_y, across_one, across_two, *rest):
+    whole, sent = rest[held:]
+    core, place, plane, half = coords[0], coords[1], coords[2], coords[3]
+    for i, apart in enumerate(planes):
+        z = plane ^ apart
+
+        def put(y, x, strips, value):
+            sent[i, y, x, strips] = value
+            whole[y, z, x, core, strips] = value
+
+        put(half, place, slice(0, 6), own[i])
+        put(half, 1 - place, slice(0, 6), by_x[i])
+        put(1 - half, place, slice(0, 6), by_y[i])
+        put(1 - half, 1 - place, slice(0, 3), across_one[i])
+        put(1 - half, 1 - place, slice(3, 6), across_two[i])
+
+
+def place_other(planes, coords, arrived, _, whole):
+    core, plane = coords[0], coords[2]
+    for i, apart in enumerate(planes):
+        for y in range(2):
+            for x in range(2):
+                whole[y, plane ^ apart, x, 1 - core] = arrived[i, y, x]
+
+
+WHOLE = (HALVES, 4, 2, 2, OWN, BLOCK, STRIP)
+
+
+def run_pack(master):
+    return call(
+        pack,
+        "pack",
+        [VMEM],
+        [(VMEM, shape_of(1, OWN, BLOCK, STRIP))],
+        [],
+        math_size(master.shape),
+        (master,),
+        mib=4,
+    )[0]
+
+
+def run_halves(by_x, by_y):
+    shape = shape_of(by_x.shape[0], 3, BLOCK, STRIP)
+    return call(
+        take_halves, "take_halves", [VMEM] * 2, [(VMEM, shape)] * 2, [], 1, (by_x, by_y), mib=4
+    )
+
+
+def run_both(one, two):
+    shape = shape_of(2, OWN, BLOCK, STRIP)
+    return call(take_both, "take_both", [VMEM] * 2, [(VMEM, shape)], [], 1, (one, two), mib=4)[0]
+
+
+def run_place_own(planes, coords, pieces, held):
+    count = len(planes)
+    return call(
+        functools.partial(place_own, len(held), planes),
+        "place_own",
+        [SMEM] + [VMEM] * (5 + len(held)),
+        [(VMEM, shape_of(*WHOLE)), (VMEM, shape_of(count, HALVES, 2, OWN, BLOCK, STRIP))],
+        [],
+        1,
+        (coords, *pieces, *held),
+        aliases={6: 0} if held else None,
+        mib=4,
+    )
+
+
+def run_place_other(planes, coords, arrived, whole):
+    return call(
+        functools.partial(place_other, planes),
+        "place_other",
+        [SMEM] + [VMEM] * 2,
+        [(VMEM, shape_of(*WHOLE))],
+        [],
+        1,
+        (coords, arrived, whole),
+        aliases={2: 0},
+        mib=4,
+    )[0]
+
+
+def neighbour_hop(value):
+    return lax.ppermute(value, "dp", OTHER_X), lax.ppermute(value, "tensor", OTHER_Y)
+
+
+def across_hop(pieces):
+    return lax.ppermute(pieces[0], "tensor", OTHER_Y), lax.ppermute(pieces[1], "dp", OTHER_X)
+
+
+def gather_split(master, coords, prepare):
+    own = run_pack(master)
+    near = lax.ppermute(own, "dp", NEAR_Z)
+    far = lax.ppermute(own, "dp", FAR_Z)
+    own_by = neighbour_hop(own)
+    own_by, near, far, own, prepared = fence(own_by, near, far, own, prepare())
+
+    other = lax.ppermute(near, "dp", FAR_Z)
+    own_across = across_hop(run_halves(*own_by))
+    both = run_both(near, far)
+    both_by = neighbour_hop(both)
+    own_across, both_by, other = fence(own_across, both_by, other)
+
+    other_by = neighbour_hop(other)
+    both_across = across_hop(run_halves(*both_by))
+    whole, sent = run_place_own((0,), coords, (own, *own_by, *own_across), ())
+    own_in = core_hop(sent)
+    both_across, other_by, own_in, whole = fence(both_across, other_by, own_in, whole)
+
+    other_across = across_hop(run_halves(*other_by))
+    whole, sent = run_place_own((1, 2), coords, (both, *both_by, *both_across), (whole,))
+    both_in = core_hop(sent)
+    whole = run_place_other((0,), coords, own_in, whole)
+    other_across, both_in, whole = fence(other_across, both_in, whole)
+
+    whole, sent = run_place_own((3,), coords, (other, *other_by, *other_across), (whole,))
+    other_in = core_hop(sent)
+    whole = run_place_other((1, 2), coords, both_in, whole)
+    other_in, whole = fence(other_in, whole)
+    whole = run_place_other((3,), coords, other_in, whole)
+    return whole.reshape(HALVES, STRIPS, BLOCK, STRIP), prepared
+
+
 def scatter_flat(strips, own):
     if own % 4 == 0:
         mine = lax.psum_scatter(
@@ -594,6 +677,10 @@
     return [(4 * a + i, 4 * b + i) for a, b in moves for i in range(4)]
 
 
+NEAR_Z = by_plane((0, 1), (1, 0), (2, 3), (3, 2))
+FAR_Z = by_plane((0, 2), (1, 3), (2, 0), (3, 1))
+
+
 def split_sum(coords, kept, arrived, sent_one, sent_two, kept_one, kept_two):
     place, half = coords[1], coords[3]
 
@@ -620,7 +707,7 @@
 
 def join_sum(coords, one, two, one_in, two_in, *outs):
     for i, out in enumerate(outs):
-        plane = 0 if len(outs) == 1 else lax.rem(coords[2] + i, 2)
+        plane = lax.rem(coords[2] + i, 2)
         out[0:3] = one[plane] + one_in[plane]
         out[3:6] = two[plane] + two_in[plane]
 
@@ -666,7 +753,7 @@
         join_sum,
         "join_sum",
         [SMEM] + [VMEM] * 4,
-        [(VMEM, shape_of(OWN, BLOCK, STRIP))] * kept[0].shape[0],
+        [(VMEM, shape_of(OWN, BLOCK, STRIP))] * 2,
         [],
         2 * math_size(kept[0].shape),
         (coords, *kept, *arrived),
@@ -710,15 +797,13 @@
 
 
 def update(
-    coords, high, high_in, one, one_in, zero, zero_in, master, stat_left, stat_right, root_left, root_right, *outs
+    coords, high, high_in, low, low_in, master, stat_left, stat_right, root_left, root_right, *outs
 ):
     grad_out, left_out, right_out, master_out, copy_out, grad = outs
-    plane = coords[2]
     strip = pl.program_id(0)
     for condition, own, arrived in (
-        (plane >= 2, high, high_in),
-        (plane == 1, one, one_in),
-        (plane == 0, zero, zero_in),
+        (coords[2] >= 2, high, high_in),
+        (coords[2] < 2, low, low_in),
     ):
 
         @pl.when(condition)
@@ -750,7 +835,7 @@
         12 * 2 * count * BLOCK**3,
         (coords, *sums, *blocks),
         grid=(count // 4,),
-        mib=12,
+        mib=4,
     )
 
 
@@ -799,16 +884,27 @@
     split = lax.axis_size("dp") == 16 and lax.axis_size("tensor") == 2
     dp_pos, half = lax.axis_index("dp"), lax.axis_index("tensor")
     coords = jnp.stack([dp_pos % 2, dp_pos // 2 % 2, dp_pos // 4, half]).astype(jnp.int32)
-    strips = gather_weights(master)
-    group_mask = token_mask.astype(F32)
-    own_mask = lax.dynamic_slice_in_dim(group_mask, half * own_caps, own_caps, 0)
-    share = (own_mask / jnp.sum(own_mask, axis=1, keepdims=True)).reshape(rows, 1)
-    mask = jnp.repeat(own_mask.reshape(rows // GROUP, CAPS, SLOTS), SLOTS, axis=1).swapaxes(1, 2)
-    cot = cotangent.astype(F32)
-    grad_out = (cot[:, None, :] * share.reshape(own_caps, SLOTS, 1)).reshape(rows, D)
-    out_low = grad_out.astype(BF16)
-    normed, qkv, attended, after, normed_two = run_forward(tokens, norm_gains, mask, strips)
-    hidden, grad_two, *held = run_mlp(coords, normed_two, out_low, strips, split)
+
+    def prepare():
+        group_mask = token_mask.astype(F32)
+        own_mask = lax.dynamic_slice_in_dim(group_mask, half * own_caps, own_caps, 0)
+        share = 1.0 / jnp.sum(own_mask, axis=1, keepdims=True)
+        mask = jnp.repeat(own_mask.reshape(rows // GROUP, CAPS, SLOTS), SLOTS, axis=1)
+        weight = own_mask * share
+        grad_out = cotangent.astype(F32)[:, None, :] * weight[:, :, None]
+        wide = jnp.broadcast_to(weight[:, :, None], (own_caps, SLOTS, PAIR)).reshape(rows, PAIR)
+        grad_out = grad_out.reshape(rows, D)
+        return mask.swapaxes(1, 2), wide, grad_out, grad_out.astype(BF16)
+
+    if split:
+        strips, prepared = gather_split(master, coords, prepare)
+    else:
+        strips, prepared = gather_weights(master), prepare()
+    mask, share, grad_out, out_low = prepared
+    normed, qkv, attended, after, normed_two, after_pooled = run_forward(
+        tokens, norm_gains, mask, share, strips
+    )
+    hidden_pooled, grad_two, *held = run_mlp(coords, normed_two, out_low, share, strips, split)
     hops = sum_hops()
     blocks = (master, stat_left, stat_right, root_left, root_right)
     if not split:
@@ -819,70 +915,63 @@
         input_grad, gain_grads = run_input(
             tokens, norm_gains, grad_mixed, grad_after, gain_two, strips
         )
-        pooled = run_mlp_out(after, hidden, share, strips)
+        pooled = run_pool(after_pooled, hidden_pooled, strips)
         for hop in hops:
             gain_grads = add_hop(gain_grads, hop)
         updated = plain_update(scatter_flat(held[0], own), *blocks)
     else:
-        upper_kept, upper_sent, one_kept, one_sent = held
+        upper_kept, upper_sent, *lower = held
         upper_in = core_hop(upper_sent)
-        grad_after, gain_two, grad_att, *one = run_output(
-            coords, norm_gains, attended, after, grad_out, grad_two, strips, (one_kept, one_sent), split
+        grad_after, gain_two, grad_att, *lower = run_output(
+            coords, norm_gains, attended, after, grad_out, grad_two, strips, lower, split
         )
-        upper_in, grad_att, one = fence(upper_in, grad_att, one)
+        upper_in, grad_att, lower = fence(upper_in, grad_att, lower)
 
         upper_sent, upper_kept = run_split(coords, upper_kept, upper_in)
-        upper_sent, grad_att, one = fence(upper_sent, grad_att, one)
+        upper_sent, grad_att, lower = fence(upper_sent, grad_att, lower)
         upper_in = first_hop(upper_sent)
-        one_in = core_hop(one[1])
-        grad_mixed, *zero = run_backward(coords, mask, normed, qkv, grad_att, [], split)
-        upper_in, one_in, grad_mixed, zero = fence(upper_in, one_in, grad_mixed, zero)
-
+        grad_mixed, *lower = run_backward(coords, mask, normed, qkv, grad_att, lower, split)
+        upper_in, grad_mixed, lower = fence(upper_in, grad_mixed, lower)
+
+        lower_in = core_hop(lower[1])
         upper_sent, upper_kept = run_again(coords, upper_kept, upper_in)
-        one_sent, one_kept = run_split(coords, one[0], one_in)
-        upper_sent, one_sent, zero, grad_mixed = fence(upper_sent, one_sent, zero, grad_mixed)
-        zero_in = core_hop(zero[1])
         upper_in = second_hop(upper_sent)
-        one_in = first_hop(one_sent)
+        lower_in, upper_sent, grad_mixed = fence(lower_in, upper_sent, grad_mixed)
+
+        lower_sent, lower_kept = run_split(coords, lower[0], lower_in)
+        lower_sent, grad_mixed = fence(lower_sent, grad_mixed)
+        lower_in = first_hop(lower_sent)
         input_grad, gain_grads = run_input(
             tokens, norm_gains, grad_mixed, grad_after, gain_two, strips
         )
-        zero_in, gain_grads, hidden = fence(zero_in, gain_grads, hidden)
-
-        zero_sent, zero_kept = run_split(coords, zero[0], zero_in)
-        zero_sent, gain_grads, hidden = fence(zero_sent, gain_grads, hidden)
-        zero_in = first_hop(zero_sent)
-        gain_grads = add_hop(gain_grads, hops[0])
-        pooled = run_mlp_out(after, hidden, share, strips)
-        upper_in, one_in, gain_grads, pooled = fence(upper_in, one_in, gain_grads, pooled)
-
-        one_sent, one_kept = run_again(coords, one_kept, one_in)
-        one_in = second_hop(one_sent)
-        high, other = run_join(coords, upper_kept, upper_in)
-        high_in = lax.ppermute(other, "dp", by_plane((0, 1), (1, 0), (2, 3), (3, 2)))
-        gain_grads = add_hop(gain_grads, hops[1])
-        zero_in, one_in, high_in, gain_grads = fence(zero_in, one_in, high_in, gain_grads)
-
-        zero_sent, zero_kept = run_again(coords, zero_kept, zero_in)
-        zero_in = second_hop(zero_sent)
-        (one_sum,) = run_join(coords, one_kept, one_in)
-        one_in = lax.ppermute(one_sum, "dp", by_plane((0, 1), (2, 3)))
+        upper_in, gain_grads = fence(upper_in, gain_grads)
+
+        high, high_sent = run_join(coords, upper_kept, upper_in)
+        high_in = lax.ppermute(high_sent, "dp", NEAR_Z)
+        gain_in = lax.ppermute(gain_grads, *hops[0])
+        pooled = run_pool(after_pooled, hidden_pooled, strips)
+        high_in, lower_in, gain_in, pooled = fence(high_in, lower_in, gain_in, pooled)
+
+        lower_sent, lower_kept = run_again(coords, lower_kept, lower_in)
+        lower_in = second_hop(lower_sent)
         high = run_sum(high, high_in)
         high_in = lax.ppermute(high, "dp", by_plane((0, 2), (1, 3)))
-        gain_grads = add_hop(gain_grads, hops[2])
-        zero_in, one_in, gain_grads = fence(zero_in, one_in, gain_grads)
-
-        (zero_sum,) = run_join(coords, zero_kept, zero_in)
-        zero_in = lax.ppermute(zero_sum, "dp", by_plane((1, 0), (3, 2)))
-        one_sum = run_sum(one_sum, one_in)
-        one_in = lax.ppermute(one_sum, "dp", by_plane((3, 1)))
-        gain_grads = add_hop(gain_grads, hops[3])
-        zero_in, high_in, gain_grads = fence(zero_in, high_in, gain_grads)
-
-        zero_sum = run_sum(zero_sum, zero_in)
-        zero_in = lax.ppermute(zero_sum, "dp", by_plane((2, 0)))
-        gain_grads = add_hop(gain_grads, hops[4])
-        updated = run_update(coords, (high, high_in, one_sum, one_in, zero_sum, zero_in), blocks)
+        gain_grads = run_sum(gain_grads, gain_in)
+        gain_in = lax.ppermute(gain_grads, *hops[1])
+        lower_in, gain_in = fence(lower_in, gain_in)
+
+        low, low_sent = run_join(coords, lower_kept, lower_in)
+        low_in = lax.ppermute(low_sent, "dp", NEAR_Z)
+        gain_grads = run_sum(gain_grads, gain_in)
+        gain_in = lax.ppermute(gain_grads, *hops[2])
+        low_in, gain_in = fence(low_in, gain_in)
+
+        low = run_sum(low, low_in)
+        low_in = lax.ppermute(low, "dp", by_plane((2, 0), (3, 1)))
+        gain_grads = run_sum(gain_grads, gain_in)
+        for hop in hops[3:]:
+            gain_grads = add_hop(gain_grads, hop)
+        updated = run_update(coords, (high, high_in, low, low_in), blocks)
     gain_grads = gain_grads.reshape(2, D)
     moments_new = DECAY_RATE * gain_moments + (1.0 - DECAY_RATE) * gain_grads * gain_grads
     gains_new = norm_gains - GAIN_RATE * gain_grads / (jnp.sqrt(moments_new) + 1e-08)

time: 308 us -> 260 us (0.84)
  waiting for transfers between devices: 131 us -> 97.9 us
  starting transfers between devices: 33.9 us -> 55.1 us
  local copies, waits for them, and re-layouts: 22.8 us -> 3.41 us
  between operations: 14.6 us -> 1.07 us
    all_gather x1 -> x0, waiting for transfers between devices: 103 us -> none  [gather_weights(): strips = lax.all_gather(strips, EVERY, axis=0, tiled=True)]
    ppermute x5 -> x21, waiting for transfers between devices: 1.86 us -> 69.8 us  [the longest x3 30.8 us: across_hop(): lax.ppermute(pieces[0], 'tensor', OTHER_Y)]
    ppermute x5 -> x21, starting transfers between devices: 6.62 us -> 27.6 us  [the longest x3 4.23 us: neighbour_hop(): lax.ppermute(value, 'dp', OTHER_X)]
    unnamed x89 -> x23, local copies, waits for them, and re-layouts: 18.5 us -> 1.41 us
    ppermute x3 -> x5, waiting for transfers between devices: 0.01 us -> 6.38 us  [core_hop(): return lax.ppermute(sent, 'dp', OTHER_CORE)]
    ppermute x5 -> x2, waiting for transfers between devices: 14 us -> 9.36 us  [add_hop(): return run_sum(value, lax.ppermute(value, *hop))]
    pallas_call x24 -> x31, Pallas kernels: 100 us -> 97.2 us  [call(): pl.pallas_call(kernel, grid=grid, in_specs=in_specs, out_specs=[spec for...]
    ppermute x3 -> x2, waiting for transfers between devices: 10 us -> 8.25 us  [second_hop(): lax.ppermute(sent[0], 'dp', OTHER_X)]
  transfers between devices with their start and end apart: 27 -> 37, of which waited for: 8 -> 22; matrix products, arithmetic and copies ran while one was open for 2% -> 2% of each run, Pallas kernels for 15% -> 14%
where the time goes in v1:
time: 260 us; the launch traced here: 259 us
  waiting for transfers between devices  97.9 us (38%)
  Pallas kernels  97.2 us (37%)
  starting transfers between devices  55.1 us (21%)
  other arithmetic  4.33 us (2%)
  local copies, waits for them, and re-layouts  3.41 us (1%)
    pallas_call x31, Pallas kernels, call(): pl.pallas_call(kernel, grid=grid, in_specs=in_specs, out_specs=[spec for...  97.2 us
    ppermute x3, waiting for transfers between devices, across_hop(): lax.ppermute(pieces[0], 'tensor', OTHER_Y)  30.8 us
    ppermute x1, waiting for transfers between devices, body(): gain_in = lax.ppermute(gain_grads, *hops[0])  12.5 us
    ppermute x2, starting transfers between devices, add_hop(): return run_sum(value, lax.ppermute(value, *hop))  12 us
    ppermute x1, waiting for transfers between devices, gather_split(): far = lax.ppermute(own, 'dp', FAR_Z)  10.7 us
    ppermute x2, waiting for transfers between devices, add_hop(): return run_sum(value, lax.ppermute(value, *hop))  9.36 us
    ppermute x2, waiting for transfers between devices, second_hop(): lax.ppermute(sent[0], 'dp', OTHER_X)  8.25 us
    ppermute x3, waiting for transfers between devices, neighbour_hop(): lax.ppermute(value, 'tensor', OTHER_Y)  7.55 us
  transfers between devices with their start and end apart: 37, of which 22 were waited for; matrix products, arithmetic and copies ran while one was open for 2% of the time, Pallas kernels for 14%

profile of v1, /device:TPU:0, one launch (start us, length us, event | category | flops | bytes accessed | tf_op | source)
XLA Modules:
  0.0 259.0 jit_solution(8667219266254663496)
XLA Ops:
  0.7 1.3 copy-done.1
  1.9 0.9 pack.1.own
  2.9 4.0 %collective-permute-start.3 = (bf16[1,6,96,384]{3,2,1,0:T(8,128)(2,1)}, bf16[1,6,96,384]{3,2,1,0:T(8,128)(2,1)}, u32[]{:S(2)}, u32[]{:S(2)}) collective-permute-start(bf16[1,6,96,384]{3,2,1,0:T(8,128)(2,1)} %pack.1.own), channel_id=1, source_target_pairs={{0,16},{2,18},{4,20},{6,22},{8,24},{10,26},{12,28},{14,30},{16,0},... | collective-permute-start | bytes 1327112 | tf_op jit(solution)/shard_map/ppermute | solution.py:627
  6.9 1.6 collective-permute-start.2
  8.5 1.5 collective-permute-start.1
  10.0 1.5 collective-permute-start
  12.6 1.6 convert_element_type.10
  15.1 1.2 fusion
  16.3 10.7 %collective-permute-done.3.two = bf16[1,6,96,384]{3,2,1,0:T(8,128)(2,1)} collective-permute-done((bf16[1,6,96,384]{3,2,1,0:T(8,128)(2,1)}, bf16[1,6,96,384]{3,2,1,0:T(8,128)(2,1)}, u32[]{:S(2)}, u32[]{:S(2)}) %collective-permute-start.3) | collective-permute-done | bytes 442400 | tf_op jit(solution)/shard_map/ppermute | solution.py:627
  27.2 0.9 broadcast_in_dim.16.share
  28.1 2.1 take_both.1.own
  30.2 1.6 collective-permute-start.7
  31.8 1.5 collective-permute-start.6
  33.3 1.3 collective-permute-start.8
  34.6 1.9 take_halves.3
  37.6 18.2 %collective-permute-done.4.across_one = bf16[1,3,96,384]{3,2,1,0:T(8,128)(2,1)} collective-permute-done((bf16[1,3,96,384]{3,2,1,0:T(8,128)(2,1)}, bf16[1,3,96,384]{3,2,1,0:T(8,128)(2,1)}, u32[]{:S(2)}, u32[]{:S(2)}) %collective-permute-start.4) | collective-permute-done | bytes 221216 | tf_op jit(solution)/shard_map/ppermute | solution.py:621
  55.9 1.0 collective-permute-done.5.across_two
  56.9 1.8 place_own.3
  58.7 0.8 collective-permute-start.12
  59.5 1.2 collective-permute-start.11
  60.8 1.5 take_halves.4
  62.3 1.6 collective-permute-start.9
  64.4 7.5 %collective-permute-done.12.by_y = bf16[1,6,96,384]{3,2,1,0:T(8,128)(2,1)S(1)} collective-permute-done((bf16[1,6,96,384]{3,2,1,0:T(8,128)(2,1)}, bf16[1,6,96,384]{3,2,1,0:T(8,128)(2,1)S(1)}, u32[]{:S(2)}, u32[]{:S(2)}) %collective-permute-start.12) | collective-permute-done | bytes 442400 | tf_op jit(solution)/shard_map/ppermute | solution.py:617
  72.8 8.2 %collective-permute-done.9.across_one = bf16[2,3,96,384]{3,2,1,0:T(8,128)(2,1)S(1)} collective-permute-done((bf16[2,3,96,384]{3,2,1,0:T(8,128)(2,1)S(1)}, bf16[2,3,96,384]{3,2,1,0:T(8,128)(2,1)S(1)}, u32[]{:S(2)}, u32[]{:S(2)}) %collective-permute-start.9) | collective-permute-done | bytes 442400 | tf_op jit(solution)/shard_map/ppermute | solution.py:621
  81.5 2.3 place_own.4
  83.9 1.3 collective-permute-start.14
  85.3 1.5 collective-permute-start.15
  87.5 4.4 %collective-permute-done.14.across_one = bf16[1,3,96,384]{3,2,1,0:T(8,128)(2,1)S(1)} collective-permute-done((bf16[1,3,96,384]{3,2,1,0:T(8,128)(2,1)S(1)}, bf16[1,3,96,384]{3,2,1,0:T(8,128)(2,1)S(1)}, u32[]{:S(2)}, u32[]{:S(2)}) %collective-permute-start.14) | collective-permute-done | bytes 221216 | tf_op jit(solution)/shard_map/ppermute | solution.py:621
  91.8 1.0 collective-permute-done.15.across_two
  92.8 1.3 place_own.5
  94.2 0.9 place_other.4._
  95.1 2.8 %collective-permute-done.17.arrived = bf16[1,2,2,6,96,384]{5,4,3,2,1,0:T(8,128)(2,1)S(1)} collective-permute-done((bf16[1,2,2,6,96,384]{5,4,3,2,1,0:T(8,128)(2,1)S(1)}, bf16[1,2,2,6,96,384]{5,4,3,2,1,0:T(8,128)(2,1)S(1)}, u32[]{:S(2)}, u32[]{:S(2)}) %collective-permute-start.17) | collective-permute-done | bytes 1769504 | tf_op jit(solution)/shard_map/ppermute | solution.py:778
  98.7 12.4 %attention_forward.1 = (bf16[768,768]{1,0:T(8,128)(2,1)S(1)}, bf16[6,768,384]{2,1,0:T(8,128)(2,1)S(1)}, bf16[768,768]{1,0:T(8,128)(2,1)S(1)}, f32[768,768]{1,0:T...) custom-call(bf16[768,768]{1,0:T(8,128)(2,1)S(1)} %copy-done, f32[2,768]{1,0:T(2,128)S(1)} %copy-done.9, ...), custom_call_target="tpu_custom_call" | custom-call | flops 1 | bytes 1 | tf_op jit(solution)/shard_map/attention_forward/pallas_call | solution.py:353
  111.1 27.2 %mlp_both.1 = (f32[4,48,768]{2,1,0:T(8,128)S(1)}, f32[768,768]{1,0:T(8,128)S(1)}, bf16[2,2,2,6,96,384]{5,4,3,2,1,0:T(8,128)(2,1)S(1)}, bf16[2,2,2,6,96,384]{5,4,...) custom-call(s32[4]{0:T(128)S(1)} %pad_add_fusion.coords, ...), custom_call_target="tpu_custom_call" | custom-call | flops 1 | bytes 1 | tf_op jit(solution)/shard_map/mlp_both/pallas_call | solution.py:353
  138.5 5.1 %output_backward.1 = (f32[768,768]{1,0:T(8,128)S(1)}, f32[1,768]{1,0:T(1,128)S(1)}, bf16[768,768]{1,0:T(8,128)(2,1)S(1)}, bf16[2,2,2,6,96,384]{5,4,3,2,1,0:T(8,128)(2,1)S(1)}, bf16[2,2,2,6,96,384]{5,4,3,2,1,0:T(8,128)(2,1)S(1)}) custom-call(s32[4]{0:T(128)S(1)} %pad_add_fusion.coords, ...), custom_call_target="tpu_custom_call", output_to_operand_aliasing={{3}: (7, {}), {4}: (8, {})} | custom-call | flops 1 | bytes 1 | tf_op jit(solution)/shard_map/output_backward/pallas_call | solution.py:353
  143.5 1.0 collective-permute-done.18.arrived
  144.6 1.1 split_sum.2
  146.5 1.2 collective-permute-start.20
  147.7 16.6 %attention_backward.1 = (bf16[6,768,384]{2,1,0:T(8,128)(2,1)S(1)}, bf16[2,2,2,6,96,384]{5,4,3,2,1,0:T(8,128)(2,1)S(1)}, bf16[2,2,2,6,96,384]{5,4,3,2,1,0:T(8,128)(2,1)S(1)}) custom-call(s32[4]{0:T(128)S(1)} %pad_add_fusion.coords, f32[6,16,128]{2,1,0:T(8,128)S(1)} %bitcast.28, ...), custom_call_target="tpu_custom_call", output_to_operand_aliasing={{1}: (5, {}), {2}: (6, {})} | custom-call | flops 1 | bytes 1 | tf_op jit(solution)/shard_map/attention_backward/pallas_call | solution.py:353
  164.3 3.1 %collective-permute-done.19.one_in = bf16[2,2,3,96,384]{4,3,2,1,0:T(8,128)(2,1)S(1)} collective-permute-done((bf16[2,2,3,96,384]{4,3,2,1,0:T(8,128)(2,1)S(1)}, bf16[2,2,3,96,384]{4,3,2,1,0:T(8,128)(2,1)S(1)}, u32[]{:S(2)}, u32[]{:S(2)}) %collective-permute-start.19) | collective-permute-done | bytes 884768 | tf_op jit(solution)/shard_map/ppermute | solution.py:782
  168.7 1.3 collective-permute-start.21
  170.0 1.5 collective-permute-start.22
  171.5 2.6 collective-permute-done.23.arrived
  174.1 1.1 split_sum.3
  175.2 1.3 collective-permute-start.25
  176.5 1.5 collective-permute-start.26
  178.0 6.4 %input_backward.1 = (f32[768,768]{1,0:T(8,128)}, f32[2,1,768]{2,1,0:T(1,128)S(1)}) custom-call(bf16[768,768]{1,0:T(8,128)(2,1)S(1)} %copy-done, f32[2,768]{1,0:T(2,128)S(1)} %copy-done.9, bf16[6,768,384]{2,1,0:T(8,128)(2,1)S(1)} %get-tuple-element.207.grad_mixed, f32[768,768]{1,0:T(8,128)S(1)} %get-tuple-element.208.grad_after, ...), custom_call_target="tpu_custom_call" | custom-call | flops 1 | bytes 1 | tf_op jit(solution)/shard_map/input_backward/pallas_call | solution.py:353
  185.1 1.7 collective-permute-start.24
  187.3 1.5 pool_out.1
  188.9 12.5 %collective-permute-done.27.right = f32[2,1,768]{2,1,0:T(1,128)S(1)} collective-permute-done((f32[2,1,768]{2,1,0:T(1,128)S(1)}, f32[2,1,768]{2,1,0:T(1,128)S(1)}, u32[]{:S(2)}, u32[]{:S(2)}) %collective-permute-start.27) | collective-permute-done | bytes 6176 | tf_op jit(solution)/shard_map/ppermute | solution.py:951
  202.3 0.8 collective-permute-start.28
  203.1 1.3 collective-permute-start.29
  204.4 1.2 collective-permute-done.30.right
  205.6 8.2 %collective-permute-done.28.one_in = bf16[2,3,96,384]{3,2,1,0:T(8,128)(2,1)S(1)} collective-permute-done((bf16[2,3,96,384]{3,2,1,0:T(8,128)(2,1)S(1)}, bf16[2,3,96,384]{3,2,1,0:T(8,128)(2,1)S(1)}, u32[]{:S(2)}, u32[]{:S(2)}) %collective-permute-start.28) | collective-permute-done | bytes 442400 | tf_op jit(solution)/shard_map/ppermute | solution.py:786
  215.0 1.5 collective-permute-start.31
  216.5 1.5 collective-permute-start.32
  218.1 5.3 %collective-permute-start.35 = (bf16[6,96,384]{2,1,0:T(8,128)(2,1)S(1)}, bf16[6,96,384]{2,1,0:T(8,128)(2,1)S(1)}, u32[]{:S(2)}, u32[]{:S(2)}) collective-permute-start(bf16[6,96,384]{2,1,0:T(8,128)(2,1)S(1)} %sum_of.12.high), channel_id=1, source_target_pairs={{0,16},{2,18},{4,20},{6,22},{8,24},{10,26},{12,28},{14,30},{1,17},... | collective-permute-start | bytes 1327112 | tf_op jit(solution)/shard_map/ppermute | solution.py:958
  223.4 3.7 %collective-permute-done.31.right = bf16[6,96,384]{2,1,0:T(8,128)(2,1)S(1)} collective-permute-done((bf16[6,96,384]{2,1,0:T(8,128)(2,1)S(1)}, bf16[6,96,384]{2,1,0:T(8,128)(2,1)S(1)}, u32[]{:S(2)}, u32[]{:S(2)}) %collective-permute-start.31) | collective-permute-done | bytes 442400 | tf_op jit(solution)/shard_map/ppermute | solution.py:964
  227.2 1.3 collective-permute-start.36
  228.5 2.5 collective-permute-start.33
  231.1 2.9 %collective-permute-done.33.right = f32[2,1,768]{2,1,0:T(1,128)S(1)} collective-permute-done((f32[2,1,768]{2,1,0:T(1,128)S(1)}, f32[2,1,768]{2,1,0:T(1,128)S(1)}, u32[]{:S(2)}, u32[]{:S(2)}) %collective-permute-start.33) | collective-permute-done | bytes 6176 | tf_op jit(solution)/shard_map/ppermute | solution.py:853
  234.0 9.4 %collective-permute-start.34 = (f32[2,1,768]{2,1,0:T(1,128)S(1)}, f32[2,1,768]{2,1,0:T(1,128)S(1)}, u32[]{:S(2)}, u32[]{:S(2)}) collective-permute-start(f32[2,1,768]{2,1,0:T(1,128)S(1)} %sum_of.10.left), channel_id=1, source_target_pairs={{0,16},{2,18},{4,20},{6,22},{8,24},{10,26},{12,28},{14,30},{16,0},... | collective-permute-start | bytes 18440 | tf_op jit(solution)/shard_map/ppermute | solution.py:853
  243.4 6.5 %collective-permute-done.34.right = f32[2,1,768]{2,1,0:T(1,128)S(1)} collective-permute-done((f32[2,1,768]{2,1,0:T(1,128)S(1)}, f32[2,1,768]{2,1,0:T(1,128)S(1)}, u32[]{:S(2)}, u32[]{:S(2)}) %collective-permute-start.34) | collective-permute-done | bytes 6176 | tf_op jit(solution)/shard_map/ppermute | solution.py:853
  250.6 8.5 %update.1 = (f32[24,96,96]{2,1,0:T(8,128)}, f32[24,96,96]{2,1,0:T(8,128)}, f32[24,96,96]{2,1,0:T(8,128)}, f32[24,96,96]{2,1,0:T(8,128)}, bf16[24,96,96]{2,1,0:T(8,128)(2,1)}) custom-call(s32[4]{0:T(128)S(1)} %pad_add_fusion.coords, bf16[6,96,384]{2,1,0:T(8,128)(2,1)S(1)} %sum_of.12.high, bf16[6,96,384]{2,1,0:T(8,128)(2,1)S(1)} %collective-permute-done.35.high_in, ...), custom_call_target="tpu_custom_call" | custom-call | flops 1 | bytes 1 | tf_op jit(solution)/shard_map/update/pallas_call | solution.py:353
  (76 shorter events, 13.2 us)
Async XLA Ops:
  0.6 1.3 copy-start.1
  2.9 24.1 %collective-permute-start.3 = (bf16[1,6,96,384]{3,2,1,0:T(8,128)(2,1)}, bf16[1,6,96,384]{3,2,1,0:T(8,128)(2,1)}, u32[]{:S(2)}, u32[]{:S(2)}) collective-permute-start(bf16[1,6,96,384]{3,2,1,0:T(8,128)(2,1)} %pack.1.own), channel_id=1, source_target_pairs={{0,16},{2,18},{4,20},{6,22},{8,24},{10,26},{12,28},{14,30},{16,0},... | collective-permute-start | bytes 1327112 | tf_op jit(solution)/shard_map/ppermute | solution.py:627
  6.9 20.3 %collective-permute-start.2 = (bf16[1,6,96,384]{3,2,1,0:T(8,128)(2,1)}, bf16[1,6,96,384]{3,2,1,0:T(8,128)(2,1)}, u32[]{:S(2)}, u32[]{:S(2)}) collective-permute-start(bf16[1,6,96,384]{3,2,1,0:T(8,128)(2,1)} %pack.1.own), channel_id=1, source_target_pairs={{0,8},{2,10},{4,12},{6,14},{8,0},{10,2},{12,4},{14,6},{16,24},{18,... | collective-permute-start | bytes 1327112 | tf_op jit(solution)/shard_map/ppermute | solution.py:626
  8.5 18.7 %collective-permute-start.1 = (bf16[1,6,96,384]{3,2,1,0:T(8,128)(2,1)}, bf16[1,6,96,384]{3,2,1,0:T(8,128)(2,1)}, u32[]{:S(2)}, u32[]{:S(2)}) collective-permute-start(bf16[1,6,96,384]{3,2,1,0:T(8,128)(2,1)} %pack.1.own), channel_id=1, source_target_pairs={{0,1},{1,0},{2,3},{3,2},{4,5},{5,4},{6,7},{7,6},{8,9},{9,8},{10,11... | collective-permute-start | bytes 1327112 | tf_op jit(solution)/shard_map/ppermute | solution.py:617
  10.0 17.2 %collective-permute-start = (bf16[1,6,96,384]{3,2,1,0:T(8,128)(2,1)}, bf16[1,6,96,384]{3,2,1,0:T(8,128)(2,1)}, u32[]{:S(2)}, u32[]{:S(2)}) collective-permute-start(bf16[1,6,96,384]{3,2,1,0:T(8,128)(2,1)} %pack.1.own), channel_id=1, source_target_pairs={{0,4},{2,6},{4,0},{6,2},{8,12},{10,14},{12,8},{14,10},{16,20},{18,... | collective-permute-start | bytes 1327112 | tf_op jit(solution)/shard_map/ppermute | solution.py:617
  30.2 26.6 %collective-permute-start.7 = (bf16[2,6,96,384]{3,2,1,0:T(8,128)(2,1)}, bf16[2,6,96,384]{3,2,1,0:T(8,128)(2,1)}, u32[]{:S(2)}, u32[]{:S(2)}) collective-permute-start(bf16[2,6,96,384]{3,2,1,0:T(8,128)(2,1)} %take_both.1.own), channel_id=1, source_target_pairs={{0,1},{1,0},{2,3},{3,2},{4,5},{5,4},{6,7},{7,6},{8,9},{9,8},{10,11... | collective-permute-start | bytes 2654216 | tf_op jit(solution)/shard_map/ppermute | solution.py:617
  31.8 25.1 %collective-permute-start.6 = (bf16[2,6,96,384]{3,2,1,0:T(8,128)(2,1)}, bf16[2,6,96,384]{3,2,1,0:T(8,128)(2,1)}, u32[]{:S(2)}, u32[]{:S(2)}) collective-permute-start(bf16[2,6,96,384]{3,2,1,0:T(8,128)(2,1)} %take_both.1.own), channel_id=1, source_target_pairs={{0,4},{2,6},{4,0},{6,2},{8,12},{10,14},{12,8},{14,10},{16,20},{18,... | collective-permute-start | bytes 2654216 | tf_op jit(solution)/shard_map/ppermute | solution.py:617
  33.3 23.6 %collective-permute-start.8 = (bf16[1,6,96,384]{3,2,1,0:T(8,128)(2,1)}, bf16[1,6,96,384]{3,2,1,0:T(8,128)(2,1)}, u32[]{:S(2)}, u32[]{:S(2)}) collective-permute-start(bf16[1,6,96,384]{3,2,1,0:T(8,128)(2,1)} %collective-permute-done.2.one), channel_id=1, source_target_pairs={{0,16},{2,18},{4,20},{6,22},{8,24},{10,26},{12,28},{14,30},{16,0},... | collective-permute-start | bytes 1327112 | tf_op jit(solution)/shard_map/ppermute | solution.py:631
  36.5 19.3 %collective-permute-start.4 = (bf16[1,3,96,384]{3,2,1,0:T(8,128)(2,1)}, bf16[1,3,96,384]{3,2,1,0:T(8,128)(2,1)}, u32[]{:S(2)}, u32[]{:S(2)}) collective-permute-start(bf16[1,3,96,384]{3,2,1,0:T(8,128)(2,1)} %get-tuple-element.131), channel_id=1, source_target_pairs={{0,1},{1,0},{2,3},{3,2},{4,5},{5,4},{6,7},{7,6},{8,9},{9,8},{10,11... | collective-permute-start | bytes 663560 | tf_op jit(solution)/shard_map/ppermute | solution.py:621
  37.0 19.8 %collective-permute-start.5 = (bf16[1,3,96,384]{3,2,1,0:T(8,128)(2,1)}, bf16[1,3,96,384]{3,2,1,0:T(8,128)(2,1)}, u32[]{:S(2)}, u32[]{:S(2)}) collective-permute-start(bf16[1,3,96,384]{3,2,1,0:T(8,128)(2,1)} %get-tuple-element.132), channel_id=1, source_target_pairs={{0,4},{2,6},{4,0},{6,2},{8,12},{10,14},{12,8},{14,10},{16,20},{18,... | collective-permute-start | bytes 663560 | tf_op jit(solution)/shard_map/ppermute | solution.py:621
  58.6 22.8 %collective-permute-start.13 = (bf16[1,2,2,6,96,384]{5,4,3,2,1,0:T(8,128)(2,1)S(1)}, bf16[1,2,2,6,96,384]{5,4,3,2,1,0:T(8,128)(2,1)S(1)}, u32[]{:S(2)}, u32[]{:S(2)}) collective-permute-start(bf16[1,2,2,6,96,384]{5,4,3,2,1,0:T(8,128)(2,1)S(1)} %get-tuple-element.143), channel_id=1, source_target_pairs={{0,2},{2,0},{4,6},{6,4},{8,10},{10,8},{12,14},{14,12},{16,18},{18,... | collective-permute-start | bytes 5308424 | tf_op jit(solution)/shard_map/ppermute | solution.py:778
  58.7 13.2 %collective-permute-start.12 = (bf16[1,6,96,384]{3,2,1,0:T(8,128)(2,1)}, bf16[1,6,96,384]{3,2,1,0:T(8,128)(2,1)S(1)}, u32[]{:S(2)}, u32[]{:S(2)}) collective-permute-start(bf16[1,6,96,384]{3,2,1,0:T(8,128)(2,1)} %collective-permute-done.8.own), channel_id=1, source_target_pairs={{0,1},{1,0},{2,3},{3,2},{4,5},{5,4},{6,7},{7,6},{8,9},{9,8},{10,11... | collective-permute-start | bytes 1327112 | tf_op jit(solution)/shard_map/ppermute | solution.py:617
  59.5 13.2 %collective-permute-start.11 = (bf16[1,6,96,384]{3,2,1,0:T(8,128)(2,1)}, bf16[1,6,96,384]{3,2,1,0:T(8,128)(2,1)S(1)}, u32[]{:S(2)}, u32[]{:S(2)}) collective-permute-start(bf16[1,6,96,384]{3,2,1,0:T(8,128)(2,1)} %collective-permute-done.8.own), channel_id=1, source_target_pairs={{0,4},{2,6},{4,0},{6,2},{8,12},{10,14},{12,8},{14,10},{16,20},{18,... | collective-permute-start | bytes 1327112 | tf_op jit(solution)/shard_map/ppermute | solution.py:617
  62.3 18.7 %collective-permute-start.9 = (bf16[2,3,96,384]{3,2,1,0:T(8,128)(2,1)S(1)}, bf16[2,3,96,384]{3,2,1,0:T(8,128)(2,1)S(1)}, u32[]{:S(2)}, u32[]{:S(2)}) collective-permute-start(bf16[2,3,96,384]{3,2,1,0:T(8,128)(2,1)S(1)} %get-tuple-element.138), channel_id=1, source_target_pairs={{0,1},{1,0},{2,3},{3,2},{4,5},{5,4},{6,7},{7,6},{8,9},{9,8},{10,11... | collective-permute-start | bytes 1327112 | tf_op jit(solution)/shard_map/ppermute | solution.py:621
  63.9 17.6 %collective-permute-start.10 = (bf16[2,3,96,384]{3,2,1,0:T(8,128)(2,1)S(1)}, bf16[2,3,96,384]{3,2,1,0:T(8,128)(2,1)S(1)}, u32[]{:S(2)}, u32[]{:S(2)}) collective-permute-start(bf16[2,3,96,384]{3,2,1,0:T(8,128)(2,1)S(1)} %get-tuple-element.139), channel_id=1, source_target_pairs={{0,4},{2,6},{4,0},{6,2},{8,12},{10,14},{12,8},{14,10},{16,20},{18,... | collective-permute-start | bytes 1327112 | tf_op jit(solution)/shard_map/ppermute | solution.py:621
  83.8 9.0 %collective-permute-start.16 = (bf16[2,2,2,6,96,384]{5,4,3,2,1,0:T(8,128)(2,1)S(1)}, bf16[2,2,2,6,96,384]{5,4,3,2,1,0:T(8,128)(2,1)S(1)}, u32[]{:S(2)}, u32[]{:S(2)}) collective-permute-start(bf16[2,2,2,6,96,384]{5,4,3,2,1,0:T(8,128)(2,1)S(1)} %get-tuple-element.152), channel_id=1, source_target_pairs={{0,2},{2,0},{4,6},{6,4},{8,10},{10,8},{12,14},{14,12},{16,18},{18,... | collective-permute-start | bytes 10616840 | tf_op jit(solution)/shard_map/ppermute | solution.py:778
  83.9 7.9 %collective-permute-start.14 = (bf16[1,3,96,384]{3,2,1,0:T(8,128)(2,1)S(1)}, bf16[1,3,96,384]{3,2,1,0:T(8,128)(2,1)S(1)}, u32[]{:S(2)}, u32[]{:S(2)}) collective-permute-start(bf16[1,3,96,384]{3,2,1,0:T(8,128)(2,1)S(1)} %get-tuple-element.147), channel_id=1, source_target_pairs={{0,1},{1,0},{2,3},{3,2},{4,5},{5,4},{6,7},{7,6},{8,9},{9,8},{10,11... | collective-permute-start | bytes 663560 | tf_op jit(solution)/shard_map/ppermute | solution.py:621
  85.3 7.5 %collective-permute-start.15 = (bf16[1,3,96,384]{3,2,1,0:T(8,128)(2,1)S(1)}, bf16[1,3,96,384]{3,2,1,0:T(8,128)(2,1)S(1)}, u32[]{:S(2)}, u32[]{:S(2)}) collective-permute-start(bf16[1,3,96,384]{3,2,1,0:T(8,128)(2,1)S(1)} %get-tuple-element.148), channel_id=1, source_target_pairs={{0,4},{2,6},{4,0},{6,2},{8,12},{10,14},{12,8},{14,10},{16,20},{18,... | collective-permute-start | bytes 663560 | tf_op jit(solution)/shard_map/ppermute | solution.py:621
  94.2 3.8 %collective-permute-start.17 = (bf16[1,2,2,6,96,384]{5,4,3,2,1,0:T(8,128)(2,1)S(1)}, bf16[1,2,2,6,96,384]{5,4,3,2,1,0:T(8,128)(2,1)S(1)}, u32[]{:S(2)}, u32[]{:S(2)}) collective-permute-start(bf16[1,2,2,6,96,384]{5,4,3,2,1,0:T(8,128)(2,1)S(1)} %get-tuple-element.158), channel_id=1, source_target_pairs={{0,2},{2,0},{4,6},{6,4},{8,10},{10,8},{12,14},{14,12},{16,18},{18,... | collective-permute-start | bytes 5308424 | tf_op jit(solution)/shard_map/ppermute | solution.py:778
  95.1 3.5 %copy-start = (bf16[768,768]{1,0:T(8,128)(2,1)S(1)}, bf16[768,768]{1,0:T(8,128)(2,1)}, u32[]{:S(2)}) copy-start(bf16[768,768]{1,0:T(8,128)(2,1)} %tok.3) | copy-start | bytes 3538948
  95.1 3.5 %copy-start.3 = (f32[768,128]{1,0:T(8,128)S(1)}, f32[768,128]{1,0:T(8,128)}, u32[]{:S(2)}) copy-start(f32[768,128]{1,0:T(8,128)} %broadcast_in_dim.16.share) | copy-start | bytes 1179652
  95.1 3.5 %copy-start.8 = (f32[6,128,16]{1,2,0:T(8,128)S(1)}, f32[6,128,16]{1,2,0:T(8,128)}, u32[]{:S(2)}) copy-start(f32[6,128,16]{1,2,0:T(8,128)} %reshape.42) | copy-start | bytes 147460
  95.1 3.5 %copy-start.9 = (f32[2,768]{1,0:T(2,128)S(1)}, f32[2,768]{1,0:T(2,128)}, u32[]{:S(2)}) copy-start(f32[2,768]{1,0:T(2,128)} %gains.5) | copy-start | bytes 18436
  138.3 6.3 %collective-permute-start.18 = (bf16[2,2,2,6,96,384]{5,4,3,2,1,0:T(8,128)(2,1)S(1)}, bf16[2,2,2,6,96,384]{5,4,3,2,1,0:T(8,128)(2,1)S(1)}, u32[]{:S(2)}, u32[]{:S(2)}) collective-permute-start(bf16[2,2,2,6,96,384]{5,4,3,2,1,0:T(8,128)(2,1)S(1)} %get-tuple-element.166), channel_id=1, source_target_pairs={{0,2},{2,0},{4,6},{6,4},{8,10},{10,8},{12,14},{14,12},{16,18},{18,... | collective-permute-start | bytes 10616840 | tf_op jit(solution)/shard_map/ppermute | solution.py:778
  145.6 21.8 %collective-permute-start.19 = (bf16[2,2,3,96,384]{4,3,2,1,0:T(8,128)(2,1)S(1)}, bf16[2,2,3,96,384]{4,3,2,1,0:T(8,128)(2,1)S(1)}, u32[]{:S(2)}, u32[]{:S(2)}) collective-permute-start(bf16[2,2,3,96,384]{4,3,2,1,0:T(8,128)(2,1)S(1)} %get-tuple-element.184), channel_id=1, source_target_pairs={{0,1},{1,0},{2,3},{3,2},{4,5},{5,4},{6,7},{7,6},{8,9},{9,8},{10,11... | collective-permute-start | bytes 2654216 | tf_op jit(solution)/shard_map/ppermute | solution.py:782
  146.5 21.4 %collective-permute-start.20 = (bf16[2,2,3,96,384]{4,3,2,1,0:T(8,128)(2,1)S(1)}, bf16[2,2,3,96,384]{4,3,2,1,0:T(8,128)(2,1)S(1)}, u32[]{:S(2)}, u32[]{:S(2)}) collective-permute-start(bf16[2,2,3,96,384]{4,3,2,1,0:T(8,128)(2,1)S(1)} %get-tuple-element.185), channel_id=1, source_target_pairs={{0,4},{2,6},{4,0},{6,2},{8,12},{10,14},{12,8},{14,10},{16,20},{18,... | collective-permute-start | bytes 2654216 | tf_op jit(solution)/shard_map/ppermute | solution.py:782
  167.9 6.2 %collective-permute-start.23 = (bf16[2,2,2,6,96,384]{5,4,3,2,1,0:T(8,128)(2,1)S(1)}, bf16[2,2,2,6,96,384]{5,4,3,2,1,0:T(8,128)(2,1)S(1)}, u32[]{:S(2)}, u32[]{:S(2)}) collective-permute-start(bf16[2,2,2,6,96,384]{5,4,3,2,1,0:T(8,128)(2,1)S(1)} %get-tuple-element.201), channel_id=1, source_target_pairs={{0,2},{2,0},{4,6},{6,4},{8,10},{10,8},{12,14},{14,12},{16,18},{18,... | collective-permute-start | bytes 10616840 | tf_op jit(solution)/shard_map/ppermute | solution.py:778
  168.7 15.7 %collective-permute-start.21 = (bf16[2,3,96,384]{3,2,1,0:T(8,128)(2,1)S(1)}, bf16[2,3,96,384]{3,2,1,0:T(8,128)(2,1)S(1)}, u32[]{:S(2)}, u32[]{:S(2)}) collective-permute-start(bf16[2,3,96,384]{3,2,1,0:T(8,128)(2,1)S(1)} %get-tuple-element.198), channel_id=1, source_target_pairs={{0,4},{2,6},{4,0},{6,2},{8,12},{10,14},{12,8},{14,10},{16,20},{18,... | collective-permute-start | bytes 1327112 | tf_op jit(solution)/shard_map/ppermute | solution.py:786
  170.0 14.4 %collective-permute-start.22 = (bf16[2,3,96,384]{3,2,1,0:T(8,128)(2,1)S(1)}, bf16[2,3,96,384]{3,2,1,0:T(8,128)(2,1)S(1)}, u32[]{:S(2)}, u32[]{:S(2)}) collective-permute-start(bf16[2,3,96,384]{3,2,1,0:T(8,128)(2,1)S(1)} %get-tuple-element.199), channel_id=1, source_target_pairs={{0,1},{1,0},{2,3},{3,2},{4,5},{5,4},{6,7},{7,6},{8,9},{9,8},{10,11... | collective-permute-start | bytes 1327112 | tf_op jit(solution)/shard_map/ppermute | solution.py:786
  175.2 26.2 %collective-permute-start.25 = (bf16[2,2,3,96,384]{4,3,2,1,0:T(8,128)(2,1)S(1)}, bf16[2,2,3,96,384]{4,3,2,1,0:T(8,128)(2,1)S(1)}, u32[]{:S(2)}, u32[]{:S(2)}) collective-permute-start(bf16[2,2,3,96,384]{4,3,2,1,0:T(8,128)(2,1)S(1)} %get-tuple-element.214), channel_id=1, source_target_pairs={{0,1},{1,0},{2,3},{3,2},{4,5},{5,4},{6,7},{7,6},{8,9},{9,8},{10,11... | collective-permute-start | bytes 2654216 | tf_op jit(solution)/shard_map/ppermute | solution.py:782
  176.5 24.9 %collective-permute-start.26 = (bf16[2,2,3,96,384]{4,3,2,1,0:T(8,128)(2,1)S(1)}, bf16[2,2,3,96,384]{4,3,2,1,0:T(8,128)(2,1)S(1)}, u32[]{:S(2)}, u32[]{:S(2)}) collective-permute-start(bf16[2,2,3,96,384]{4,3,2,1,0:T(8,128)(2,1)S(1)} %get-tuple-element.215), channel_id=1, source_target_pairs={{0,4},{2,6},{4,0},{6,2},{8,12},{10,14},{12,8},{14,10},{16,20},{18,... | collective-permute-start | bytes 2654216 | tf_op jit(solution)/shard_map/ppermute | solution.py:782
  185.1 16.3 %collective-permute-start.24 = (bf16[6,96,384]{2,1,0:T(8,128)(2,1)S(1)}, bf16[6,96,384]{2,1,0:T(8,128)(2,1)S(1)}, u32[]{:S(2)}, u32[]{:S(2)}) collective-permute-start(bf16[6,96,384]{2,1,0:T(8,128)(2,1)S(1)} %get-tuple-element.213), channel_id=1, source_target_pairs={{0,8},{2,10},{4,12},{6,14},{8,0},{10,2},{12,4},{14,6},{16,24},{18,... | collective-permute-start | bytes 1327112 | tf_op jit(solution)/shard_map/ppermute | solution.py:950
  186.8 14.6 %collective-permute-start.27 = (f32[2,1,768]{2,1,0:T(1,128)S(1)}, f32[2,1,768]{2,1,0:T(1,128)S(1)}, u32[]{:S(2)}, u32[]{:S(2)}) collective-permute-start(f32[2,1,768]{2,1,0:T(1,128)S(1)} %get-tuple-element.216.left), channel_id=1, source_target_pairs={{0,1},{1,0},{2,3},{3,2},{4,5},{5,4},{6,7},{7,6},{8,9},{9,8},{10,11... | collective-permute-start | bytes 18440 | tf_op jit(solution)/shard_map/ppermute | solution.py:951
  201.4 49.1 %copy-start.6 = (f32[24,96,96]{2,1,0:T(8,128)S(1)}, f32[24,96,96]{2,1,0:T(8,128)}, u32[]{:S(2)}) copy-start(f32[24,96,96]{2,1,0:T(8,128)} %root_left.1) | copy-start | bytes 2654212
  201.4 49.1 %copy-start.7 = (f32[24,96,96]{2,1,0:T(8,128)S(1)}, f32[24,96,96]{2,1,0:T(8,128)}, u32[]{:S(2)}) copy-start(f32[24,96,96]{2,1,0:T(8,128)} %root_right.1) | copy-start | bytes 2654212
  202.2 47.6 %copy-start.10 = (f32[2,768]{1,0:T(2,128)S(1)}, f32[2,768]{1,0:T(2,128)}, u32[]{:S(2)}) copy-start(f32[2,768]{1,0:T(2,128)} %param.13) | copy-start | bytes 18436
  202.2 48.3 %copy-start.2 = (f32[24,96,96]{2,1,0:T(8,128)S(1)}, f32[24,96,96]{2,1,0:T(8,128)}, u32[]{:S(2)}) copy-start(f32[24,96,96]{2,1,0:T(8,128)} %master.3) | copy-start | bytes 2654212
  202.3 48.3 %copy-start.4 = (f32[24,96,96]{2,1,0:T(8,128)S(1)}, f32[24,96,96]{2,1,0:T(8,128)}, u32[]{:S(2)}) copy-start(f32[24,96,96]{2,1,0:T(8,128)} %stat_left.1) | copy-start | bytes 2654212
  202.3 48.3 %copy-start.5 = (f32[24,96,96]{2,1,0:T(8,128)S(1)}, f32[24,96,96]{2,1,0:T(8,128)}, u32[]{:S(2)}) copy-start(f32[24,96,96]{2,1,0:T(8,128)} %stat_right.1) | copy-start | bytes 2654212
  202.3 11.5 %collective-permute-start.28 = (bf16[2,3,96,384]{3,2,1,0:T(8,128)(2,1)S(1)}, bf16[2,3,96,384]{3,2,1,0:T(8,128)(2,1)S(1)}, u32[]{:S(2)}, u32[]{:S(2)}) collective-permute-start(bf16[2,3,96,384]{3,2,1,0:T(8,128)(2,1)S(1)} %get-tuple-element.226), channel_id=1, source_target_pairs={{0,4},{2,6},{4,0},{6,2},{8,12},{10,14},{12,8},{14,10},{16,20},{18,... | collective-permute-start | bytes 1327112 | tf_op jit(solution)/shard_map/ppermute | solution.py:786
  203.1 11.2 %collective-permute-start.29 = (bf16[2,3,96,384]{3,2,1,0:T(8,128)(2,1)S(1)}, bf16[2,3,96,384]{3,2,1,0:T(8,128)(2,1)S(1)}, u32[]{:S(2)}, u32[]{:S(2)}) collective-permute-start(bf16[2,3,96,384]{3,2,1,0:T(8,128)(2,1)S(1)} %get-tuple-element.227), channel_id=1, source_target_pairs={{0,1},{1,0},{2,3},{3,2},{4,5},{5,4},{6,7},{7,6},{8,9},{9,8},{10,11... | collective-permute-start | bytes 1327112 | tf_op jit(solution)/shard_map/ppermute | solution.py:786
  204.4 1.2 collective-permute-start.30
  215.0 12.1 %collective-permute-start.31 = (bf16[6,96,384]{2,1,0:T(8,128)(2,1)S(1)}, bf16[6,96,384]{2,1,0:T(8,128)(2,1)S(1)}, u32[]{:S(2)}, u32[]{:S(2)}) collective-permute-start(bf16[6,96,384]{2,1,0:T(8,128)(2,1)S(1)} %get-tuple-element.233), channel_id=1, source_target_pairs={{0,8},{2,10},{4,12},{6,14},{8,0},{10,2},{12,4},{14,6},{16,24},{18,... | collective-permute-start | bytes 1327112 | tf_op jit(solution)/shard_map/ppermute | solution.py:964
  216.5 6.9 %collective-permute-start.32 = (f32[2,1,768]{2,1,0:T(1,128)S(1)}, f32[2,1,768]{2,1,0:T(1,128)S(1)}, u32[]{:S(2)}, u32[]{:S(2)}) collective-permute-start(f32[2,1,768]{2,1,0:T(1,128)S(1)} %sum_of.8.left), channel_id=1, source_target_pairs={{0,4},{2,6},{4,0},{6,2},{8,12},{10,14},{12,8},{14,10},{16,20},{18,... | collective-permute-start | bytes 18440 | tf_op jit(solution)/shard_map/ppermute | solution.py:966
  218.1 32.4 %collective-permute-start.35 = (bf16[6,96,384]{2,1,0:T(8,128)(2,1)S(1)}, bf16[6,96,384]{2,1,0:T(8,128)(2,1)S(1)}, u32[]{:S(2)}, u32[]{:S(2)}) collective-permute-start(bf16[6,96,384]{2,1,0:T(8,128)(2,1)S(1)} %sum_of.12.high), channel_id=1, source_target_pairs={{0,16},{2,18},{4,20},{6,22},{8,24},{10,26},{12,28},{14,30},{1,17},... | collective-permute-start | bytes 1327112 | tf_op jit(solution)/shard_map/ppermute | solution.py:958
  227.2 23.3 %collective-permute-start.36 = (bf16[6,96,384]{2,1,0:T(8,128)(2,1)S(1)}, bf16[6,96,384]{2,1,0:T(8,128)(2,1)S(1)}, u32[]{:S(2)}, u32[]{:S(2)}) collective-permute-start(bf16[6,96,384]{2,1,0:T(8,128)(2,1)S(1)} %sum_of.13.low), channel_id=1, source_target_pairs={{16,0},{18,2},{20,4},{22,6},{24,8},{26,10},{28,12},{30,14},{17,1},... | collective-permute-start | bytes 1327112 | tf_op jit(solution)/shard_map/ppermute | solution.py:970
  228.5 5.4 %collective-permute-start.33 = (f32[2,1,768]{2,1,0:T(1,128)S(1)}, f32[2,1,768]{2,1,0:T(1,128)S(1)}, u32[]{:S(2)}, u32[]{:S(2)}) collective-permute-start(f32[2,1,768]{2,1,0:T(1,128)S(1)} %sum_of.9.left), channel_id=1, source_target_pairs={{0,8},{2,10},{4,12},{6,14},{8,0},{10,2},{12,4},{14,6},{16,24},{18,... | collective-permute-start | bytes 18440 | tf_op jit(solution)/shard_map/ppermute | solution.py:853
  234.0 15.9 %collective-permute-start.34 = (f32[2,1,768]{2,1,0:T(1,128)S(1)}, f32[2,1,768]{2,1,0:T(1,128)S(1)}, u32[]{:S(2)}, u32[]{:S(2)}) collective-permute-start(f32[2,1,768]{2,1,0:T(1,128)S(1)} %sum_of.10.left), channel_id=1, source_target_pairs={{0,16},{2,18},{4,20},{6,22},{8,24},{10,26},{12,28},{14,30},{16,0},... | collective-permute-start | bytes 18440 | tf_op jit(solution)/shard_map/ppermute | solution.py:853

commit v2 on v1

--- a/solution.py
+++ b/solution.py
@@ -39,13 +39,16 @@
     )
 
 
-def weight_of(ref, half, rows, columns):
-    parts = [ref[half, rows, column].reshape(-1, STRIP) for column in columns]
+def weight_of(strips, half, first, rows, width, columns):
+    parts = [
+        jnp.concatenate([strips[half, first + width * row + column] for row in range(rows)], axis=0)
+        for column in columns
+    ]
     return jnp.concatenate(parts, axis=1)
 
 
-def out_weight(by_two):
-    halves = [weight_of(by_two, half, slice(12, 16), (0, 1)) for half in range(HALVES)]
+def out_weight(strips):
+    halves = [weight_of(strips, half, 24, 4, 2, (0, 1)) for half in range(HALVES)]
     return jnp.concatenate(halves, axis=0)
 
 
@@ -95,19 +98,59 @@
     )
 
 
-def pair_probs(queries, key_rows, bias, caption):
-    scores = compact(mm(key_rows, queries, 1, 1), caption) * HD ** (-0.5) + bias
+def softmax_of(scores, bias):
+    scores = scores * HD ** (-0.5) + bias
     shifted = jnp.exp(scores - jnp.max(scores, axis=0, keepdims=True))
     return shifted / jnp.sum(shifted, axis=0, keepdims=True)
 
 
+def pairs_of():
+    for half in range(HALVES):
+        for start in range(0, STRIP, PAIR):
+            yield half, slice(start, start + PAIR), slice(half * STRIP + start, half * STRIP + start + PAIR)
+
+
+def columns(values, i):
+    return values[:, 2 * GROUP * i : 2 * GROUP * (i + 1)]
+
+
 def key_bias(mask):
     bias = jnp.where(mask > 0, 0.0, MASKED_SCORE)
-    return jnp.concatenate([bias, bias], axis=1)
+    return jnp.concatenate([bias] * HEADS, axis=1)
 
 
 def span_of(i, size=GROUP):
     return pl.ds(pl.multiple_of(i * size, size), size)
+
+
+def prepare(coords, token_mask, cot, mask, share, out_wide, inverse):
+    captions = cot.shape[0]
+    first = pl.multiple_of(coords[3] * captions, captions)
+    own = token_mask[pl.ds(first, captions), :].astype(F32)
+    count = jnp.broadcast_to(jnp.sum(own, axis=1, keepdims=True), (captions, PAIR))
+    inverse[...] = 1.0 / count
+    key = lax.broadcasted_iota(jnp.int32, (SLOTS, GROUP), 0).astype(F32)
+    here = (
+        lax.broadcasted_iota(jnp.int32, (CAPS, GROUP), 0)
+        == lax.broadcasted_iota(jnp.int32, (CAPS, GROUP), 1) // SLOTS
+    )
+    slot = lax.broadcasted_iota(jnp.int32, (CAPS, SLOTS, PAIR), 1).astype(F32)
+    caption = lax.broadcasted_iota(jnp.int32, (CAPS, SLOTS, PAIR), 0)
+    lane = lax.broadcasted_iota(jnp.int32, (CAPS, SLOTS, PAIR), 2)
+    for i in range(captions // CAPS):
+        span, caps = slice(i * GROUP, (i + 1) * GROUP), slice(i * CAPS, (i + 1) * CAPS)
+        number = count[caps]
+        by_query = jnp.sum(jnp.where(here, number, 0.0), axis=0, keepdims=True)
+        mask[i] = jnp.where(key < by_query, 1.0, 0.0)
+        true = slot < number[:, None, :]
+        weight = jnp.where(true, 1.0 / number[:, None, :], 0.0)
+        share[span, :] = weight.reshape(GROUP, PAIR)
+        seen = jnp.where(true & (caption + i * CAPS == lane), 1.0, 0.0)
+        out_wide[span, D:] = seen.reshape(GROUP, PAIR).astype(BF16)
+        for j in range(0, D, PAIR):
+            lanes = slice(j, j + PAIR)
+            value = (cot[caps, lanes].astype(F32)[:, None, :] * weight).reshape(GROUP, PAIR)
+            out_wide[span, lanes] = value.astype(BF16)
 
 
 def pool(values, share):
@@ -119,7 +162,7 @@
 
 
 def attention_forward(
-    tok, gains, mask, share, by_three, by_two, normed, qkv, attended, after, normed_two, after_pooled
+    tok, gains, mask, share, strips, normed, qkv, attended, after, normed_two, after_pooled
 ):
     rows = tok.shape[0]
 
@@ -130,29 +173,29 @@
         normed[span, :] = (xhat * gains[0:1, :]).astype(BF16)
 
     for half in range(HALVES):
-        mixed = mm(normed[...], weight_of(by_three, half, slice(0, 8), range(3))).astype(BF16)
+        mixed = mm(normed[...], weight_of(strips, half, 0, 8, 3, range(3))).astype(BF16)
         for part in range(3):
             qkv[3 * half + part] = mixed[:, part * STRIP : (part + 1) * STRIP]
 
     @pl.loop(0, rows // GROUP)
     def _(i):
         span = span_of(i)
-        bias = key_bias(mask[i])
         caption = caption_of()
-        for half in range(HALVES):
-            for pair in range(STRIP // PAIR):
-                lanes = slice(pair * PAIR, (pair + 1) * PAIR)
-                wide = slice(half * STRIP + pair * PAIR, half * STRIP + (pair + 1) * PAIR)
-                probs = pair_probs(
-                    split_pair(qkv[3 * half, span, lanes]),
-                    qkv[3 * half + 1, span, lanes],
-                    bias,
-                    caption,
-                )
-                mixed = mm(expand(probs, caption), qkv[3 * half + 2, span, lanes], 0, 0)
-                attended[span, wide] = join_pair(mixed).astype(BF16)
-
-    after[...] = mm(attended[...], out_weight(by_two))
+        pairs = list(pairs_of())
+        scores = [
+            compact(
+                mm(qkv[3 * half + 1, span, lanes], split_pair(qkv[3 * half, span, lanes]), 1, 1),
+                caption,
+            )
+            for half, lanes, _ in pairs
+        ]
+        probs = softmax_of(jnp.concatenate(scores, axis=1), key_bias(mask[i]))
+        for pair, (half, lanes, wide) in enumerate(pairs):
+            spread = expand(columns(probs, pair), caption)
+            mixed = mm(spread, qkv[3 * half + 2, span, lanes], 0, 0)
+            attended[span, wide] = join_pair(mixed).astype(BF16)
+
+    after[...] = mm(attended[...], out_weight(strips))
 
     @pl.loop(0, rows // GROUP)
     def _(i):
@@ -182,30 +225,36 @@
         self.whole = targets[0] if len(targets) == 1 else None
         self.batches = [] if self.whole is not None else list(zip(runs, targets[0::2], targets[1::2]))
 
-    def store(self, value, half, strip, planes):
+    def store(self, pieces, here=True):
         if self.whole is not None:
-            self.whole[half, strip] = value
+
+            @pl.when(here)
+            def _():
+                for value, half, strip in pieces:
+                    self.whole[half, strip] = value
+
             return
-        plane = strip // (4 * OWN)
-        place = (strip // (2 * OWN)) % 2
-        owner = (strip // OWN) % 2
-        for run, kept, sent in self.batches:
-            inside = [z for z in planes if z in run]
-            if not inside:
-                continue
-            here = len(inside) == len(planes) or (plane >= run[0]) & (plane <= run[-1])
-            spot = (plane - run[0], half, place, strip % OWN)
-
-            @pl.when(here & (owner == self.core))
+        for core in range(2):
+
+            @pl.when((self.core == core) & here)
             def _():
-                kept[spot] = value
-
-            @pl.when(here & (owner != self.core))
-            def _():
-                sent[spot] = value
-
-
-def mlp_both(coords, normed_two, out_low, share, by_four, by_two, *rest):
+                for value, half, strip in pieces:
+                    plane, place = strip // (4 * OWN), strip // (2 * OWN) % 2
+                    for run, kept, sent in self.batches:
+                        if plane in run:
+                            target = kept if strip // OWN % 2 == core else sent
+                            target[plane - run[0], half, place, strip % OWN] = value
+
+
+def strips_of(grad, rows, columns):
+    return [
+        (i, j, grad[i * BLOCK : (i + 1) * BLOCK, j * STRIP : (j + 1) * STRIP])
+        for i in range(rows)
+        for j in range(columns)
+    ]
+
+
+def mlp_both(coords, normed_two, out_wide, strips, *rest):
     hidden_pooled, grad_normed_two, *targets, hidden, grad_up = rest
     step = pl.program_id(0)
     rows = normed_two.shape[0]
@@ -217,43 +266,43 @@
     def _():
         grad_normed_two[...] = jnp.zeros_like(grad_normed_two)
 
-    up_weight = weight_of(by_four, half, slice(8, 16), (2 * column, 2 * column + 1))
-    down_weight = weight_of(by_two, half, pl.ds(32 + 8 * column, 8), (0, 1))
+    up_weight = weight_of(strips, half, 32 + 2 * column, 8, 4, (0, 1))
+    down_weight = weight_of(strips, half, 64 + 16 * column, 8, 2, (0, 1))
     chunk = 256
     for i in range(rows // chunk):
         span = slice(i * chunk, (i + 1) * chunk)
         act, slope = gelu_both(mm(normed_two[span, :], up_weight))
-        act = act.astype(BF16)
-        hidden[span, :] = act
-        caps = slice(i * chunk // SLOTS, (i + 1) * chunk // SLOTS)
-        hidden_pooled[step, caps, :] = pool(act.astype(F32), share[span, :])
-        grad = (mm(out_low[span, :], down_weight, 1, 1) * slope).astype(BF16)
+        hidden[span, :] = act.astype(BF16)
+        grad = (mm(out_wide[span, :D], down_weight, 1, 1) * slope).astype(BF16)
         grad_up[span, :] = grad
         grad_normed_two[span, :] += mm(grad, up_weight, 1, 1)
 
-    down_grad = mm(hidden[...], out_low[...], 0, 0).astype(BF16)
-    up_grad = mm(normed_two[...], grad_up[...], 0, 0).astype(BF16)
-    for row in range(8):
-        for part in range(2):
-            block = slice(row * BLOCK, (row + 1) * BLOCK), slice(part * STRIP, (part + 1) * STRIP)
-            emit.store(down_grad[block], half, 64 + 16 * column + 2 * row + part, (2, 3))
-            planes = (1,) if row < 4 else (2,)
-            emit.store(up_grad[block], half, 32 + 4 * row + 2 * column + part, planes)
-
-
-def pool_out(after_pooled, hidden_pooled, by_two, pooled):
+    both = mm(hidden[...], out_wide[...], 0, 0)
+    hidden_pooled[step] = both[:, D:]
+    down_strips = strips_of(both[:, :D].astype(BF16), 8, 2)
+    up_strips = strips_of(mm(normed_two[...], grad_up[...], 0, 0).astype(BF16), 8, 2)
+    for i in range(2):
+        pieces = [(value, half, 64 + 16 * i + 2 * row + part) for row, part, value in down_strips]
+        pieces += [(value, half, 32 + 4 * row + 2 * i + part) for row, part, value in up_strips]
+        emit.store(pieces, column == i)
+
+
+def pool_out(after_pooled, hidden_pooled, inverse, strips, pooled):
+    captions = pooled.shape[0]
     pooled[...] = after_pooled[...]
     for step in range(4):
         value = hidden_pooled[step]
         high = value.astype(BF16)
         low = (value - high.astype(F32)).astype(BF16)
-        start = 32 + 8 * (step % 2)
-        weight = weight_of(by_two, step // 2, slice(start, start + 8), (0, 1))
-        both = mm(jnp.concatenate([high, low], axis=0), weight)
-        pooled[...] += both[: value.shape[0]] + both[value.shape[0] :]
-
-
-def output_backward(held, coords, gains, attended, after, grad_out, grad_normed_two, by_two, *rest):
+        weight = weight_of(strips, step // 2, 64 + 16 * (step % 2), 8, 2, (0, 1))
+        both = mm(jnp.concatenate([high, low], axis=1), weight, 0, 0)
+        total = both[:captions] + both[PAIR : PAIR + captions]
+        pooled[...] += total * jnp.concatenate([inverse[...]] * (D // PAIR), axis=1)
+
+
+def output_backward(
+    held, coords, gains, attended, after, cot, share, grad_normed_two, strips, *rest
+):
     grad_after, gain_part, grad_att, *targets, after_low = rest[held:]
     rows = after.shape[0]
     emit = Emitter(targets, (LOWER,), coords)
@@ -265,18 +314,24 @@
         xhat, inverse = norm_parts(after[span, :])
         grad = grad_normed_two[span, :]
         gain_part[...] += jnp.sum(grad * xhat, axis=0, keepdims=True)
-        value = grad_out[span, :] + norm_back(xhat, inverse, gains[1:2, :], grad)
+        weight = share[span, :].reshape(CAPS, SLOTS, PAIR)
+        parts = [
+            (cot[span_of(i, CAPS), j : j + PAIR].astype(F32)[:, None, :] * weight)
+            for j in range(0, D, PAIR)
+        ]
+        grad_out = jnp.concatenate([part.reshape(GROUP, PAIR) for part in parts], axis=1)
+        value = grad_out + norm_back(xhat, inverse, gains[1:2, :], grad)
         grad_after[span, :] = value
         after_low[span, :] = value.astype(BF16)
 
-    grad_att[...] = mm(after_low[...], out_weight(by_two), 1, 1).astype(BF16)
+    grad_att[...] = mm(after_low[...], out_weight(strips), 1, 1).astype(BF16)
     grad_w = mm(attended[...], after_low[...], 0, 0).astype(BF16)
-    for half in range(HALVES):
-        for row in range(4):
-            for part in range(2):
-                top = (4 * half + row) * BLOCK
-                value = grad_w[top : top + BLOCK, part * STRIP : (part + 1) * STRIP]
-                emit.store(value, half, 24 + 2 * row + part, (1,))
+    emit.store(
+        [
+            (value, row // 4, 24 + 2 * (row % 4) + part)
+            for row, part, value in strips_of(grad_w, 8, 2)
+        ]
+    )
 
 
 def attention_backward(held, coords, mask, normed, qkv, grad_att, *rest):
@@ -287,45 +342,47 @@
     @pl.loop(0, rows // GROUP)
     def _(i):
         span = span_of(i)
-        bias = key_bias(mask[i])
         caption = caption_of()
         scale = HD ** (-0.5)
-        for half in range(HALVES):
-            for pair in range(STRIP // PAIR):
-                lanes = slice(pair * PAIR, (pair + 1) * PAIR)
-                wide = slice(half * STRIP + pair * PAIR, half * STRIP + (pair + 1) * PAIR)
-                queries = split_pair(qkv[3 * half, span, lanes])
-                key_rows = qkv[3 * half + 1, span, lanes]
-                value_rows = qkv[3 * half + 2, span, lanes]
-                probs = pair_probs(queries, key_rows, bias, caption)
-                grads = split_pair(grad_att[span, wide])
-                grad_probs = compact(mm(value_rows, grads, 1, 1), caption)
-                inner = jnp.sum(probs * grad_probs, axis=0, keepdims=True)
-                grad_scores = expand(probs * (grad_probs - inner), caption)
-                grad_mixed[3 * half, span, lanes] = (
-                    join_pair(mm(grad_scores, key_rows, 0, 0)) * scale
-                ).astype(BF16)
-                grad_mixed[3 * half + 1, span, lanes] = (mm(grad_scores, queries) * scale).astype(
-                    BF16
-                )
-                grad_mixed[3 * half + 2, span, lanes] = mm(expand(probs, caption), grads).astype(
-                    BF16
-                )
+        pairs = list(pairs_of())
+        scores = [
+            compact(
+                mm(qkv[3 * half + 1, span, lanes], split_pair(qkv[3 * half, span, lanes]), 1, 1),
+                caption,
+            )
+            for half, lanes, _ in pairs
+        ]
+        grad_probs = [
+            compact(
+                mm(qkv[3 * half + 2, span, lanes], split_pair(grad_att[span, wide]), 1, 1), caption
+            )
+            for half, lanes, wide in pairs
+        ]
+        probs = softmax_of(jnp.concatenate(scores, axis=1), key_bias(mask[i]))
+        grad_probs = jnp.concatenate(grad_probs, axis=1)
+        inner = jnp.sum(probs * grad_probs, axis=0, keepdims=True)
+        grad_scores = probs * (grad_probs - inner)
+        for pair, (half, lanes, wide) in enumerate(pairs):
+            spread = expand(columns(grad_scores, pair), caption)
+            back = mm(spread, qkv[3 * half + 1, span, lanes], 0, 0)
+            grad_mixed[3 * half, span, lanes] = (join_pair(back) * scale).astype(BF16)
+            back = mm(spread, split_pair(qkv[3 * half, span, lanes]))
+            grad_mixed[3 * half + 1, span, lanes] = (back * scale).astype(BF16)
+            spread = expand(columns(probs, pair), caption)
+            grad_mixed[3 * half + 2, span, lanes] = mm(
+                spread, split_pair(grad_att[span, wide])
+            ).astype(BF16)
 
     for half in range(HALVES):
         grads = jnp.concatenate([grad_mixed[3 * half + part] for part in range(3)], axis=1)
         grad_w = mm(normed[...], grads, 0, 0).astype(BF16)
-        for row in range(8):
-            for part in range(3):
-                strip = 3 * row + part
-                value = grad_w[row * BLOCK : (row + 1) * BLOCK, part * STRIP : (part + 1) * STRIP]
-                emit.store(value, half, strip, (0,))
-
-
-def input_backward(tok, gains, grad_mixed, grad_after, gain_two, by_three, input_grad, gain_part):
+        emit.store([(value, half, 3 * row + part) for row, part, value in strips_of(grad_w, 8, 3)])
+
+
+def input_backward(tok, gains, grad_mixed, grad_after, gain_two, strips, input_grad, gain_part):
     rows = tok.shape[0]
     grads = jnp.concatenate([grad_mixed[part] for part in range(6)], axis=1)
-    halves = [weight_of(by_three, half, slice(0, 8), range(3)) for half in range(HALVES)]
+    halves = [weight_of(strips, half, 0, 8, 3, range(3)) for half in range(HALVES)]
     input_grad[...] = mm(grads, jnp.concatenate(halves, axis=1), 1, 1)
     gain_part[0] = jnp.zeros_like(gain_two)
     gain_part[1] = gain_two[...]
@@ -376,8 +433,24 @@
 UNIT = 2 * 768 * 768 * 768
 
 
-def by_count(strips, count):
-    return strips.reshape(HALVES, STRIPS // count, count, BLOCK, STRIP)
+def run_prepare(coords, token_mask, cot):
+    captions = cot.shape[0]
+    rows = captions * SLOTS
+    return call(
+        prepare,
+        "prepare",
+        [SMEM, VMEM, VMEM],
+        [
+            (VMEM, shape_of(rows // GROUP, SLOTS, GROUP, dtype=F32)),
+            (VMEM, shape_of(rows, PAIR, dtype=F32)),
+            (VMEM, shape_of(rows, D + PAIR)),
+            (VMEM, shape_of(captions, PAIR, dtype=F32)),
+        ],
+        [],
+        1,
+        (coords, token_mask, cot),
+        mib=6,
+    )
 
 
 def run_forward(tok, gains, mask, share, strips):
@@ -385,7 +458,7 @@
     return call(
         attention_forward,
         "attention_forward",
-        [VMEM] * 6,
+        [VMEM] * 5,
         [
             (VMEM, shape_of(rows, D)),
             (VMEM, shape_of(6, rows, STRIP)),
@@ -396,7 +469,7 @@
         ],
         [],
         5 * UNIT,
-        (tok, gains, mask, share, by_count(strips, 3), by_count(strips, 2)),
+        (tok, gains, mask, share, strips),
         mib=3,
     )
 
@@ -409,44 +482,41 @@
     return [(VMEM, shape) for shape in shapes]
 
 
-def run_mlp(coords, normed_two, out_low, share, strips, split):
+def run_mlp(coords, normed_two, out_wide, strips, split):
     rows = normed_two.shape[0]
     return call(
         mlp_both,
         "mlp_both",
-        [SMEM] + [VMEM] * 5,
-        [
-            (VMEM, shape_of(4, rows // SLOTS, D, dtype=F32)),
-            (VMEM, shape_of(rows, D, dtype=F32)),
-        ]
+        [SMEM] + [VMEM] * 3,
+        [(VMEM, shape_of(4, D, PAIR, dtype=F32)), (VMEM, shape_of(rows, D, dtype=F32))]
         + targets_of((UPPER, LOWER), split),
         [pltpu.VMEM((rows, D), BF16), pltpu.VMEM((rows, D), BF16)],
         20 * UNIT,
-        (coords, normed_two, out_low, share, by_count(strips, 4), by_count(strips, 2)),
+        (coords, normed_two, out_wide, strips),
         grid=(4,),
-        mib=7,
-    )
-
-
-def run_pool(after_pooled, hidden_pooled, strips):
+        mib=8 if split else 44,
+    )
+
+
+def run_pool(after_pooled, hidden_pooled, inverse, strips):
     return call(
         pool_out,
         "pool_out",
-        [VMEM] * 3,
+        [VMEM] * 4,
         [(VMEM, jax.ShapeDtypeStruct(after_pooled.shape, F32))],
         [],
         UNIT // 2,
-        (after_pooled, hidden_pooled, by_count(strips, 2)),
-        mib=4,
+        (after_pooled, hidden_pooled, inverse, strips),
+        mib=6,
     )[0]
 
 
-def run_output(coords, gains, attended, after, grad_out, grad_two, strips, held, split):
+def run_output(coords, gains, attended, after, cot, share, grad_two, strips, held, split):
     rows = after.shape[0]
     return call(
         functools.partial(output_backward, len(held)),
         "output_backward",
-        [SMEM] + [VMEM] * (6 + len(held)),
+        [SMEM] + [VMEM] * (7 + len(held)),
         [
             (VMEM, shape_of(rows, D, dtype=F32)),
             (VMEM, shape_of(1, D, dtype=F32)),
@@ -455,9 +525,9 @@
         + targets_of((LOWER,), split),
         [pltpu.VMEM((rows, D), BF16)],
         2 * UNIT,
-        (coords, gains, attended, after, grad_out, grad_two, by_count(strips, 2), *held),
-        aliases={7 + i: 3 + i for i in range(len(held))},
-        mib=6,
+        (coords, gains, attended, after, cot, share, grad_two, strips, *held),
+        aliases={8 + i: 3 + i for i in range(len(held))},
+        mib=6 if split else 56,
     )
 
 
@@ -472,7 +542,7 @@
         7 * UNIT,
         (coords, mask, normed, qkv, grad_att, *held),
         aliases={5 + i: 1 + i for i in range(len(held))},
-        mib=6,
+        mib=6 if split else 56,
     )
 
 
@@ -485,7 +555,7 @@
         [(VMEM, shape_of(rows, D, dtype=F32)), (VMEM, shape_of(2, 1, D, dtype=F32))],
         [],
         3 * UNIT,
-        (tok, gains, grad_mixed, grad_after, gain_two, by_count(strips, 3)),
+        (tok, gains, grad_mixed, grad_after, gain_two, strips),
         mib=5,
     )
 
@@ -712,6 +782,27 @@
         out[3:6] = two[plane] + two_in[plane]
 
 
+def pick_sum(coords, high, high_in, low, low_in, mine, sent):
+    @pl.when(coords[2] >= 2)
+    def _():
+        mine[...] = high[...] + high_in[...]
+        sent[...] = low[...] + low_in[...]
+
+    @pl.when(coords[2] < 2)
+    def _():
+        mine[...] = low[...] + low_in[...]
+        sent[...] = high[...] + high_in[...]
+
+
+def renew_gains(grads, arrived, moments, gains, grads_out, moments_out, gains_out):
+    for i in range(2):
+        grad = grads[i] + arrived[i]
+        moment = DECAY_RATE * moments[i : i + 1] + (1.0 - DECAY_RATE) * grad * grad
+        grads_out[i : i + 1] = grad
+        moments_out[i : i + 1] = moment
+        gains_out[i : i + 1] = gains[i : i + 1] - GAIN_RATE * grad / (jnp.sqrt(moment) + 1e-08)
+
+
 def sum_of(left, right, out):
     @pl.loop(0, left.shape[0])
     def _(i):
@@ -761,6 +852,19 @@
     )
 
 
+def run_pick(coords, high, high_in, low, low_in):
+    return call(
+        pick_sum,
+        "pick_sum",
+        [SMEM] + [VMEM] * 4,
+        [(VMEM, shape_of(OWN, BLOCK, STRIP))] * 2,
+        [],
+        1,
+        (coords, high, high_in, low, low_in),
+        mib=4,
+    )
+
+
 def run_sum(left, right):
     return call(
         sum_of,
@@ -772,6 +876,19 @@
         (left, right),
         mib=4,
     )[0]
+
+
+def run_gains(grads, arrived, moments, gains):
+    return call(
+        renew_gains,
+        "renew_gains",
+        [VMEM] * 4,
+        [(VMEM, shape_of(2, D, dtype=F32))] * 3,
+        [],
+        1,
+        (grads, arrived, moments, gains),
+        mib=4,
+    )
 
 
 def core_hop(sent):
@@ -796,20 +913,10 @@
     return mm(left_high, right_high, left_dim, right_dim) + small
 
 
-def update(
-    coords, high, high_in, low, low_in, master, stat_left, stat_right, root_left, root_right, *outs
-):
-    grad_out, left_out, right_out, master_out, copy_out, grad = outs
+def update(mine, arrived, master, stat_left, stat_right, root_left, root_right, *outs):
+    grad_out, left_out, right_out, master_out, copy_out = outs
     strip = pl.program_id(0)
-    for condition, own, arrived in (
-        (coords[2] >= 2, high, high_in),
-        (coords[2] < 2, low, low_in),
-    ):
-
-        @pl.when(condition)
-        def _():
-            grad[...] = own[strip].astype(F32) + arrived[strip].astype(F32)
-
+    grad = mine[strip].astype(F32) + arrived[strip].astype(F32)
     for i in range(4):
         block = 4 * strip + i
         g = grad[:, i * BLOCK : (i + 1) * BLOCK]
@@ -822,18 +929,18 @@
         copy_out[i] = new.astype(BF16)
 
 
-def run_update(coords, sums, blocks):
+def run_update(sums, blocks):
     count = blocks[0].shape[0]
     tile = pl.BlockSpec((4, BLOCK, BLOCK), lambda i: (i, 0, 0))
     shape = shape_of(count, BLOCK, BLOCK, dtype=F32)
     return call(
         update,
         "update",
-        [SMEM] + [VMEM] * (len(sums) + len(blocks)),
+        [VMEM] * (len(sums) + len(blocks)),
         [(tile, shape)] * 4 + [(tile, shape_of(count, BLOCK, BLOCK))],
-        [pltpu.VMEM((BLOCK, STRIP), F32)],
+        [],
         12 * 2 * count * BLOCK**3,
-        (coords, *sums, *blocks),
+        (*sums, *blocks),
         grid=(count // 4,),
         mib=4,
     )
@@ -847,10 +954,6 @@
             hops.append((axis, [(i, i ^ step) for i in range(size)]))
             step *= 2
     return hops
-
-
-def add_hop(value, hop):
-    return run_sum(value, lax.ppermute(value, *hop))
 
 
 def plain_update(grad, master, stat_left, stat_right, root_left, root_right):
@@ -885,45 +988,39 @@
     dp_pos, half = lax.axis_index("dp"), lax.axis_index("tensor")
     coords = jnp.stack([dp_pos % 2, dp_pos // 2 % 2, dp_pos // 4, half]).astype(jnp.int32)
 
-    def prepare():
-        group_mask = token_mask.astype(F32)
-        own_mask = lax.dynamic_slice_in_dim(group_mask, half * own_caps, own_caps, 0)
-        share = 1.0 / jnp.sum(own_mask, axis=1, keepdims=True)
-        mask = jnp.repeat(own_mask.reshape(rows // GROUP, CAPS, SLOTS), SLOTS, axis=1)
-        weight = own_mask * share
-        grad_out = cotangent.astype(F32)[:, None, :] * weight[:, :, None]
-        wide = jnp.broadcast_to(weight[:, :, None], (own_caps, SLOTS, PAIR)).reshape(rows, PAIR)
-        grad_out = grad_out.reshape(rows, D)
-        return mask.swapaxes(1, 2), wide, grad_out, grad_out.astype(BF16)
-
+    coords, master = fence(coords, master)
     if split:
-        strips, prepared = gather_split(master, coords, prepare)
+        strips, prepared = gather_split(
+            master, coords, lambda: run_prepare(coords, token_mask, cotangent)
+        )
     else:
-        strips, prepared = gather_weights(master), prepare()
-    mask, share, grad_out, out_low = prepared
+        strips, prepared = gather_weights(master), run_prepare(coords, token_mask, cotangent)
+    mask, share, out_wide, inverse = prepared
     normed, qkv, attended, after, normed_two, after_pooled = run_forward(
         tokens, norm_gains, mask, share, strips
     )
-    hidden_pooled, grad_two, *held = run_mlp(coords, normed_two, out_low, share, strips, split)
+    hidden_pooled, grad_two, *held = run_mlp(coords, normed_two, out_wide, strips, split)
     hops = sum_hops()
     blocks = (master, stat_left, stat_right, root_left, root_right)
     if not split:
         grad_after, gain_two, grad_att, *held = run_output(
-            coords, norm_gains, attended, after, grad_out, grad_two, strips, held, split
+            coords, norm_gains, attended, after, cotangent, share, grad_two, strips, held, split
         )
         grad_mixed, *held = run_backward(coords, mask, normed, qkv, grad_att, held, split)
         input_grad, gain_grads = run_input(
             tokens, norm_gains, grad_mixed, grad_after, gain_two, strips
         )
-        pooled = run_pool(after_pooled, hidden_pooled, strips)
-        for hop in hops:
-            gain_grads = add_hop(gain_grads, hop)
+        pooled = run_pool(after_pooled, hidden_pooled, inverse, strips)
+        for hop in hops[:-1]:
+            gain_grads = run_sum(gain_grads, lax.ppermute(gain_grads, *hop))
+        gain_in = lax.ppermute(gain_grads, *hops[-1])
+        gain_results = run_gains(gain_grads, gain_in, gain_moments, norm_gains)
         updated = plain_update(scatter_flat(held[0], own), *blocks)
     else:
         upper_kept, upper_sent, *lower = held
         upper_in = core_hop(upper_sent)
         grad_after, gain_two, grad_att, *lower = run_output(
-            coords, norm_gains, attended, after, grad_out, grad_two, strips, lower, split
+            coords, norm_gains, attended, after, cotangent, share, grad_two, strips, lower, split
         )
         upper_in, grad_att, lower = fence(upper_in, grad_att, lower)
 
@@ -946,16 +1043,14 @@
         )
         upper_in, gain_grads = fence(upper_in, gain_grads)
 
+        gain_in = lax.ppermute(gain_grads, *hops[0])
+        pooled = run_pool(after_pooled, hidden_pooled, inverse, strips)
         high, high_sent = run_join(coords, upper_kept, upper_in)
         high_in = lax.ppermute(high_sent, "dp", NEAR_Z)
-        gain_in = lax.ppermute(gain_grads, *hops[0])
-        pooled = run_pool(after_pooled, hidden_pooled, strips)
         high_in, lower_in, gain_in, pooled = fence(high_in, lower_in, gain_in, pooled)
 
         lower_sent, lower_kept = run_again(coords, lower_kept, lower_in)
         lower_in = second_hop(lower_sent)
-        high = run_sum(high, high_in)
-        high_in = lax.ppermute(high, "dp", by_plane((0, 2), (1, 3)))
         gain_grads = run_sum(gain_grads, gain_in)
         gain_in = lax.ppermute(gain_grads, *hops[1])
         lower_in, gain_in = fence(lower_in, gain_in)
@@ -966,16 +1061,17 @@
         gain_in = lax.ppermute(gain_grads, *hops[2])
         low_in, gain_in = fence(low_in, gain_in)
 
-        low = run_sum(low, low_in)
-        low_in = lax.ppermute(low, "dp", by_plane((2, 0), (3, 1)))
+        mine, sent = run_pick(coords, high, high_in, low, low_in)
+        arrived = lax.ppermute(sent, "dp", FAR_Z)
         gain_grads = run_sum(gain_grads, gain_in)
-        for hop in hops[3:]:
-            gain_grads = add_hop(gain_grads, hop)
-        updated = run_update(coords, (high, high_in, low, low_in), blocks)
-    gain_grads = gain_grads.reshape(2, D)
-    moments_new = DECAY_RATE * gain_moments + (1.0 - DECAY_RATE) * gain_grads * gain_grads
-    gains_new = norm_gains - GAIN_RATE * gain_grads / (jnp.sqrt(moments_new) + 1e-08)
-    return (pooled, input_grad, gain_grads, moments_new, gains_new, *updated)
+        gain_in = lax.ppermute(gain_grads, *hops[3])
+        gain_grads = run_sum(gain_grads, gain_in)
+        gain_in = lax.ppermute(gain_grads, *hops[4])
+        gain_results = run_gains(gain_grads, gain_in, gain_moments, norm_gains)
+        arrived, gain_results = fence(arrived, gain_results)
+
+        updated = run_update((mine, arrived), blocks)
+    return (pooled, input_grad, *gain_results, *updated)
 
 
 def solution(mesh):

time: 260 us -> 245 us (0.942)
  waiting for transfers between devices: 97.9 us -> 116 us
  Pallas kernels: 97.2 us -> 80.1 us
  starting transfers between devices: 55.1 us -> 43.8 us
  other arithmetic: 4.33 us -> 0.08 us
    pallas_call x31, Pallas kernels: 97.2 us -> 80.1 us  [call(): pl.pallas_call(kernel, grid=grid, in_specs=in_specs, out_specs=[spec for...]
    ppermute x4 -> x3, starting transfers between devices: 18.6 us -> 7.08 us  [the longest x1 3.14 us: body(): arrived = lax.ppermute(sent, 'dp', FAR_Z)]
    ppermute x2, waiting for transfers between devices: 3.12 us -> 9.81 us  [first_hop(): lax.ppermute(sent[0], 'tensor', OTHER_Y)]
    ppermute x4 -> x3, waiting for transfers between devices: 9.36 us -> 13.7 us  [the longest x1 8.04 us: body(): gain_in = lax.ppermute(gain_grads, *hops[4])]
    convert_element_type x2 -> x0, other arithmetic: 2.77 us -> none  [the longest x1 1.57 us: prepare(): grad_out = cotangent.astype(F32)[:, None, :] * weight[:, :, None]]
  transfers between devices with their start and end apart: 37 -> 36, of which waited for: 22 -> 23; matrix products, arithmetic and copies ran while one was open for 2% -> 0% of each run, Pallas kernels for 14% -> 12%
where the time goes in v2:
time: 245 us; the launch traced here: 244 us
  waiting for transfers between devices  116 us (47%)
  Pallas kernels  80.1 us (33%)
  starting transfers between devices  43.8 us (18%)
  local copies, waits for them, and re-layouts  2.99 us (1%)
    pallas_call x31, Pallas kernels, call(): pl.pallas_call(kernel, grid=grid, in_specs=in_specs, out_specs=[spec for...  80.1 us
    ppermute x3, waiting for transfers between devices, across_hop(): lax.ppermute(pieces[0], 'tensor', OTHER_Y)  32.4 us
    ppermute x1, waiting for transfers between devices, gather_split(): far = lax.ppermute(own, 'dp', FAR_Z)  12.5 us
    ppermute x1, waiting for transfers between devices, body(): gain_in = lax.ppermute(gain_grads, *hops[0])  11.9 us
    ppermute x2, waiting for transfers between devices, first_hop(): lax.ppermute(sent[0], 'tensor', OTHER_Y)  9.81 us
    ppermute x3, waiting for transfers between devices, neighbour_hop(): lax.ppermute(value, 'tensor', OTHER_Y)  8.78 us
    ppermute x2, waiting for transfers between devices, second_hop(): lax.ppermute(sent[0], 'dp', OTHER_X)  8.25 us
    ppermute x1, waiting for transfers between devices, body(): gain_in = lax.ppermute(gain_grads, *hops[4])  8.04 us
  transfers between devices with their start and end apart: 36, of which 23 were waited for; matrix products, arithmetic and copies ran while one was open for 0% of the time, Pallas kernels for 12%

profile of v2, /device:TPU:0, one launch (start us, length us, event | category | flops | bytes accessed | tf_op | source)
XLA Modules:
  0.0 244.4 jit_solution(15623269553396230345)
XLA Ops:
  0.8 1.3 copy-done
  2.2 4.1 %collective-permute-start.3 = (bf16[1,6,96,384]{3,2,1,0:T(8,128)(2,1)S(1)}, bf16[1,6,96,384]{3,2,1,0:T(8,128)(2,1)S(1)}, u32[]{:S(2)}, u32[]{:S(2)}) collective-permute-start(bf16[1,6,96,384]{3,2,1,0:T(8,128)(2,1)S(1)} %pack.1.own), channel_id=1, source_target_pairs={{0,16},{2,18},{4,20},{6,22},{8,24},{10,26},{12,28},{14,30},{16,0},... | collective-permute-start | bytes 1327112 | tf_op jit(solution)/shard_map/ppermute | solution.py:697
  6.3 1.6 collective-permute-start.2
  7.9 1.5 collective-permute-start.1
  9.4 1.5 collective-permute-start
  10.9 0.8 copy.29.token_mask
  11.7 0.9 copy-done.7
  12.6 1.0 prepare.1
  13.5 12.5 %collective-permute-done.3.two = bf16[1,6,96,384]{3,2,1,0:T(8,128)(2,1)S(1)} collective-permute-done((bf16[1,6,96,384]{3,2,1,0:T(8,128)(2,1)S(1)}, bf16[1,6,96,384]{3,2,1,0:T(8,128)(2,1)S(1)}, u32[]{:S(2)}, u32[]{:S(2)}) %collective-permute-start.3) | collective-permute-done | bytes 442400 | tf_op jit(solution)/shard_map/ppermute | solution.py:697
  26.4 1.6 collective-permute-start.7
  28.0 1.5 collective-permute-start.6
  29.5 1.3 collective-permute-start.8
  32.0 19.8 %collective-permute-done.4.across_one = bf16[1,3,96,384]{3,2,1,0:T(8,128)(2,1)S(1)} collective-permute-done((bf16[1,3,96,384]{3,2,1,0:T(8,128)(2,1)S(1)}, bf16[1,3,96,384]{3,2,1,0:T(8,128)(2,1)S(1)}, u32[]{:S(2)}, u32[]{:S(2)}) %collective-permute-start.4) | collective-permute-done | bytes 221216 | tf_op jit(solution)/shard_map/ppermute | solution.py:691
  51.8 1.0 collective-permute-done.5.across_two
  52.8 0.9 place_own.3
  53.7 0.8 collective-permute-start.12
  54.5 1.2 collective-permute-start.11
  55.8 1.6 collective-permute-start.9
  58.0 8.8 %collective-permute-done.12.by_y = bf16[1,6,96,384]{3,2,1,0:T(8,128)(2,1)S(1)} collective-permute-done((bf16[1,6,96,384]{3,2,1,0:T(8,128)(2,1)S(1)}, bf16[1,6,96,384]{3,2,1,0:T(8,128)(2,1)S(1)}, u32[]{:S(2)}, u32[]{:S(2)}) %collective-permute-start.12) | collective-permute-done | bytes 442400 | tf_op jit(solution)/shard_map/ppermute | solution.py:687
  66.7 0.8 collective-permute-done.11.by_x
  67.5 8.2 %collective-permute-done.9.across_one = bf16[2,3,96,384]{3,2,1,0:T(8,128)(2,1)S(1)} collective-permute-done((bf16[2,3,96,384]{3,2,1,0:T(8,128)(2,1)S(1)}, bf16[2,3,96,384]{3,2,1,0:T(8,128)(2,1)S(1)}, u32[]{:S(2)}, u32[]{:S(2)}) %collective-permute-start.9) | collective-permute-done | bytes 442400 | tf_op jit(solution)/shard_map/ppermute | solution.py:691
  76.2 1.2 place_own.4
  77.5 1.3 collective-permute-start.14
  78.9 1.5 collective-permute-start.15
  81.1 4.4 %collective-permute-done.14.across_one = bf16[1,3,96,384]{3,2,1,0:T(8,128)(2,1)S(1)} collective-permute-done((bf16[1,3,96,384]{3,2,1,0:T(8,128)(2,1)S(1)}, bf16[1,3,96,384]{3,2,1,0:T(8,128)(2,1)S(1)}, u32[]{:S(2)}, u32[]{:S(2)}) %collective-permute-start.14) | collective-permute-done | bytes 221216 | tf_op jit(solution)/shard_map/ppermute | solution.py:691
  85.4 1.0 collective-permute-done.15.across_two
  86.4 0.9 place_own.5
  87.4 0.9 place_other.4._
  88.2 2.8 %collective-permute-done.17.arrived = bf16[1,2,2,6,96,384]{5,4,3,2,1,0:T(8,128)(2,1)S(1)} collective-permute-done((bf16[1,2,2,6,96,384]{5,4,3,2,1,0:T(8,128)(2,1)S(1)}, bf16[1,2,2,6,96,384]{5,4,3,2,1,0:T(8,128)(2,1)S(1)}, u32[]{:S(2)}, u32[]{:S(2)}) %collective-permute-start.17) | collective-permute-done | bytes 1769504 | tf_op jit(solution)/shard_map/ppermute | solution.py:895
  91.8 10.7 %attention_forward.1 = (bf16[768,768]{1,0:T(8,128)(2,1)S(1)}, bf16[6,768,384]{2,1,0:T(8,128)(2,1)S(1)}, bf16[768,768]{1,0:T(8,128)(2,1)S(1)}, f32[768,768]{1,0:T...) custom-call(bf16[768,768]{1,0:T(8,128)(2,1)S(1)} %copy-done.2, f32[2,768]{1,0:T(2,128)S(1)} %copy-done.9, ...), custom_call_target="tpu_custom_call" | custom-call | flops 1 | bytes 1 | tf_op jit(solution)/shard_map/attention_forward/pallas_call | solution.py:410
  102.4 25.1 %mlp_both.1 = (f32[4,768,128]{2,1,0:T(8,128)S(1)}, f32[768,768]{1,0:T(8,128)S(1)}, bf16[2,2,2,6,96,384]{5,4,3,2,1,0:T(8,128)(2,1)S(1)}, bf16[2,2,2,6,96,384]{5,4...) custom-call(s32[4]{0:T(128)S(1)} %pad_add_fusion.coords, ...), custom_call_target="tpu_custom_call" | custom-call | flops 1 | bytes 1 | tf_op jit(solution)/shard_map/mlp_both/pallas_call | solution.py:410
  127.8 5.2 %output_backward.1 = (f32[768,768]{1,0:T(8,128)S(1)}, f32[1,768]{1,0:T(1,128)S(1)}, bf16[768,768]{1,0:T(8,128)(2,1)S(1)}, bf16[2,2,2,6,96,384]{5,4,3,2,1,0:T(8,128)(2,1)S(1)}, bf16[2,2,2,6,96,384]{5,4,3,2,1,0:T(8,128)(2,1)S(1)}) custom-call(s32[4]{0:T(128)S(1)} %pad_add_fusion.coords, ...), custom_call_target="tpu_custom_call", output_to_operand_aliasing={{3}: (8, {}), {4}: (9, {})} | custom-call | flops 1 | bytes 1 | tf_op jit(solution)/shard_map/output_backward/pallas_call | solution.py:410
  133.0 0.8 collective-permute-done.18.arrived
  133.8 1.1 split_sum.2
  134.9 0.8 collective-permute-start.19
  135.7 1.2 collective-permute-start.20
  136.9 9.9 %attention_backward.1 = (bf16[6,768,384]{2,1,0:T(8,128)(2,1)S(1)}, bf16[2,2,2,6,96,384]{5,4,3,2,1,0:T(8,128)(2,1)S(1)}, bf16[2,2,2,6,96,384]{5,4,3,2,1,0:T(8,128)(2,1)S(1)}) custom-call(s32[4]{0:T(128)S(1)} %pad_add_fusion.coords, f32[6,16,128]{2,1,0:T(8,128)S(1)} %get-tuple-element.148.mask, ...), custom_call_target="tpu_custom_call", output_to_operand_aliasing={{1}: (5, {}), {2}: (6, {})} | custom-call | flops 1 | bytes 1 | tf_op jit(solution)/shard_map/attention_backward/pallas_call | solution.py:410
  146.9 9.8 %collective-permute-done.19.one_in = bf16[2,2,3,96,384]{4,3,2,1,0:T(8,128)(2,1)S(1)} collective-permute-done((bf16[2,2,3,96,384]{4,3,2,1,0:T(8,128)(2,1)S(1)}, bf16[2,2,3,96,384]{4,3,2,1,0:T(8,128)(2,1)S(1)}, u32[]{:S(2)}, u32[]{:S(2)}) %collective-permute-start.19) | collective-permute-done | bytes 884768 | tf_op jit(solution)/shard_map/ppermute | solution.py:899
  157.1 0.8 split_again.2
  158.0 1.3 collective-permute-start.21
  159.3 1.5 collective-permute-start.22
  160.8 2.5 %collective-permute-done.23.arrived = bf16[2,2,2,6,96,384]{5,4,3,2,1,0:T(8,128)(2,1)S(1)} collective-permute-done((bf16[2,2,2,6,96,384]{5,4,3,2,1,0:T(8,128)(2,1)S(1)}, bf16[2,2,2,6,96,384]{5,4,3,2,1,0:T(8,128)(2,1)S(1)}, u32[]{:S(2)}, u32[]{:S(2)}) %collective-permute-start.23) | collective-permute-done | bytes 3538976 | tf_op jit(solution)/shard_map/ppermute | solution.py:895
  163.3 1.1 split_sum.3
  164.4 1.4 collective-permute-start.25
  165.8 1.5 collective-permute-start.26
  167.2 6.5 %input_backward.1 = (f32[768,768]{1,0:T(8,128)}, f32[2,1,768]{2,1,0:T(1,128)S(1)}) custom-call(bf16[768,768]{1,0:T(8,128)(2,1)S(1)} %copy-done.2, f32[2,768]{1,0:T(2,128)S(1)} %copy-done.9, bf16[6,768,384]{2,1,0:T(8,128)(2,1)S(1)} %get-tuple-element.227.grad_mixed, f32[768,768]{1,0:T(8,128)S(1)} %get-tuple-element.228.grad_after, ...), custom_call_target="tpu_custom_call" | custom-call | flops 1 | bytes 1 | tf_op jit(solution)/shard_map/input_backward/pallas_call | solution.py:410
  174.5 1.7 collective-permute-start.24
  176.7 2.1 pool_out.1
  178.8 11.9 %collective-permute-done.27.right = f32[2,1,768]{2,1,0:T(1,128)S(1)} collective-permute-done((f32[2,1,768]{2,1,0:T(1,128)S(1)}, f32[2,1,768]{2,1,0:T(1,128)S(1)}, u32[]{:S(2)}, u32[]{:S(2)}) %collective-permute-start.27) | collective-permute-done | bytes 6176 | tf_op jit(solution)/shard_map/ppermute | solution.py:1046
  190.7 0.8 split_again.3
  191.6 0.8 collective-permute-start.28
  192.5 1.3 collective-permute-start.29
  193.8 1.2 collective-permute-done.30.right
  194.9 8.2 %collective-permute-done.28.one_in = bf16[2,3,96,384]{3,2,1,0:T(8,128)(2,1)S(1)} collective-permute-done((bf16[2,3,96,384]{3,2,1,0:T(8,128)(2,1)S(1)}, bf16[2,3,96,384]{3,2,1,0:T(8,128)(2,1)S(1)}, u32[]{:S(2)}, u32[]{:S(2)}) %collective-permute-start.28) | collective-permute-done | bytes 442400 | tf_op jit(solution)/shard_map/ppermute | solution.py:903
  204.4 1.5 collective-permute-start.31
  205.8 1.5 collective-permute-start.32
  207.3 2.1 collective-permute-done.32.right
  209.5 5.2 %collective-permute-done.31.low_in = bf16[6,96,384]{2,1,0:T(8,128)(2,1)S(1)} collective-permute-done((bf16[6,96,384]{2,1,0:T(8,128)(2,1)S(1)}, bf16[6,96,384]{2,1,0:T(8,128)(2,1)S(1)}, u32[]{:S(2)}, u32[]{:S(2)}) %collective-permute-start.31) | collective-permute-done | bytes 442400 | tf_op jit(solution)/shard_map/ppermute | solution.py:1059
  215.4 3.1 %collective-permute-start.33 = (bf16[6,96,384]{2,1,0:T(8,128)(2,1)S(1)}, bf16[6,96,384]{2,1,0:T(8,128)(2,1)S(1)}, u32[]{:S(2)}, u32[]{:S(2)}) collective-permute-start(bf16[6,96,384]{2,1,0:T(8,128)(2,1)S(1)} %get-tuple-element.259), channel_id=1, source_target_pairs={{0,16},{2,18},{4,20},{6,22},{8,24},{10,26},{12,28},{14,30},{16,0},... | collective-permute-start | bytes 1327112 | tf_op jit(solution)/shard_map/ppermute | solution.py:1065
  218.5 1.7 collective-permute-start.34
  220.3 5.7 %collective-permute-done.34.right = f32[2,1,768]{2,1,0:T(1,128)S(1)} collective-permute-done((f32[2,1,768]{2,1,0:T(1,128)S(1)}, f32[2,1,768]{2,1,0:T(1,128)S(1)}, u32[]{:S(2)}, u32[]{:S(2)}) %collective-permute-start.34) | collective-permute-done | bytes 6176 | tf_op jit(solution)/shard_map/ppermute | solution.py:1067
  226.0 2.2 collective-permute-start.35
  228.2 8.0 %collective-permute-done.35.arrived = f32[2,1,768]{2,1,0:T(1,128)S(1)} collective-permute-done((f32[2,1,768]{2,1,0:T(1,128)S(1)}, f32[2,1,768]{2,1,0:T(1,128)S(1)}, u32[]{:S(2)}, u32[]{:S(2)}) %collective-permute-start.35) | collective-permute-done | bytes 6176 | tf_op jit(solution)/shard_map/ppermute | solution.py:1069
  236.8 7.6 %update.1 = (f32[24,96,96]{2,1,0:T(8,128)}, f32[24,96,96]{2,1,0:T(8,128)}, f32[24,96,96]{2,1,0:T(8,128)}, f32[24,96,96]{2,1,0:T(8,128)}, bf16[24,96,96]{2,1,0:T(8,128)(2,1)}) custom-call(bf16[6,96,384]{2,1,0:T(8,128)(2,1)S(1)} %get-tuple-element.267.mine, bf16[6,96,384]{2,1,0:T(8,128)(2,1)S(1)} %collective-permute-done.33.arrived, ...), custom_call_target="tpu_custom_call" | custom-call | flops 1 | bytes 1 | tf_op jit(solution)/shard_map/update/pallas_call | solution.py:410
  (63 shorter events, 8.9 us)
Async XLA Ops:
  0.8 1.3 copy-start
  2.2 23.9 %collective-permute-start.3 = (bf16[1,6,96,384]{3,2,1,0:T(8,128)(2,1)S(1)}, bf16[1,6,96,384]{3,2,1,0:T(8,128)(2,1)S(1)}, u32[]{:S(2)}, u32[]{:S(2)}) collective-permute-start(bf16[1,6,96,384]{3,2,1,0:T(8,128)(2,1)S(1)} %pack.1.own), channel_id=1, source_target_pairs={{0,16},{2,18},{4,20},{6,22},{8,24},{10,26},{12,28},{14,30},{16,0},... | collective-permute-start | bytes 1327112 | tf_op jit(solution)/shard_map/ppermute | solution.py:697
  6.3 19.9 %collective-permute-start.2 = (bf16[1,6,96,384]{3,2,1,0:T(8,128)(2,1)S(1)}, bf16[1,6,96,384]{3,2,1,0:T(8,128)(2,1)S(1)}, u32[]{:S(2)}, u32[]{:S(2)}) collective-permute-start(bf16[1,6,96,384]{3,2,1,0:T(8,128)(2,1)S(1)} %pack.1.own), channel_id=1, source_target_pairs={{0,8},{2,10},{4,12},{6,14},{8,0},{10,2},{12,4},{14,6},{16,24},{18,... | collective-permute-start | bytes 1327112 | tf_op jit(solution)/shard_map/ppermute | solution.py:696
  7.9 18.4 %collective-permute-start.1 = (bf16[1,6,96,384]{3,2,1,0:T(8,128)(2,1)S(1)}, bf16[1,6,96,384]{3,2,1,0:T(8,128)(2,1)S(1)}, u32[]{:S(2)}, u32[]{:S(2)}) collective-permute-start(bf16[1,6,96,384]{3,2,1,0:T(8,128)(2,1)S(1)} %pack.1.own), channel_id=1, source_target_pairs={{0,1},{1,0},{2,3},{3,2},{4,5},{5,4},{6,7},{7,6},{8,9},{9,8},{10,11... | collective-permute-start | bytes 1327112 | tf_op jit(solution)/shard_map/ppermute | solution.py:687
  9.4 16.9 %collective-permute-start = (bf16[1,6,96,384]{3,2,1,0:T(8,128)(2,1)S(1)}, bf16[1,6,96,384]{3,2,1,0:T(8,128)(2,1)S(1)}, u32[]{:S(2)}, u32[]{:S(2)}) collective-permute-start(bf16[1,6,96,384]{3,2,1,0:T(8,128)(2,1)S(1)} %pack.1.own), channel_id=1, source_target_pairs={{0,4},{2,6},{4,0},{6,2},{8,12},{10,14},{12,8},{14,10},{16,20},{18,... | collective-permute-start | bytes 1327112 | tf_op jit(solution)/shard_map/ppermute | solution.py:687
  11.7 0.9 copy-start.7
  26.4 26.4 %collective-permute-start.7 = (bf16[2,6,96,384]{3,2,1,0:T(8,128)(2,1)S(1)}, bf16[2,6,96,384]{3,2,1,0:T(8,128)(2,1)S(1)}, u32[]{:S(2)}, u32[]{:S(2)}) collective-permute-start(bf16[2,6,96,384]{3,2,1,0:T(8,128)(2,1)S(1)} %take_both.1.own), channel_id=1, source_target_pairs={{0,1},{1,0},{2,3},{3,2},{4,5},{5,4},{6,7},{7,6},{8,9},{9,8},{10,11... | collective-permute-start | bytes 2654216 | tf_op jit(solution)/shard_map/ppermute | solution.py:687
  28.0 24.8 %collective-permute-start.6 = (bf16[2,6,96,384]{3,2,1,0:T(8,128)(2,1)S(1)}, bf16[2,6,96,384]{3,2,1,0:T(8,128)(2,1)S(1)}, u32[]{:S(2)}, u32[]{:S(2)}) collective-permute-start(bf16[2,6,96,384]{3,2,1,0:T(8,128)(2,1)S(1)} %take_both.1.own), channel_id=1, source_target_pairs={{0,4},{2,6},{4,0},{6,2},{8,12},{10,14},{12,8},{14,10},{16,20},{18,... | collective-permute-start | bytes 2654216 | tf_op jit(solution)/shard_map/ppermute | solution.py:687
  29.5 23.3 %collective-permute-start.8 = (bf16[1,6,96,384]{3,2,1,0:T(8,128)(2,1)S(1)}, bf16[1,6,96,384]{3,2,1,0:T(8,128)(2,1)S(1)}, u32[]{:S(2)}, u32[]{:S(2)}) collective-permute-start(bf16[1,6,96,384]{3,2,1,0:T(8,128)(2,1)S(1)} %collective-permute-done.2.one), channel_id=1, source_target_pairs={{0,16},{2,18},{4,20},{6,22},{8,24},{10,26},{12,28},{14,30},{16,0},... | collective-permute-start | bytes 1327112 | tf_op jit(solution)/shard_map/ppermute | solution.py:701
  30.9 20.9 %collective-permute-start.4 = (bf16[1,3,96,384]{3,2,1,0:T(8,128)(2,1)S(1)}, bf16[1,3,96,384]{3,2,1,0:T(8,128)(2,1)S(1)}, u32[]{:S(2)}, u32[]{:S(2)}) collective-permute-start(bf16[1,3,96,384]{3,2,1,0:T(8,128)(2,1)S(1)} %get-tuple-element.152), channel_id=1, source_target_pairs={{0,1},{1,0},{2,3},{3,2},{4,5},{5,4},{6,7},{7,6},{8,9},{9,8},{10,11... | collective-permute-start | bytes 663560 | tf_op jit(solution)/shard_map/ppermute | solution.py:691
  31.4 21.3 %collective-permute-start.5 = (bf16[1,3,96,384]{3,2,1,0:T(8,128)(2,1)S(1)}, bf16[1,3,96,384]{3,2,1,0:T(8,128)(2,1)S(1)}, u32[]{:S(2)}, u32[]{:S(2)}) collective-permute-start(bf16[1,3,96,384]{3,2,1,0:T(8,128)(2,1)S(1)} %get-tuple-element.153), channel_id=1, source_target_pairs={{0,4},{2,6},{4,0},{6,2},{8,12},{10,14},{12,8},{14,10},{16,20},{18,... | collective-permute-start | bytes 663560 | tf_op jit(solution)/shard_map/ppermute | solution.py:691
  53.6 22.6 %collective-permute-start.13 = (bf16[1,2,2,6,96,384]{5,4,3,2,1,0:T(8,128)(2,1)S(1)}, bf16[1,2,2,6,96,384]{5,4,3,2,1,0:T(8,128)(2,1)S(1)}, u32[]{:S(2)}, u32[]{:S(2)}) collective-permute-start(bf16[1,2,2,6,96,384]{5,4,3,2,1,0:T(8,128)(2,1)S(1)} %get-tuple-element.164), channel_id=1, source_target_pairs={{0,2},{2,0},{4,6},{6,4},{8,10},{10,8},{12,14},{14,12},{16,18},{18,... | collective-permute-start | bytes 5308424 | tf_op jit(solution)/shard_map/ppermute | solution.py:895
  53.7 13.0 %collective-permute-start.12 = (bf16[1,6,96,384]{3,2,1,0:T(8,128)(2,1)S(1)}, bf16[1,6,96,384]{3,2,1,0:T(8,128)(2,1)S(1)}, u32[]{:S(2)}, u32[]{:S(2)}) collective-permute-start(bf16[1,6,96,384]{3,2,1,0:T(8,128)(2,1)S(1)} %collective-permute-done.8.own), channel_id=1, source_target_pairs={{0,1},{1,0},{2,3},{3,2},{4,5},{5,4},{6,7},{7,6},{8,9},{9,8},{10,11... | collective-permute-start | bytes 1327112 | tf_op jit(solution)/shard_map/ppermute | solution.py:687
  54.5 13.0 %collective-permute-start.11 = (bf16[1,6,96,384]{3,2,1,0:T(8,128)(2,1)S(1)}, bf16[1,6,96,384]{3,2,1,0:T(8,128)(2,1)S(1)}, u32[]{:S(2)}, u32[]{:S(2)}) collective-permute-start(bf16[1,6,96,384]{3,2,1,0:T(8,128)(2,1)S(1)} %collective-permute-done.8.own), channel_id=1, source_target_pairs={{0,4},{2,6},{4,0},{6,2},{8,12},{10,14},{12,8},{14,10},{16,20},{18,... | collective-permute-start | bytes 1327112 | tf_op jit(solution)/shard_map/ppermute | solution.py:687
  55.8 19.9 %collective-permute-start.9 = (bf16[2,3,96,384]{3,2,1,0:T(8,128)(2,1)S(1)}, bf16[2,3,96,384]{3,2,1,0:T(8,128)(2,1)S(1)}, u32[]{:S(2)}, u32[]{:S(2)}) collective-permute-start(bf16[2,3,96,384]{3,2,1,0:T(8,128)(2,1)S(1)} %get-tuple-element.159), channel_id=1, source_target_pairs={{0,1},{1,0},{2,3},{3,2},{4,5},{5,4},{6,7},{7,6},{8,9},{9,8},{10,11... | collective-permute-start | bytes 1327112 | tf_op jit(solution)/shard_map/ppermute | solution.py:691
  57.4 18.8 %collective-permute-start.10 = (bf16[2,3,96,384]{3,2,1,0:T(8,128)(2,1)S(1)}, bf16[2,3,96,384]{3,2,1,0:T(8,128)(2,1)S(1)}, u32[]{:S(2)}, u32[]{:S(2)}) collective-permute-start(bf16[2,3,96,384]{3,2,1,0:T(8,128)(2,1)S(1)} %get-tuple-element.160), channel_id=1, source_target_pairs={{0,4},{2,6},{4,0},{6,2},{8,12},{10,14},{12,8},{14,10},{16,20},{18,... | collective-permute-start | bytes 1327112 | tf_op jit(solution)/shard_map/ppermute | solution.py:691
  77.4 9.0 %collective-permute-start.16 = (bf16[2,2,2,6,96,384]{5,4,3,2,1,0:T(8,128)(2,1)S(1)}, bf16[2,2,2,6,96,384]{5,4,3,2,1,0:T(8,128)(2,1)S(1)}, u32[]{:S(2)}, u32[]{:S(2)}) collective-permute-start(bf16[2,2,2,6,96,384]{5,4,3,2,1,0:T(8,128)(2,1)S(1)} %get-tuple-element.173), channel_id=1, source_target_pairs={{0,2},{2,0},{4,6},{6,4},{8,10},{10,8},{12,14},{14,12},{16,18},{18,... | collective-permute-start | bytes 10616840 | tf_op jit(solution)/shard_map/ppermute | solution.py:895
  77.5 7.9 %collective-permute-start.14 = (bf16[1,3,96,384]{3,2,1,0:T(8,128)(2,1)S(1)}, bf16[1,3,96,384]{3,2,1,0:T(8,128)(2,1)S(1)}, u32[]{:S(2)}, u32[]{:S(2)}) collective-permute-start(bf16[1,3,96,384]{3,2,1,0:T(8,128)(2,1)S(1)} %get-tuple-element.168), channel_id=1, source_target_pairs={{0,1},{1,0},{2,3},{3,2},{4,5},{5,4},{6,7},{7,6},{8,9},{9,8},{10,11... | collective-permute-start | bytes 663560 | tf_op jit(solution)/shard_map/ppermute | solution.py:691
  78.9 7.5 %collective-permute-start.15 = (bf16[1,3,96,384]{3,2,1,0:T(8,128)(2,1)S(1)}, bf16[1,3,96,384]{3,2,1,0:T(8,128)(2,1)S(1)}, u32[]{:S(2)}, u32[]{:S(2)}) collective-permute-start(bf16[1,3,96,384]{3,2,1,0:T(8,128)(2,1)S(1)} %get-tuple-element.169), channel_id=1, source_target_pairs={{0,4},{2,6},{4,0},{6,2},{8,12},{10,14},{12,8},{14,10},{16,20},{18,... | collective-permute-start | bytes 663560 | tf_op jit(solution)/shard_map/ppermute | solution.py:691
  87.3 3.8 %collective-permute-start.17 = (bf16[1,2,2,6,96,384]{5,4,3,2,1,0:T(8,128)(2,1)S(1)}, bf16[1,2,2,6,96,384]{5,4,3,2,1,0:T(8,128)(2,1)S(1)}, u32[]{:S(2)}, u32[]{:S(2)}) collective-permute-start(bf16[1,2,2,6,96,384]{5,4,3,2,1,0:T(8,128)(2,1)S(1)} %get-tuple-element.179), channel_id=1, source_target_pairs={{0,2},{2,0},{4,6},{6,4},{8,10},{10,8},{12,14},{14,12},{16,18},{18,... | collective-permute-start | bytes 5308424 | tf_op jit(solution)/shard_map/ppermute | solution.py:895
  88.2 3.5 %copy-start.2 = (bf16[768,768]{1,0:T(8,128)(2,1)S(1)}, bf16[768,768]{1,0:T(8,128)(2,1)}, u32[]{:S(2)}) copy-start(bf16[768,768]{1,0:T(8,128)(2,1)} %tok.3) | copy-start | bytes 3538948
  88.2 3.5 %copy-start.9 = (f32[2,768]{1,0:T(2,128)S(1)}, f32[2,768]{1,0:T(2,128)}, u32[]{:S(2)}) copy-start(f32[2,768]{1,0:T(2,128)} %gains.7) | copy-start | bytes 18436
  102.4 25.3 %copy-start.8 = (bf16[48,768]{1,0:T(8,128)(2,1)S(1)}, bf16[48,768]{1,0:T(8,128)(2,1)}, u32[]{:S(2)}) copy-start(bf16[48,768]{1,0:T(8,128)(2,1)} %cot.3) | copy-start | bytes 221188
  127.5 6.3 %collective-permute-start.18 = (bf16[2,2,2,6,96,384]{5,4,3,2,1,0:T(8,128)(2,1)S(1)}, bf16[2,2,2,6,96,384]{5,4,3,2,1,0:T(8,128)(2,1)S(1)}, u32[]{:S(2)}, u32[]{:S(2)}) collective-permute-start(bf16[2,2,2,6,96,384]{5,4,3,2,1,0:T(8,128)(2,1)S(1)} %get-tuple-element.187), channel_id=1, source_target_pairs={{0,2},{2,0},{4,6},{6,4},{8,10},{10,8},{12,14},{14,12},{16,18},{18,... | collective-permute-start | bytes 10616840 | tf_op jit(solution)/shard_map/ppermute | solution.py:895
  134.9 21.8 %collective-permute-start.19 = (bf16[2,2,3,96,384]{4,3,2,1,0:T(8,128)(2,1)S(1)}, bf16[2,2,3,96,384]{4,3,2,1,0:T(8,128)(2,1)S(1)}, u32[]{:S(2)}, u32[]{:S(2)}) collective-permute-start(bf16[2,2,3,96,384]{4,3,2,1,0:T(8,128)(2,1)S(1)} %get-tuple-element.204), channel_id=1, source_target_pairs={{0,1},{1,0},{2,3},{3,2},{4,5},{5,4},{6,7},{7,6},{8,9},{9,8},{10,11... | collective-permute-start | bytes 2654216 | tf_op jit(solution)/shard_map/ppermute | solution.py:899
  135.7 21.4 %collective-permute-start.20 = (bf16[2,2,3,96,384]{4,3,2,1,0:T(8,128)(2,1)S(1)}, bf16[2,2,3,96,384]{4,3,2,1,0:T(8,128)(2,1)S(1)}, u32[]{:S(2)}, u32[]{:S(2)}) collective-permute-start(bf16[2,2,3,96,384]{4,3,2,1,0:T(8,128)(2,1)S(1)} %get-tuple-element.205), channel_id=1, source_target_pairs={{0,4},{2,6},{4,0},{6,2},{8,12},{10,14},{12,8},{14,10},{16,20},{18,... | collective-permute-start | bytes 2654216 | tf_op jit(solution)/shard_map/ppermute | solution.py:899
  157.1 6.2 %collective-permute-start.23 = (bf16[2,2,2,6,96,384]{5,4,3,2,1,0:T(8,128)(2,1)S(1)}, bf16[2,2,2,6,96,384]{5,4,3,2,1,0:T(8,128)(2,1)S(1)}, u32[]{:S(2)}, u32[]{:S(2)}) collective-permute-start(bf16[2,2,2,6,96,384]{5,4,3,2,1,0:T(8,128)(2,1)S(1)} %get-tuple-element.221), channel_id=1, source_target_pairs={{0,2},{2,0},{4,6},{6,4},{8,10},{10,8},{12,14},{14,12},{16,18},{18,... | collective-permute-start | bytes 10616840 | tf_op jit(solution)/shard_map/ppermute | solution.py:895
  158.0 15.8 %collective-permute-start.21 = (bf16[2,3,96,384]{3,2,1,0:T(8,128)(2,1)S(1)}, bf16[2,3,96,384]{3,2,1,0:T(8,128)(2,1)S(1)}, u32[]{:S(2)}, u32[]{:S(2)}) collective-permute-start(bf16[2,3,96,384]{3,2,1,0:T(8,128)(2,1)S(1)} %get-tuple-element.218), channel_id=1, source_target_pairs={{0,4},{2,6},{4,0},{6,2},{8,12},{10,14},{12,8},{14,10},{16,20},{18,... | collective-permute-start | bytes 1327112 | tf_op jit(solution)/shard_map/ppermute | solution.py:903
  159.3 14.4 %collective-permute-start.22 = (bf16[2,3,96,384]{3,2,1,0:T(8,128)(2,1)S(1)}, bf16[2,3,96,384]{3,2,1,0:T(8,128)(2,1)S(1)}, u32[]{:S(2)}, u32[]{:S(2)}) collective-permute-start(bf16[2,3,96,384]{3,2,1,0:T(8,128)(2,1)S(1)} %get-tuple-element.219), channel_id=1, source_target_pairs={{0,1},{1,0},{2,3},{3,2},{4,5},{5,4},{6,7},{7,6},{8,9},{9,8},{10,11... | collective-permute-start | bytes 1327112 | tf_op jit(solution)/shard_map/ppermute | solution.py:903
  164.4 26.3 %collective-permute-start.25 = (bf16[2,2,3,96,384]{4,3,2,1,0:T(8,128)(2,1)S(1)}, bf16[2,2,3,96,384]{4,3,2,1,0:T(8,128)(2,1)S(1)}, u32[]{:S(2)}, u32[]{:S(2)}) collective-permute-start(bf16[2,2,3,96,384]{4,3,2,1,0:T(8,128)(2,1)S(1)} %get-tuple-element.234), channel_id=1, source_target_pairs={{0,1},{1,0},{2,3},{3,2},{4,5},{5,4},{6,7},{7,6},{8,9},{9,8},{10,11... | collective-permute-start | bytes 2654216 | tf_op jit(solution)/shard_map/ppermute | solution.py:899
  165.8 24.9 %collective-permute-start.26 = (bf16[2,2,3,96,384]{4,3,2,1,0:T(8,128)(2,1)S(1)}, bf16[2,2,3,96,384]{4,3,2,1,0:T(8,128)(2,1)S(1)}, u32[]{:S(2)}, u32[]{:S(2)}) collective-permute-start(bf16[2,2,3,96,384]{4,3,2,1,0:T(8,128)(2,1)S(1)} %get-tuple-element.235), channel_id=1, source_target_pairs={{0,4},{2,6},{4,0},{6,2},{8,12},{10,14},{12,8},{14,10},{16,20},{18,... | collective-permute-start | bytes 2654216 | tf_op jit(solution)/shard_map/ppermute | solution.py:899
  174.5 16.2 %collective-permute-start.24 = (bf16[6,96,384]{2,1,0:T(8,128)(2,1)S(1)}, bf16[6,96,384]{2,1,0:T(8,128)(2,1)S(1)}, u32[]{:S(2)}, u32[]{:S(2)}) collective-permute-start(bf16[6,96,384]{2,1,0:T(8,128)(2,1)S(1)} %get-tuple-element.233), channel_id=1, source_target_pairs={{0,8},{2,10},{4,12},{6,14},{8,0},{10,2},{12,4},{14,6},{16,24},{18,... | collective-permute-start | bytes 1327112 | tf_op jit(solution)/shard_map/ppermute | solution.py:1049
  176.2 14.5 %collective-permute-start.27 = (f32[2,1,768]{2,1,0:T(1,128)S(1)}, f32[2,1,768]{2,1,0:T(1,128)S(1)}, u32[]{:S(2)}, u32[]{:S(2)}) collective-permute-start(f32[2,1,768]{2,1,0:T(1,128)S(1)} %get-tuple-element.236.left), channel_id=1, source_target_pairs={{0,1},{1,0},{2,3},{3,2},{4,5},{5,4},{6,7},{7,6},{8,9},{9,8},{10,11... | collective-permute-start | bytes 18440 | tf_op jit(solution)/shard_map/ppermute | solution.py:1046
  190.7 46.1 %copy-start.5 = (f32[24,96,96]{2,1,0:T(8,128)S(1)}, f32[24,96,96]{2,1,0:T(8,128)}, u32[]{:S(2)}) copy-start(f32[24,96,96]{2,1,0:T(8,128)} %root_left.1) | copy-start | bytes 2654212
  190.7 46.1 %copy-start.6 = (f32[24,96,96]{2,1,0:T(8,128)S(1)}, f32[24,96,96]{2,1,0:T(8,128)}, u32[]{:S(2)}) copy-start(f32[24,96,96]{2,1,0:T(8,128)} %root_right.1) | copy-start | bytes 2654212
  191.6 44.6 %copy-start.10 = (f32[2,768]{1,0:T(2,128)S(1)}, f32[2,768]{1,0:T(2,128)}, u32[]{:S(2)}) copy-start(f32[2,768]{1,0:T(2,128)} %moments.1) | copy-start | bytes 18436
  191.6 45.2 %copy-start.1 = (f32[24,96,96]{2,1,0:T(8,128)S(1)}, f32[24,96,96]{2,1,0:T(8,128)}, u32[]{:S(2)}) copy-start(f32[24,96,96]{2,1,0:T(8,128)} %master.1) | copy-start | bytes 2654212
  191.6 45.2 %copy-start.3 = (f32[24,96,96]{2,1,0:T(8,128)S(1)}, f32[24,96,96]{2,1,0:T(8,128)}, u32[]{:S(2)}) copy-start(f32[24,96,96]{2,1,0:T(8,128)} %stat_left.1) | copy-start | bytes 2654212
  191.6 45.2 %copy-start.4 = (f32[24,96,96]{2,1,0:T(8,128)S(1)}, f32[24,96,96]{2,1,0:T(8,128)}, u32[]{:S(2)}) copy-start(f32[24,96,96]{2,1,0:T(8,128)} %stat_right.1) | copy-start | bytes 2654212
  191.6 11.5 %collective-permute-start.28 = (bf16[2,3,96,384]{3,2,1,0:T(8,128)(2,1)S(1)}, bf16[2,3,96,384]{3,2,1,0:T(8,128)(2,1)S(1)}, u32[]{:S(2)}, u32[]{:S(2)}) collective-permute-start(bf16[2,3,96,384]{3,2,1,0:T(8,128)(2,1)S(1)} %get-tuple-element.250), channel_id=1, source_target_pairs={{0,4},{2,6},{4,0},{6,2},{8,12},{10,14},{12,8},{14,10},{16,20},{18,... | collective-permute-start | bytes 1327112 | tf_op jit(solution)/shard_map/ppermute | solution.py:903
  192.5 11.2 %collective-permute-start.29 = (bf16[2,3,96,384]{3,2,1,0:T(8,128)(2,1)S(1)}, bf16[2,3,96,384]{3,2,1,0:T(8,128)(2,1)S(1)}, u32[]{:S(2)}, u32[]{:S(2)}) collective-permute-start(bf16[2,3,96,384]{3,2,1,0:T(8,128)(2,1)S(1)} %get-tuple-element.251), channel_id=1, source_target_pairs={{0,1},{1,0},{2,3},{3,2},{4,5},{5,4},{6,7},{7,6},{8,9},{9,8},{10,11... | collective-permute-start | bytes 1327112 | tf_op jit(solution)/shard_map/ppermute | solution.py:903
  193.8 1.2 collective-permute-start.30
  204.4 10.3 %collective-permute-start.31 = (bf16[6,96,384]{2,1,0:T(8,128)(2,1)S(1)}, bf16[6,96,384]{2,1,0:T(8,128)(2,1)S(1)}, u32[]{:S(2)}, u32[]{:S(2)}) collective-permute-start(bf16[6,96,384]{2,1,0:T(8,128)(2,1)S(1)} %get-tuple-element.256), channel_id=1, source_target_pairs={{0,8},{2,10},{4,12},{6,14},{8,0},{10,2},{12,4},{14,6},{16,24},{18,... | collective-permute-start | bytes 1327112 | tf_op jit(solution)/shard_map/ppermute | solution.py:1059
  205.8 3.6 %collective-permute-start.32 = (f32[2,1,768]{2,1,0:T(1,128)S(1)}, f32[2,1,768]{2,1,0:T(1,128)S(1)}, u32[]{:S(2)}, u32[]{:S(2)}) collective-permute-start(f32[2,1,768]{2,1,0:T(1,128)S(1)} %sum_of.5.left), channel_id=1, source_target_pairs={{0,4},{2,6},{4,0},{6,2},{8,12},{10,14},{12,8},{14,10},{16,20},{18,... | collective-permute-start | bytes 18440 | tf_op jit(solution)/shard_map/ppermute | solution.py:1061
  215.4 21.4 %collective-permute-start.33 = (bf16[6,96,384]{2,1,0:T(8,128)(2,1)S(1)}, bf16[6,96,384]{2,1,0:T(8,128)(2,1)S(1)}, u32[]{:S(2)}, u32[]{:S(2)}) collective-permute-start(bf16[6,96,384]{2,1,0:T(8,128)(2,1)S(1)} %get-tuple-element.259), channel_id=1, source_target_pairs={{0,16},{2,18},{4,20},{6,22},{8,24},{10,26},{12,28},{14,30},{16,0},... | collective-permute-start | bytes 1327112 | tf_op jit(solution)/shard_map/ppermute | solution.py:1065
  218.5 7.4 %collective-permute-start.34 = (f32[2,1,768]{2,1,0:T(1,128)S(1)}, f32[2,1,768]{2,1,0:T(1,128)S(1)}, u32[]{:S(2)}, u32[]{:S(2)}) collective-permute-start(f32[2,1,768]{2,1,0:T(1,128)S(1)} %sum_of.6.left), channel_id=1, source_target_pairs={{0,8},{2,10},{4,12},{6,14},{8,0},{10,2},{12,4},{14,6},{16,24},{18,... | collective-permute-start | bytes 18440 | tf_op jit(solution)/shard_map/ppermute | solution.py:1067
  226.0 10.2 %collective-permute-start.35 = (f32[2,1,768]{2,1,0:T(1,128)S(1)}, f32[2,1,768]{2,1,0:T(1,128)S(1)}, u32[]{:S(2)}, u32[]{:S(2)}) collective-permute-start(f32[2,1,768]{2,1,0:T(1,128)S(1)} %sum_of.7.grads), channel_id=1, source_target_pairs={{0,16},{2,18},{4,20},{6,22},{8,24},{10,26},{12,28},{14,30},{16,0},... | collective-permute-start | bytes 18440 | tf_op jit(solution)/shard_map/ppermute | solution.py:1069

commit v3 on v2

--- a/solution.py
+++ b/solution.py
@@ -123,7 +123,7 @@
     return pl.ds(pl.multiple_of(i * size, size), size)
 
 
-def prepare(coords, token_mask, cot, mask, share, out_wide, inverse):
+def prepare(coords, token_mask, cot, tok, gains, mask, share, out_wide, inverse, normed):
     captions = cot.shape[0]
     first = pl.multiple_of(coords[3] * captions, captions)
     own = token_mask[pl.ds(first, captions), :].astype(F32)
@@ -151,6 +151,8 @@
             lanes = slice(j, j + PAIR)
             value = (cot[caps, lanes].astype(F32)[:, None, :] * weight).reshape(GROUP, PAIR)
             out_wide[span, lanes] = value.astype(BF16)
+        xhat, _ = norm_parts(tok[span, :].astype(F32))
+        normed[span, :] = (xhat * gains[0:1, :]).astype(BF16)
 
 
 def pool(values, share):
@@ -162,15 +164,9 @@
 
 
 def attention_forward(
-    tok, gains, mask, share, strips, normed, qkv, attended, after, normed_two, after_pooled
+    tok, gains, normed, mask, share, strips, qkv, attended, after, normed_two, after_pooled
 ):
     rows = tok.shape[0]
-
-    @pl.loop(0, rows // GROUP)
-    def _(i):
-        span = span_of(i)
-        xhat, _ = norm_parts(tok[span, :].astype(F32))
-        normed[span, :] = (xhat * gains[0:1, :]).astype(BF16)
 
     for half in range(HALVES):
         mixed = mm(normed[...], weight_of(strips, half, 0, 8, 3, range(3))).astype(BF16)
@@ -433,34 +429,34 @@
 UNIT = 2 * 768 * 768 * 768
 
 
-def run_prepare(coords, token_mask, cot):
+def run_prepare(coords, token_mask, cot, tok, gains):
     captions = cot.shape[0]
     rows = captions * SLOTS
     return call(
         prepare,
         "prepare",
-        [SMEM, VMEM, VMEM],
+        [SMEM] + [VMEM] * 4,
         [
             (VMEM, shape_of(rows // GROUP, SLOTS, GROUP, dtype=F32)),
             (VMEM, shape_of(rows, PAIR, dtype=F32)),
             (VMEM, shape_of(rows, D + PAIR)),
             (VMEM, shape_of(captions, PAIR, dtype=F32)),
+            (VMEM, shape_of(rows, D)),
         ],
         [],
         1,
-        (coords, token_mask, cot),
+        (coords, token_mask, cot, tok, gains),
         mib=6,
     )
 
 
-def run_forward(tok, gains, mask, share, strips):
+def run_forward(tok, gains, normed, mask, share, strips):
     rows = tok.shape[0]
     return call(
         attention_forward,
         "attention_forward",
-        [VMEM] * 5,
+        [VMEM] * 6,
         [
-            (VMEM, shape_of(rows, D)),
             (VMEM, shape_of(6, rows, STRIP)),
             (VMEM, shape_of(rows, D)),
             (VMEM, shape_of(rows, D, dtype=F32)),
@@ -469,7 +465,7 @@
         ],
         [],
         5 * UNIT,
-        (tok, gains, mask, share, strips),
+        (tok, gains, normed, mask, share, strips),
         mib=3,
     )
 
@@ -494,7 +490,7 @@
         20 * UNIT,
         (coords, normed_two, out_wide, strips),
         grid=(4,),
-        mib=8 if split else 44,
+        mib=6 if split else 44,
     )
 
 
@@ -917,14 +913,17 @@
     grad_out, left_out, right_out, master_out, copy_out = outs
     strip = pl.program_id(0)
     grad = mine[strip].astype(F32) + arrived[strip].astype(F32)
-    for i in range(4):
-        block = 4 * strip + i
-        g = grad[:, i * BLOCK : (i + 1) * BLOCK]
-        grad_out[i] = g
-        left_out[i] = DECAY_RATE * stat_left[block] + (1.0 - DECAY_RATE) * precise(g, g, 1, 1)
-        right_out[i] = DECAY_RATE * stat_right[block] + (1.0 - DECAY_RATE) * precise(g, g, 0, 0)
-        direction = precise(root_left[block], precise(g, root_right[block]))
-        new = master[block] - STEP_RATE * direction
+    blocks = [4 * strip + i for i in range(4)]
+    grads = [grad[:, i * BLOCK : (i + 1) * BLOCK] for i in range(4)]
+    sides = [precise(g, root_right[block]) for g, block in zip(grads, blocks)]
+    lefts = [precise(g, g, 1, 1) for g in grads]
+    rights = [precise(g, g, 0, 0) for g in grads]
+    directions = [precise(root_left[block], side) for side, block in zip(sides, blocks)]
+    for i, block in enumerate(blocks):
+        grad_out[i] = grads[i]
+        left_out[i] = DECAY_RATE * stat_left[block] + (1.0 - DECAY_RATE) * lefts[i]
+        right_out[i] = DECAY_RATE * stat_right[block] + (1.0 - DECAY_RATE) * rights[i]
+        new = master[block] - STEP_RATE * directions[i]
         master_out[i] = new
         copy_out[i] = new.astype(BF16)
 
@@ -989,15 +988,14 @@
     coords = jnp.stack([dp_pos % 2, dp_pos // 2 % 2, dp_pos // 4, half]).astype(jnp.int32)
 
     coords, master = fence(coords, master)
+    first = functools.partial(run_prepare, coords, token_mask, cotangent, tokens, norm_gains)
     if split:
-        strips, prepared = gather_split(
-            master, coords, lambda: run_prepare(coords, token_mask, cotangent)
-        )
+        strips, prepared = gather_split(master, coords, first)
     else:
-        strips, prepared = gather_weights(master), run_prepare(coords, token_mask, cotangent)
-    mask, share, out_wide, inverse = prepared
-    normed, qkv, attended, after, normed_two, after_pooled = run_forward(
-        tokens, norm_gains, mask, share, strips
+        strips, prepared = gather_weights(master), first()
+    mask, share, out_wide, inverse, normed = prepared
+    qkv, attended, after, normed_two, after_pooled = run_forward(
+        tokens, norm_gains, normed, mask, share, strips
     )
     hidden_pooled, grad_two, *held = run_mlp(coords, normed_two, out_wide, strips, split)
     hops = sum_hops()

time: 245 us -> 241 us (0.984)
  Pallas kernels: 80.1 us -> 76.8 us
    pallas_call x31, Pallas kernels: 80.1 us -> 76.8 us  [call(): pl.pallas_call(kernel, grid=grid, in_specs=in_specs, out_specs=[spec for...]
  transfers between devices with their start and end apart: 36 -> 36, of which waited for: 23 -> 23; matrix products, arithmetic and copies ran while one was open for 0% -> 0% of each run, Pallas kernels for 12% -> 13%
where the time goes in v3:
time: 241 us
  waiting for transfers between devices  115 us (48%)
  Pallas kernels  76.8 us (32%)
  starting transfers between devices  43.8 us (18%)
  local copies, waits for them, and re-layouts  3.76 us (2%)
    pallas_call x31, Pallas kernels, call(): pl.pallas_call(kernel, grid=grid, in_specs=in_specs, out_specs=[spec for...  76.8 us
    ppermute x3, waiting for transfers between devices, across_hop(): lax.ppermute(pieces[0], 'tensor', OTHER_Y)  32.4 us
    ppermute x1, waiting for transfers between devices, body(): gain_in = lax.ppermute(gain_grads, *hops[0])  11.8 us
    ppermute x1, waiting for transfers between devices, gather_split(): far = lax.ppermute(own, 'dp', FAR_Z)  11.1 us
    ppermute x2, waiting for transfers between devices, first_hop(): lax.ppermute(sent[0], 'tensor', OTHER_Y)  9.76 us
    ppermute x3, waiting for transfers between devices, neighbour_hop(): lax.ppermute(value, 'tensor', OTHER_Y)  8.78 us
    ppermute x2, waiting for transfers between devices, second_hop(): lax.ppermute(sent[0], 'dp', OTHER_X)  8.25 us
    ppermute x1, waiting for transfers between devices, body(): gain_in = lax.ppermute(gain_grads, *hops[4])  8.04 us
  transfers between devices with their start and end apart: 36, of which 23 were waited for; matrix products, arithmetic and copies ran while one was open for 0% of the time, Pallas kernels for 13%

profile of v3, /device:TPU:0, one launch (start us, length us, event | category | flops | bytes accessed | tf_op | source)
XLA Modules:
  0.0 240.7 jit_solution(18040135970480622777)
XLA Ops:
  0.8 1.3 copy-done.1
  2.3 4.1 %collective-permute-start.3 = (bf16[1,6,96,384]{3,2,1,0:T(8,128)(2,1)S(1)}, bf16[1,6,96,384]{3,2,1,0:T(8,128)(2,1)S(1)}, u32[]{:S(2)}, u32[]{:S(2)}) collective-permute-start(bf16[1,6,96,384]{3,2,1,0:T(8,128)(2,1)S(1)} %pack.1.own), channel_id=1, source_target_pairs={{0,16},{2,18},{4,20},{6,22},{8,24},{10,26},{12,28},{14,30},{16,0},... | collective-permute-start | bytes 1327112 | tf_op jit(solution)/shard_map/ppermute | solution.py:693
  6.4 1.6 collective-permute-start.2
  8.0 1.5 collective-permute-start.1
  9.5 1.5 collective-permute-start
  11.0 0.8 copy.29.token_mask
  11.8 0.9 copy-done.7
  13.4 1.7 prepare.1
  15.1 11.1 %collective-permute-done.3.two = bf16[1,6,96,384]{3,2,1,0:T(8,128)(2,1)S(1)} collective-permute-done((bf16[1,6,96,384]{3,2,1,0:T(8,128)(2,1)S(1)}, bf16[1,6,96,384]{3,2,1,0:T(8,128)(2,1)S(1)}, u32[]{:S(2)}, u32[]{:S(2)}) %collective-permute-start.3) | collective-permute-done | bytes 442400 | tf_op jit(solution)/shard_map/ppermute | solution.py:693
  26.4 1.6 collective-permute-start.7
  28.1 1.5 collective-permute-start.6
  29.6 1.3 collective-permute-start.8
  32.0 19.8 %collective-permute-done.4.across_one = bf16[1,3,96,384]{3,2,1,0:T(8,128)(2,1)S(1)} collective-permute-done((bf16[1,3,96,384]{3,2,1,0:T(8,128)(2,1)S(1)}, bf16[1,3,96,384]{3,2,1,0:T(8,128)(2,1)S(1)}, u32[]{:S(2)}, u32[]{:S(2)}) %collective-permute-start.4) | collective-permute-done | bytes 221216 | tf_op jit(solution)/shard_map/ppermute | solution.py:687
  51.8 1.0 collective-permute-done.5.across_two
  52.8 0.9 place_own.3
  53.8 0.8 collective-permute-start.12
  54.6 1.2 collective-permute-start.11
  55.9 1.6 collective-permute-start.9
  58.0 8.8 %collective-permute-done.12.by_y = bf16[1,6,96,384]{3,2,1,0:T(8,128)(2,1)S(1)} collective-permute-done((bf16[1,6,96,384]{3,2,1,0:T(8,128)(2,1)S(1)}, bf16[1,6,96,384]{3,2,1,0:T(8,128)(2,1)S(1)}, u32[]{:S(2)}, u32[]{:S(2)}) %collective-permute-start.12) | collective-permute-done | bytes 442400 | tf_op jit(solution)/shard_map/ppermute | solution.py:683
  66.8 0.8 collective-permute-done.11.by_x
  67.6 8.2 %collective-permute-done.9.across_one = bf16[2,3,96,384]{3,2,1,0:T(8,128)(2,1)S(1)} collective-permute-done((bf16[2,3,96,384]{3,2,1,0:T(8,128)(2,1)S(1)}, bf16[2,3,96,384]{3,2,1,0:T(8,128)(2,1)S(1)}, u32[]{:S(2)}, u32[]{:S(2)}) %collective-permute-start.9) | collective-permute-done | bytes 442400 | tf_op jit(solution)/shard_map/ppermute | solution.py:687
  76.3 1.2 place_own.4
  77.6 1.3 collective-permute-start.14
  79.0 1.5 collective-permute-start.15
  81.1 4.4 %collective-permute-done.14.across_one = bf16[1,3,96,384]{3,2,1,0:T(8,128)(2,1)S(1)} collective-permute-done((bf16[1,3,96,384]{3,2,1,0:T(8,128)(2,1)S(1)}, bf16[1,3,96,384]{3,2,1,0:T(8,128)(2,1)S(1)}, u32[]{:S(2)}, u32[]{:S(2)}) %collective-permute-start.14) | collective-permute-done | bytes 221216 | tf_op jit(solution)/shard_map/ppermute | solution.py:687
  85.5 1.0 collective-permute-done.15.across_two
  86.5 0.9 place_own.5
  87.4 0.9 place_other.4._
  88.3 2.8 %collective-permute-done.17.arrived = bf16[1,2,2,6,96,384]{5,4,3,2,1,0:T(8,128)(2,1)S(1)} collective-permute-done((bf16[1,2,2,6,96,384]{5,4,3,2,1,0:T(8,128)(2,1)S(1)}, bf16[1,2,2,6,96,384]{5,4,3,2,1,0:T(8,128)(2,1)S(1)}, u32[]{:S(2)}, u32[]{:S(2)}) %collective-permute-start.17) | collective-permute-done | bytes 1769504 | tf_op jit(solution)/shard_map/ppermute | solution.py:891
  91.8 9.3 %attention_forward.1 = (bf16[6,768,384]{2,1,0:T(8,128)(2,1)S(1)}, bf16[768,768]{1,0:T(8,128)(2,1)S(1)}, f32[768,768]{1,0:T(8,128)S(1)}, bf16[768,768]{1,0:T(8,128)(2,1)S(1)}, f32[48,768]{1,0:T(8,128)S(1)}) custom-call(bf16[768,768]{1,0:T(8,128)(2,1)S(1)} %copy-done, f32[2,768]{1,0:T(2,128)S(1)} %copy-done.10, ...), custom_call_target="tpu_custom_call" | custom-call | flops 1 | bytes 1 | tf_op jit(solution)/shard_map/attention_forward/pallas_call | solution.py:406
  101.2 25.0 %mlp_both.1 = (f32[4,768,128]{2,1,0:T(8,128)S(1)}, f32[768,768]{1,0:T(8,128)S(1)}, bf16[2,2,2,6,96,384]{5,4,3,2,1,0:T(8,128)(2,1)S(1)}, bf16[2,2,2,6,96,384]{5,4...) custom-call(s32[4]{0:T(128)S(1)} %pad_add_fusion.coords, ...), custom_call_target="tpu_custom_call" | custom-call | flops 1 | bytes 1 | tf_op jit(solution)/shard_map/mlp_both/pallas_call | solution.py:406
  126.4 5.0 %output_backward.1 = (f32[768,768]{1,0:T(8,128)S(1)}, f32[1,768]{1,0:T(1,128)S(1)}, bf16[768,768]{1,0:T(8,128)(2,1)S(1)}, bf16[2,2,2,6,96,384]{5,4,3,2,1,0:T(8,128)(2,1)S(1)}, bf16[2,2,2,6,96,384]{5,4,3,2,1,0:T(8,128)(2,1)S(1)}) custom-call(s32[4]{0:T(128)S(1)} %pad_add_fusion.coords, ...), custom_call_target="tpu_custom_call", output_to_operand_aliasing={{3}: (8, {}), {4}: (9, {})} | custom-call | flops 1 | bytes 1 | tf_op jit(solution)/shard_map/output_backward/pallas_call | solution.py:406
  131.4 1.0 collective-permute-done.18.arrived
  132.4 1.3 split_sum.2
  133.7 0.8 collective-permute-start.19
  134.5 1.2 collective-permute-start.20
  135.8 9.9 %attention_backward.1 = (bf16[6,768,384]{2,1,0:T(8,128)(2,1)S(1)}, bf16[2,2,2,6,96,384]{5,4,3,2,1,0:T(8,128)(2,1)S(1)}, bf16[2,2,2,6,96,384]{5,4,3,2,1,0:T(8,128)(2,1)S(1)}) custom-call(s32[4]{0:T(128)S(1)} %pad_add_fusion.coords, f32[6,16,128]{2,1,0:T(8,128)S(1)} %get-tuple-element.151.mask, ...), custom_call_target="tpu_custom_call", output_to_operand_aliasing={{1}: (5, {}), {2}: (6, {})} | custom-call | flops 1 | bytes 1 | tf_op jit(solution)/shard_map/attention_backward/pallas_call | solution.py:406
  145.7 9.8 %collective-permute-done.19.one_in = bf16[2,2,3,96,384]{4,3,2,1,0:T(8,128)(2,1)S(1)} collective-permute-done((bf16[2,2,3,96,384]{4,3,2,1,0:T(8,128)(2,1)S(1)}, bf16[2,2,3,96,384]{4,3,2,1,0:T(8,128)(2,1)S(1)}, u32[]{:S(2)}, u32[]{:S(2)}) %collective-permute-start.19) | collective-permute-done | bytes 884768 | tf_op jit(solution)/shard_map/ppermute | solution.py:895
  156.0 0.8 split_again.2
  156.8 1.3 collective-permute-start.21
  158.1 1.5 collective-permute-start.22
  159.6 2.6 %collective-permute-done.23.arrived = bf16[2,2,2,6,96,384]{5,4,3,2,1,0:T(8,128)(2,1)S(1)} collective-permute-done((bf16[2,2,2,6,96,384]{5,4,3,2,1,0:T(8,128)(2,1)S(1)}, bf16[2,2,2,6,96,384]{5,4,3,2,1,0:T(8,128)(2,1)S(1)}, u32[]{:S(2)}, u32[]{:S(2)}) %collective-permute-start.23) | collective-permute-done | bytes 3538976 | tf_op jit(solution)/shard_map/ppermute | solution.py:891
  162.2 1.1 split_sum.3
  163.3 1.3 collective-permute-start.25
  164.6 1.5 collective-permute-start.26
  166.1 6.5 %input_backward.1 = (f32[768,768]{1,0:T(8,128)}, f32[2,1,768]{2,1,0:T(1,128)S(1)}) custom-call(bf16[768,768]{1,0:T(8,128)(2,1)S(1)} %copy-done, f32[2,768]{1,0:T(2,128)S(1)} %copy-done.10, bf16[6,768,384]{2,1,0:T(8,128)(2,1)S(1)} %get-tuple-element.229.grad_mixed, f32[768,768]{1,0:T(8,128)S(1)} %get-tuple-element.230.grad_after, ...), custom_call_target="tpu_custom_call" | custom-call | flops 1 | bytes 1 | tf_op jit(solution)/shard_map/input_backward/pallas_call | solution.py:406
  173.3 1.7 collective-permute-start.24
  175.5 2.1 pool_out.1
  177.6 11.8 %collective-permute-done.27.right = f32[2,1,768]{2,1,0:T(1,128)S(1)} collective-permute-done((f32[2,1,768]{2,1,0:T(1,128)S(1)}, f32[2,1,768]{2,1,0:T(1,128)S(1)}, u32[]{:S(2)}, u32[]{:S(2)}) %collective-permute-start.27) | collective-permute-done | bytes 6176 | tf_op jit(solution)/shard_map/ppermute | solution.py:1044
  189.5 0.9 split_again.3
  190.4 0.8 collective-permute-start.28
  191.3 1.3 collective-permute-start.29
  192.6 1.2 collective-permute-done.30.right
  193.7 8.2 %collective-permute-done.28.one_in = bf16[2,3,96,384]{3,2,1,0:T(8,128)(2,1)S(1)} collective-permute-done((bf16[2,3,96,384]{3,2,1,0:T(8,128)(2,1)S(1)}, bf16[2,3,96,384]{3,2,1,0:T(8,128)(2,1)S(1)}, u32[]{:S(2)}, u32[]{:S(2)}) %collective-permute-start.28) | collective-permute-done | bytes 442400 | tf_op jit(solution)/shard_map/ppermute | solution.py:899
  203.2 1.5 collective-permute-start.31
  204.6 1.5 collective-permute-start.32
  206.1 2.1 collective-permute-done.32.right
  208.3 5.2 %collective-permute-done.31.low_in = bf16[6,96,384]{2,1,0:T(8,128)(2,1)S(1)} collective-permute-done((bf16[6,96,384]{2,1,0:T(8,128)(2,1)S(1)}, bf16[6,96,384]{2,1,0:T(8,128)(2,1)S(1)}, u32[]{:S(2)}, u32[]{:S(2)}) %collective-permute-start.31) | collective-permute-done | bytes 442400 | tf_op jit(solution)/shard_map/ppermute | solution.py:1057
  214.2 3.1 %collective-permute-start.33 = (bf16[6,96,384]{2,1,0:T(8,128)(2,1)S(1)}, bf16[6,96,384]{2,1,0:T(8,128)(2,1)S(1)}, u32[]{:S(2)}, u32[]{:S(2)}) collective-permute-start(bf16[6,96,384]{2,1,0:T(8,128)(2,1)S(1)} %get-tuple-element.261), channel_id=1, source_target_pairs={{0,16},{2,18},{4,20},{6,22},{8,24},{10,26},{12,28},{14,30},{16,0},... | collective-permute-start | bytes 1327112 | tf_op jit(solution)/shard_map/ppermute | solution.py:1063
  217.4 1.7 collective-permute-start.34
  219.1 5.7 %collective-permute-done.34.right = f32[2,1,768]{2,1,0:T(1,128)S(1)} collective-permute-done((f32[2,1,768]{2,1,0:T(1,128)S(1)}, f32[2,1,768]{2,1,0:T(1,128)S(1)}, u32[]{:S(2)}, u32[]{:S(2)}) %collective-permute-start.34) | collective-permute-done | bytes 6176 | tf_op jit(solution)/shard_map/ppermute | solution.py:1065
  224.8 2.2 collective-permute-start.35
  227.0 8.0 %collective-permute-done.35.arrived = f32[2,1,768]{2,1,0:T(1,128)S(1)} collective-permute-done((f32[2,1,768]{2,1,0:T(1,128)S(1)}, f32[2,1,768]{2,1,0:T(1,128)S(1)}, u32[]{:S(2)}, u32[]{:S(2)}) %collective-permute-start.35) | collective-permute-done | bytes 6176 | tf_op jit(solution)/shard_map/ppermute | solution.py:1067
  235.7 5.0 %update.1 = (f32[24,96,96]{2,1,0:T(8,128)}, f32[24,96,96]{2,1,0:T(8,128)}, f32[24,96,96]{2,1,0:T(8,128)}, f32[24,96,96]{2,1,0:T(8,128)}, bf16[24,96,96]{2,1,0:T(8,128)(2,1)}) custom-call(bf16[6,96,384]{2,1,0:T(8,128)(2,1)S(1)} %get-tuple-element.269.mine, bf16[6,96,384]{2,1,0:T(8,128)(2,1)S(1)} %collective-permute-done.33.arrived, ...), custom_call_target="tpu_custom_call" | custom-call | flops 1 | bytes 1 | tf_op jit(solution)/shard_map/update/pallas_call | solution.py:406
  (65 shorter events, 9.6 us)
Async XLA Ops:
  0.6 11.1 %copy-start = (bf16[768,768]{1,0:T(8,128)(2,1)S(1)}, bf16[768,768]{1,0:T(8,128)(2,1)}, u32[]{:S(2)}) copy-start(bf16[768,768]{1,0:T(8,128)(2,1)} %tok.5) | copy-start | bytes 3538948
  0.8 1.3 copy-start.1
  2.3 23.9 %collective-permute-start.3 = (bf16[1,6,96,384]{3,2,1,0:T(8,128)(2,1)S(1)}, bf16[1,6,96,384]{3,2,1,0:T(8,128)(2,1)S(1)}, u32[]{:S(2)}, u32[]{:S(2)}) collective-permute-start(bf16[1,6,96,384]{3,2,1,0:T(8,128)(2,1)S(1)} %pack.1.own), channel_id=1, source_target_pairs={{0,16},{2,18},{4,20},{6,22},{8,24},{10,26},{12,28},{14,30},{16,0},... | collective-permute-start | bytes 1327112 | tf_op jit(solution)/shard_map/ppermute | solution.py:693
  6.4 19.9 %collective-permute-start.2 = (bf16[1,6,96,384]{3,2,1,0:T(8,128)(2,1)S(1)}, bf16[1,6,96,384]{3,2,1,0:T(8,128)(2,1)S(1)}, u32[]{:S(2)}, u32[]{:S(2)}) collective-permute-start(bf16[1,6,96,384]{3,2,1,0:T(8,128)(2,1)S(1)} %pack.1.own), channel_id=1, source_target_pairs={{0,8},{2,10},{4,12},{6,14},{8,0},{10,2},{12,4},{14,6},{16,24},{18,... | collective-permute-start | bytes 1327112 | tf_op jit(solution)/shard_map/ppermute | solution.py:692
  8.0 18.4 %collective-permute-start.1 = (bf16[1,6,96,384]{3,2,1,0:T(8,128)(2,1)S(1)}, bf16[1,6,96,384]{3,2,1,0:T(8,128)(2,1)S(1)}, u32[]{:S(2)}, u32[]{:S(2)}) collective-permute-start(bf16[1,6,96,384]{3,2,1,0:T(8,128)(2,1)S(1)} %pack.1.own), channel_id=1, source_target_pairs={{0,1},{1,0},{2,3},{3,2},{4,5},{5,4},{6,7},{7,6},{8,9},{9,8},{10,11... | collective-permute-start | bytes 1327112 | tf_op jit(solution)/shard_map/ppermute | solution.py:683
  9.5 16.9 %collective-permute-start = (bf16[1,6,96,384]{3,2,1,0:T(8,128)(2,1)S(1)}, bf16[1,6,96,384]{3,2,1,0:T(8,128)(2,1)S(1)}, u32[]{:S(2)}, u32[]{:S(2)}) collective-permute-start(bf16[1,6,96,384]{3,2,1,0:T(8,128)(2,1)S(1)} %pack.1.own), channel_id=1, source_target_pairs={{0,4},{2,6},{4,0},{6,2},{8,12},{10,14},{12,8},{14,10},{16,20},{18,... | collective-permute-start | bytes 1327112 | tf_op jit(solution)/shard_map/ppermute | solution.py:683
  11.8 0.9 copy-start.7
  12.7 0.7 copy-start.9
  26.4 26.4 %collective-permute-start.7 = (bf16[2,6,96,384]{3,2,1,0:T(8,128)(2,1)S(1)}, bf16[2,6,96,384]{3,2,1,0:T(8,128)(2,1)S(1)}, u32[]{:S(2)}, u32[]{:S(2)}) collective-permute-start(bf16[2,6,96,384]{3,2,1,0:T(8,128)(2,1)S(1)} %take_both.1.own), channel_id=1, source_target_pairs={{0,1},{1,0},{2,3},{3,2},{4,5},{5,4},{6,7},{7,6},{8,9},{9,8},{10,11... | collective-permute-start | bytes 2654216 | tf_op jit(solution)/shard_map/ppermute | solution.py:683
  28.1 24.8 %collective-permute-start.6 = (bf16[2,6,96,384]{3,2,1,0:T(8,128)(2,1)S(1)}, bf16[2,6,96,384]{3,2,1,0:T(8,128)(2,1)S(1)}, u32[]{:S(2)}, u32[]{:S(2)}) collective-permute-start(bf16[2,6,96,384]{3,2,1,0:T(8,128)(2,1)S(1)} %take_both.1.own), channel_id=1, source_target_pairs={{0,4},{2,6},{4,0},{6,2},{8,12},{10,14},{12,8},{14,10},{16,20},{18,... | collective-permute-start | bytes 2654216 | tf_op jit(solution)/shard_map/ppermute | solution.py:683
  29.6 23.3 %collective-permute-start.8 = (bf16[1,6,96,384]{3,2,1,0:T(8,128)(2,1)S(1)}, bf16[1,6,96,384]{3,2,1,0:T(8,128)(2,1)S(1)}, u32[]{:S(2)}, u32[]{:S(2)}) collective-permute-start(bf16[1,6,96,384]{3,2,1,0:T(8,128)(2,1)S(1)} %collective-permute-done.2.one), channel_id=1, source_target_pairs={{0,16},{2,18},{4,20},{6,22},{8,24},{10,26},{12,28},{14,30},{16,0},... | collective-permute-start | bytes 1327112 | tf_op jit(solution)/shard_map/ppermute | solution.py:697
  30.9 20.9 %collective-permute-start.4 = (bf16[1,3,96,384]{3,2,1,0:T(8,128)(2,1)S(1)}, bf16[1,3,96,384]{3,2,1,0:T(8,128)(2,1)S(1)}, u32[]{:S(2)}, u32[]{:S(2)}) collective-permute-start(bf16[1,3,96,384]{3,2,1,0:T(8,128)(2,1)S(1)} %get-tuple-element.155), channel_id=1, source_target_pairs={{0,1},{1,0},{2,3},{3,2},{4,5},{5,4},{6,7},{7,6},{8,9},{9,8},{10,11... | collective-permute-start | bytes 663560 | tf_op jit(solution)/shard_map/ppermute | solution.py:687
  31.5 21.3 %collective-permute-start.5 = (bf16[1,3,96,384]{3,2,1,0:T(8,128)(2,1)S(1)}, bf16[1,3,96,384]{3,2,1,0:T(8,128)(2,1)S(1)}, u32[]{:S(2)}, u32[]{:S(2)}) collective-permute-start(bf16[1,3,96,384]{3,2,1,0:T(8,128)(2,1)S(1)} %get-tuple-element.156), channel_id=1, source_target_pairs={{0,4},{2,6},{4,0},{6,2},{8,12},{10,14},{12,8},{14,10},{16,20},{18,... | collective-permute-start | bytes 663560 | tf_op jit(solution)/shard_map/ppermute | solution.py:687
  53.7 22.6 %collective-permute-start.13 = (bf16[1,2,2,6,96,384]{5,4,3,2,1,0:T(8,128)(2,1)S(1)}, bf16[1,2,2,6,96,384]{5,4,3,2,1,0:T(8,128)(2,1)S(1)}, u32[]{:S(2)}, u32[]{:S(2)}) collective-permute-start(bf16[1,2,2,6,96,384]{5,4,3,2,1,0:T(8,128)(2,1)S(1)} %get-tuple-element.167), channel_id=1, source_target_pairs={{0,2},{2,0},{4,6},{6,4},{8,10},{10,8},{12,14},{14,12},{16,18},{18,... | collective-permute-start | bytes 5308424 | tf_op jit(solution)/shard_map/ppermute | solution.py:891
  53.8 13.0 %collective-permute-start.12 = (bf16[1,6,96,384]{3,2,1,0:T(8,128)(2,1)S(1)}, bf16[1,6,96,384]{3,2,1,0:T(8,128)(2,1)S(1)}, u32[]{:S(2)}, u32[]{:S(2)}) collective-permute-start(bf16[1,6,96,384]{3,2,1,0:T(8,128)(2,1)S(1)} %collective-permute-done.8.own), channel_id=1, source_target_pairs={{0,1},{1,0},{2,3},{3,2},{4,5},{5,4},{6,7},{7,6},{8,9},{9,8},{10,11... | collective-permute-start | bytes 1327112 | tf_op jit(solution)/shard_map/ppermute | solution.py:683
  54.6 13.0 %collective-permute-start.11 = (bf16[1,6,96,384]{3,2,1,0:T(8,128)(2,1)S(1)}, bf16[1,6,96,384]{3,2,1,0:T(8,128)(2,1)S(1)}, u32[]{:S(2)}, u32[]{:S(2)}) collective-permute-start(bf16[1,6,96,384]{3,2,1,0:T(8,128)(2,1)S(1)} %collective-permute-done.8.own), channel_id=1, source_target_pairs={{0,4},{2,6},{4,0},{6,2},{8,12},{10,14},{12,8},{14,10},{16,20},{18,... | collective-permute-start | bytes 1327112 | tf_op jit(solution)/shard_map/ppermute | solution.py:683
  55.9 19.9 %collective-permute-start.9 = (bf16[2,3,96,384]{3,2,1,0:T(8,128)(2,1)S(1)}, bf16[2,3,96,384]{3,2,1,0:T(8,128)(2,1)S(1)}, u32[]{:S(2)}, u32[]{:S(2)}) collective-permute-start(bf16[2,3,96,384]{3,2,1,0:T(8,128)(2,1)S(1)} %get-tuple-element.162), channel_id=1, source_target_pairs={{0,1},{1,0},{2,3},{3,2},{4,5},{5,4},{6,7},{7,6},{8,9},{9,8},{10,11... | collective-permute-start | bytes 1327112 | tf_op jit(solution)/shard_map/ppermute | solution.py:687
  57.5 18.8 %collective-permute-start.10 = (bf16[2,3,96,384]{3,2,1,0:T(8,128)(2,1)S(1)}, bf16[2,3,96,384]{3,2,1,0:T(8,128)(2,1)S(1)}, u32[]{:S(2)}, u32[]{:S(2)}) collective-permute-start(bf16[2,3,96,384]{3,2,1,0:T(8,128)(2,1)S(1)} %get-tuple-element.163), channel_id=1, source_target_pairs={{0,4},{2,6},{4,0},{6,2},{8,12},{10,14},{12,8},{14,10},{16,20},{18,... | collective-permute-start | bytes 1327112 | tf_op jit(solution)/shard_map/ppermute | solution.py:687
  77.5 9.0 %collective-permute-start.16 = (bf16[2,2,2,6,96,384]{5,4,3,2,1,0:T(8,128)(2,1)S(1)}, bf16[2,2,2,6,96,384]{5,4,3,2,1,0:T(8,128)(2,1)S(1)}, u32[]{:S(2)}, u32[]{:S(2)}) collective-permute-start(bf16[2,2,2,6,96,384]{5,4,3,2,1,0:T(8,128)(2,1)S(1)} %get-tuple-element.176), channel_id=1, source_target_pairs={{0,2},{2,0},{4,6},{6,4},{8,10},{10,8},{12,14},{14,12},{16,18},{18,... | collective-permute-start | bytes 10616840 | tf_op jit(solution)/shard_map/ppermute | solution.py:891
  77.6 7.9 %collective-permute-start.14 = (bf16[1,3,96,384]{3,2,1,0:T(8,128)(2,1)S(1)}, bf16[1,3,96,384]{3,2,1,0:T(8,128)(2,1)S(1)}, u32[]{:S(2)}, u32[]{:S(2)}) collective-permute-start(bf16[1,3,96,384]{3,2,1,0:T(8,128)(2,1)S(1)} %get-tuple-element.171), channel_id=1, source_target_pairs={{0,1},{1,0},{2,3},{3,2},{4,5},{5,4},{6,7},{7,6},{8,9},{9,8},{10,11... | collective-permute-start | bytes 663560 | tf_op jit(solution)/shard_map/ppermute | solution.py:687
  79.0 7.5 %collective-permute-start.15 = (bf16[1,3,96,384]{3,2,1,0:T(8,128)(2,1)S(1)}, bf16[1,3,96,384]{3,2,1,0:T(8,128)(2,1)S(1)}, u32[]{:S(2)}, u32[]{:S(2)}) collective-permute-start(bf16[1,3,96,384]{3,2,1,0:T(8,128)(2,1)S(1)} %get-tuple-element.172), channel_id=1, source_target_pairs={{0,4},{2,6},{4,0},{6,2},{8,12},{10,14},{12,8},{14,10},{16,20},{18,... | collective-permute-start | bytes 663560 | tf_op jit(solution)/shard_map/ppermute | solution.py:687
  87.4 3.8 %collective-permute-start.17 = (bf16[1,2,2,6,96,384]{5,4,3,2,1,0:T(8,128)(2,1)S(1)}, bf16[1,2,2,6,96,384]{5,4,3,2,1,0:T(8,128)(2,1)S(1)}, u32[]{:S(2)}, u32[]{:S(2)}) collective-permute-start(bf16[1,2,2,6,96,384]{5,4,3,2,1,0:T(8,128)(2,1)S(1)} %get-tuple-element.182), channel_id=1, source_target_pairs={{0,2},{2,0},{4,6},{6,4},{8,10},{10,8},{12,14},{14,12},{16,18},{18,... | collective-permute-start | bytes 5308424 | tf_op jit(solution)/shard_map/ppermute | solution.py:891
  88.3 3.5 %copy-start.10 = (f32[2,768]{1,0:T(2,128)S(1)}, f32[2,768]{1,0:T(2,128)}, u32[]{:S(2)}) copy-start(f32[2,768]{1,0:T(2,128)} %gains.9) | copy-start | bytes 18436
  101.2 25.2 %copy-start.8 = (bf16[48,768]{1,0:T(8,128)(2,1)S(1)}, bf16[48,768]{1,0:T(8,128)(2,1)}, u32[]{:S(2)}) copy-start(bf16[48,768]{1,0:T(8,128)(2,1)} %cot.3) | copy-start | bytes 221188
  126.1 6.3 %collective-permute-start.18 = (bf16[2,2,2,6,96,384]{5,4,3,2,1,0:T(8,128)(2,1)S(1)}, bf16[2,2,2,6,96,384]{5,4,3,2,1,0:T(8,128)(2,1)S(1)}, u32[]{:S(2)}, u32[]{:S(2)}) collective-permute-start(bf16[2,2,2,6,96,384]{5,4,3,2,1,0:T(8,128)(2,1)S(1)} %get-tuple-element.190), channel_id=1, source_target_pairs={{0,2},{2,0},{4,6},{6,4},{8,10},{10,8},{12,14},{14,12},{16,18},{18,... | collective-permute-start | bytes 10616840 | tf_op jit(solution)/shard_map/ppermute | solution.py:891
  133.7 21.8 %collective-permute-start.19 = (bf16[2,2,3,96,384]{4,3,2,1,0:T(8,128)(2,1)S(1)}, bf16[2,2,3,96,384]{4,3,2,1,0:T(8,128)(2,1)S(1)}, u32[]{:S(2)}, u32[]{:S(2)}) collective-permute-start(bf16[2,2,3,96,384]{4,3,2,1,0:T(8,128)(2,1)S(1)} %get-tuple-element.207), channel_id=1, source_target_pairs={{0,1},{1,0},{2,3},{3,2},{4,5},{5,4},{6,7},{7,6},{8,9},{9,8},{10,11... | collective-permute-start | bytes 2654216 | tf_op jit(solution)/shard_map/ppermute | solution.py:895
  134.5 21.4 %collective-permute-start.20 = (bf16[2,2,3,96,384]{4,3,2,1,0:T(8,128)(2,1)S(1)}, bf16[2,2,3,96,384]{4,3,2,1,0:T(8,128)(2,1)S(1)}, u32[]{:S(2)}, u32[]{:S(2)}) collective-permute-start(bf16[2,2,3,96,384]{4,3,2,1,0:T(8,128)(2,1)S(1)} %get-tuple-element.208), channel_id=1, source_target_pairs={{0,4},{2,6},{4,0},{6,2},{8,12},{10,14},{12,8},{14,10},{16,20},{18,... | collective-permute-start | bytes 2654216 | tf_op jit(solution)/shard_map/ppermute | solution.py:895
  156.0 6.2 %collective-permute-start.23 = (bf16[2,2,2,6,96,384]{5,4,3,2,1,0:T(8,128)(2,1)S(1)}, bf16[2,2,2,6,96,384]{5,4,3,2,1,0:T(8,128)(2,1)S(1)}, u32[]{:S(2)}, u32[]{:S(2)}) collective-permute-start(bf16[2,2,2,6,96,384]{5,4,3,2,1,0:T(8,128)(2,1)S(1)} %get-tuple-element.223), channel_id=1, source_target_pairs={{0,2},{2,0},{4,6},{6,4},{8,10},{10,8},{12,14},{14,12},{16,18},{18,... | collective-permute-start | bytes 10616840 | tf_op jit(solution)/shard_map/ppermute | solution.py:891
  156.8 15.8 %collective-permute-start.21 = (bf16[2,3,96,384]{3,2,1,0:T(8,128)(2,1)S(1)}, bf16[2,3,96,384]{3,2,1,0:T(8,128)(2,1)S(1)}, u32[]{:S(2)}, u32[]{:S(2)}) collective-permute-start(bf16[2,3,96,384]{3,2,1,0:T(8,128)(2,1)S(1)} %get-tuple-element.220), channel_id=1, source_target_pairs={{0,4},{2,6},{4,0},{6,2},{8,12},{10,14},{12,8},{14,10},{16,20},{18,... | collective-permute-start | bytes 1327112 | tf_op jit(solution)/shard_map/ppermute | solution.py:899
  158.1 14.5 %collective-permute-start.22 = (bf16[2,3,96,384]{3,2,1,0:T(8,128)(2,1)S(1)}, bf16[2,3,96,384]{3,2,1,0:T(8,128)(2,1)S(1)}, u32[]{:S(2)}, u32[]{:S(2)}) collective-permute-start(bf16[2,3,96,384]{3,2,1,0:T(8,128)(2,1)S(1)} %get-tuple-element.221), channel_id=1, source_target_pairs={{0,1},{1,0},{2,3},{3,2},{4,5},{5,4},{6,7},{7,6},{8,9},{9,8},{10,11... | collective-permute-start | bytes 1327112 | tf_op jit(solution)/shard_map/ppermute | solution.py:899
  163.3 26.2 %collective-permute-start.25 = (bf16[2,2,3,96,384]{4,3,2,1,0:T(8,128)(2,1)S(1)}, bf16[2,2,3,96,384]{4,3,2,1,0:T(8,128)(2,1)S(1)}, u32[]{:S(2)}, u32[]{:S(2)}) collective-permute-start(bf16[2,2,3,96,384]{4,3,2,1,0:T(8,128)(2,1)S(1)} %get-tuple-element.236), channel_id=1, source_target_pairs={{0,1},{1,0},{2,3},{3,2},{4,5},{5,4},{6,7},{7,6},{8,9},{9,8},{10,11... | collective-permute-start | bytes 2654216 | tf_op jit(solution)/shard_map/ppermute | solution.py:895
  164.6 24.9 %collective-permute-start.26 = (bf16[2,2,3,96,384]{4,3,2,1,0:T(8,128)(2,1)S(1)}, bf16[2,2,3,96,384]{4,3,2,1,0:T(8,128)(2,1)S(1)}, u32[]{:S(2)}, u32[]{:S(2)}) collective-permute-start(bf16[2,2,3,96,384]{4,3,2,1,0:T(8,128)(2,1)S(1)} %get-tuple-element.237), channel_id=1, source_target_pairs={{0,4},{2,6},{4,0},{6,2},{8,12},{10,14},{12,8},{14,10},{16,20},{18,... | collective-permute-start | bytes 2654216 | tf_op jit(solution)/shard_map/ppermute | solution.py:895
  173.3 16.2 %collective-permute-start.24 = (bf16[6,96,384]{2,1,0:T(8,128)(2,1)S(1)}, bf16[6,96,384]{2,1,0:T(8,128)(2,1)S(1)}, u32[]{:S(2)}, u32[]{:S(2)}) collective-permute-start(bf16[6,96,384]{2,1,0:T(8,128)(2,1)S(1)} %get-tuple-element.235), channel_id=1, source_target_pairs={{0,8},{2,10},{4,12},{6,14},{8,0},{10,2},{12,4},{14,6},{16,24},{18,... | collective-permute-start | bytes 1327112 | tf_op jit(solution)/shard_map/ppermute | solution.py:1047
  175.0 14.5 %collective-permute-start.27 = (f32[2,1,768]{2,1,0:T(1,128)S(1)}, f32[2,1,768]{2,1,0:T(1,128)S(1)}, u32[]{:S(2)}, u32[]{:S(2)}) collective-permute-start(f32[2,1,768]{2,1,0:T(1,128)S(1)} %get-tuple-element.238.left), channel_id=1, source_target_pairs={{0,1},{1,0},{2,3},{3,2},{4,5},{5,4},{6,7},{7,6},{8,9},{9,8},{10,11... | collective-permute-start | bytes 18440 | tf_op jit(solution)/shard_map/ppermute | solution.py:1044
  189.5 46.2 %copy-start.5 = (f32[24,96,96]{2,1,0:T(8,128)S(1)}, f32[24,96,96]{2,1,0:T(8,128)}, u32[]{:S(2)}) copy-start(f32[24,96,96]{2,1,0:T(8,128)} %root_left.1) | copy-start | bytes 2654212
  189.5 46.1 %copy-start.6 = (f32[24,96,96]{2,1,0:T(8,128)S(1)}, f32[24,96,96]{2,1,0:T(8,128)}, u32[]{:S(2)}) copy-start(f32[24,96,96]{2,1,0:T(8,128)} %root_right.1) | copy-start | bytes 2654212
  190.4 44.6 %copy-start.11 = (f32[2,768]{1,0:T(2,128)S(1)}, f32[2,768]{1,0:T(2,128)}, u32[]{:S(2)}) copy-start(f32[2,768]{1,0:T(2,128)} %moments.1) | copy-start | bytes 18436
  190.4 45.3 %copy-start.2 = (f32[24,96,96]{2,1,0:T(8,128)S(1)}, f32[24,96,96]{2,1,0:T(8,128)}, u32[]{:S(2)}) copy-start(f32[24,96,96]{2,1,0:T(8,128)} %master.1) | copy-start | bytes 2654212
  190.4 45.3 %copy-start.3 = (f32[24,96,96]{2,1,0:T(8,128)S(1)}, f32[24,96,96]{2,1,0:T(8,128)}, u32[]{:S(2)}) copy-start(f32[24,96,96]{2,1,0:T(8,128)} %stat_left.1) | copy-start | bytes 2654212
  190.4 45.2 %copy-start.4 = (f32[24,96,96]{2,1,0:T(8,128)S(1)}, f32[24,96,96]{2,1,0:T(8,128)}, u32[]{:S(2)}) copy-start(f32[24,96,96]{2,1,0:T(8,128)} %stat_right.1) | copy-start | bytes 2654212
  190.4 11.5 %collective-permute-start.28 = (bf16[2,3,96,384]{3,2,1,0:T(8,128)(2,1)S(1)}, bf16[2,3,96,384]{3,2,1,0:T(8,128)(2,1)S(1)}, u32[]{:S(2)}, u32[]{:S(2)}) collective-permute-start(bf16[2,3,96,384]{3,2,1,0:T(8,128)(2,1)S(1)} %get-tuple-element.252), channel_id=1, source_target_pairs={{0,4},{2,6},{4,0},{6,2},{8,12},{10,14},{12,8},{14,10},{16,20},{18,... | collective-permute-start | bytes 1327112 | tf_op jit(solution)/shard_map/ppermute | solution.py:899
  191.3 11.2 %collective-permute-start.29 = (bf16[2,3,96,384]{3,2,1,0:T(8,128)(2,1)S(1)}, bf16[2,3,96,384]{3,2,1,0:T(8,128)(2,1)S(1)}, u32[]{:S(2)}, u32[]{:S(2)}) collective-permute-start(bf16[2,3,96,384]{3,2,1,0:T(8,128)(2,1)S(1)} %get-tuple-element.253), channel_id=1, source_target_pairs={{0,1},{1,0},{2,3},{3,2},{4,5},{5,4},{6,7},{7,6},{8,9},{9,8},{10,11... | collective-permute-start | bytes 1327112 | tf_op jit(solution)/shard_map/ppermute | solution.py:899
  192.6 1.2 collective-permute-start.30
  203.2 10.3 %collective-permute-start.31 = (bf16[6,96,384]{2,1,0:T(8,128)(2,1)S(1)}, bf16[6,96,384]{2,1,0:T(8,128)(2,1)S(1)}, u32[]{:S(2)}, u32[]{:S(2)}) collective-permute-start(bf16[6,96,384]{2,1,0:T(8,128)(2,1)S(1)} %get-tuple-element.258), channel_id=1, source_target_pairs={{0,8},{2,10},{4,12},{6,14},{8,0},{10,2},{12,4},{14,6},{16,24},{18,... | collective-permute-start | bytes 1327112 | tf_op jit(solution)/shard_map/ppermute | solution.py:1057
  204.6 3.6 %collective-permute-start.32 = (f32[2,1,768]{2,1,0:T(1,128)S(1)}, f32[2,1,768]{2,1,0:T(1,128)S(1)}, u32[]{:S(2)}, u32[]{:S(2)}) collective-permute-start(f32[2,1,768]{2,1,0:T(1,128)S(1)} %sum_of.5.left), channel_id=1, source_target_pairs={{0,4},{2,6},{4,0},{6,2},{8,12},{10,14},{12,8},{14,10},{16,20},{18,... | collective-permute-start | bytes 18440 | tf_op jit(solution)/shard_map/ppermute | solution.py:1059
  214.2 21.4 %collective-permute-start.33 = (bf16[6,96,384]{2,1,0:T(8,128)(2,1)S(1)}, bf16[6,96,384]{2,1,0:T(8,128)(2,1)S(1)}, u32[]{:S(2)}, u32[]{:S(2)}) collective-permute-start(bf16[6,96,384]{2,1,0:T(8,128)(2,1)S(1)} %get-tuple-element.261), channel_id=1, source_target_pairs={{0,16},{2,18},{4,20},{6,22},{8,24},{10,26},{12,28},{14,30},{16,0},... | collective-permute-start | bytes 1327112 | tf_op jit(solution)/shard_map/ppermute | solution.py:1063
  217.4 7.4 %collective-permute-start.34 = (f32[2,1,768]{2,1,0:T(1,128)S(1)}, f32[2,1,768]{2,1,0:T(1,128)S(1)}, u32[]{:S(2)}, u32[]{:S(2)}) collective-permute-start(f32[2,1,768]{2,1,0:T(1,128)S(1)} %sum_of.6.left), channel_id=1, source_target_pairs={{0,8},{2,10},{4,12},{6,14},{8,0},{10,2},{12,4},{14,6},{16,24},{18,... | collective-permute-start | bytes 18440 | tf_op jit(solution)/shard_map/ppermute | solution.py:1065
  224.8 10.2 %collective-permute-start.35 = (f32[2,1,768]{2,1,0:T(1,128)S(1)}, f32[2,1,768]{2,1,0:T(1,128)S(1)}, u32[]{:S(2)}, u32[]{:S(2)}) collective-permute-start(f32[2,1,768]{2,1,0:T(1,128)S(1)} %sum_of.7.grads), channel_id=1, source_target_pairs={{0,16},{2,18},{4,20},{6,22},{8,24},{10,26},{12,28},{14,30},{16,0},... | collective-permute-start | bytes 18440 | tf_op jit(solution)/shard_map/ppermute | solution.py:1067

commit v4 on v3

--- a/solution.py
+++ b/solution.py
@@ -692,14 +692,13 @@
     near = lax.ppermute(own, "dp", NEAR_Z)
     far = lax.ppermute(own, "dp", FAR_Z)
     own_by = neighbour_hop(own)
-    own_by, near, far, own, prepared = fence(own_by, near, far, own, prepare())
-
-    other = lax.ppermute(near, "dp", FAR_Z)
+    own_by, prepared = fence(own_by, prepare())
     own_across = across_hop(run_halves(*own_by))
+    near, far, own_across, own_by, own, prepared = fence(near, far, own_across, own_by, own, prepared)
+
     both = run_both(near, far)
     both_by = neighbour_hop(both)
-    own_across, both_by, other = fence(own_across, both_by, other)
-
+    other = lax.ppermute(far, "dp", NEAR_Z)
     other_by = neighbour_hop(other)
     both_across = across_hop(run_halves(*both_by))
     whole, sent = run_place_own((0,), coords, (own, *own_by, *own_across), ())
@@ -1031,15 +1030,12 @@
         lower_in = core_hop(lower[1])
         upper_sent, upper_kept = run_again(coords, upper_kept, upper_in)
         upper_in = second_hop(upper_sent)
-        lower_in, upper_sent, grad_mixed = fence(lower_in, upper_sent, grad_mixed)
 
         lower_sent, lower_kept = run_split(coords, lower[0], lower_in)
-        lower_sent, grad_mixed = fence(lower_sent, grad_mixed)
         lower_in = first_hop(lower_sent)
         input_grad, gain_grads = run_input(
             tokens, norm_gains, grad_mixed, grad_after, gain_two, strips
         )
-        upper_in, gain_grads = fence(upper_in, gain_grads)
 
         gain_in = lax.ppermute(gain_grads, *hops[0])
         pooled = run_pool(after_pooled, hidden_pooled, inverse, strips)

time: 241 us -> 235 us (0.975)
  starting transfers between devices: 43.8 us -> 40.8 us
  waiting for transfers between devices: 115 us -> 112 us
    ppermute x3, waiting for transfers between devices: 32.4 us -> 13.6 us  [across_hop(): lax.ppermute(pieces[0], 'tensor', OTHER_Y)]
    ppermute x1, waiting for transfers between devices: 0.01 us -> 10.5 us  [gather_split(): other = lax.ppermute(far, 'dp', NEAR_Z)]
    ppermute x1, waiting for transfers between devices: 11.8 us -> 6.01 us  [body(): gain_in = lax.ppermute(gain_grads, *hops[0])]
    ppermute x3, waiting for transfers between devices: 8.78 us -> 13.6 us  [neighbour_hop(): lax.ppermute(value, 'tensor', OTHER_Y)]
    ppermute x2, waiting for transfers between devices: 8.25 us -> 11.7 us  [second_hop(): lax.ppermute(sent[0], 'dp', OTHER_X)]
  transfers between devices with their start and end apart: 36 -> 36, of which waited for: 23 -> 28; matrix products, arithmetic and copies ran while one was open for 0% -> 0% of each run, Pallas kernels for 13% -> 13%
where the time goes in v4:
time: 235 us
  waiting for transfers between devices  112 us (48%)
  Pallas kernels  76.7 us (33%)
  starting transfers between devices  40.8 us (17%)
  local copies, waits for them, and re-layouts  3.76 us (2%)
    pallas_call x31, Pallas kernels, call(): pl.pallas_call(kernel, grid=grid, in_specs=in_specs, out_specs=[spec for...  76.7 us
    ppermute x3, waiting for transfers between devices, across_hop(): lax.ppermute(pieces[0], 'tensor', OTHER_Y)  13.6 us
    ppermute x3, waiting for transfers between devices, neighbour_hop(): lax.ppermute(value, 'tensor', OTHER_Y)  13.6 us
    ppermute x2, waiting for transfers between devices, second_hop(): lax.ppermute(sent[0], 'dp', OTHER_X)  11.7 us
    ppermute x2, waiting for transfers between devices, first_hop(): lax.ppermute(sent[0], 'tensor', OTHER_Y)  10.8 us
    ppermute x1, waiting for transfers between devices, gather_split(): other = lax.ppermute(far, 'dp', NEAR_Z)  10.5 us
    ppermute x1, waiting for transfers between devices, gather_split(): far = lax.ppermute(own, 'dp', FAR_Z)  9.59 us
    ppermute x1, waiting for transfers between devices, body(): gain_in = lax.ppermute(gain_grads, *hops[4])  8.06 us
  transfers between devices with their start and end apart: 36, of which 28 were waited for; matrix products, arithmetic and copies ran while one was open for 0% of the time, Pallas kernels for 13%

profile of v4, /device:TPU:0, one launch (start us, length us, event | category | flops | bytes accessed | tf_op | source)
XLA Modules:
  0.0 234.8 jit_solution(10200207381727538996)
XLA Ops:
  0.8 1.3 copy-done.1
  2.3 3.0 %collective-permute-start.3 = (bf16[1,6,96,384]{3,2,1,0:T(8,128)(2,1)S(1)}, bf16[1,6,96,384]{3,2,1,0:T(8,128)(2,1)S(1)}, u32[]{:S(2)}, u32[]{:S(2)}) collective-permute-start(bf16[1,6,96,384]{3,2,1,0:T(8,128)(2,1)S(1)} %pack.1.own), channel_id=1, source_target_pairs={{0,1},{1,0},{2,3},{3,2},{4,5},{5,4},{6,7},{7,6},{8,9},{9,8},{10,11... | collective-permute-start | bytes 1327112 | tf_op jit(solution)/shard_map/ppermute | solution.py:683
  5.3 1.5 collective-permute-start.2
  6.8 2.6 %collective-permute-start.1 = (bf16[1,6,96,384]{3,2,1,0:T(8,128)(2,1)S(1)}, bf16[1,6,96,384]{3,2,1,0:T(8,128)(2,1)S(1)}, u32[]{:S(2)}, u32[]{:S(2)}) collective-permute-start(bf16[1,6,96,384]{3,2,1,0:T(8,128)(2,1)S(1)} %pack.1.own), channel_id=1, source_target_pairs={{0,16},{2,18},{4,20},{6,22},{8,24},{10,26},{12,28},{14,30},{16,0},... | collective-permute-start | bytes 1327112 | tf_op jit(solution)/shard_map/ppermute | solution.py:693
  9.4 1.6 collective-permute-start
  11.0 0.8 copy.29.token_mask
  11.8 0.9 copy-done.7
  12.7 0.7 copy-done.9
  13.4 1.7 prepare.1
  15.5 1.5 collective-permute-done.2.by_x
  17.4 1.6 collective-permute-start.5
  19.1 9.6 %collective-permute-done.1.two = bf16[1,6,96,384]{3,2,1,0:T(8,128)(2,1)S(1)} collective-permute-done((bf16[1,6,96,384]{3,2,1,0:T(8,128)(2,1)S(1)}, bf16[1,6,96,384]{3,2,1,0:T(8,128)(2,1)S(1)}, u32[]{:S(2)}, u32[]{:S(2)}) %collective-permute-start.1) | collective-permute-done | bytes 442400 | tf_op jit(solution)/shard_map/ppermute | solution.py:693
  28.9 0.9 place_own.3
  30.9 1.5 collective-permute-start.6
  32.4 10.5 %collective-permute-done.6.own = bf16[1,6,96,384]{3,2,1,0:T(8,128)(2,1)S(1)} collective-permute-done((bf16[1,6,96,384]{3,2,1,0:T(8,128)(2,1)S(1)}, bf16[1,6,96,384]{3,2,1,0:T(8,128)(2,1)S(1)}, u32[]{:S(2)}, u32[]{:S(2)}) %collective-permute-start.6) | collective-permute-done | bytes 442400 | tf_op jit(solution)/shard_map/ppermute | solution.py:701
  42.9 1.6 collective-permute-start.12
  44.5 1.5 collective-permute-start.11
  46.0 6.4 %collective-permute-done.8.by_y = bf16[2,6,96,384]{3,2,1,0:T(8,128)(2,1)S(1)} collective-permute-done((bf16[2,6,96,384]{3,2,1,0:T(8,128)(2,1)S(1)}, bf16[2,6,96,384]{3,2,1,0:T(8,128)(2,1)S(1)}, u32[]{:S(2)}, u32[]{:S(2)}) %collective-permute-start.8) | collective-permute-done | bytes 884768 | tf_op jit(solution)/shard_map/ppermute | solution.py:683
  53.0 1.6 collective-permute-start.9
  55.1 6.7 %collective-permute-done.12.by_y = bf16[1,6,96,384]{3,2,1,0:T(8,128)(2,1)S(1)} collective-permute-done((bf16[1,6,96,384]{3,2,1,0:T(8,128)(2,1)S(1)}, bf16[1,6,96,384]{3,2,1,0:T(8,128)(2,1)S(1)}, u32[]{:S(2)}, u32[]{:S(2)}) %collective-permute-start.12) | collective-permute-done | bytes 442400 | tf_op jit(solution)/shard_map/ppermute | solution.py:683
  62.4 8.5 %collective-permute-done.9.across_one = bf16[2,3,96,384]{3,2,1,0:T(8,128)(2,1)S(1)} collective-permute-done((bf16[2,3,96,384]{3,2,1,0:T(8,128)(2,1)S(1)}, bf16[2,3,96,384]{3,2,1,0:T(8,128)(2,1)S(1)}, u32[]{:S(2)}, u32[]{:S(2)}) %collective-permute-start.9) | collective-permute-done | bytes 442400 | tf_op jit(solution)/shard_map/ppermute | solution.py:687
  71.2 1.2 place_own.4
  72.5 1.6 collective-permute-start.14
  74.6 0.7 place_other.3.rest_0_
  75.3 5.1 %collective-permute-done.14.across_one = bf16[1,3,96,384]{3,2,1,0:T(8,128)(2,1)S(1)} collective-permute-done((bf16[1,3,96,384]{3,2,1,0:T(8,128)(2,1)S(1)}, bf16[1,3,96,384]{3,2,1,0:T(8,128)(2,1)S(1)}, u32[]{:S(2)}, u32[]{:S(2)}) %collective-permute-start.14) | collective-permute-done | bytes 221216 | tf_op jit(solution)/shard_map/ppermute | solution.py:687
  80.4 1.2 collective-permute-done.15.across_two
  81.6 0.9 place_own.5
  82.5 0.9 place_other.4._
  83.4 2.8 %collective-permute-done.17.arrived = bf16[1,2,2,6,96,384]{5,4,3,2,1,0:T(8,128)(2,1)S(1)} collective-permute-done((bf16[1,2,2,6,96,384]{5,4,3,2,1,0:T(8,128)(2,1)S(1)}, bf16[1,2,2,6,96,384]{5,4,3,2,1,0:T(8,128)(2,1)S(1)}, u32[]{:S(2)}, u32[]{:S(2)}) %collective-permute-start.17) | collective-permute-done | bytes 1769504 | tf_op jit(solution)/shard_map/ppermute | solution.py:890
  86.2 0.7 place_other.5
  86.9 9.3 %attention_forward.1 = (bf16[6,768,384]{2,1,0:T(8,128)(2,1)S(1)}, bf16[768,768]{1,0:T(8,128)(2,1)S(1)}, f32[768,768]{1,0:T(8,128)S(1)}, bf16[768,768]{1,0:T(8,128)(2,1)S(1)}, f32[48,768]{1,0:T(8,128)S(1)}) custom-call(bf16[768,768]{1,0:T(8,128)(2,1)S(1)} %copy-done, f32[2,768]{1,0:T(2,128)S(1)} %copy-done.10, ...), custom_call_target="tpu_custom_call" | custom-call | flops 1 | bytes 1 | tf_op jit(solution)/shard_map/attention_forward/pallas_call | solution.py:406
  96.3 25.0 %mlp_both.1 = (f32[4,768,128]{2,1,0:T(8,128)S(1)}, f32[768,768]{1,0:T(8,128)S(1)}, bf16[2,2,2,6,96,384]{5,4,3,2,1,0:T(8,128)(2,1)S(1)}, bf16[2,2,2,6,96,384]{5,4...) custom-call(s32[4]{0:T(128)S(1)} %pad_add_fusion.coords, ...), custom_call_target="tpu_custom_call" | custom-call | flops 1 | bytes 1 | tf_op jit(solution)/shard_map/mlp_both/pallas_call | solution.py:406
  121.4 5.0 %output_backward.1 = (f32[768,768]{1,0:T(8,128)S(1)}, f32[1,768]{1,0:T(1,128)S(1)}, bf16[768,768]{1,0:T(8,128)(2,1)S(1)}, bf16[2,2,2,6,96,384]{5,4,3,2,1,0:T(8,128)(2,1)S(1)}, bf16[2,2,2,6,96,384]{5,4,3,2,1,0:T(8,128)(2,1)S(1)}) custom-call(s32[4]{0:T(128)S(1)} %pad_add_fusion.coords, ...), custom_call_target="tpu_custom_call", output_to_operand_aliasing={{3}: (8, {}), {4}: (9, {})} | custom-call | flops 1 | bytes 1 | tf_op jit(solution)/shard_map/output_backward/pallas_call | solution.py:406
  126.5 1.1 collective-permute-done.18.arrived
  127.5 1.3 split_sum.2
  129.9 9.9 %attention_backward.1 = (bf16[6,768,384]{2,1,0:T(8,128)(2,1)S(1)}, bf16[2,2,2,6,96,384]{5,4,3,2,1,0:T(8,128)(2,1)S(1)}, bf16[2,2,2,6,96,384]{5,4,3,2,1,0:T(8,128)(2,1)S(1)}) custom-call(s32[4]{0:T(128)S(1)} %pad_add_fusion.coords, f32[6,16,128]{2,1,0:T(8,128)S(1)} %get-tuple-element.156.mask, ...), custom_call_target="tpu_custom_call", output_to_operand_aliasing={{1}: (5, {}), {2}: (6, {})} | custom-call | flops 1 | bytes 1 | tf_op jit(solution)/shard_map/attention_backward/pallas_call | solution.py:406
  139.8 10.8 %collective-permute-done.19.one_in = bf16[2,2,3,96,384]{4,3,2,1,0:T(8,128)(2,1)S(1)} collective-permute-done((bf16[2,2,3,96,384]{4,3,2,1,0:T(8,128)(2,1)S(1)}, bf16[2,2,3,96,384]{4,3,2,1,0:T(8,128)(2,1)S(1)}, u32[]{:S(2)}, u32[]{:S(2)}) %collective-permute-start.19) | collective-permute-done | bytes 884768 | tf_op jit(solution)/shard_map/ppermute | solution.py:894
  150.8 0.8 split_again.2
  152.2 1.6 collective-permute-start.22
  153.7 3.3 %collective-permute-done.24.arrived = bf16[2,2,2,6,96,384]{5,4,3,2,1,0:T(8,128)(2,1)S(1)} collective-permute-done((bf16[2,2,2,6,96,384]{5,4,3,2,1,0:T(8,128)(2,1)S(1)}, bf16[2,2,2,6,96,384]{5,4,3,2,1,0:T(8,128)(2,1)S(1)}, u32[]{:S(2)}, u32[]{:S(2)}) %collective-permute-start.24) | collective-permute-done | bytes 3538976 | tf_op jit(solution)/shard_map/ppermute | solution.py:890
  157.0 1.1 split_sum.3
  158.1 1.6 collective-permute-start.25
  160.2 4.4 %collective-permute-done.21.one_in = bf16[2,3,96,384]{3,2,1,0:T(8,128)(2,1)S(1)} collective-permute-done((bf16[2,3,96,384]{3,2,1,0:T(8,128)(2,1)S(1)}, bf16[2,3,96,384]{3,2,1,0:T(8,128)(2,1)S(1)}, u32[]{:S(2)}, u32[]{:S(2)}) %collective-permute-start.21) | collective-permute-done | bytes 442400 | tf_op jit(solution)/shard_map/ppermute | solution.py:898
  165.8 1.6 collective-permute-start.23
  167.4 6.5 %input_backward.1 = (f32[768,768]{1,0:T(8,128)}, f32[2,1,768]{2,1,0:T(1,128)S(1)}) custom-call(bf16[768,768]{1,0:T(8,128)(2,1)S(1)} %copy-done, f32[2,768]{1,0:T(2,128)S(1)} %copy-done.10, bf16[6,768,384]{2,1,0:T(8,128)(2,1)S(1)} %get-tuple-element.227.grad_mixed, f32[768,768]{1,0:T(8,128)S(1)} %get-tuple-element.228.grad_after, ...), custom_call_target="tpu_custom_call" | custom-call | flops 1 | bytes 1 | tf_op jit(solution)/shard_map/input_backward/pallas_call | solution.py:406
  173.9 1.5 collective-permute-start.27
  175.4 2.1 pool_out.1
  177.5 6.0 %collective-permute-done.27.right = f32[2,1,768]{2,1,0:T(1,128)S(1)} collective-permute-done((f32[2,1,768]{2,1,0:T(1,128)S(1)}, f32[2,1,768]{2,1,0:T(1,128)S(1)}, u32[]{:S(2)}, u32[]{:S(2)}) %collective-permute-start.27) | collective-permute-done | bytes 6176 | tf_op jit(solution)/shard_map/ppermute | solution.py:1040
  183.6 0.9 split_again.3
  184.5 1.6 collective-permute-start.28
  186.1 1.5 collective-permute-start.29
  187.7 1.2 collective-permute-done.30.right
  188.8 7.2 %collective-permute-done.28.one_in = bf16[2,3,96,384]{3,2,1,0:T(8,128)(2,1)S(1)} collective-permute-done((bf16[2,3,96,384]{3,2,1,0:T(8,128)(2,1)S(1)}, bf16[2,3,96,384]{3,2,1,0:T(8,128)(2,1)S(1)}, u32[]{:S(2)}, u32[]{:S(2)}) %collective-permute-start.28) | collective-permute-done | bytes 442400 | tf_op jit(solution)/shard_map/ppermute | solution.py:898
  196.1 1.3 collective-permute-done.29.two_in
  198.0 1.5 collective-permute-start.31
  200.1 3.1 %collective-permute-done.32.right = f32[2,1,768]{2,1,0:T(1,128)S(1)} collective-permute-done((f32[2,1,768]{2,1,0:T(1,128)S(1)}, f32[2,1,768]{2,1,0:T(1,128)S(1)}, u32[]{:S(2)}, u32[]{:S(2)}) %collective-permute-start.32) | collective-permute-done | bytes 6176 | tf_op jit(solution)/shard_map/ppermute | solution.py:1055
  203.1 5.2 %collective-permute-done.31.low_in = bf16[6,96,384]{2,1,0:T(8,128)(2,1)S(1)} collective-permute-done((bf16[6,96,384]{2,1,0:T(8,128)(2,1)S(1)}, bf16[6,96,384]{2,1,0:T(8,128)(2,1)S(1)}, u32[]{:S(2)}, u32[]{:S(2)}) %collective-permute-start.31) | collective-permute-done | bytes 442400 | tf_op jit(solution)/shard_map/ppermute | solution.py:1053
  208.4 0.7 pick_sum.1
  209.0 2.1 collective-permute-start.33
  211.1 1.7 collective-permute-start.34
  212.9 5.7 %collective-permute-done.34.right = f32[2,1,768]{2,1,0:T(1,128)S(1)} collective-permute-done((f32[2,1,768]{2,1,0:T(1,128)S(1)}, f32[2,1,768]{2,1,0:T(1,128)S(1)}, u32[]{:S(2)}, u32[]{:S(2)}) %collective-permute-start.34) | collective-permute-done | bytes 6176 | tf_op jit(solution)/shard_map/ppermute | solution.py:1061
  218.5 2.5 %collective-permute-start.35 = (f32[2,1,768]{2,1,0:T(1,128)S(1)}, f32[2,1,768]{2,1,0:T(1,128)S(1)}, u32[]{:S(2)}, u32[]{:S(2)}) collective-permute-start(f32[2,1,768]{2,1,0:T(1,128)S(1)} %sum_of.7.grads), channel_id=1, source_target_pairs={{0,16},{2,18},{4,20},{6,22},{8,24},{10,26},{12,28},{14,30},{16,0},... | collective-permute-start | bytes 18440 | tf_op jit(solution)/shard_map/ppermute | solution.py:1063
  221.0 8.1 %collective-permute-done.35.arrived = f32[2,1,768]{2,1,0:T(1,128)S(1)} collective-permute-done((f32[2,1,768]{2,1,0:T(1,128)S(1)}, f32[2,1,768]{2,1,0:T(1,128)S(1)}, u32[]{:S(2)}, u32[]{:S(2)}) %collective-permute-start.35) | collective-permute-done | bytes 6176 | tf_op jit(solution)/shard_map/ppermute | solution.py:1063
  229.8 5.0 %update.1 = (f32[24,96,96]{2,1,0:T(8,128)}, f32[24,96,96]{2,1,0:T(8,128)}, f32[24,96,96]{2,1,0:T(8,128)}, f32[24,96,96]{2,1,0:T(8,128)}, bf16[24,96,96]{2,1,0:T(8,128)(2,1)}) custom-call(bf16[6,96,384]{2,1,0:T(8,128)(2,1)S(1)} %get-tuple-element.261.mine, bf16[6,96,384]{2,1,0:T(8,128)(2,1)S(1)} %collective-permute-done.33.arrived, ...), custom_call_target="tpu_custom_call" | custom-call | flops 1 | bytes 1 | tf_op jit(solution)/shard_map/update/pallas_call | solution.py:406
  (65 shorter events, 10.9 us)
Async XLA Ops:
  0.6 11.1 %copy-start = (bf16[768,768]{1,0:T(8,128)(2,1)S(1)}, bf16[768,768]{1,0:T(8,128)(2,1)}, u32[]{:S(2)}) copy-start(bf16[768,768]{1,0:T(8,128)(2,1)} %tok.5) | copy-start | bytes 3538948
  0.8 1.3 copy-start.1
  2.3 13.2 %collective-permute-start.3 = (bf16[1,6,96,384]{3,2,1,0:T(8,128)(2,1)S(1)}, bf16[1,6,96,384]{3,2,1,0:T(8,128)(2,1)S(1)}, u32[]{:S(2)}, u32[]{:S(2)}) collective-permute-start(bf16[1,6,96,384]{3,2,1,0:T(8,128)(2,1)S(1)} %pack.1.own), channel_id=1, source_target_pairs={{0,1},{1,0},{2,3},{3,2},{4,5},{5,4},{6,7},{7,6},{8,9},{9,8},{10,11... | collective-permute-start | bytes 1327112 | tf_op jit(solution)/shard_map/ppermute | solution.py:683
  5.3 11.6 %collective-permute-start.2 = (bf16[1,6,96,384]{3,2,1,0:T(8,128)(2,1)S(1)}, bf16[1,6,96,384]{3,2,1,0:T(8,128)(2,1)S(1)}, u32[]{:S(2)}, u32[]{:S(2)}) collective-permute-start(bf16[1,6,96,384]{3,2,1,0:T(8,128)(2,1)S(1)} %pack.1.own), channel_id=1, source_target_pairs={{0,4},{2,6},{4,0},{6,2},{8,12},{10,14},{12,8},{14,10},{16,20},{18,... | collective-permute-start | bytes 1327112 | tf_op jit(solution)/shard_map/ppermute | solution.py:683
  6.8 21.8 %collective-permute-start.1 = (bf16[1,6,96,384]{3,2,1,0:T(8,128)(2,1)S(1)}, bf16[1,6,96,384]{3,2,1,0:T(8,128)(2,1)S(1)}, u32[]{:S(2)}, u32[]{:S(2)}) collective-permute-start(bf16[1,6,96,384]{3,2,1,0:T(8,128)(2,1)S(1)} %pack.1.own), channel_id=1, source_target_pairs={{0,16},{2,18},{4,20},{6,22},{8,24},{10,26},{12,28},{14,30},{16,0},... | collective-permute-start | bytes 1327112 | tf_op jit(solution)/shard_map/ppermute | solution.py:693
  9.4 19.4 %collective-permute-start = (bf16[1,6,96,384]{3,2,1,0:T(8,128)(2,1)S(1)}, bf16[1,6,96,384]{3,2,1,0:T(8,128)(2,1)S(1)}, u32[]{:S(2)}, u32[]{:S(2)}) collective-permute-start(bf16[1,6,96,384]{3,2,1,0:T(8,128)(2,1)S(1)} %pack.1.own), channel_id=1, source_target_pairs={{0,8},{2,10},{4,12},{6,14},{8,0},{10,2},{12,4},{14,6},{16,24},{18,... | collective-permute-start | bytes 1327112 | tf_op jit(solution)/shard_map/ppermute | solution.py:692
  11.8 0.9 copy-start.7
  12.7 0.7 copy-start.9
  17.0 11.8 %collective-permute-start.4 = (bf16[1,3,96,384]{3,2,1,0:T(8,128)(2,1)S(1)}, bf16[1,3,96,384]{3,2,1,0:T(8,128)(2,1)S(1)}, u32[]{:S(2)}, u32[]{:S(2)}) collective-permute-start(bf16[1,3,96,384]{3,2,1,0:T(8,128)(2,1)S(1)} %get-tuple-element.148), channel_id=1, source_target_pairs={{0,1},{1,0},{2,3},{3,2},{4,5},{5,4},{6,7},{7,6},{8,9},{9,8},{10,11... | collective-permute-start | bytes 663560 | tf_op jit(solution)/shard_map/ppermute | solution.py:687
  17.4 11.4 %collective-permute-start.5 = (bf16[1,3,96,384]{3,2,1,0:T(8,128)(2,1)S(1)}, bf16[1,3,96,384]{3,2,1,0:T(8,128)(2,1)S(1)}, u32[]{:S(2)}, u32[]{:S(2)}) collective-permute-start(bf16[1,3,96,384]{3,2,1,0:T(8,128)(2,1)S(1)} %get-tuple-element.149), channel_id=1, source_target_pairs={{0,4},{2,6},{4,0},{6,2},{8,12},{10,14},{12,8},{14,10},{16,20},{18,... | collective-permute-start | bytes 663560 | tf_op jit(solution)/shard_map/ppermute | solution.py:687
  29.7 41.5 %collective-permute-start.13 = (bf16[1,2,2,6,96,384]{5,4,3,2,1,0:T(8,128)(2,1)S(1)}, bf16[1,2,2,6,96,384]{5,4,3,2,1,0:T(8,128)(2,1)S(1)}, u32[]{:S(2)}, u32[]{:S(2)}) collective-permute-start(bf16[1,2,2,6,96,384]{5,4,3,2,1,0:T(8,128)(2,1)S(1)} %get-tuple-element.167), channel_id=1, source_target_pairs={{0,2},{2,0},{4,6},{6,4},{8,10},{10,8},{12,14},{14,12},{16,18},{18,... | collective-permute-start | bytes 5308424 | tf_op jit(solution)/shard_map/ppermute | solution.py:890
  29.9 22.5 %collective-permute-start.8 = (bf16[2,6,96,384]{3,2,1,0:T(8,128)(2,1)S(1)}, bf16[2,6,96,384]{3,2,1,0:T(8,128)(2,1)S(1)}, u32[]{:S(2)}, u32[]{:S(2)}) collective-permute-start(bf16[2,6,96,384]{3,2,1,0:T(8,128)(2,1)S(1)} %take_both.1.own), channel_id=1, source_target_pairs={{0,1},{1,0},{2,3},{3,2},{4,5},{5,4},{6,7},{7,6},{8,9},{9,8},{10,11... | collective-permute-start | bytes 2654216 | tf_op jit(solution)/shard_map/ppermute | solution.py:683
  30.5 22.5 %collective-permute-start.7 = (bf16[2,6,96,384]{3,2,1,0:T(8,128)(2,1)S(1)}, bf16[2,6,96,384]{3,2,1,0:T(8,128)(2,1)S(1)}, u32[]{:S(2)}, u32[]{:S(2)}) collective-permute-start(bf16[2,6,96,384]{3,2,1,0:T(8,128)(2,1)S(1)} %take_both.1.own), channel_id=1, source_target_pairs={{0,4},{2,6},{4,0},{6,2},{8,12},{10,14},{12,8},{14,10},{16,20},{18,... | collective-permute-start | bytes 2654216 | tf_op jit(solution)/shard_map/ppermute | solution.py:683
  30.9 12.0 %collective-permute-start.6 = (bf16[1,6,96,384]{3,2,1,0:T(8,128)(2,1)S(1)}, bf16[1,6,96,384]{3,2,1,0:T(8,128)(2,1)S(1)}, u32[]{:S(2)}, u32[]{:S(2)}) collective-permute-start(bf16[1,6,96,384]{3,2,1,0:T(8,128)(2,1)S(1)} %collective-permute-done.1.two), channel_id=1, source_target_pairs={{0,8},{2,10},{4,12},{6,14},{8,0},{10,2},{12,4},{14,6},{16,24},{18,... | collective-permute-start | bytes 1327112 | tf_op jit(solution)/shard_map/ppermute | solution.py:701
  42.9 18.9 %collective-permute-start.12 = (bf16[1,6,96,384]{3,2,1,0:T(8,128)(2,1)S(1)}, bf16[1,6,96,384]{3,2,1,0:T(8,128)(2,1)S(1)}, u32[]{:S(2)}, u32[]{:S(2)}) collective-permute-start(bf16[1,6,96,384]{3,2,1,0:T(8,128)(2,1)S(1)} %collective-permute-done.6.own), channel_id=1, source_target_pairs={{0,1},{1,0},{2,3},{3,2},{4,5},{5,4},{6,7},{7,6},{8,9},{9,8},{10,11... | collective-permute-start | bytes 1327112 | tf_op jit(solution)/shard_map/ppermute | solution.py:683
  44.5 17.9 %collective-permute-start.11 = (bf16[1,6,96,384]{3,2,1,0:T(8,128)(2,1)S(1)}, bf16[1,6,96,384]{3,2,1,0:T(8,128)(2,1)S(1)}, u32[]{:S(2)}, u32[]{:S(2)}) collective-permute-start(bf16[1,6,96,384]{3,2,1,0:T(8,128)(2,1)S(1)} %collective-permute-done.6.own), channel_id=1, source_target_pairs={{0,4},{2,6},{4,0},{6,2},{8,12},{10,14},{12,8},{14,10},{16,20},{18,... | collective-permute-start | bytes 1327112 | tf_op jit(solution)/shard_map/ppermute | solution.py:683
  53.0 17.9 %collective-permute-start.9 = (bf16[2,3,96,384]{3,2,1,0:T(8,128)(2,1)S(1)}, bf16[2,3,96,384]{3,2,1,0:T(8,128)(2,1)S(1)}, u32[]{:S(2)}, u32[]{:S(2)}) collective-permute-start(bf16[2,3,96,384]{3,2,1,0:T(8,128)(2,1)S(1)} %get-tuple-element.160), channel_id=1, source_target_pairs={{0,1},{1,0},{2,3},{3,2},{4,5},{5,4},{6,7},{7,6},{8,9},{9,8},{10,11... | collective-permute-start | bytes 1327112 | tf_op jit(solution)/shard_map/ppermute | solution.py:687
  54.6 16.6 %collective-permute-start.10 = (bf16[2,3,96,384]{3,2,1,0:T(8,128)(2,1)S(1)}, bf16[2,3,96,384]{3,2,1,0:T(8,128)(2,1)S(1)}, u32[]{:S(2)}, u32[]{:S(2)}) collective-permute-start(bf16[2,3,96,384]{3,2,1,0:T(8,128)(2,1)S(1)} %get-tuple-element.161), channel_id=1, source_target_pairs={{0,4},{2,6},{4,0},{6,2},{8,12},{10,14},{12,8},{14,10},{16,20},{18,... | collective-permute-start | bytes 1327112 | tf_op jit(solution)/shard_map/ppermute | solution.py:687
  72.3 9.3 %collective-permute-start.16 = (bf16[2,2,2,6,96,384]{5,4,3,2,1,0:T(8,128)(2,1)S(1)}, bf16[2,2,2,6,96,384]{5,4,3,2,1,0:T(8,128)(2,1)S(1)}, u32[]{:S(2)}, u32[]{:S(2)}) collective-permute-start(bf16[2,2,2,6,96,384]{5,4,3,2,1,0:T(8,128)(2,1)S(1)} %get-tuple-element.176), channel_id=1, source_target_pairs={{0,2},{2,0},{4,6},{6,4},{8,10},{10,8},{12,14},{14,12},{16,18},{18,... | collective-permute-start | bytes 10616840 | tf_op jit(solution)/shard_map/ppermute | solution.py:890
  72.5 7.9 %collective-permute-start.14 = (bf16[1,3,96,384]{3,2,1,0:T(8,128)(2,1)S(1)}, bf16[1,3,96,384]{3,2,1,0:T(8,128)(2,1)S(1)}, u32[]{:S(2)}, u32[]{:S(2)}) collective-permute-start(bf16[1,3,96,384]{3,2,1,0:T(8,128)(2,1)S(1)} %get-tuple-element.171), channel_id=1, source_target_pairs={{0,1},{1,0},{2,3},{3,2},{4,5},{5,4},{6,7},{7,6},{8,9},{9,8},{10,11... | collective-permute-start | bytes 663560 | tf_op jit(solution)/shard_map/ppermute | solution.py:687
  74.1 7.5 %collective-permute-start.15 = (bf16[1,3,96,384]{3,2,1,0:T(8,128)(2,1)S(1)}, bf16[1,3,96,384]{3,2,1,0:T(8,128)(2,1)S(1)}, u32[]{:S(2)}, u32[]{:S(2)}) collective-permute-start(bf16[1,3,96,384]{3,2,1,0:T(8,128)(2,1)S(1)} %get-tuple-element.172), channel_id=1, source_target_pairs={{0,4},{2,6},{4,0},{6,2},{8,12},{10,14},{12,8},{14,10},{16,20},{18,... | collective-permute-start | bytes 663560 | tf_op jit(solution)/shard_map/ppermute | solution.py:687
  82.5 3.8 %collective-permute-start.17 = (bf16[1,2,2,6,96,384]{5,4,3,2,1,0:T(8,128)(2,1)S(1)}, bf16[1,2,2,6,96,384]{5,4,3,2,1,0:T(8,128)(2,1)S(1)}, u32[]{:S(2)}, u32[]{:S(2)}) collective-permute-start(bf16[1,2,2,6,96,384]{5,4,3,2,1,0:T(8,128)(2,1)S(1)} %get-tuple-element.182), channel_id=1, source_target_pairs={{0,2},{2,0},{4,6},{6,4},{8,10},{10,8},{12,14},{14,12},{16,18},{18,... | collective-permute-start | bytes 5308424 | tf_op jit(solution)/shard_map/ppermute | solution.py:890
  83.4 3.5 %copy-start.10 = (f32[2,768]{1,0:T(2,128)S(1)}, f32[2,768]{1,0:T(2,128)}, u32[]{:S(2)}) copy-start(f32[2,768]{1,0:T(2,128)} %gains.9) | copy-start | bytes 18436
  96.3 25.2 %copy-start.8 = (bf16[48,768]{1,0:T(8,128)(2,1)S(1)}, bf16[48,768]{1,0:T(8,128)(2,1)}, u32[]{:S(2)}) copy-start(bf16[48,768]{1,0:T(8,128)(2,1)} %cot.3) | copy-start | bytes 221188
  121.2 6.3 %collective-permute-start.18 = (bf16[2,2,2,6,96,384]{5,4,3,2,1,0:T(8,128)(2,1)S(1)}, bf16[2,2,2,6,96,384]{5,4,3,2,1,0:T(8,128)(2,1)S(1)}, u32[]{:S(2)}, u32[]{:S(2)}) collective-permute-start(bf16[2,2,2,6,96,384]{5,4,3,2,1,0:T(8,128)(2,1)S(1)} %get-tuple-element.190), channel_id=1, source_target_pairs={{0,2},{2,0},{4,6},{6,4},{8,10},{10,8},{12,14},{14,12},{16,18},{18,... | collective-permute-start | bytes 10616840 | tf_op jit(solution)/shard_map/ppermute | solution.py:890
  128.8 21.8 %collective-permute-start.19 = (bf16[2,2,3,96,384]{4,3,2,1,0:T(8,128)(2,1)S(1)}, bf16[2,2,3,96,384]{4,3,2,1,0:T(8,128)(2,1)S(1)}, u32[]{:S(2)}, u32[]{:S(2)}) collective-permute-start(bf16[2,2,3,96,384]{4,3,2,1,0:T(8,128)(2,1)S(1)} %get-tuple-element.207), channel_id=1, source_target_pairs={{0,1},{1,0},{2,3},{3,2},{4,5},{5,4},{6,7},{7,6},{8,9},{9,8},{10,11... | collective-permute-start | bytes 2654216 | tf_op jit(solution)/shard_map/ppermute | solution.py:894
  129.4 21.4 %collective-permute-start.20 = (bf16[2,2,3,96,384]{4,3,2,1,0:T(8,128)(2,1)S(1)}, bf16[2,2,3,96,384]{4,3,2,1,0:T(8,128)(2,1)S(1)}, u32[]{:S(2)}, u32[]{:S(2)}) collective-permute-start(bf16[2,2,3,96,384]{4,3,2,1,0:T(8,128)(2,1)S(1)} %get-tuple-element.208), channel_id=1, source_target_pairs={{0,4},{2,6},{4,0},{6,2},{8,12},{10,14},{12,8},{14,10},{16,20},{18,... | collective-permute-start | bytes 2654216 | tf_op jit(solution)/shard_map/ppermute | solution.py:894
  150.8 6.2 %collective-permute-start.24 = (bf16[2,2,2,6,96,384]{5,4,3,2,1,0:T(8,128)(2,1)S(1)}, bf16[2,2,2,6,96,384]{5,4,3,2,1,0:T(8,128)(2,1)S(1)}, u32[]{:S(2)}, u32[]{:S(2)}) collective-permute-start(bf16[2,2,2,6,96,384]{5,4,3,2,1,0:T(8,128)(2,1)S(1)} %get-tuple-element.224), channel_id=1, source_target_pairs={{0,2},{2,0},{4,6},{6,4},{8,10},{10,8},{12,14},{14,12},{16,18},{18,... | collective-permute-start | bytes 10616840 | tf_op jit(solution)/shard_map/ppermute | solution.py:890
  151.6 13.0 %collective-permute-start.21 = (bf16[2,3,96,384]{3,2,1,0:T(8,128)(2,1)S(1)}, bf16[2,3,96,384]{3,2,1,0:T(8,128)(2,1)S(1)}, u32[]{:S(2)}, u32[]{:S(2)}) collective-permute-start(bf16[2,3,96,384]{3,2,1,0:T(8,128)(2,1)S(1)} %get-tuple-element.220), channel_id=1, source_target_pairs={{0,4},{2,6},{4,0},{6,2},{8,12},{10,14},{12,8},{14,10},{16,20},{18,... | collective-permute-start | bytes 1327112 | tf_op jit(solution)/shard_map/ppermute | solution.py:898
  152.2 13.0 %collective-permute-start.22 = (bf16[2,3,96,384]{3,2,1,0:T(8,128)(2,1)S(1)}, bf16[2,3,96,384]{3,2,1,0:T(8,128)(2,1)S(1)}, u32[]{:S(2)}, u32[]{:S(2)}) collective-permute-start(bf16[2,3,96,384]{3,2,1,0:T(8,128)(2,1)S(1)} %get-tuple-element.221), channel_id=1, source_target_pairs={{0,1},{1,0},{2,3},{3,2},{4,5},{5,4},{6,7},{7,6},{8,9},{9,8},{10,11... | collective-permute-start | bytes 1327112 | tf_op jit(solution)/shard_map/ppermute | solution.py:898
  158.1 25.5 %collective-permute-start.25 = (bf16[2,2,3,96,384]{4,3,2,1,0:T(8,128)(2,1)S(1)}, bf16[2,2,3,96,384]{4,3,2,1,0:T(8,128)(2,1)S(1)}, u32[]{:S(2)}, u32[]{:S(2)}) collective-permute-start(bf16[2,2,3,96,384]{4,3,2,1,0:T(8,128)(2,1)S(1)} %get-tuple-element.225), channel_id=1, source_target_pairs={{0,1},{1,0},{2,3},{3,2},{4,5},{5,4},{6,7},{7,6},{8,9},{9,8},{10,11... | collective-permute-start | bytes 2654216 | tf_op jit(solution)/shard_map/ppermute | solution.py:894
  159.7 23.9 %collective-permute-start.26 = (bf16[2,2,3,96,384]{4,3,2,1,0:T(8,128)(2,1)S(1)}, bf16[2,2,3,96,384]{4,3,2,1,0:T(8,128)(2,1)S(1)}, u32[]{:S(2)}, u32[]{:S(2)}) collective-permute-start(bf16[2,2,3,96,384]{4,3,2,1,0:T(8,128)(2,1)S(1)} %get-tuple-element.226), channel_id=1, source_target_pairs={{0,4},{2,6},{4,0},{6,2},{8,12},{10,14},{12,8},{14,10},{16,20},{18,... | collective-permute-start | bytes 2654216 | tf_op jit(solution)/shard_map/ppermute | solution.py:894
  165.8 17.7 %collective-permute-start.23 = (bf16[6,96,384]{2,1,0:T(8,128)(2,1)S(1)}, bf16[6,96,384]{2,1,0:T(8,128)(2,1)S(1)}, u32[]{:S(2)}, u32[]{:S(2)}) collective-permute-start(bf16[6,96,384]{2,1,0:T(8,128)(2,1)S(1)} %get-tuple-element.222), channel_id=1, source_target_pairs={{0,8},{2,10},{4,12},{6,14},{8,0},{10,2},{12,4},{14,6},{16,24},{18,... | collective-permute-start | bytes 1327112 | tf_op jit(solution)/shard_map/ppermute | solution.py:1043
  173.9 9.7 %collective-permute-start.27 = (f32[2,1,768]{2,1,0:T(1,128)S(1)}, f32[2,1,768]{2,1,0:T(1,128)S(1)}, u32[]{:S(2)}, u32[]{:S(2)}) collective-permute-start(f32[2,1,768]{2,1,0:T(1,128)S(1)} %get-tuple-element.230.left), channel_id=1, source_target_pairs={{0,1},{1,0},{2,3},{3,2},{4,5},{5,4},{6,7},{7,6},{8,9},{9,8},{10,11... | collective-permute-start | bytes 18440 | tf_op jit(solution)/shard_map/ppermute | solution.py:1040
  183.6 46.2 %copy-start.5 = (f32[24,96,96]{2,1,0:T(8,128)S(1)}, f32[24,96,96]{2,1,0:T(8,128)}, u32[]{:S(2)}) copy-start(f32[24,96,96]{2,1,0:T(8,128)} %root_left.1) | copy-start | bytes 2654212
  183.6 46.2 %copy-start.6 = (f32[24,96,96]{2,1,0:T(8,128)S(1)}, f32[24,96,96]{2,1,0:T(8,128)}, u32[]{:S(2)}) copy-start(f32[24,96,96]{2,1,0:T(8,128)} %root_right.1) | copy-start | bytes 2654212
  184.5 44.6 %copy-start.11 = (f32[2,768]{1,0:T(2,128)S(1)}, f32[2,768]{1,0:T(2,128)}, u32[]{:S(2)}) copy-start(f32[2,768]{1,0:T(2,128)} %moments.1) | copy-start | bytes 18436
  184.5 45.3 %copy-start.2 = (f32[24,96,96]{2,1,0:T(8,128)S(1)}, f32[24,96,96]{2,1,0:T(8,128)}, u32[]{:S(2)}) copy-start(f32[24,96,96]{2,1,0:T(8,128)} %master.1) | copy-start | bytes 2654212
  184.5 45.3 %copy-start.3 = (f32[24,96,96]{2,1,0:T(8,128)S(1)}, f32[24,96,96]{2,1,0:T(8,128)}, u32[]{:S(2)}) copy-start(f32[24,96,96]{2,1,0:T(8,128)} %stat_left.1) | copy-start | bytes 2654212
  184.5 45.3 %copy-start.4 = (f32[24,96,96]{2,1,0:T(8,128)S(1)}, f32[24,96,96]{2,1,0:T(8,128)}, u32[]{:S(2)}) copy-start(f32[24,96,96]{2,1,0:T(8,128)} %stat_right.1) | copy-start | bytes 2654212
  184.5 11.5 %collective-permute-start.28 = (bf16[2,3,96,384]{3,2,1,0:T(8,128)(2,1)S(1)}, bf16[2,3,96,384]{3,2,1,0:T(8,128)(2,1)S(1)}, u32[]{:S(2)}, u32[]{:S(2)}) collective-permute-start(bf16[2,3,96,384]{3,2,1,0:T(8,128)(2,1)S(1)} %get-tuple-element.244), channel_id=1, source_target_pairs={{0,4},{2,6},{4,0},{6,2},{8,12},{10,14},{12,8},{14,10},{16,20},{18,... | collective-permute-start | bytes 1327112 | tf_op jit(solution)/shard_map/ppermute | solution.py:898
  186.1 11.2 %collective-permute-start.29 = (bf16[2,3,96,384]{3,2,1,0:T(8,128)(2,1)S(1)}, bf16[2,3,96,384]{3,2,1,0:T(8,128)(2,1)S(1)}, u32[]{:S(2)}, u32[]{:S(2)}) collective-permute-start(bf16[2,3,96,384]{3,2,1,0:T(8,128)(2,1)S(1)} %get-tuple-element.245), channel_id=1, source_target_pairs={{0,1},{1,0},{2,3},{3,2},{4,5},{5,4},{6,7},{7,6},{8,9},{9,8},{10,11... | collective-permute-start | bytes 1327112 | tf_op jit(solution)/shard_map/ppermute | solution.py:898
  187.7 1.2 collective-permute-start.30
  198.0 10.3 %collective-permute-start.31 = (bf16[6,96,384]{2,1,0:T(8,128)(2,1)S(1)}, bf16[6,96,384]{2,1,0:T(8,128)(2,1)S(1)}, u32[]{:S(2)}, u32[]{:S(2)}) collective-permute-start(bf16[6,96,384]{2,1,0:T(8,128)(2,1)S(1)} %get-tuple-element.250), channel_id=1, source_target_pairs={{0,8},{2,10},{4,12},{6,14},{8,0},{10,2},{12,4},{14,6},{16,24},{18,... | collective-permute-start | bytes 1327112 | tf_op jit(solution)/shard_map/ppermute | solution.py:1053
  199.5 3.6 %collective-permute-start.32 = (f32[2,1,768]{2,1,0:T(1,128)S(1)}, f32[2,1,768]{2,1,0:T(1,128)S(1)}, u32[]{:S(2)}, u32[]{:S(2)}) collective-permute-start(f32[2,1,768]{2,1,0:T(1,128)S(1)} %sum_of.5.left), channel_id=1, source_target_pairs={{0,4},{2,6},{4,0},{6,2},{8,12},{10,14},{12,8},{14,10},{16,20},{18,... | collective-permute-start | bytes 18440 | tf_op jit(solution)/shard_map/ppermute | solution.py:1055
  209.0 20.7 %collective-permute-start.33 = (bf16[6,96,384]{2,1,0:T(8,128)(2,1)S(1)}, bf16[6,96,384]{2,1,0:T(8,128)(2,1)S(1)}, u32[]{:S(2)}, u32[]{:S(2)}) collective-permute-start(bf16[6,96,384]{2,1,0:T(8,128)(2,1)S(1)} %get-tuple-element.253), channel_id=1, source_target_pairs={{0,16},{2,18},{4,20},{6,22},{8,24},{10,26},{12,28},{14,30},{16,0},... | collective-permute-start | bytes 1327112 | tf_op jit(solution)/shard_map/ppermute | solution.py:1059
  211.1 7.4 %collective-permute-start.34 = (f32[2,1,768]{2,1,0:T(1,128)S(1)}, f32[2,1,768]{2,1,0:T(1,128)S(1)}, u32[]{:S(2)}, u32[]{:S(2)}) collective-permute-start(f32[2,1,768]{2,1,0:T(1,128)S(1)} %sum_of.6.left), channel_id=1, source_target_pairs={{0,8},{2,10},{4,12},{6,14},{8,0},{10,2},{12,4},{14,6},{16,24},{18,... | collective-permute-start | bytes 18440 | tf_op jit(solution)/shard_map/ppermute | solution.py:1061
  218.5 10.6 %collective-permute-start.35 = (f32[2,1,768]{2,1,0:T(1,128)S(1)}, f32[2,1,768]{2,1,0:T(1,128)S(1)}, u32[]{:S(2)}, u32[]{:S(2)}) collective-permute-start(f32[2,1,768]{2,1,0:T(1,128)S(1)} %sum_of.7.grads), channel_id=1, source_target_pairs={{0,16},{2,18},{4,20},{6,22},{8,24},{10,26},{12,28},{14,30},{16,0},... | collective-permute-start | bytes 18440 | tf_op jit(solution)/shard_map/ppermute | solution.py:1063

commit v5 on v4

--- a/solution.py
+++ b/solution.py
@@ -614,6 +614,25 @@
         put(1 - half, 1 - place, slice(3, 6), across_two[i])
 
 
+def place_most(apart, coords, own, by_x, by_y, _, whole, sent):
+    core, place, plane, half = coords[0], coords[1], coords[2], coords[3]
+    for i, (y, x, value) in enumerate(
+        ((half, place, own), (half, 1 - place, by_x), (1 - half, place, by_y))
+    ):
+        sent[i] = value[0]
+        whole[y, plane ^ apart, x, core] = value[0]
+
+
+def place_last(apart, coords, most_in, one_in, two_in, one, two, _, whole):
+    core, place, plane, half = coords[0], coords[1], coords[2], coords[3]
+    z = plane ^ apart
+    for i, (y, x) in enumerate(((half, place), (half, 1 - place), (1 - half, place))):
+        whole[y, z, x, 1 - core] = most_in[i]
+    for strips, mine, other in ((pl.ds(0, 3), one, one_in), (pl.ds(3, 3), two, two_in)):
+        whole[1 - half, z, 1 - place, core, strips] = mine[0]
+        whole[1 - half, z, 1 - place, 1 - core, strips] = other[0]
+
+
 def place_other(planes, coords, arrived, _, whole):
     core, plane = coords[0], coords[2]
     for i, apart in enumerate(planes):
@@ -663,6 +682,34 @@
         aliases={6: 0} if held else None,
         mib=4,
     )
+
+
+def run_place_most(apart, coords, pieces, whole):
+    return call(
+        functools.partial(place_most, apart),
+        "place_most",
+        [SMEM] + [VMEM] * 4,
+        [(VMEM, shape_of(*WHOLE)), (VMEM, shape_of(3, OWN, BLOCK, STRIP))],
+        [],
+        1,
+        (coords, *pieces, whole),
+        aliases={4: 0},
+        mib=4,
+    )
+
+
+def run_place_last(apart, coords, pieces, whole):
+    return call(
+        functools.partial(place_last, apart),
+        "place_last",
+        [SMEM] + [VMEM] * 6,
+        [(VMEM, shape_of(*WHOLE))],
+        [],
+        1,
+        (coords, *pieces, whole),
+        aliases={6: 0},
+        mib=4,
+    )[0]
 
 
 def run_place_other(planes, coords, arrived, whole):
@@ -708,14 +755,15 @@
     other_across = across_hop(run_halves(*other_by))
     whole, sent = run_place_own((1, 2), coords, (both, *both_by, *both_across), (whole,))
     both_in = core_hop(sent)
+    whole, sent = run_place_most(3, coords, (other, *other_by), whole)
+    other_in = core_hop(sent)
     whole = run_place_other((0,), coords, own_in, whole)
-    other_across, both_in, whole = fence(other_across, both_in, whole)
-
-    whole, sent = run_place_own((3,), coords, (other, *other_by, *other_across), (whole,))
-    other_in = core_hop(sent)
+    other_across, both_in, other_in, whole = fence(other_across, both_in, other_in, whole)
+
+    across_in = core_hop(other_across[0]), core_hop(other_across[1])
     whole = run_place_other((1, 2), coords, both_in, whole)
-    other_in, whole = fence(other_in, whole)
-    whole = run_place_other((3,), coords, other_in, whole)
+    across_in, whole = fence(across_in, whole)
+    whole = run_place_last(3, coords, (other_in, *across_in, *other_across), whole)
     return whole.reshape(HALVES, STRIPS, BLOCK, STRIP), prepared
 
 
@@ -910,10 +958,14 @@
 
 def update(mine, arrived, master, stat_left, stat_right, root_left, root_right, *outs):
     grad_out, left_out, right_out, master_out, copy_out = outs
-    strip = pl.program_id(0)
-    grad = mine[strip].astype(F32) + arrived[strip].astype(F32)
-    blocks = [4 * strip + i for i in range(4)]
-    grads = [grad[:, i * BLOCK : (i + 1) * BLOCK] for i in range(4)]
+    count = grad_out.shape[0]
+    first = pl.program_id(0) * count
+    grads = []
+    for i in range(count // 4):
+        strip = first // 4 + i
+        grad = mine[strip].astype(F32) + arrived[strip].astype(F32)
+        grads += [grad[:, j * BLOCK : (j + 1) * BLOCK] for j in range(4)]
+    blocks = [first + i for i in range(count)]
     sides = [precise(g, root_right[block]) for g, block in zip(grads, blocks)]
     lefts = [precise(g, g, 1, 1) for g in grads]
     rights = [precise(g, g, 0, 0) for g in grads]
@@ -929,7 +981,8 @@
 
 def run_update(sums, blocks):
     count = blocks[0].shape[0]
-    tile = pl.BlockSpec((4, BLOCK, BLOCK), lambda i: (i, 0, 0))
+    step = 8 if count % 8 == 0 else 4
+    tile = pl.BlockSpec((step, BLOCK, BLOCK), lambda i: (i, 0, 0))
     shape = shape_of(count, BLOCK, BLOCK, dtype=F32)
     return call(
         update,
@@ -939,8 +992,8 @@
         [],
         12 * 2 * count * BLOCK**3,
         (*sums, *blocks),
-        grid=(count // 4,),
-        mib=4,
+        grid=(count // step,),
+        mib=8,
     )
 
 

time: 235 us -> 233 us (level)
  waiting for transfers between devices: 112 us -> 109 us
    ppermute x5 -> x7, waiting for transfers between devices: 7.19 us -> 4.68 us  [core_hop(): return lax.ppermute(sent, 'dp', OTHER_CORE)]
  transfers between devices with their start and end apart: 36 -> 38, of which waited for: 28 -> 29; matrix products, arithmetic and copies ran while one was open for 0% -> 0% of each run, Pallas kernels for 13% -> 13%
where the time goes in v5:
time: 233 us; the launch traced here: 232 us
  waiting for transfers between devices  109 us (47%)
  Pallas kernels  76.1 us (33%)
  starting transfers between devices  42 us (18%)
  local copies, waits for them, and re-layouts  3.76 us (2%)
    pallas_call x31, Pallas kernels, call(): pl.pallas_call(kernel, grid=grid, in_specs=in_specs, out_specs=[spec for...  76.1 us
    ppermute x3, waiting for transfers between devices, neighbour_hop(): lax.ppermute(value, 'tensor', OTHER_Y)  13.6 us
    ppermute x3, waiting for transfers between devices, across_hop(): lax.ppermute(pieces[0], 'tensor', OTHER_Y)  13.1 us
    ppermute x2, waiting for transfers between devices, second_hop(): lax.ppermute(sent[0], 'dp', OTHER_X)  11.6 us
    ppermute x2, waiting for transfers between devices, first_hop(): lax.ppermute(sent[0], 'tensor', OTHER_Y)  10.8 us
    ppermute x1, waiting for transfers between devices, gather_split(): other = lax.ppermute(far, 'dp', NEAR_Z)  10.5 us
    ppermute x1, waiting for transfers between devices, gather_split(): far = lax.ppermute(own, 'dp', FAR_Z)  9.59 us
    ppermute x1, waiting for transfers between devices, body(): gain_in = lax.ppermute(gain_grads, *hops[4])  8.05 us
  transfers between devices with their start and end apart: 38, of which 29 were waited for; matrix products, arithmetic and copies ran while one was open for 0% of the time, Pallas kernels for 13%

profile of v5, /device:TPU:0, one launch (start us, length us, event | category | flops | bytes accessed | tf_op | source)
XLA Modules:
  0.0 232.3 jit_solution(7022017839967223823)
XLA Ops:
  0.8 1.3 copy-done.1
  2.3 3.0 %collective-permute-start.3 = (bf16[1,6,96,384]{3,2,1,0:T(8,128)(2,1)S(1)}, bf16[1,6,96,384]{3,2,1,0:T(8,128)(2,1)S(1)}, u32[]{:S(2)}, u32[]{:S(2)}) collective-permute-start(bf16[1,6,96,384]{3,2,1,0:T(8,128)(2,1)S(1)} %pack.1.own), channel_id=1, source_target_pairs={{0,1},{1,0},{2,3},{3,2},{4,5},{5,4},{6,7},{7,6},{8,9},{9,8},{10,11... | collective-permute-start | bytes 1327112 | tf_op jit(solution)/shard_map/ppermute | solution.py:730
  5.3 1.5 collective-permute-start.2
  6.8 2.6 %collective-permute-start.1 = (bf16[1,6,96,384]{3,2,1,0:T(8,128)(2,1)S(1)}, bf16[1,6,96,384]{3,2,1,0:T(8,128)(2,1)S(1)}, u32[]{:S(2)}, u32[]{:S(2)}) collective-permute-start(bf16[1,6,96,384]{3,2,1,0:T(8,128)(2,1)S(1)} %pack.1.own), channel_id=1, source_target_pairs={{0,16},{2,18},{4,20},{6,22},{8,24},{10,26},{12,28},{14,30},{16,0},... | collective-permute-start | bytes 1327112 | tf_op jit(solution)/shard_map/ppermute | solution.py:740
  9.4 1.6 collective-permute-start
  11.0 0.8 copy.29.token_mask
  11.8 0.9 copy-done.7
  12.7 0.7 copy-done.9
  13.4 1.7 prepare.1
  15.5 1.5 collective-permute-done.2.by_x
  17.4 1.6 collective-permute-start.5
  19.1 9.6 %collective-permute-done.1.two = bf16[1,6,96,384]{3,2,1,0:T(8,128)(2,1)S(1)} collective-permute-done((bf16[1,6,96,384]{3,2,1,0:T(8,128)(2,1)S(1)}, bf16[1,6,96,384]{3,2,1,0:T(8,128)(2,1)S(1)}, u32[]{:S(2)}, u32[]{:S(2)}) %collective-permute-start.1) | collective-permute-done | bytes 442400 | tf_op jit(solution)/shard_map/ppermute | solution.py:740
  28.9 0.9 place_own.2
  30.9 1.5 collective-permute-start.10
  32.4 10.5 %collective-permute-done.10.own = bf16[1,6,96,384]{3,2,1,0:T(8,128)(2,1)S(1)} collective-permute-done((bf16[1,6,96,384]{3,2,1,0:T(8,128)(2,1)S(1)}, bf16[1,6,96,384]{3,2,1,0:T(8,128)(2,1)S(1)}, u32[]{:S(2)}, u32[]{:S(2)}) %collective-permute-start.10) | collective-permute-done | bytes 442400 | tf_op jit(solution)/shard_map/ppermute | solution.py:748
  42.9 1.6 collective-permute-start.12
  44.5 1.5 collective-permute-start.11
  46.0 6.4 %collective-permute-done.7.by_y = bf16[2,6,96,384]{3,2,1,0:T(8,128)(2,1)S(1)} collective-permute-done((bf16[2,6,96,384]{3,2,1,0:T(8,128)(2,1)S(1)}, bf16[2,6,96,384]{3,2,1,0:T(8,128)(2,1)S(1)}, u32[]{:S(2)}, u32[]{:S(2)}) %collective-permute-start.7) | collective-permute-done | bytes 884768 | tf_op jit(solution)/shard_map/ppermute | solution.py:730
  53.0 1.6 collective-permute-start.8
  55.1 6.7 %collective-permute-done.12.by_y = bf16[1,6,96,384]{3,2,1,0:T(8,128)(2,1)S(1)} collective-permute-done((bf16[1,6,96,384]{3,2,1,0:T(8,128)(2,1)S(1)}, bf16[1,6,96,384]{3,2,1,0:T(8,128)(2,1)S(1)}, u32[]{:S(2)}, u32[]{:S(2)}) %collective-permute-start.12) | collective-permute-done | bytes 442400 | tf_op jit(solution)/shard_map/ppermute | solution.py:730
  62.4 8.5 %collective-permute-done.8.across_one = bf16[2,3,96,384]{3,2,1,0:T(8,128)(2,1)S(1)} collective-permute-done((bf16[2,3,96,384]{3,2,1,0:T(8,128)(2,1)S(1)}, bf16[2,3,96,384]{3,2,1,0:T(8,128)(2,1)S(1)}, u32[]{:S(2)}, u32[]{:S(2)}) %collective-permute-start.8) | collective-permute-done | bytes 442400 | tf_op jit(solution)/shard_map/ppermute | solution.py:734
  71.2 1.2 place_own.3
  72.4 0.8 place_most.1
  73.8 1.6 collective-permute-start.14
  75.9 0.7 place_other.2._
  76.6 4.6 %collective-permute-done.14.one = bf16[1,3,96,384]{3,2,1,0:T(8,128)(2,1)S(1)} collective-permute-done((bf16[1,3,96,384]{3,2,1,0:T(8,128)(2,1)S(1)}, bf16[1,3,96,384]{3,2,1,0:T(8,128)(2,1)S(1)}, u32[]{:S(2)}, u32[]{:S(2)}) %collective-permute-start.14) | collective-permute-done | bytes 221216 | tf_op jit(solution)/shard_map/ppermute | solution.py:734
  81.2 1.2 collective-permute-done.15.two
  83.0 0.8 place_other.3._
  84.3 0.7 place_last.1
  85.0 9.3 %attention_forward.1 = (bf16[6,768,384]{2,1,0:T(8,128)(2,1)S(1)}, bf16[768,768]{1,0:T(8,128)(2,1)S(1)}, f32[768,768]{1,0:T(8,128)S(1)}, bf16[768,768]{1,0:T(8,128)(2,1)S(1)}, f32[48,768]{1,0:T(8,128)S(1)}) custom-call(bf16[768,768]{1,0:T(8,128)(2,1)S(1)} %copy-done, f32[2,768]{1,0:T(2,128)S(1)} %copy-done.10, ...), custom_call_target="tpu_custom_call" | custom-call | flops 1 | bytes 1 | tf_op jit(solution)/shard_map/attention_forward/pallas_call | solution.py:406
  94.3 25.0 %mlp_both.1 = (f32[4,768,128]{2,1,0:T(8,128)S(1)}, f32[768,768]{1,0:T(8,128)S(1)}, bf16[2,2,2,6,96,384]{5,4,3,2,1,0:T(8,128)(2,1)S(1)}, bf16[2,2,2,6,96,384]{5,4...) custom-call(s32[4]{0:T(128)S(1)} %pad_add_fusion.coords, ...), custom_call_target="tpu_custom_call" | custom-call | flops 1 | bytes 1 | tf_op jit(solution)/shard_map/mlp_both/pallas_call | solution.py:406
  119.6 5.0 %output_backward.1 = (f32[768,768]{1,0:T(8,128)S(1)}, f32[1,768]{1,0:T(1,128)S(1)}, bf16[768,768]{1,0:T(8,128)(2,1)S(1)}, bf16[2,2,2,6,96,384]{5,4,3,2,1,0:T(8,128)(2,1)S(1)}, bf16[2,2,2,6,96,384]{5,4,3,2,1,0:T(8,128)(2,1)S(1)}) custom-call(s32[4]{0:T(128)S(1)} %pad_add_fusion.coords, ...), custom_call_target="tpu_custom_call", output_to_operand_aliasing={{3}: (8, {}), {4}: (9, {})} | custom-call | flops 1 | bytes 1 | tf_op jit(solution)/shard_map/output_backward/pallas_call | solution.py:406
  124.6 1.0 collective-permute-done.20.arrived
  125.6 1.3 split_sum.2
  127.9 9.9 %attention_backward.1 = (bf16[6,768,384]{2,1,0:T(8,128)(2,1)S(1)}, bf16[2,2,2,6,96,384]{5,4,3,2,1,0:T(8,128)(2,1)S(1)}, bf16[2,2,2,6,96,384]{5,4,3,2,1,0:T(8,128)(2,1)S(1)}) custom-call(s32[4]{0:T(128)S(1)} %pad_add_fusion.coords, f32[6,16,128]{2,1,0:T(8,128)S(1)} %get-tuple-element.158.mask, ...), custom_call_target="tpu_custom_call", output_to_operand_aliasing={{1}: (5, {}), {2}: (6, {})} | custom-call | flops 1 | bytes 1 | tf_op jit(solution)/shard_map/attention_backward/pallas_call | solution.py:406
  137.9 10.8 %collective-permute-done.21.one_in = bf16[2,2,3,96,384]{4,3,2,1,0:T(8,128)(2,1)S(1)} collective-permute-done((bf16[2,2,3,96,384]{4,3,2,1,0:T(8,128)(2,1)S(1)}, bf16[2,2,3,96,384]{4,3,2,1,0:T(8,128)(2,1)S(1)}, u32[]{:S(2)}, u32[]{:S(2)}) %collective-permute-start.21) | collective-permute-done | bytes 884768 | tf_op jit(solution)/shard_map/ppermute | solution.py:942
  149.0 0.8 split_again.2
  150.3 1.6 collective-permute-start.24
  151.9 3.3 %collective-permute-done.26.arrived = bf16[2,2,2,6,96,384]{5,4,3,2,1,0:T(8,128)(2,1)S(1)} collective-permute-done((bf16[2,2,2,6,96,384]{5,4,3,2,1,0:T(8,128)(2,1)S(1)}, bf16[2,2,2,6,96,384]{5,4,3,2,1,0:T(8,128)(2,1)S(1)}, u32[]{:S(2)}, u32[]{:S(2)}) %collective-permute-start.26) | collective-permute-done | bytes 3538976 | tf_op jit(solution)/shard_map/ppermute | solution.py:938
  155.2 1.1 split_sum.3
  156.3 1.6 collective-permute-start.27
  158.4 4.4 %collective-permute-done.23.one_in = bf16[2,3,96,384]{3,2,1,0:T(8,128)(2,1)S(1)} collective-permute-done((bf16[2,3,96,384]{3,2,1,0:T(8,128)(2,1)S(1)}, bf16[2,3,96,384]{3,2,1,0:T(8,128)(2,1)S(1)}, u32[]{:S(2)}, u32[]{:S(2)}) %collective-permute-start.23) | collective-permute-done | bytes 442400 | tf_op jit(solution)/shard_map/ppermute | solution.py:946
  163.3 0.7 join_sum.2
  164.0 1.6 collective-permute-start.25
  165.5 6.5 %input_backward.1 = (f32[768,768]{1,0:T(8,128)}, f32[2,1,768]{2,1,0:T(1,128)S(1)}) custom-call(bf16[768,768]{1,0:T(8,128)(2,1)S(1)} %copy-done, f32[2,768]{1,0:T(2,128)S(1)} %copy-done.10, bf16[6,768,384]{2,1,0:T(8,128)(2,1)S(1)} %get-tuple-element.231.grad_mixed, f32[768,768]{1,0:T(8,128)S(1)} %get-tuple-element.232.grad_after, ...), custom_call_target="tpu_custom_call" | custom-call | flops 1 | bytes 1 | tf_op jit(solution)/shard_map/input_backward/pallas_call | solution.py:406
  172.0 1.5 collective-permute-start.29
  173.6 2.1 pool_out.1
  175.7 6.0 %collective-permute-done.29.right = f32[2,1,768]{2,1,0:T(1,128)S(1)} collective-permute-done((f32[2,1,768]{2,1,0:T(1,128)S(1)}, f32[2,1,768]{2,1,0:T(1,128)S(1)}, u32[]{:S(2)}, u32[]{:S(2)}) %collective-permute-start.29) | collective-permute-done | bytes 6176 | tf_op jit(solution)/shard_map/ppermute | solution.py:1093
  181.7 0.9 split_again.3
  182.7 1.6 collective-permute-start.30
  184.3 1.5 collective-permute-start.31
  185.8 1.2 collective-permute-done.32.right
  187.0 7.2 %collective-permute-done.30.one_in = bf16[2,3,96,384]{3,2,1,0:T(8,128)(2,1)S(1)} collective-permute-done((bf16[2,3,96,384]{3,2,1,0:T(8,128)(2,1)S(1)}, bf16[2,3,96,384]{3,2,1,0:T(8,128)(2,1)S(1)}, u32[]{:S(2)}, u32[]{:S(2)}) %collective-permute-start.30) | collective-permute-done | bytes 442400 | tf_op jit(solution)/shard_map/ppermute | solution.py:946
  194.2 1.3 collective-permute-done.31.two_in
  196.2 1.5 collective-permute-start.33
  198.2 3.1 %collective-permute-done.34.right = f32[2,1,768]{2,1,0:T(1,128)S(1)} collective-permute-done((f32[2,1,768]{2,1,0:T(1,128)S(1)}, f32[2,1,768]{2,1,0:T(1,128)S(1)}, u32[]{:S(2)}, u32[]{:S(2)}) %collective-permute-start.34) | collective-permute-done | bytes 6176 | tf_op jit(solution)/shard_map/ppermute | solution.py:1108
  201.3 5.2 %collective-permute-done.33.low_in = bf16[6,96,384]{2,1,0:T(8,128)(2,1)S(1)} collective-permute-done((bf16[6,96,384]{2,1,0:T(8,128)(2,1)S(1)}, bf16[6,96,384]{2,1,0:T(8,128)(2,1)S(1)}, u32[]{:S(2)}, u32[]{:S(2)}) %collective-permute-start.33) | collective-permute-done | bytes 442400 | tf_op jit(solution)/shard_map/ppermute | solution.py:1106
  206.5 0.7 pick_sum.1
  207.2 2.1 collective-permute-start.35
  209.3 1.7 collective-permute-start.36
  211.0 5.7 %collective-permute-done.36.right = f32[2,1,768]{2,1,0:T(1,128)S(1)} collective-permute-done((f32[2,1,768]{2,1,0:T(1,128)S(1)}, f32[2,1,768]{2,1,0:T(1,128)S(1)}, u32[]{:S(2)}, u32[]{:S(2)}) %collective-permute-start.36) | collective-permute-done | bytes 6176 | tf_op jit(solution)/shard_map/ppermute | solution.py:1114
  216.7 2.5 %collective-permute-start.37 = (f32[2,1,768]{2,1,0:T(1,128)S(1)}, f32[2,1,768]{2,1,0:T(1,128)S(1)}, u32[]{:S(2)}, u32[]{:S(2)}) collective-permute-start(f32[2,1,768]{2,1,0:T(1,128)S(1)} %sum_of.7.grads), channel_id=1, source_target_pairs={{0,16},{2,18},{4,20},{6,22},{8,24},{10,26},{12,28},{14,30},{16,0},... | collective-permute-start | bytes 18440 | tf_op jit(solution)/shard_map/ppermute | solution.py:1116
  219.2 8.1 %collective-permute-done.37.arrived = f32[2,1,768]{2,1,0:T(1,128)S(1)} collective-permute-done((f32[2,1,768]{2,1,0:T(1,128)S(1)}, f32[2,1,768]{2,1,0:T(1,128)S(1)}, u32[]{:S(2)}, u32[]{:S(2)}) %collective-permute-start.37) | collective-permute-done | bytes 6176 | tf_op jit(solution)/shard_map/ppermute | solution.py:1116
  227.9 4.4 %update.1 = (f32[24,96,96]{2,1,0:T(8,128)}, f32[24,96,96]{2,1,0:T(8,128)}, f32[24,96,96]{2,1,0:T(8,128)}, f32[24,96,96]{2,1,0:T(8,128)}, bf16[24,96,96]{2,1,0:T(8,128)(2,1)}) custom-call(bf16[6,96,384]{2,1,0:T(8,128)(2,1)S(1)} %get-tuple-element.265.mine, bf16[6,96,384]{2,1,0:T(8,128)(2,1)S(1)} %collective-permute-done.35.arrived, ...), custom_call_target="tpu_custom_call" | custom-call | flops 1 | bytes 1 | tf_op jit(solution)/shard_map/update/pallas_call | solution.py:406
  (69 shorter events, 11.7 us)
Async XLA Ops:
  0.6 11.1 %copy-start = (bf16[768,768]{1,0:T(8,128)(2,1)S(1)}, bf16[768,768]{1,0:T(8,128)(2,1)}, u32[]{:S(2)}) copy-start(bf16[768,768]{1,0:T(8,128)(2,1)} %tok.5) | copy-start | bytes 3538948
  0.8 1.3 copy-start.1
  2.3 13.2 %collective-permute-start.3 = (bf16[1,6,96,384]{3,2,1,0:T(8,128)(2,1)S(1)}, bf16[1,6,96,384]{3,2,1,0:T(8,128)(2,1)S(1)}, u32[]{:S(2)}, u32[]{:S(2)}) collective-permute-start(bf16[1,6,96,384]{3,2,1,0:T(8,128)(2,1)S(1)} %pack.1.own), channel_id=1, source_target_pairs={{0,1},{1,0},{2,3},{3,2},{4,5},{5,4},{6,7},{7,6},{8,9},{9,8},{10,11... | collective-permute-start | bytes 1327112 | tf_op jit(solution)/shard_map/ppermute | solution.py:730
  5.3 11.6 %collective-permute-start.2 = (bf16[1,6,96,384]{3,2,1,0:T(8,128)(2,1)S(1)}, bf16[1,6,96,384]{3,2,1,0:T(8,128)(2,1)S(1)}, u32[]{:S(2)}, u32[]{:S(2)}) collective-permute-start(bf16[1,6,96,384]{3,2,1,0:T(8,128)(2,1)S(1)} %pack.1.own), channel_id=1, source_target_pairs={{0,4},{2,6},{4,0},{6,2},{8,12},{10,14},{12,8},{14,10},{16,20},{18,... | collective-permute-start | bytes 1327112 | tf_op jit(solution)/shard_map/ppermute | solution.py:730
  6.8 21.8 %collective-permute-start.1 = (bf16[1,6,96,384]{3,2,1,0:T(8,128)(2,1)S(1)}, bf16[1,6,96,384]{3,2,1,0:T(8,128)(2,1)S(1)}, u32[]{:S(2)}, u32[]{:S(2)}) collective-permute-start(bf16[1,6,96,384]{3,2,1,0:T(8,128)(2,1)S(1)} %pack.1.own), channel_id=1, source_target_pairs={{0,16},{2,18},{4,20},{6,22},{8,24},{10,26},{12,28},{14,30},{16,0},... | collective-permute-start | bytes 1327112 | tf_op jit(solution)/shard_map/ppermute | solution.py:740
  9.4 19.4 %collective-permute-start = (bf16[1,6,96,384]{3,2,1,0:T(8,128)(2,1)S(1)}, bf16[1,6,96,384]{3,2,1,0:T(8,128)(2,1)S(1)}, u32[]{:S(2)}, u32[]{:S(2)}) collective-permute-start(bf16[1,6,96,384]{3,2,1,0:T(8,128)(2,1)S(1)} %pack.1.own), channel_id=1, source_target_pairs={{0,8},{2,10},{4,12},{6,14},{8,0},{10,2},{12,4},{14,6},{16,24},{18,... | collective-permute-start | bytes 1327112 | tf_op jit(solution)/shard_map/ppermute | solution.py:739
  11.8 0.9 copy-start.7
  12.7 0.7 copy-start.9
  17.0 11.8 %collective-permute-start.4 = (bf16[1,3,96,384]{3,2,1,0:T(8,128)(2,1)S(1)}, bf16[1,3,96,384]{3,2,1,0:T(8,128)(2,1)S(1)}, u32[]{:S(2)}, u32[]{:S(2)}) collective-permute-start(bf16[1,3,96,384]{3,2,1,0:T(8,128)(2,1)S(1)} %get-tuple-element.150), channel_id=1, source_target_pairs={{0,1},{1,0},{2,3},{3,2},{4,5},{5,4},{6,7},{7,6},{8,9},{9,8},{10,11... | collective-permute-start | bytes 663560 | tf_op jit(solution)/shard_map/ppermute | solution.py:734
  17.4 11.4 %collective-permute-start.5 = (bf16[1,3,96,384]{3,2,1,0:T(8,128)(2,1)S(1)}, bf16[1,3,96,384]{3,2,1,0:T(8,128)(2,1)S(1)}, u32[]{:S(2)}, u32[]{:S(2)}) collective-permute-start(bf16[1,3,96,384]{3,2,1,0:T(8,128)(2,1)S(1)} %get-tuple-element.151), channel_id=1, source_target_pairs={{0,4},{2,6},{4,0},{6,2},{8,12},{10,14},{12,8},{14,10},{16,20},{18,... | collective-permute-start | bytes 663560 | tf_op jit(solution)/shard_map/ppermute | solution.py:734
  29.7 41.5 %collective-permute-start.13 = (bf16[1,2,2,6,96,384]{5,4,3,2,1,0:T(8,128)(2,1)S(1)}, bf16[1,2,2,6,96,384]{5,4,3,2,1,0:T(8,128)(2,1)S(1)}, u32[]{:S(2)}, u32[]{:S(2)}) collective-permute-start(bf16[1,2,2,6,96,384]{5,4,3,2,1,0:T(8,128)(2,1)S(1)} %get-tuple-element.169), channel_id=1, source_target_pairs={{0,2},{2,0},{4,6},{6,4},{8,10},{10,8},{12,14},{14,12},{16,18},{18,... | collective-permute-start | bytes 5308424 | tf_op jit(solution)/shard_map/ppermute | solution.py:938
  29.9 22.5 %collective-permute-start.7 = (bf16[2,6,96,384]{3,2,1,0:T(8,128)(2,1)S(1)}, bf16[2,6,96,384]{3,2,1,0:T(8,128)(2,1)S(1)}, u32[]{:S(2)}, u32[]{:S(2)}) collective-permute-start(bf16[2,6,96,384]{3,2,1,0:T(8,128)(2,1)S(1)} %take_both.1.own), channel_id=1, source_target_pairs={{0,1},{1,0},{2,3},{3,2},{4,5},{5,4},{6,7},{7,6},{8,9},{9,8},{10,11... | collective-permute-start | bytes 2654216 | tf_op jit(solution)/shard_map/ppermute | solution.py:730
  30.5 22.5 %collective-permute-start.6 = (bf16[2,6,96,384]{3,2,1,0:T(8,128)(2,1)S(1)}, bf16[2,6,96,384]{3,2,1,0:T(8,128)(2,1)S(1)}, u32[]{:S(2)}, u32[]{:S(2)}) collective-permute-start(bf16[2,6,96,384]{3,2,1,0:T(8,128)(2,1)S(1)} %take_both.1.own), channel_id=1, source_target_pairs={{0,4},{2,6},{4,0},{6,2},{8,12},{10,14},{12,8},{14,10},{16,20},{18,... | collective-permute-start | bytes 2654216 | tf_op jit(solution)/shard_map/ppermute | solution.py:730
  30.9 12.0 %collective-permute-start.10 = (bf16[1,6,96,384]{3,2,1,0:T(8,128)(2,1)S(1)}, bf16[1,6,96,384]{3,2,1,0:T(8,128)(2,1)S(1)}, u32[]{:S(2)}, u32[]{:S(2)}) collective-permute-start(bf16[1,6,96,384]{3,2,1,0:T(8,128)(2,1)S(1)} %collective-permute-done.1.two), channel_id=1, source_target_pairs={{0,8},{2,10},{4,12},{6,14},{8,0},{10,2},{12,4},{14,6},{16,24},{18,... | collective-permute-start | bytes 1327112 | tf_op jit(solution)/shard_map/ppermute | solution.py:748
  42.9 18.9 %collective-permute-start.12 = (bf16[1,6,96,384]{3,2,1,0:T(8,128)(2,1)S(1)}, bf16[1,6,96,384]{3,2,1,0:T(8,128)(2,1)S(1)}, u32[]{:S(2)}, u32[]{:S(2)}) collective-permute-start(bf16[1,6,96,384]{3,2,1,0:T(8,128)(2,1)S(1)} %collective-permute-done.10.own), channel_id=1, source_target_pairs={{0,1},{1,0},{2,3},{3,2},{4,5},{5,4},{6,7},{7,6},{8,9},{9,8},{10,11... | collective-permute-start | bytes 1327112 | tf_op jit(solution)/shard_map/ppermute | solution.py:730
  44.5 17.9 %collective-permute-start.11 = (bf16[1,6,96,384]{3,2,1,0:T(8,128)(2,1)S(1)}, bf16[1,6,96,384]{3,2,1,0:T(8,128)(2,1)S(1)}, u32[]{:S(2)}, u32[]{:S(2)}) collective-permute-start(bf16[1,6,96,384]{3,2,1,0:T(8,128)(2,1)S(1)} %collective-permute-done.10.own), channel_id=1, source_target_pairs={{0,4},{2,6},{4,0},{6,2},{8,12},{10,14},{12,8},{14,10},{16,20},{18,... | collective-permute-start | bytes 1327112 | tf_op jit(solution)/shard_map/ppermute | solution.py:730
  53.0 17.9 %collective-permute-start.8 = (bf16[2,3,96,384]{3,2,1,0:T(8,128)(2,1)S(1)}, bf16[2,3,96,384]{3,2,1,0:T(8,128)(2,1)S(1)}, u32[]{:S(2)}, u32[]{:S(2)}) collective-permute-start(bf16[2,3,96,384]{3,2,1,0:T(8,128)(2,1)S(1)} %get-tuple-element.162), channel_id=1, source_target_pairs={{0,1},{1,0},{2,3},{3,2},{4,5},{5,4},{6,7},{7,6},{8,9},{9,8},{10,11... | collective-permute-start | bytes 1327112 | tf_op jit(solution)/shard_map/ppermute | solution.py:734
  54.6 16.6 %collective-permute-start.9 = (bf16[2,3,96,384]{3,2,1,0:T(8,128)(2,1)S(1)}, bf16[2,3,96,384]{3,2,1,0:T(8,128)(2,1)S(1)}, u32[]{:S(2)}, u32[]{:S(2)}) collective-permute-start(bf16[2,3,96,384]{3,2,1,0:T(8,128)(2,1)S(1)} %get-tuple-element.163), channel_id=1, source_target_pairs={{0,4},{2,6},{4,0},{6,2},{8,12},{10,14},{12,8},{14,10},{16,20},{18,... | collective-permute-start | bytes 1327112 | tf_op jit(solution)/shard_map/ppermute | solution.py:734
  72.3 10.1 %collective-permute-start.16 = (bf16[2,2,2,6,96,384]{5,4,3,2,1,0:T(8,128)(2,1)S(1)}, bf16[2,2,2,6,96,384]{5,4,3,2,1,0:T(8,128)(2,1)S(1)}, u32[]{:S(2)}, u32[]{:S(2)}) collective-permute-start(bf16[2,2,2,6,96,384]{5,4,3,2,1,0:T(8,128)(2,1)S(1)} %get-tuple-element.178), channel_id=1, source_target_pairs={{0,2},{2,0},{4,6},{6,4},{8,10},{10,8},{12,14},{14,12},{16,18},{18,... | collective-permute-start | bytes 10616840 | tf_op jit(solution)/shard_map/ppermute | solution.py:938
  73.2 9.3 %collective-permute-start.17 = (bf16[3,6,96,384]{3,2,1,0:T(8,128)(2,1)S(1)}, bf16[3,6,96,384]{3,2,1,0:T(8,128)(2,1)S(1)}, u32[]{:S(2)}, u32[]{:S(2)}) collective-permute-start(bf16[3,6,96,384]{3,2,1,0:T(8,128)(2,1)S(1)} %get-tuple-element.180), channel_id=1, source_target_pairs={{0,2},{2,0},{4,6},{6,4},{8,10},{10,8},{12,14},{14,12},{16,18},{18,... | collective-permute-start | bytes 3981320 | tf_op jit(solution)/shard_map/ppermute | solution.py:938
  73.8 7.4 %collective-permute-start.14 = (bf16[1,3,96,384]{3,2,1,0:T(8,128)(2,1)S(1)}, bf16[1,3,96,384]{3,2,1,0:T(8,128)(2,1)S(1)}, u32[]{:S(2)}, u32[]{:S(2)}) collective-permute-start(bf16[1,3,96,384]{3,2,1,0:T(8,128)(2,1)S(1)} %get-tuple-element.173), channel_id=1, source_target_pairs={{0,1},{1,0},{2,3},{3,2},{4,5},{5,4},{6,7},{7,6},{8,9},{9,8},{10,11... | collective-permute-start | bytes 663560 | tf_op jit(solution)/shard_map/ppermute | solution.py:734
  75.4 7.1 %collective-permute-start.15 = (bf16[1,3,96,384]{3,2,1,0:T(8,128)(2,1)S(1)}, bf16[1,3,96,384]{3,2,1,0:T(8,128)(2,1)S(1)}, u32[]{:S(2)}, u32[]{:S(2)}) collective-permute-start(bf16[1,3,96,384]{3,2,1,0:T(8,128)(2,1)S(1)} %get-tuple-element.174), channel_id=1, source_target_pairs={{0,4},{2,6},{4,0},{6,2},{8,12},{10,14},{12,8},{14,10},{16,20},{18,... | collective-permute-start | bytes 663560 | tf_op jit(solution)/shard_map/ppermute | solution.py:734
  82.5 1.5 collective-permute-start.18
  82.5 1.8 collective-permute-start.19
  83.8 1.2 copy-start.10
  94.3 25.3 %copy-start.8 = (bf16[48,768]{1,0:T(8,128)(2,1)S(1)}, bf16[48,768]{1,0:T(8,128)(2,1)}, u32[]{:S(2)}) copy-start(bf16[48,768]{1,0:T(8,128)(2,1)} %cot.3) | copy-start | bytes 221188
  119.3 6.3 %collective-permute-start.20 = (bf16[2,2,2,6,96,384]{5,4,3,2,1,0:T(8,128)(2,1)S(1)}, bf16[2,2,2,6,96,384]{5,4,3,2,1,0:T(8,128)(2,1)S(1)}, u32[]{:S(2)}, u32[]{:S(2)}) collective-permute-start(bf16[2,2,2,6,96,384]{5,4,3,2,1,0:T(8,128)(2,1)S(1)} %get-tuple-element.194), channel_id=1, source_target_pairs={{0,2},{2,0},{4,6},{6,4},{8,10},{10,8},{12,14},{14,12},{16,18},{18,... | collective-permute-start | bytes 10616840 | tf_op jit(solution)/shard_map/ppermute | solution.py:938
  126.9 21.8 %collective-permute-start.21 = (bf16[2,2,3,96,384]{4,3,2,1,0:T(8,128)(2,1)S(1)}, bf16[2,2,3,96,384]{4,3,2,1,0:T(8,128)(2,1)S(1)}, u32[]{:S(2)}, u32[]{:S(2)}) collective-permute-start(bf16[2,2,3,96,384]{4,3,2,1,0:T(8,128)(2,1)S(1)} %get-tuple-element.211), channel_id=1, source_target_pairs={{0,1},{1,0},{2,3},{3,2},{4,5},{5,4},{6,7},{7,6},{8,9},{9,8},{10,11... | collective-permute-start | bytes 2654216 | tf_op jit(solution)/shard_map/ppermute | solution.py:942
  127.5 21.5 %collective-permute-start.22 = (bf16[2,2,3,96,384]{4,3,2,1,0:T(8,128)(2,1)S(1)}, bf16[2,2,3,96,384]{4,3,2,1,0:T(8,128)(2,1)S(1)}, u32[]{:S(2)}, u32[]{:S(2)}) collective-permute-start(bf16[2,2,3,96,384]{4,3,2,1,0:T(8,128)(2,1)S(1)} %get-tuple-element.212), channel_id=1, source_target_pairs={{0,4},{2,6},{4,0},{6,2},{8,12},{10,14},{12,8},{14,10},{16,20},{18,... | collective-permute-start | bytes 2654216 | tf_op jit(solution)/shard_map/ppermute | solution.py:942
  149.0 6.2 %collective-permute-start.26 = (bf16[2,2,2,6,96,384]{5,4,3,2,1,0:T(8,128)(2,1)S(1)}, bf16[2,2,2,6,96,384]{5,4,3,2,1,0:T(8,128)(2,1)S(1)}, u32[]{:S(2)}, u32[]{:S(2)}) collective-permute-start(bf16[2,2,2,6,96,384]{5,4,3,2,1,0:T(8,128)(2,1)S(1)} %get-tuple-element.228), channel_id=1, source_target_pairs={{0,2},{2,0},{4,6},{6,4},{8,10},{10,8},{12,14},{14,12},{16,18},{18,... | collective-permute-start | bytes 10616840 | tf_op jit(solution)/shard_map/ppermute | solution.py:938
  149.8 13.0 %collective-permute-start.23 = (bf16[2,3,96,384]{3,2,1,0:T(8,128)(2,1)S(1)}, bf16[2,3,96,384]{3,2,1,0:T(8,128)(2,1)S(1)}, u32[]{:S(2)}, u32[]{:S(2)}) collective-permute-start(bf16[2,3,96,384]{3,2,1,0:T(8,128)(2,1)S(1)} %get-tuple-element.224), channel_id=1, source_target_pairs={{0,4},{2,6},{4,0},{6,2},{8,12},{10,14},{12,8},{14,10},{16,20},{18,... | collective-permute-start | bytes 1327112 | tf_op jit(solution)/shard_map/ppermute | solution.py:946
  150.3 13.0 %collective-permute-start.24 = (bf16[2,3,96,384]{3,2,1,0:T(8,128)(2,1)S(1)}, bf16[2,3,96,384]{3,2,1,0:T(8,128)(2,1)S(1)}, u32[]{:S(2)}, u32[]{:S(2)}) collective-permute-start(bf16[2,3,96,384]{3,2,1,0:T(8,128)(2,1)S(1)} %get-tuple-element.225), channel_id=1, source_target_pairs={{0,1},{1,0},{2,3},{3,2},{4,5},{5,4},{6,7},{7,6},{8,9},{9,8},{10,11... | collective-permute-start | bytes 1327112 | tf_op jit(solution)/shard_map/ppermute | solution.py:946
  156.3 25.5 %collective-permute-start.27 = (bf16[2,2,3,96,384]{4,3,2,1,0:T(8,128)(2,1)S(1)}, bf16[2,2,3,96,384]{4,3,2,1,0:T(8,128)(2,1)S(1)}, u32[]{:S(2)}, u32[]{:S(2)}) collective-permute-start(bf16[2,2,3,96,384]{4,3,2,1,0:T(8,128)(2,1)S(1)} %get-tuple-element.229), channel_id=1, source_target_pairs={{0,1},{1,0},{2,3},{3,2},{4,5},{5,4},{6,7},{7,6},{8,9},{9,8},{10,11... | collective-permute-start | bytes 2654216 | tf_op jit(solution)/shard_map/ppermute | solution.py:942
  157.8 23.9 %collective-permute-start.28 = (bf16[2,2,3,96,384]{4,3,2,1,0:T(8,128)(2,1)S(1)}, bf16[2,2,3,96,384]{4,3,2,1,0:T(8,128)(2,1)S(1)}, u32[]{:S(2)}, u32[]{:S(2)}) collective-permute-start(bf16[2,2,3,96,384]{4,3,2,1,0:T(8,128)(2,1)S(1)} %get-tuple-element.230), channel_id=1, source_target_pairs={{0,4},{2,6},{4,0},{6,2},{8,12},{10,14},{12,8},{14,10},{16,20},{18,... | collective-permute-start | bytes 2654216 | tf_op jit(solution)/shard_map/ppermute | solution.py:942
  164.0 17.7 %collective-permute-start.25 = (bf16[6,96,384]{2,1,0:T(8,128)(2,1)S(1)}, bf16[6,96,384]{2,1,0:T(8,128)(2,1)S(1)}, u32[]{:S(2)}, u32[]{:S(2)}) collective-permute-start(bf16[6,96,384]{2,1,0:T(8,128)(2,1)S(1)} %get-tuple-element.226), channel_id=1, source_target_pairs={{0,8},{2,10},{4,12},{6,14},{8,0},{10,2},{12,4},{14,6},{16,24},{18,... | collective-permute-start | bytes 1327112 | tf_op jit(solution)/shard_map/ppermute | solution.py:1096
  172.0 9.7 %collective-permute-start.29 = (f32[2,1,768]{2,1,0:T(1,128)S(1)}, f32[2,1,768]{2,1,0:T(1,128)S(1)}, u32[]{:S(2)}, u32[]{:S(2)}) collective-permute-start(f32[2,1,768]{2,1,0:T(1,128)S(1)} %get-tuple-element.234.left), channel_id=1, source_target_pairs={{0,1},{1,0},{2,3},{3,2},{4,5},{5,4},{6,7},{7,6},{8,9},{9,8},{10,11... | collective-permute-start | bytes 18440 | tf_op jit(solution)/shard_map/ppermute | solution.py:1093
  181.7 46.2 %copy-start.5 = (f32[24,96,96]{2,1,0:T(8,128)S(1)}, f32[24,96,96]{2,1,0:T(8,128)}, u32[]{:S(2)}) copy-start(f32[24,96,96]{2,1,0:T(8,128)} %root_left.1) | copy-start | bytes 2654212
  181.7 46.2 %copy-start.6 = (f32[24,96,96]{2,1,0:T(8,128)S(1)}, f32[24,96,96]{2,1,0:T(8,128)}, u32[]{:S(2)}) copy-start(f32[24,96,96]{2,1,0:T(8,128)} %root_right.1) | copy-start | bytes 2654212
  182.6 44.6 %copy-start.11 = (f32[2,768]{1,0:T(2,128)S(1)}, f32[2,768]{1,0:T(2,128)}, u32[]{:S(2)}) copy-start(f32[2,768]{1,0:T(2,128)} %moments.1) | copy-start | bytes 18436
  182.6 45.3 %copy-start.2 = (f32[24,96,96]{2,1,0:T(8,128)S(1)}, f32[24,96,96]{2,1,0:T(8,128)}, u32[]{:S(2)}) copy-start(f32[24,96,96]{2,1,0:T(8,128)} %master.1) | copy-start | bytes 2654212
  182.7 45.3 %copy-start.3 = (f32[24,96,96]{2,1,0:T(8,128)S(1)}, f32[24,96,96]{2,1,0:T(8,128)}, u32[]{:S(2)}) copy-start(f32[24,96,96]{2,1,0:T(8,128)} %stat_left.1) | copy-start | bytes 2654212
  182.7 45.3 %copy-start.4 = (f32[24,96,96]{2,1,0:T(8,128)S(1)}, f32[24,96,96]{2,1,0:T(8,128)}, u32[]{:S(2)}) copy-start(f32[24,96,96]{2,1,0:T(8,128)} %stat_right.1) | copy-start | bytes 2654212
  182.7 11.5 %collective-permute-start.30 = (bf16[2,3,96,384]{3,2,1,0:T(8,128)(2,1)S(1)}, bf16[2,3,96,384]{3,2,1,0:T(8,128)(2,1)S(1)}, u32[]{:S(2)}, u32[]{:S(2)}) collective-permute-start(bf16[2,3,96,384]{3,2,1,0:T(8,128)(2,1)S(1)} %get-tuple-element.248), channel_id=1, source_target_pairs={{0,4},{2,6},{4,0},{6,2},{8,12},{10,14},{12,8},{14,10},{16,20},{18,... | collective-permute-start | bytes 1327112 | tf_op jit(solution)/shard_map/ppermute | solution.py:946
  184.3 11.2 %collective-permute-start.31 = (bf16[2,3,96,384]{3,2,1,0:T(8,128)(2,1)S(1)}, bf16[2,3,96,384]{3,2,1,0:T(8,128)(2,1)S(1)}, u32[]{:S(2)}, u32[]{:S(2)}) collective-permute-start(bf16[2,3,96,384]{3,2,1,0:T(8,128)(2,1)S(1)} %get-tuple-element.249), channel_id=1, source_target_pairs={{0,1},{1,0},{2,3},{3,2},{4,5},{5,4},{6,7},{7,6},{8,9},{9,8},{10,11... | collective-permute-start | bytes 1327112 | tf_op jit(solution)/shard_map/ppermute | solution.py:946
  185.8 1.2 collective-permute-start.32
  196.2 10.3 %collective-permute-start.33 = (bf16[6,96,384]{2,1,0:T(8,128)(2,1)S(1)}, bf16[6,96,384]{2,1,0:T(8,128)(2,1)S(1)}, u32[]{:S(2)}, u32[]{:S(2)}) collective-permute-start(bf16[6,96,384]{2,1,0:T(8,128)(2,1)S(1)} %get-tuple-element.254), channel_id=1, source_target_pairs={{0,8},{2,10},{4,12},{6,14},{8,0},{10,2},{12,4},{14,6},{16,24},{18,... | collective-permute-start | bytes 1327112 | tf_op jit(solution)/shard_map/ppermute | solution.py:1106
  197.7 3.6 %collective-permute-start.34 = (f32[2,1,768]{2,1,0:T(1,128)S(1)}, f32[2,1,768]{2,1,0:T(1,128)S(1)}, u32[]{:S(2)}, u32[]{:S(2)}) collective-permute-start(f32[2,1,768]{2,1,0:T(1,128)S(1)} %sum_of.5.left), channel_id=1, source_target_pairs={{0,4},{2,6},{4,0},{6,2},{8,12},{10,14},{12,8},{14,10},{16,20},{18,... | collective-permute-start | bytes 18440 | tf_op jit(solution)/shard_map/ppermute | solution.py:1108
  207.2 20.7 %collective-permute-start.35 = (bf16[6,96,384]{2,1,0:T(8,128)(2,1)S(1)}, bf16[6,96,384]{2,1,0:T(8,128)(2,1)S(1)}, u32[]{:S(2)}, u32[]{:S(2)}) collective-permute-start(bf16[6,96,384]{2,1,0:T(8,128)(2,1)S(1)} %get-tuple-element.257), channel_id=1, source_target_pairs={{0,16},{2,18},{4,20},{6,22},{8,24},{10,26},{12,28},{14,30},{16,0},... | collective-permute-start | bytes 1327112 | tf_op jit(solution)/shard_map/ppermute | solution.py:1112
  209.3 7.4 %collective-permute-start.36 = (f32[2,1,768]{2,1,0:T(1,128)S(1)}, f32[2,1,768]{2,1,0:T(1,128)S(1)}, u32[]{:S(2)}, u32[]{:S(2)}) collective-permute-start(f32[2,1,768]{2,1,0:T(1,128)S(1)} %sum_of.6.left), channel_id=1, source_target_pairs={{0,8},{2,10},{4,12},{6,14},{8,0},{10,2},{12,4},{14,6},{16,24},{18,... | collective-permute-start | bytes 18440 | tf_op jit(solution)/shard_map/ppermute | solution.py:1114
  216.7 10.6 %collective-permute-start.37 = (f32[2,1,768]{2,1,0:T(1,128)S(1)}, f32[2,1,768]{2,1,0:T(1,128)S(1)}, u32[]{:S(2)}, u32[]{:S(2)}) collective-permute-start(f32[2,1,768]{2,1,0:T(1,128)S(1)} %sum_of.7.grads), channel_id=1, source_target_pairs={{0,16},{2,18},{4,20},{6,22},{8,24},{10,26},{12,28},{14,30},{16,0},... | collective-permute-start | bytes 18440 | tf_op jit(solution)/shard_map/ppermute | solution.py:1116

commit v6 on v5

--- a/solution.py
+++ b/solution.py
@@ -1078,7 +1078,10 @@
         upper_sent, grad_att, lower = fence(upper_sent, grad_att, lower)
         upper_in = first_hop(upper_sent)
         grad_mixed, *lower = run_backward(coords, mask, normed, qkv, grad_att, lower, split)
-        upper_in, grad_mixed, lower = fence(upper_in, grad_mixed, lower)
+        input_grad, gain_grads = run_input(
+            tokens, norm_gains, grad_mixed, grad_after, gain_two, strips
+        )
+        upper_in, gain_grads, lower = fence(upper_in, gain_grads, lower)
 
         lower_in = core_hop(lower[1])
         upper_sent, upper_kept = run_again(coords, upper_kept, upper_in)
@@ -1086,9 +1089,6 @@
 
         lower_sent, lower_kept = run_split(coords, lower[0], lower_in)
         lower_in = first_hop(lower_sent)
-        input_grad, gain_grads = run_input(
-            tokens, norm_gains, grad_mixed, grad_after, gain_two, strips
-        )
 
         gain_in = lax.ppermute(gain_grads, *hops[0])
         pooled = run_pool(after_pooled, hidden_pooled, inverse, strips)

time: 233 us -> 233 us (level)
    ppermute x1, waiting for transfers between devices: 6.02 us -> 12.5 us  [body(): gain_in = lax.ppermute(gain_grads, *hops[0])]
    ppermute x2, waiting for transfers between devices: 10.8 us -> 4.36 us  [first_hop(): lax.ppermute(sent[0], 'tensor', OTHER_Y)]
where the time goes in v6:
time: 233 us; the launch traced here: 232 us
  waiting for transfers between devices  109 us (47%)
  Pallas kernels  76 us (33%)
  starting transfers between devices  42 us (18%)
  local copies, waits for them, and re-layouts  3.76 us (2%)
    pallas_call x31, Pallas kernels, call(): pl.pallas_call(kernel, grid=grid, in_specs=in_specs, out_specs=[spec for...  76 us
    ppermute x3, waiting for transfers between devices, neighbour_hop(): lax.ppermute(value, 'tensor', OTHER_Y)  13.6 us
    ppermute x3, waiting for transfers between devices, across_hop(): lax.ppermute(pieces[0], 'tensor', OTHER_Y)  13.1 us
    ppermute x1, waiting for transfers between devices, body(): gain_in = lax.ppermute(gain_grads, *hops[0])  12.5 us
    ppermute x2, waiting for transfers between devices, second_hop(): lax.ppermute(sent[0], 'dp', OTHER_X)  11.6 us
    ppermute x1, waiting for transfers between devices, gather_split(): other = lax.ppermute(far, 'dp', NEAR_Z)  10.5 us
    ppermute x1, waiting for transfers between devices, gather_split(): far = lax.ppermute(own, 'dp', FAR_Z)  9.59 us
    ppermute x1, waiting for transfers between devices, body(): gain_in = lax.ppermute(gain_grads, *hops[4])  8.05 us
  transfers between devices with their start and end apart: 38, of which 29 were waited for; matrix products, arithmetic and copies ran while one was open for 0% of the time, Pallas kernels for 13%

profile of v6, /device:TPU:0, one launch (start us, length us, event | category | flops | bytes accessed | tf_op | source)
XLA Modules:
  0.0 232.3 jit_solution(8673797528753984023)
XLA Ops:
  0.8 1.3 copy-done.1
  2.3 3.0 %collective-permute-start.3 = (bf16[1,6,96,384]{3,2,1,0:T(8,128)(2,1)S(1)}, bf16[1,6,96,384]{3,2,1,0:T(8,128)(2,1)S(1)}, u32[]{:S(2)}, u32[]{:S(2)}) collective-permute-start(bf16[1,6,96,384]{3,2,1,0:T(8,128)(2,1)S(1)} %pack.1.own), channel_id=1, source_target_pairs={{0,1},{1,0},{2,3},{3,2},{4,5},{5,4},{6,7},{7,6},{8,9},{9,8},{10,11... | collective-permute-start | bytes 1327112 | tf_op jit(solution)/shard_map/ppermute | solution.py:730
  5.3 1.5 collective-permute-start.2
  6.8 2.6 %collective-permute-start.1 = (bf16[1,6,96,384]{3,2,1,0:T(8,128)(2,1)S(1)}, bf16[1,6,96,384]{3,2,1,0:T(8,128)(2,1)S(1)}, u32[]{:S(2)}, u32[]{:S(2)}) collective-permute-start(bf16[1,6,96,384]{3,2,1,0:T(8,128)(2,1)S(1)} %pack.1.own), channel_id=1, source_target_pairs={{0,16},{2,18},{4,20},{6,22},{8,24},{10,26},{12,28},{14,30},{16,0},... | collective-permute-start | bytes 1327112 | tf_op jit(solution)/shard_map/ppermute | solution.py:740
  9.4 1.6 collective-permute-start
  11.0 0.8 copy.29.token_mask
  11.8 0.9 copy-done.7
  12.7 0.7 copy-done.9
  13.4 1.7 prepare.1
  15.5 1.5 collective-permute-done.2.by_x
  17.4 1.6 collective-permute-start.5
  19.1 9.6 %collective-permute-done.1.two = bf16[1,6,96,384]{3,2,1,0:T(8,128)(2,1)S(1)} collective-permute-done((bf16[1,6,96,384]{3,2,1,0:T(8,128)(2,1)S(1)}, bf16[1,6,96,384]{3,2,1,0:T(8,128)(2,1)S(1)}, u32[]{:S(2)}, u32[]{:S(2)}) %collective-permute-start.1) | collective-permute-done | bytes 442400 | tf_op jit(solution)/shard_map/ppermute | solution.py:740
  28.9 0.9 place_own.2
  30.9 1.5 collective-permute-start.10
  32.4 10.5 %collective-permute-done.10.own = bf16[1,6,96,384]{3,2,1,0:T(8,128)(2,1)S(1)} collective-permute-done((bf16[1,6,96,384]{3,2,1,0:T(8,128)(2,1)S(1)}, bf16[1,6,96,384]{3,2,1,0:T(8,128)(2,1)S(1)}, u32[]{:S(2)}, u32[]{:S(2)}) %collective-permute-start.10) | collective-permute-done | bytes 442400 | tf_op jit(solution)/shard_map/ppermute | solution.py:748
  42.9 1.6 collective-permute-start.12
  44.5 1.5 collective-permute-start.11
  46.0 6.4 %collective-permute-done.7.by_y = bf16[2,6,96,384]{3,2,1,0:T(8,128)(2,1)S(1)} collective-permute-done((bf16[2,6,96,384]{3,2,1,0:T(8,128)(2,1)S(1)}, bf16[2,6,96,384]{3,2,1,0:T(8,128)(2,1)S(1)}, u32[]{:S(2)}, u32[]{:S(2)}) %collective-permute-start.7) | collective-permute-done | bytes 884768 | tf_op jit(solution)/shard_map/ppermute | solution.py:730
  53.0 1.6 collective-permute-start.8
  55.1 6.7 %collective-permute-done.12.by_y = bf16[1,6,96,384]{3,2,1,0:T(8,128)(2,1)S(1)} collective-permute-done((bf16[1,6,96,384]{3,2,1,0:T(8,128)(2,1)S(1)}, bf16[1,6,96,384]{3,2,1,0:T(8,128)(2,1)S(1)}, u32[]{:S(2)}, u32[]{:S(2)}) %collective-permute-start.12) | collective-permute-done | bytes 442400 | tf_op jit(solution)/shard_map/ppermute | solution.py:730
  62.4 8.5 %collective-permute-done.8.across_one = bf16[2,3,96,384]{3,2,1,0:T(8,128)(2,1)S(1)} collective-permute-done((bf16[2,3,96,384]{3,2,1,0:T(8,128)(2,1)S(1)}, bf16[2,3,96,384]{3,2,1,0:T(8,128)(2,1)S(1)}, u32[]{:S(2)}, u32[]{:S(2)}) %collective-permute-start.8) | collective-permute-done | bytes 442400 | tf_op jit(solution)/shard_map/ppermute | solution.py:734
  71.2 1.2 place_own.3
  72.4 0.8 place_most.1
  73.8 1.6 collective-permute-start.14
  75.9 0.7 place_other.2._
  76.6 4.6 %collective-permute-done.14.one = bf16[1,3,96,384]{3,2,1,0:T(8,128)(2,1)S(1)} collective-permute-done((bf16[1,3,96,384]{3,2,1,0:T(8,128)(2,1)S(1)}, bf16[1,3,96,384]{3,2,1,0:T(8,128)(2,1)S(1)}, u32[]{:S(2)}, u32[]{:S(2)}) %collective-permute-start.14) | collective-permute-done | bytes 221216 | tf_op jit(solution)/shard_map/ppermute | solution.py:734
  81.2 1.2 collective-permute-done.15.two
  83.0 0.8 place_other.3._
  84.3 0.7 place_last.1
  85.0 9.3 %attention_forward.1 = (bf16[6,768,384]{2,1,0:T(8,128)(2,1)S(1)}, bf16[768,768]{1,0:T(8,128)(2,1)S(1)}, f32[768,768]{1,0:T(8,128)S(1)}, bf16[768,768]{1,0:T(8,128)(2,1)S(1)}, f32[48,768]{1,0:T(8,128)S(1)}) custom-call(bf16[768,768]{1,0:T(8,128)(2,1)S(1)} %copy-done, f32[2,768]{1,0:T(2,128)S(1)} %copy-done.10, ...), custom_call_target="tpu_custom_call" | custom-call | flops 1 | bytes 1 | tf_op jit(solution)/shard_map/attention_forward/pallas_call | solution.py:406
  94.3 25.0 %mlp_both.1 = (f32[4,768,128]{2,1,0:T(8,128)S(1)}, f32[768,768]{1,0:T(8,128)S(1)}, bf16[2,2,2,6,96,384]{5,4,3,2,1,0:T(8,128)(2,1)S(1)}, bf16[2,2,2,6,96,384]{5,4...) custom-call(s32[4]{0:T(128)S(1)} %pad_add_fusion.coords, ...), custom_call_target="tpu_custom_call" | custom-call | flops 1 | bytes 1 | tf_op jit(solution)/shard_map/mlp_both/pallas_call | solution.py:406
  119.6 5.0 %output_backward.1 = (f32[768,768]{1,0:T(8,128)S(1)}, f32[1,768]{1,0:T(1,128)S(1)}, bf16[768,768]{1,0:T(8,128)(2,1)S(1)}, bf16[2,2,2,6,96,384]{5,4,3,2,1,0:T(8,128)(2,1)S(1)}, bf16[2,2,2,6,96,384]{5,4,3,2,1,0:T(8,128)(2,1)S(1)}) custom-call(s32[4]{0:T(128)S(1)} %pad_add_fusion.coords, ...), custom_call_target="tpu_custom_call", output_to_operand_aliasing={{3}: (8, {}), {4}: (9, {})} | custom-call | flops 1 | bytes 1 | tf_op jit(solution)/shard_map/output_backward/pallas_call | solution.py:406
  124.6 1.0 collective-permute-done.20.arrived
  125.6 1.3 split_sum.2
  127.9 9.9 %attention_backward.1 = (bf16[6,768,384]{2,1,0:T(8,128)(2,1)S(1)}, bf16[2,2,2,6,96,384]{5,4,3,2,1,0:T(8,128)(2,1)S(1)}, bf16[2,2,2,6,96,384]{5,4,3,2,1,0:T(8,128)(2,1)S(1)}) custom-call(s32[4]{0:T(128)S(1)} %pad_add_fusion.coords, f32[6,16,128]{2,1,0:T(8,128)S(1)} %get-tuple-element.158.mask, ...), custom_call_target="tpu_custom_call", output_to_operand_aliasing={{1}: (5, {}), {2}: (6, {})} | custom-call | flops 1 | bytes 1 | tf_op jit(solution)/shard_map/attention_backward/pallas_call | solution.py:406
  137.9 6.5 %input_backward.1 = (f32[768,768]{1,0:T(8,128)}, f32[2,1,768]{2,1,0:T(1,128)S(1)}) custom-call(bf16[768,768]{1,0:T(8,128)(2,1)S(1)} %copy-done, f32[2,768]{1,0:T(2,128)S(1)} %copy-done.10, bf16[6,768,384]{2,1,0:T(8,128)(2,1)S(1)} %get-tuple-element.217.grad_mixed, f32[768,768]{1,0:T(8,128)S(1)} %get-tuple-element.218.grad_after, ...), custom_call_target="tpu_custom_call" | custom-call | flops 1 | bytes 1 | tf_op jit(solution)/shard_map/input_backward/pallas_call | solution.py:406
  144.4 4.4 %collective-permute-done.21.one_in = bf16[2,2,3,96,384]{4,3,2,1,0:T(8,128)(2,1)S(1)} collective-permute-done((bf16[2,2,3,96,384]{4,3,2,1,0:T(8,128)(2,1)S(1)}, bf16[2,2,3,96,384]{4,3,2,1,0:T(8,128)(2,1)S(1)}, u32[]{:S(2)}, u32[]{:S(2)}) %collective-permute-start.21) | collective-permute-done | bytes 884768 | tf_op jit(solution)/shard_map/ppermute | solution.py:942
  149.0 0.8 split_again.2
  150.3 1.6 collective-permute-start.24
  151.9 3.3 %collective-permute-done.26.arrived = bf16[2,2,2,6,96,384]{5,4,3,2,1,0:T(8,128)(2,1)S(1)} collective-permute-done((bf16[2,2,2,6,96,384]{5,4,3,2,1,0:T(8,128)(2,1)S(1)}, bf16[2,2,2,6,96,384]{5,4,3,2,1,0:T(8,128)(2,1)S(1)}, u32[]{:S(2)}, u32[]{:S(2)}) %collective-permute-start.26) | collective-permute-done | bytes 3538976 | tf_op jit(solution)/shard_map/ppermute | solution.py:938
  155.2 1.1 split_sum.3
  156.3 1.6 collective-permute-start.27
  158.4 4.4 %collective-permute-done.23.one_in = bf16[2,3,96,384]{3,2,1,0:T(8,128)(2,1)S(1)} collective-permute-done((bf16[2,3,96,384]{3,2,1,0:T(8,128)(2,1)S(1)}, bf16[2,3,96,384]{3,2,1,0:T(8,128)(2,1)S(1)}, u32[]{:S(2)}, u32[]{:S(2)}) %collective-permute-start.23) | collective-permute-done | bytes 442400 | tf_op jit(solution)/shard_map/ppermute | solution.py:946
  164.0 1.6 collective-permute-start.25
  165.5 1.5 collective-permute-start.29
  167.1 2.1 pool_out.1
  169.2 12.5 %collective-permute-done.29.right = f32[2,1,768]{2,1,0:T(1,128)S(1)} collective-permute-done((f32[2,1,768]{2,1,0:T(1,128)S(1)}, f32[2,1,768]{2,1,0:T(1,128)S(1)}, u32[]{:S(2)}, u32[]{:S(2)}) %collective-permute-start.29) | collective-permute-done | bytes 6176 | tf_op jit(solution)/shard_map/ppermute | solution.py:1093
  181.7 0.8 split_again.3
  182.6 1.6 collective-permute-start.30
  184.2 1.5 collective-permute-start.31
  185.7 1.2 collective-permute-done.32.right
  186.9 7.2 %collective-permute-done.30.one_in = bf16[2,3,96,384]{3,2,1,0:T(8,128)(2,1)S(1)} collective-permute-done((bf16[2,3,96,384]{3,2,1,0:T(8,128)(2,1)S(1)}, bf16[2,3,96,384]{3,2,1,0:T(8,128)(2,1)S(1)}, u32[]{:S(2)}, u32[]{:S(2)}) %collective-permute-start.30) | collective-permute-done | bytes 442400 | tf_op jit(solution)/shard_map/ppermute | solution.py:946
  194.1 1.3 collective-permute-done.31.two_in
  195.4 0.7 join_sum.3
  196.1 1.5 collective-permute-start.33
  198.2 3.1 %collective-permute-done.34.right = f32[2,1,768]{2,1,0:T(1,128)S(1)} collective-permute-done((f32[2,1,768]{2,1,0:T(1,128)S(1)}, f32[2,1,768]{2,1,0:T(1,128)S(1)}, u32[]{:S(2)}, u32[]{:S(2)}) %collective-permute-start.34) | collective-permute-done | bytes 6176 | tf_op jit(solution)/shard_map/ppermute | solution.py:1108
  201.3 5.2 %collective-permute-done.33.low_in = bf16[6,96,384]{2,1,0:T(8,128)(2,1)S(1)} collective-permute-done((bf16[6,96,384]{2,1,0:T(8,128)(2,1)S(1)}, bf16[6,96,384]{2,1,0:T(8,128)(2,1)S(1)}, u32[]{:S(2)}, u32[]{:S(2)}) %collective-permute-start.33) | collective-permute-done | bytes 442400 | tf_op jit(solution)/shard_map/ppermute | solution.py:1106
  206.5 0.7 pick_sum.1
  207.1 2.1 collective-permute-start.35
  209.2 1.7 collective-permute-start.36
  210.9 5.7 %collective-permute-done.36.right = f32[2,1,768]{2,1,0:T(1,128)S(1)} collective-permute-done((f32[2,1,768]{2,1,0:T(1,128)S(1)}, f32[2,1,768]{2,1,0:T(1,128)S(1)}, u32[]{:S(2)}, u32[]{:S(2)}) %collective-permute-start.36) | collective-permute-done | bytes 6176 | tf_op jit(solution)/shard_map/ppermute | solution.py:1114
  216.6 2.5 %collective-permute-start.37 = (f32[2,1,768]{2,1,0:T(1,128)S(1)}, f32[2,1,768]{2,1,0:T(1,128)S(1)}, u32[]{:S(2)}, u32[]{:S(2)}) collective-permute-start(f32[2,1,768]{2,1,0:T(1,128)S(1)} %sum_of.7.grads), channel_id=1, source_target_pairs={{0,16},{2,18},{4,20},{6,22},{8,24},{10,26},{12,28},{14,30},{16,0},... | collective-permute-start | bytes 18440 | tf_op jit(solution)/shard_map/ppermute | solution.py:1116
  219.1 8.1 %collective-permute-done.37.arrived = f32[2,1,768]{2,1,0:T(1,128)S(1)} collective-permute-done((f32[2,1,768]{2,1,0:T(1,128)S(1)}, f32[2,1,768]{2,1,0:T(1,128)S(1)}, u32[]{:S(2)}, u32[]{:S(2)}) %collective-permute-start.37) | collective-permute-done | bytes 6176 | tf_op jit(solution)/shard_map/ppermute | solution.py:1116
  227.9 4.4 %update.1 = (f32[24,96,96]{2,1,0:T(8,128)}, f32[24,96,96]{2,1,0:T(8,128)}, f32[24,96,96]{2,1,0:T(8,128)}, f32[24,96,96]{2,1,0:T(8,128)}, bf16[24,96,96]{2,1,0:T(8,128)(2,1)}) custom-call(bf16[6,96,384]{2,1,0:T(8,128)(2,1)S(1)} %get-tuple-element.265.mine, bf16[6,96,384]{2,1,0:T(8,128)(2,1)S(1)} %collective-permute-done.35.arrived, ...), custom_call_target="tpu_custom_call" | custom-call | flops 1 | bytes 1 | tf_op jit(solution)/shard_map/update/pallas_call | solution.py:406
  (69 shorter events, 11.7 us)
Async XLA Ops:
  0.6 11.1 %copy-start = (bf16[768,768]{1,0:T(8,128)(2,1)S(1)}, bf16[768,768]{1,0:T(8,128)(2,1)}, u32[]{:S(2)}) copy-start(bf16[768,768]{1,0:T(8,128)(2,1)} %tok.5) | copy-start | bytes 3538948
  0.8 1.3 copy-start.1
  2.3 13.2 %collective-permute-start.3 = (bf16[1,6,96,384]{3,2,1,0:T(8,128)(2,1)S(1)}, bf16[1,6,96,384]{3,2,1,0:T(8,128)(2,1)S(1)}, u32[]{:S(2)}, u32[]{:S(2)}) collective-permute-start(bf16[1,6,96,384]{3,2,1,0:T(8,128)(2,1)S(1)} %pack.1.own), channel_id=1, source_target_pairs={{0,1},{1,0},{2,3},{3,2},{4,5},{5,4},{6,7},{7,6},{8,9},{9,8},{10,11... | collective-permute-start | bytes 1327112 | tf_op jit(solution)/shard_map/ppermute | solution.py:730
  5.3 11.6 %collective-permute-start.2 = (bf16[1,6,96,384]{3,2,1,0:T(8,128)(2,1)S(1)}, bf16[1,6,96,384]{3,2,1,0:T(8,128)(2,1)S(1)}, u32[]{:S(2)}, u32[]{:S(2)}) collective-permute-start(bf16[1,6,96,384]{3,2,1,0:T(8,128)(2,1)S(1)} %pack.1.own), channel_id=1, source_target_pairs={{0,4},{2,6},{4,0},{6,2},{8,12},{10,14},{12,8},{14,10},{16,20},{18,... | collective-permute-start | bytes 1327112 | tf_op jit(solution)/shard_map/ppermute | solution.py:730
  6.8 21.8 %collective-permute-start.1 = (bf16[1,6,96,384]{3,2,1,0:T(8,128)(2,1)S(1)}, bf16[1,6,96,384]{3,2,1,0:T(8,128)(2,1)S(1)}, u32[]{:S(2)}, u32[]{:S(2)}) collective-permute-start(bf16[1,6,96,384]{3,2,1,0:T(8,128)(2,1)S(1)} %pack.1.own), channel_id=1, source_target_pairs={{0,16},{2,18},{4,20},{6,22},{8,24},{10,26},{12,28},{14,30},{16,0},... | collective-permute-start | bytes 1327112 | tf_op jit(solution)/shard_map/ppermute | solution.py:740
  9.4 19.4 %collective-permute-start = (bf16[1,6,96,384]{3,2,1,0:T(8,128)(2,1)S(1)}, bf16[1,6,96,384]{3,2,1,0:T(8,128)(2,1)S(1)}, u32[]{:S(2)}, u32[]{:S(2)}) collective-permute-start(bf16[1,6,96,384]{3,2,1,0:T(8,128)(2,1)S(1)} %pack.1.own), channel_id=1, source_target_pairs={{0,8},{2,10},{4,12},{6,14},{8,0},{10,2},{12,4},{14,6},{16,24},{18,... | collective-permute-start | bytes 1327112 | tf_op jit(solution)/shard_map/ppermute | solution.py:739
  11.8 0.9 copy-start.7
  12.7 0.7 copy-start.9
  17.0 11.8 %collective-permute-start.4 = (bf16[1,3,96,384]{3,2,1,0:T(8,128)(2,1)S(1)}, bf16[1,3,96,384]{3,2,1,0:T(8,128)(2,1)S(1)}, u32[]{:S(2)}, u32[]{:S(2)}) collective-permute-start(bf16[1,3,96,384]{3,2,1,0:T(8,128)(2,1)S(1)} %get-tuple-element.150), channel_id=1, source_target_pairs={{0,1},{1,0},{2,3},{3,2},{4,5},{5,4},{6,7},{7,6},{8,9},{9,8},{10,11... | collective-permute-start | bytes 663560 | tf_op jit(solution)/shard_map/ppermute | solution.py:734
  17.4 11.4 %collective-permute-start.5 = (bf16[1,3,96,384]{3,2,1,0:T(8,128)(2,1)S(1)}, bf16[1,3,96,384]{3,2,1,0:T(8,128)(2,1)S(1)}, u32[]{:S(2)}, u32[]{:S(2)}) collective-permute-start(bf16[1,3,96,384]{3,2,1,0:T(8,128)(2,1)S(1)} %get-tuple-element.151), channel_id=1, source_target_pairs={{0,4},{2,6},{4,0},{6,2},{8,12},{10,14},{12,8},{14,10},{16,20},{18,... | collective-permute-start | bytes 663560 | tf_op jit(solution)/shard_map/ppermute | solution.py:734
  29.7 41.5 %collective-permute-start.13 = (bf16[1,2,2,6,96,384]{5,4,3,2,1,0:T(8,128)(2,1)S(1)}, bf16[1,2,2,6,96,384]{5,4,3,2,1,0:T(8,128)(2,1)S(1)}, u32[]{:S(2)}, u32[]{:S(2)}) collective-permute-start(bf16[1,2,2,6,96,384]{5,4,3,2,1,0:T(8,128)(2,1)S(1)} %get-tuple-element.169), channel_id=1, source_target_pairs={{0,2},{2,0},{4,6},{6,4},{8,10},{10,8},{12,14},{14,12},{16,18},{18,... | collective-permute-start | bytes 5308424 | tf_op jit(solution)/shard_map/ppermute | solution.py:938
  29.9 22.5 %collective-permute-start.7 = (bf16[2,6,96,384]{3,2,1,0:T(8,128)(2,1)S(1)}, bf16[2,6,96,384]{3,2,1,0:T(8,128)(2,1)S(1)}, u32[]{:S(2)}, u32[]{:S(2)}) collective-permute-start(bf16[2,6,96,384]{3,2,1,0:T(8,128)(2,1)S(1)} %take_both.1.own), channel_id=1, source_target_pairs={{0,1},{1,0},{2,3},{3,2},{4,5},{5,4},{6,7},{7,6},{8,9},{9,8},{10,11... | collective-permute-start | bytes 2654216 | tf_op jit(solution)/shard_map/ppermute | solution.py:730
  30.5 22.5 %collective-permute-start.6 = (bf16[2,6,96,384]{3,2,1,0:T(8,128)(2,1)S(1)}, bf16[2,6,96,384]{3,2,1,0:T(8,128)(2,1)S(1)}, u32[]{:S(2)}, u32[]{:S(2)}) collective-permute-start(bf16[2,6,96,384]{3,2,1,0:T(8,128)(2,1)S(1)} %take_both.1.own), channel_id=1, source_target_pairs={{0,4},{2,6},{4,0},{6,2},{8,12},{10,14},{12,8},{14,10},{16,20},{18,... | collective-permute-start | bytes 2654216 | tf_op jit(solution)/shard_map/ppermute | solution.py:730
  30.9 12.0 %collective-permute-start.10 = (bf16[1,6,96,384]{3,2,1,0:T(8,128)(2,1)S(1)}, bf16[1,6,96,384]{3,2,1,0:T(8,128)(2,1)S(1)}, u32[]{:S(2)}, u32[]{:S(2)}) collective-permute-start(bf16[1,6,96,384]{3,2,1,0:T(8,128)(2,1)S(1)} %collective-permute-done.1.two), channel_id=1, source_target_pairs={{0,8},{2,10},{4,12},{6,14},{8,0},{10,2},{12,4},{14,6},{16,24},{18,... | collective-permute-start | bytes 1327112 | tf_op jit(solution)/shard_map/ppermute | solution.py:748
  42.9 18.9 %collective-permute-start.12 = (bf16[1,6,96,384]{3,2,1,0:T(8,128)(2,1)S(1)}, bf16[1,6,96,384]{3,2,1,0:T(8,128)(2,1)S(1)}, u32[]{:S(2)}, u32[]{:S(2)}) collective-permute-start(bf16[1,6,96,384]{3,2,1,0:T(8,128)(2,1)S(1)} %collective-permute-done.10.own), channel_id=1, source_target_pairs={{0,1},{1,0},{2,3},{3,2},{4,5},{5,4},{6,7},{7,6},{8,9},{9,8},{10,11... | collective-permute-start | bytes 1327112 | tf_op jit(solution)/shard_map/ppermute | solution.py:730
  44.5 17.9 %collective-permute-start.11 = (bf16[1,6,96,384]{3,2,1,0:T(8,128)(2,1)S(1)}, bf16[1,6,96,384]{3,2,1,0:T(8,128)(2,1)S(1)}, u32[]{:S(2)}, u32[]{:S(2)}) collective-permute-start(bf16[1,6,96,384]{3,2,1,0:T(8,128)(2,1)S(1)} %collective-permute-done.10.own), channel_id=1, source_target_pairs={{0,4},{2,6},{4,0},{6,2},{8,12},{10,14},{12,8},{14,10},{16,20},{18,... | collective-permute-start | bytes 1327112 | tf_op jit(solution)/shard_map/ppermute | solution.py:730
  53.0 17.9 %collective-permute-start.8 = (bf16[2,3,96,384]{3,2,1,0:T(8,128)(2,1)S(1)}, bf16[2,3,96,384]{3,2,1,0:T(8,128)(2,1)S(1)}, u32[]{:S(2)}, u32[]{:S(2)}) collective-permute-start(bf16[2,3,96,384]{3,2,1,0:T(8,128)(2,1)S(1)} %get-tuple-element.162), channel_id=1, source_target_pairs={{0,1},{1,0},{2,3},{3,2},{4,5},{5,4},{6,7},{7,6},{8,9},{9,8},{10,11... | collective-permute-start | bytes 1327112 | tf_op jit(solution)/shard_map/ppermute | solution.py:734
  54.6 16.6 %collective-permute-start.9 = (bf16[2,3,96,384]{3,2,1,0:T(8,128)(2,1)S(1)}, bf16[2,3,96,384]{3,2,1,0:T(8,128)(2,1)S(1)}, u32[]{:S(2)}, u32[]{:S(2)}) collective-permute-start(bf16[2,3,96,384]{3,2,1,0:T(8,128)(2,1)S(1)} %get-tuple-element.163), channel_id=1, source_target_pairs={{0,4},{2,6},{4,0},{6,2},{8,12},{10,14},{12,8},{14,10},{16,20},{18,... | collective-permute-start | bytes 1327112 | tf_op jit(solution)/shard_map/ppermute | solution.py:734
  72.3 10.1 %collective-permute-start.16 = (bf16[2,2,2,6,96,384]{5,4,3,2,1,0:T(8,128)(2,1)S(1)}, bf16[2,2,2,6,96,384]{5,4,3,2,1,0:T(8,128)(2,1)S(1)}, u32[]{:S(2)}, u32[]{:S(2)}) collective-permute-start(bf16[2,2,2,6,96,384]{5,4,3,2,1,0:T(8,128)(2,1)S(1)} %get-tuple-element.178), channel_id=1, source_target_pairs={{0,2},{2,0},{4,6},{6,4},{8,10},{10,8},{12,14},{14,12},{16,18},{18,... | collective-permute-start | bytes 10616840 | tf_op jit(solution)/shard_map/ppermute | solution.py:938
  73.2 9.3 %collective-permute-start.17 = (bf16[3,6,96,384]{3,2,1,0:T(8,128)(2,1)S(1)}, bf16[3,6,96,384]{3,2,1,0:T(8,128)(2,1)S(1)}, u32[]{:S(2)}, u32[]{:S(2)}) collective-permute-start(bf16[3,6,96,384]{3,2,1,0:T(8,128)(2,1)S(1)} %get-tuple-element.180), channel_id=1, source_target_pairs={{0,2},{2,0},{4,6},{6,4},{8,10},{10,8},{12,14},{14,12},{16,18},{18,... | collective-permute-start | bytes 3981320 | tf_op jit(solution)/shard_map/ppermute | solution.py:938
  73.8 7.4 %collective-permute-start.14 = (bf16[1,3,96,384]{3,2,1,0:T(8,128)(2,1)S(1)}, bf16[1,3,96,384]{3,2,1,0:T(8,128)(2,1)S(1)}, u32[]{:S(2)}, u32[]{:S(2)}) collective-permute-start(bf16[1,3,96,384]{3,2,1,0:T(8,128)(2,1)S(1)} %get-tuple-element.173), channel_id=1, source_target_pairs={{0,1},{1,0},{2,3},{3,2},{4,5},{5,4},{6,7},{7,6},{8,9},{9,8},{10,11... | collective-permute-start | bytes 663560 | tf_op jit(solution)/shard_map/ppermute | solution.py:734
  75.4 7.1 %collective-permute-start.15 = (bf16[1,3,96,384]{3,2,1,0:T(8,128)(2,1)S(1)}, bf16[1,3,96,384]{3,2,1,0:T(8,128)(2,1)S(1)}, u32[]{:S(2)}, u32[]{:S(2)}) collective-permute-start(bf16[1,3,96,384]{3,2,1,0:T(8,128)(2,1)S(1)} %get-tuple-element.174), channel_id=1, source_target_pairs={{0,4},{2,6},{4,0},{6,2},{8,12},{10,14},{12,8},{14,10},{16,20},{18,... | collective-permute-start | bytes 663560 | tf_op jit(solution)/shard_map/ppermute | solution.py:734
  82.5 1.5 collective-permute-start.18
  82.5 1.8 collective-permute-start.19
  83.8 1.2 copy-start.10
  94.3 25.3 %copy-start.8 = (bf16[48,768]{1,0:T(8,128)(2,1)S(1)}, bf16[48,768]{1,0:T(8,128)(2,1)}, u32[]{:S(2)}) copy-start(bf16[48,768]{1,0:T(8,128)(2,1)} %cot.3) | copy-start | bytes 221188
  119.3 6.3 %collective-permute-start.20 = (bf16[2,2,2,6,96,384]{5,4,3,2,1,0:T(8,128)(2,1)S(1)}, bf16[2,2,2,6,96,384]{5,4,3,2,1,0:T(8,128)(2,1)S(1)}, u32[]{:S(2)}, u32[]{:S(2)}) collective-permute-start(bf16[2,2,2,6,96,384]{5,4,3,2,1,0:T(8,128)(2,1)S(1)} %get-tuple-element.194), channel_id=1, source_target_pairs={{0,2},{2,0},{4,6},{6,4},{8,10},{10,8},{12,14},{14,12},{16,18},{18,... | collective-permute-start | bytes 10616840 | tf_op jit(solution)/shard_map/ppermute | solution.py:938
  126.9 21.8 %collective-permute-start.21 = (bf16[2,2,3,96,384]{4,3,2,1,0:T(8,128)(2,1)S(1)}, bf16[2,2,3,96,384]{4,3,2,1,0:T(8,128)(2,1)S(1)}, u32[]{:S(2)}, u32[]{:S(2)}) collective-permute-start(bf16[2,2,3,96,384]{4,3,2,1,0:T(8,128)(2,1)S(1)} %get-tuple-element.211), channel_id=1, source_target_pairs={{0,1},{1,0},{2,3},{3,2},{4,5},{5,4},{6,7},{7,6},{8,9},{9,8},{10,11... | collective-permute-start | bytes 2654216 | tf_op jit(solution)/shard_map/ppermute | solution.py:942
  127.5 21.5 %collective-permute-start.22 = (bf16[2,2,3,96,384]{4,3,2,1,0:T(8,128)(2,1)S(1)}, bf16[2,2,3,96,384]{4,3,2,1,0:T(8,128)(2,1)S(1)}, u32[]{:S(2)}, u32[]{:S(2)}) collective-permute-start(bf16[2,2,3,96,384]{4,3,2,1,0:T(8,128)(2,1)S(1)} %get-tuple-element.212), channel_id=1, source_target_pairs={{0,4},{2,6},{4,0},{6,2},{8,12},{10,14},{12,8},{14,10},{16,20},{18,... | collective-permute-start | bytes 2654216 | tf_op jit(solution)/shard_map/ppermute | solution.py:942
  149.0 6.2 %collective-permute-start.26 = (bf16[2,2,2,6,96,384]{5,4,3,2,1,0:T(8,128)(2,1)S(1)}, bf16[2,2,2,6,96,384]{5,4,3,2,1,0:T(8,128)(2,1)S(1)}, u32[]{:S(2)}, u32[]{:S(2)}) collective-permute-start(bf16[2,2,2,6,96,384]{5,4,3,2,1,0:T(8,128)(2,1)S(1)} %get-tuple-element.231), channel_id=1, source_target_pairs={{0,2},{2,0},{4,6},{6,4},{8,10},{10,8},{12,14},{14,12},{16,18},{18,... | collective-permute-start | bytes 10616840 | tf_op jit(solution)/shard_map/ppermute | solution.py:938
  149.8 13.0 %collective-permute-start.23 = (bf16[2,3,96,384]{3,2,1,0:T(8,128)(2,1)S(1)}, bf16[2,3,96,384]{3,2,1,0:T(8,128)(2,1)S(1)}, u32[]{:S(2)}, u32[]{:S(2)}) collective-permute-start(bf16[2,3,96,384]{3,2,1,0:T(8,128)(2,1)S(1)} %get-tuple-element.227), channel_id=1, source_target_pairs={{0,4},{2,6},{4,0},{6,2},{8,12},{10,14},{12,8},{14,10},{16,20},{18,... | collective-permute-start | bytes 1327112 | tf_op jit(solution)/shard_map/ppermute | solution.py:946
  150.3 13.0 %collective-permute-start.24 = (bf16[2,3,96,384]{3,2,1,0:T(8,128)(2,1)S(1)}, bf16[2,3,96,384]{3,2,1,0:T(8,128)(2,1)S(1)}, u32[]{:S(2)}, u32[]{:S(2)}) collective-permute-start(bf16[2,3,96,384]{3,2,1,0:T(8,128)(2,1)S(1)} %get-tuple-element.228), channel_id=1, source_target_pairs={{0,1},{1,0},{2,3},{3,2},{4,5},{5,4},{6,7},{7,6},{8,9},{9,8},{10,11... | collective-permute-start | bytes 1327112 | tf_op jit(solution)/shard_map/ppermute | solution.py:946
  156.3 25.5 %collective-permute-start.27 = (bf16[2,2,3,96,384]{4,3,2,1,0:T(8,128)(2,1)S(1)}, bf16[2,2,3,96,384]{4,3,2,1,0:T(8,128)(2,1)S(1)}, u32[]{:S(2)}, u32[]{:S(2)}) collective-permute-start(bf16[2,2,3,96,384]{4,3,2,1,0:T(8,128)(2,1)S(1)} %get-tuple-element.232), channel_id=1, source_target_pairs={{0,1},{1,0},{2,3},{3,2},{4,5},{5,4},{6,7},{7,6},{8,9},{9,8},{10,11... | collective-permute-start | bytes 2654216 | tf_op jit(solution)/shard_map/ppermute | solution.py:942
  157.8 23.9 %collective-permute-start.28 = (bf16[2,2,3,96,384]{4,3,2,1,0:T(8,128)(2,1)S(1)}, bf16[2,2,3,96,384]{4,3,2,1,0:T(8,128)(2,1)S(1)}, u32[]{:S(2)}, u32[]{:S(2)}) collective-permute-start(bf16[2,2,3,96,384]{4,3,2,1,0:T(8,128)(2,1)S(1)} %get-tuple-element.233), channel_id=1, source_target_pairs={{0,4},{2,6},{4,0},{6,2},{8,12},{10,14},{12,8},{14,10},{16,20},{18,... | collective-permute-start | bytes 2654216 | tf_op jit(solution)/shard_map/ppermute | solution.py:942
  164.0 17.7 %collective-permute-start.25 = (bf16[6,96,384]{2,1,0:T(8,128)(2,1)S(1)}, bf16[6,96,384]{2,1,0:T(8,128)(2,1)S(1)}, u32[]{:S(2)}, u32[]{:S(2)}) collective-permute-start(bf16[6,96,384]{2,1,0:T(8,128)(2,1)S(1)} %get-tuple-element.229), channel_id=1, source_target_pairs={{0,8},{2,10},{4,12},{6,14},{8,0},{10,2},{12,4},{14,6},{16,24},{18,... | collective-permute-start | bytes 1327112 | tf_op jit(solution)/shard_map/ppermute | solution.py:1096
  165.5 16.2 %collective-permute-start.29 = (f32[2,1,768]{2,1,0:T(1,128)S(1)}, f32[2,1,768]{2,1,0:T(1,128)S(1)}, u32[]{:S(2)}, u32[]{:S(2)}) collective-permute-start(f32[2,1,768]{2,1,0:T(1,128)S(1)} %get-tuple-element.234.left), channel_id=1, source_target_pairs={{0,1},{1,0},{2,3},{3,2},{4,5},{5,4},{6,7},{7,6},{8,9},{9,8},{10,11... | collective-permute-start | bytes 18440 | tf_op jit(solution)/shard_map/ppermute | solution.py:1093
  181.7 46.1 %copy-start.5 = (f32[24,96,96]{2,1,0:T(8,128)S(1)}, f32[24,96,96]{2,1,0:T(8,128)}, u32[]{:S(2)}) copy-start(f32[24,96,96]{2,1,0:T(8,128)} %root_left.1) | copy-start | bytes 2654212
  181.7 46.1 %copy-start.6 = (f32[24,96,96]{2,1,0:T(8,128)S(1)}, f32[24,96,96]{2,1,0:T(8,128)}, u32[]{:S(2)}) copy-start(f32[24,96,96]{2,1,0:T(8,128)} %root_right.1) | copy-start | bytes 2654212
  182.5 44.7 %copy-start.11 = (f32[2,768]{1,0:T(2,128)S(1)}, f32[2,768]{1,0:T(2,128)}, u32[]{:S(2)}) copy-start(f32[2,768]{1,0:T(2,128)} %moments.1) | copy-start | bytes 18436
  182.6 45.3 %copy-start.2 = (f32[24,96,96]{2,1,0:T(8,128)S(1)}, f32[24,96,96]{2,1,0:T(8,128)}, u32[]{:S(2)}) copy-start(f32[24,96,96]{2,1,0:T(8,128)} %master.1) | copy-start | bytes 2654212
  182.6 45.3 %copy-start.3 = (f32[24,96,96]{2,1,0:T(8,128)S(1)}, f32[24,96,96]{2,1,0:T(8,128)}, u32[]{:S(2)}) copy-start(f32[24,96,96]{2,1,0:T(8,128)} %stat_left.1) | copy-start | bytes 2654212
  182.6 45.3 %copy-start.4 = (f32[24,96,96]{2,1,0:T(8,128)S(1)}, f32[24,96,96]{2,1,0:T(8,128)}, u32[]{:S(2)}) copy-start(f32[24,96,96]{2,1,0:T(8,128)} %stat_right.1) | copy-start | bytes 2654212
  182.6 11.5 %collective-permute-start.30 = (bf16[2,3,96,384]{3,2,1,0:T(8,128)(2,1)S(1)}, bf16[2,3,96,384]{3,2,1,0:T(8,128)(2,1)S(1)}, u32[]{:S(2)}, u32[]{:S(2)}) collective-permute-start(bf16[2,3,96,384]{3,2,1,0:T(8,128)(2,1)S(1)} %get-tuple-element.248), channel_id=1, source_target_pairs={{0,4},{2,6},{4,0},{6,2},{8,12},{10,14},{12,8},{14,10},{16,20},{18,... | collective-permute-start | bytes 1327112 | tf_op jit(solution)/shard_map/ppermute | solution.py:946
  184.2 11.2 %collective-permute-start.31 = (bf16[2,3,96,384]{3,2,1,0:T(8,128)(2,1)S(1)}, bf16[2,3,96,384]{3,2,1,0:T(8,128)(2,1)S(1)}, u32[]{:S(2)}, u32[]{:S(2)}) collective-permute-start(bf16[2,3,96,384]{3,2,1,0:T(8,128)(2,1)S(1)} %get-tuple-element.249), channel_id=1, source_target_pairs={{0,1},{1,0},{2,3},{3,2},{4,5},{5,4},{6,7},{7,6},{8,9},{9,8},{10,11... | collective-permute-start | bytes 1327112 | tf_op jit(solution)/shard_map/ppermute | solution.py:946
  185.7 1.2 collective-permute-start.32
  196.1 10.3 %collective-permute-start.33 = (bf16[6,96,384]{2,1,0:T(8,128)(2,1)S(1)}, bf16[6,96,384]{2,1,0:T(8,128)(2,1)S(1)}, u32[]{:S(2)}, u32[]{:S(2)}) collective-permute-start(bf16[6,96,384]{2,1,0:T(8,128)(2,1)S(1)} %get-tuple-element.254), channel_id=1, source_target_pairs={{0,8},{2,10},{4,12},{6,14},{8,0},{10,2},{12,4},{14,6},{16,24},{18,... | collective-permute-start | bytes 1327112 | tf_op jit(solution)/shard_map/ppermute | solution.py:1106
  197.6 3.6 %collective-permute-start.34 = (f32[2,1,768]{2,1,0:T(1,128)S(1)}, f32[2,1,768]{2,1,0:T(1,128)S(1)}, u32[]{:S(2)}, u32[]{:S(2)}) collective-permute-start(f32[2,1,768]{2,1,0:T(1,128)S(1)} %sum_of.5.left), channel_id=1, source_target_pairs={{0,4},{2,6},{4,0},{6,2},{8,12},{10,14},{12,8},{14,10},{16,20},{18,... | collective-permute-start | bytes 18440 | tf_op jit(solution)/shard_map/ppermute | solution.py:1108
  207.1 20.7 %collective-permute-start.35 = (bf16[6,96,384]{2,1,0:T(8,128)(2,1)S(1)}, bf16[6,96,384]{2,1,0:T(8,128)(2,1)S(1)}, u32[]{:S(2)}, u32[]{:S(2)}) collective-permute-start(bf16[6,96,384]{2,1,0:T(8,128)(2,1)S(1)} %get-tuple-element.257), channel_id=1, source_target_pairs={{0,16},{2,18},{4,20},{6,22},{8,24},{10,26},{12,28},{14,30},{16,0},... | collective-permute-start | bytes 1327112 | tf_op jit(solution)/shard_map/ppermute | solution.py:1112
  209.2 7.4 %collective-permute-start.36 = (f32[2,1,768]{2,1,0:T(1,128)S(1)}, f32[2,1,768]{2,1,0:T(1,128)S(1)}, u32[]{:S(2)}, u32[]{:S(2)}) collective-permute-start(f32[2,1,768]{2,1,0:T(1,128)S(1)} %sum_of.6.left), channel_id=1, source_target_pairs={{0,8},{2,10},{4,12},{6,14},{8,0},{10,2},{12,4},{14,6},{16,24},{18,... | collective-permute-start | bytes 18440 | tf_op jit(solution)/shard_map/ppermute | solution.py:1114
  216.6 10.6 %collective-permute-start.37 = (f32[2,1,768]{2,1,0:T(1,128)S(1)}, f32[2,1,768]{2,1,0:T(1,128)S(1)}, u32[]{:S(2)}, u32[]{:S(2)}) collective-permute-start(f32[2,1,768]{2,1,0:T(1,128)S(1)} %sum_of.7.grads), channel_id=1, source_target_pairs={{0,16},{2,18},{4,20},{6,22},{8,24},{10,26},{12,28},{14,30},{16,0},... | collective-permute-start | bytes 18440 | tf_op jit(solution)/shard_map/ppermute | solution.py:1116
